TPU v7x, 128 devices: a whole 4x4x4 slice. The times are simulated.
128 devices in a mesh: ctx: 16 (over x, y), tensor: 8 (over z, core).
Axes of the slice: x: 4, y: 4, z: 4, core: 2. Of those that a mesh axis runs over, the one named last changes fastest.
Arguments:
- queries: bfloat16 [16384, 4096], P('ctx', 'tensor'), may hold values from -6 to 6
- keys: bfloat16 [16384, 4096], P('ctx', 'tensor'), may hold values from -6 to 6
- values: bfloat16 [16384, 4096], P('ctx', 'tensor'), may hold values from -6 to 6
- doc_ids: int32 [16384], P('ctx'), may hold values from 0 to 7, never falling along the last dimension, each value on 1 to 8192 neighbouring positions
- out_weight: bfloat16 [4096, 6144], P('tensor'), may hold values from -0.125 to 0.125
- grad_out: bfloat16 [16384, 6144], P('ctx', 'tensor'), may hold values from -6 to 6
Outputs:
- attended: bfloat16 [16384, 6144], P('ctx', 'tensor')
- grad_queries: bfloat16 [16384, 4096], P('ctx', 'tensor')
- grad_keys: bfloat16 [16384, 4096], P('ctx', 'tensor')
- grad_values: bfloat16 [16384, 4096], P('ctx', 'tensor')
- grad_weight: float32 [4096, 6144], P('tensor', 'ctx')
Inputs may be any that keep to these rules, and one draw needn't show every extreme that they name: `doc_ids`: never falling along the sequence; each document has 1 to 8192 positions, and one has exactly 8192.
All inputs are finite; a program needn't handle non-finite values.
Results may differ from a plain program's by a relative error of at most 0.015.
Values may be sent and summed in bfloat16 or wider, within the bound.
No kernel may reach another device: no remote copies, remote signals or barrier semaphores. Data moves between devices by JAX's collectives and lax.ppermute only.
A program may use at most 192 MiB of HBM per device.

v0:
```python
import jax
import jax.numpy as jnp
from jax import lax
from jax.experimental import pallas as pl
from jax.experimental.pallas import tpu as pltpu
from jax.sharding import Mesh
from jax.sharding import PartitionSpec as P

HEAD = 128
CHUNK = 256
CTX = ("cx", "cy")
TENSOR = ("z", "core")
EPSILON = 1e-06
F32 = jnp.float32
BF16 = jnp.bfloat16
NT = (((1,), (1,)), ((), ()))
TN = (((0,), (0,)), ((), ()))
NN = (((1,), (0,)), ((), ()))


def dot(a, b, dims):
    return lax.dot_general(a, b, dims, preferred_element_type=F32)


def whole(shape):
    return pl.BlockSpec(shape, lambda *_: (0,) * len(shape))


def rows_of(width, count=None):
    if count is None:
        return pl.BlockSpec((CHUNK, width), lambda i: (i, 0))
    return pl.BlockSpec((CHUNK, width), lambda i: (count - 1 - i, 0))


def head_cols(h):
    return slice(h * HEAD, (h + 1) * HEAD)


def params():
    return pltpu.CompilerParams(vmem_limit_bytes=56 << 20, dimension_semantics=("arbitrary",))


def state_of(ref):
    return ref[:-16, :].astype(F32), ref[-16:-15, :].astype(F32)


def entering_state(beside, rows, doc, place):
    total = None
    for s, ref in enumerate(beside):
        state, found = state_of(ref)
        part = jnp.where((found == doc) & (place > s + 0.5), state, 0.0)
        total = part if total is None else total + part
    for ref in rows:
        state, found = state_of(ref)
        total = total + jnp.where(found == doc, state, 0.0)
    return total


def row_kernel(latest, *refs):
    states = [state_of(ref) for ref in refs[:-1]]
    out = refs[-1]
    doc = states[0][1]
    for _, found in states[1:]:
        doc = jnp.maximum(doc, found) if latest else jnp.minimum(doc, found)
    total = None
    for state, found in states:
        part = jnp.where(found == doc, state, 0.0)
        total = part if total is None else total + part
    out[:-16, :] = total.astype(BF16)
    out[-16:, :] = jnp.broadcast_to(doc, (16, HEAD)).astype(BF16)


def tail_kernel(k, v, dcol, table, out):
    heads = k.shape[1] // HEAD
    last = table[7:8, :]
    tail = dcol[...] == last
    for h in range(heads):
        c = head_cols(h)
        kept = jnp.where(tail, k[:, c].astype(F32), 0.0).astype(BF16)
        out[c, :] = dot(kept, v[:, c], TN).astype(BF16)
    out[heads * HEAD :, :] = jnp.broadcast_to(last, (16, HEAD)).astype(BF16)


def forward_kernel(q, k, v, dcol, drow, table, *refs):
    arrived, (opened, low, turned, states, carry) = refs[:-5], refs[-5:]
    i = pl.program_id(0)
    heads = q.shape[1] // HEAD
    first = table[pl.ds(i, 1), :]
    following = table[pl.ds(i + 1, 1), :]

    @pl.when(i == 0)
    def _():
        carry[...] = entering_state(arrived[:3], arrived[3:], first, table[8:9, :])

    docs = dcol[...]
    joined = docs == first
    tail = docs == following
    keep = following == first
    t = lax.broadcasted_iota(jnp.int32, (CHUNK, CHUNK), 0)
    u = lax.broadcasted_iota(jnp.int32, (CHUNK, CHUNK), 1)
    mask = (t >= u) & (docs[:, :1] == drow[...])
    for h in range(heads):
        c = head_cols(h)
        qh, kh, vh = q[:, c], k[:, c], v[:, c]
        state = carry[c, :]
        state_low = state.astype(BF16)
        states[0, c, :] = state_low
        scores = jnp.where(mask, dot(qh, kh, NT), 0.0).astype(BF16)
        out = dot(scores, vh, NN) + jnp.where(joined, dot(qh, state_low, NN), 0.0)
        opened[:, c] = out
        inverse = lax.rsqrt(jnp.mean(out * out, axis=-1, keepdims=True) + EPSILON)
        normed = (out * inverse).astype(BF16)
        low[:, c] = normed
        turned[c, :] = normed.T
        kept = jnp.where(tail, kh.astype(F32), 0.0).astype(BF16)
        carry[c, :] = jnp.where(keep, state, 0.0) + dot(kept, vh, TN)


def cotangent_kernel(grad, weight, opened, q, dcol, table, grad_opened, out, carry):
    i = pl.program_id(0)
    heads = q.shape[1] // HEAD
    width = grad.shape[2]
    gn = dot(grad[0], weight[:, :width], NT)
    for j in range(1, grad.shape[0]):
        gn = gn + dot(grad[j], weight[:, j * width : (j + 1) * width], NT)

    @pl.when(i == 0)
    def _():
        carry[...] = jnp.zeros_like(carry)

    first = table[0:1, :]
    starts = dcol[...] == first
    for h in range(heads):
        c = head_cols(h)
        opened_h = opened[:, c]
        gh = gn[:, c]
        inverse = lax.rsqrt(jnp.mean(opened_h * opened_h, axis=-1, keepdims=True) + EPSILON)
        normed = opened_h * inverse
        go = inverse * (gh - normed * jnp.mean(gh * normed, axis=-1, keepdims=True))
        grad_opened[:, c] = go
        kept = jnp.where(starts, q[:, c].astype(F32), 0.0).astype(BF16)
        carry[c, :] += dot(kept, go.astype(BF16), TN)

    @pl.when(i == pl.num_programs(0) - 1)
    def _():
        size = heads * HEAD
        out[:size, :] = carry[...].astype(BF16)
        out[size:, :] = jnp.broadcast_to(first, (16, HEAD)).astype(BF16)


def split(value):
    high = value.astype(BF16)
    return high, (value - high.astype(F32)).astype(BF16)


def query_kernel(go, k, v, dcol, drow, table, states, out):
    i = pl.program_id(0)
    heads = k.shape[1] // HEAD
    first = table[pl.ds(i, 1), :]
    docs = dcol[...]
    joined = docs == first
    t = lax.broadcasted_iota(jnp.int32, (CHUNK, CHUNK), 0)
    u = lax.broadcasted_iota(jnp.int32, (CHUNK, CHUNK), 1)
    mask = (t >= u) & (docs[:, :1] == drow[...])
    for h in range(heads):
        c = head_cols(h)
        high, rest = split(go[:, c])
        vh = v[:, c]
        both = jnp.concatenate([high, rest], axis=1)
        twice = jnp.concatenate([vh, vh], axis=1)
        scores = jnp.where(mask, dot(both, twice, NT), 0.0).astype(BF16)
        carried = jnp.where(joined, dot(high, states[0, c, :], NT), 0.0)
        out[:, c] = (dot(scores, k[:, c], NN) + carried).astype(BF16)


def key_value_kernel(go, q, k, v, dcol, drow, table, *refs):
    arrived, (grad_k, grad_v, carry) = refs[:-3], refs[-3:]
    step = pl.program_id(0)
    i = pl.num_programs(0) - 1 - step
    heads = k.shape[1] // HEAD
    last = table[pl.ds(4 + i, 1), :]
    previous = table[pl.ds(3 + i, 1), :]

    @pl.when(step == 0)
    def _():
        carry[...] = entering_state(arrived[:3], arrived[3:], last, table[9:10, :])

    docs = dcol[...]
    joined = docs == last
    ahead = docs == previous
    keep = previous == last
    u = lax.broadcasted_iota(jnp.int32, (CHUNK, CHUNK), 0)
    t = lax.broadcasted_iota(jnp.int32, (CHUNK, CHUNK), 1)
    mask = (t >= u) & (docs[:, :1] == drow[...])
    for h in range(heads):
        c = head_cols(h)
        high, rest = split(go[:, c])
        qh, kh, vh = q[:, c], k[:, c], v[:, c]
        state = carry[c, :]
        state_low = state.astype(BF16)
        both = jnp.concatenate([high, rest], axis=1)
        twice = jnp.concatenate([vh, vh], axis=1)
        scores = jnp.where(mask, dot(kh, qh, NT), 0.0).astype(BF16)
        grad_scores = jnp.where(mask, dot(twice, both, NT), 0.0).astype(BF16)
        grad_v[:, c] = (
            dot(scores, high, NN) + jnp.where(joined, dot(kh, state_low, NN), 0.0)
        ).astype(BF16)
        grad_k[:, c] = (
            dot(grad_scores, qh, NN) + jnp.where(joined, dot(vh, state_low, NT), 0.0)
        ).astype(BF16)
        kept = jnp.where(ahead, qh.astype(F32), 0.0).astype(BF16)
        carry[c, :] = jnp.where(keep, state, 0.0) + dot(kept, high, TN)


def weight_kernel(turned, grad, first, second):
    part = dot(turned[...], grad[0], NN).astype(BF16)
    rows, cols = part.shape[0] // 2, part.shape[1] // 2
    for h in range(2):
        c = slice(h * cols, (h + 1) * cols)
        first[h, 0] = part[:rows, c]
        second[0, h] = part[rows:, c]


def middle_sum_kernel(places, a, a1, a2, a3, b, b1, b2, b3, *outs):
    for own, others, base in ((a, (a1, a2, a3), 0), (b, (b1, b2, b3), 4)):
        total = own[0, 0].astype(F32)
        for other in others:
            total = total + other[0].astype(F32)
        for s in range(4):

            @pl.when(pl.program_id(0) == s)
            def _():
                outs[base + s][...] = total.astype(outs[base + s].dtype)


def last_sum_kernel(a, a1, a2, a3, b, b1, b2, b3, out):
    half = a.shape[0]
    for parts, rows in (((a, a1, a2, a3), slice(0, half)), ((b, b1, b2, b3), slice(half, 2 * half))):
        total = parts[0][...].astype(F32)
        for part in parts[1:]:
            total = total + part[...].astype(F32)
        out[rows, :] = total


def attended_kernel(places, low, own, right, left, far_a, far_b, out, columns, sems):
    i = pl.program_id(0)
    lines = 4
    half = lines // 2

    def copies():
        for y, pieces in enumerate(((own,), (right,), (far_a, far_b), (left,))):
            for x in range(lines):
                piece = pieces[0] if len(pieces) == 1 else pieces[x // half]
                at = x if len(pieces) == 1 else x % half
                for o in range(2):
                    group = places[2 * y + o]
                    row = pl.multiple_of(places[8 + x] * HEAD, HEAD)
                    to = columns.at[group, pl.ds(row, HEAD)]
                    yield pltpu.make_async_copy(piece.at[at, o], to, sems.at[8 * y + 2 * x + o])

    @pl.when(i == 0)
    def _():
        for copy in copies():
            copy.start()
        for copy in copies():
            copy.wait()

    total = None
    for j in range(low.shape[0]):
        part = dot(low[j], columns[j], NN)
        total = part if total is None else total + part
    out[...] = total.astype(BF16)


def turned_by(value, axis, step):
    size = lax.axis_size(axis)
    return lax.ppermute(value, axis, [(i, (i + step) % size) for i in range(size)])


def moved_by(value, axis, step):
    size = lax.axis_size(axis)
    pairs = [(i, i + step) for i in range(size) if 0 <= i + step < size]
    return lax.ppermute(value, axis, pairs)


def swapped(value):
    return lax.ppermute(value, "core", [(0, 1), (1, 0)])


def pick(value, index, axis=0):
    return lax.dynamic_index_in_dim(value, index, axis, keepdims=False)


def exchanged(state, step):
    beside = [turned_by(state, "cy", step * s) for s in range(1, 4)]
    row = pl.pallas_call(
        lambda *refs: row_kernel(step > 0, *refs),
        out_shape=jax.ShapeDtypeStruct(state.shape, state.dtype),
        name="row_state",
    )(state, *beside)
    return beside + [moved_by(row, "cx", step * s) for s in range(1, 3)]


def column_pieces(out_weight, share, cx, core):
    cy, z = lax.axis_index("cy"), lax.axis_index("z")
    at = (cx * HEAD, (z - cy) % 4 * 2 * share)
    sent = lax.dynamic_slice(out_weight, at, (HEAD, 2 * share))
    pairs = [(4 * y + (i + y) % 4, 4 * y + i) for y in range(4) for i in range(4)]
    held = lax.ppermute(sent, ("cy", "z"), pairs)
    mine = lax.dynamic_slice(held, (0, core * share), (HEAD, share))
    other = lax.dynamic_slice(held, (0, (1 - core) * share), (HEAD, share))
    both = jnp.stack([mine, swapped(other)])
    return jnp.stack([both] + [turned_by(both, "cx", s) for s in range(1, 4)])


def scattered_sum(first, second, cx, cy):
    half, part = first.shape[2:]
    to_y = [turned_by(pick(first, (cy + s) % 4), "cy", s) for s in range(1, 4)]
    to_x = [turned_by(pick(second, (cx + s) % 4), "cx", s) for s in range(1, 4)]

    def own(line, start):
        shape = (1, 1, half, part)
        return pl.BlockSpec(shape, lambda i, p: (p[line], (p[start] + i) % 4, 0, 0))

    def piece(start):
        return pl.BlockSpec((1, half, part), lambda i, p: ((p[start] + i) % 4, 0, 0))

    kinds = [F32, BF16, BF16, BF16] * 2
    sums = pl.pallas_call(
        middle_sum_kernel,
        grid_spec=pltpu.PrefetchScalarGridSpec(
            num_scalar_prefetch=1,
            grid=(4,),
            in_specs=[own(1, 0)] + [piece(0)] * 3 + [own(0, 1)] + [piece(1)] * 3,
            out_specs=[pl.BlockSpec((half, part), lambda i, p: (0, 0))] * 8,
        ),
        out_shape=[jax.ShapeDtypeStruct((half, part), kind) for kind in kinds],
        compiler_params=params(),
        name="middle_sum",
    )(jnp.stack([cx, cy]), first, *to_y, second, *to_x)
    to_x = [turned_by(sums[s], "cx", s) for s in range(1, 4)]
    to_y = [turned_by(sums[4 + s], "cy", s) for s in range(1, 4)]
    return pl.pallas_call(
        last_sum_kernel,
        out_shape=jax.ShapeDtypeStruct((2 * half, part), F32),
        name="last_sum",
    )(sums[0], *to_x, sums[4], *to_y)


def body(queries, keys, values, doc_ids, out_weight, grad_out):
    rows, width = queries.shape
    blocks = rows // CHUNK
    groups = lax.axis_size(TENSOR)
    share = grad_out.shape[1]
    size = width
    payload = jax.ShapeDtypeStruct((size + 16, HEAD), BF16)
    cx, cy = lax.axis_index("cx"), lax.axis_index("cy")
    z, core = lax.axis_index("z"), lax.axis_index("core")

    grad_whole = lax.all_gather(grad_out, TENSOR, axis=0)

    docs = doc_ids.astype(F32)
    dcol = jnp.broadcast_to(docs[:, None], (rows, HEAD))
    drow = docs[None, :]
    chunked = docs.reshape(blocks, CHUNK)
    place = cy.astype(F32)[None]
    table = jnp.concatenate([chunked[:, 0], chunked[:, -1], place, 3 - place, jnp.zeros((6,), F32)])
    table = jnp.broadcast_to(table[:, None], (16, HEAD))

    tail = pl.pallas_call(tail_kernel, out_shape=payload, name="tail")(keys, values, dcol, table)
    arrived = exchanged(tail, 1)

    own = column_pieces(out_weight, share, cx, core)
    arrived, own = lax.optimization_barrier((arrived, own))

    row_block = pl.BlockSpec((1, CHUNK), lambda i: (0, i))
    state_block = pl.BlockSpec((1, size, HEAD), lambda i: (i, 0, 0))
    opened, low, turned, states = pl.pallas_call(
        forward_kernel,
        grid=(blocks,),
        in_specs=[rows_of(width)] * 3
        + [rows_of(HEAD), row_block, whole(table.shape)]
        + [whole(payload.shape)] * len(arrived),
        out_specs=[
            rows_of(width),
            rows_of(width),
            pl.BlockSpec((width, CHUNK), lambda i: (0, i)),
            state_block,
        ],
        out_shape=[
            jax.ShapeDtypeStruct((rows, width), F32),
            jax.ShapeDtypeStruct((rows, width), BF16),
            jax.ShapeDtypeStruct((width, rows), BF16),
            jax.ShapeDtypeStruct((blocks, size, HEAD), BF16),
        ],
        scratch_shapes=[pltpu.VMEM((size, HEAD), F32)],
        compiler_params=params(),
        name="forward",
    )(queries, keys, values, dcol, drow, table, *arrived)

    low_whole = lax.all_gather(low, TENSOR, axis=0)

    right = turned_by(own, "cy", -1)
    left = turned_by(own, "cy", 1)
    turned, right, left = lax.optimization_barrier((turned, right, left))

    pair = (width // 2, share // 2)
    first, second = pl.pallas_call(
        weight_kernel,
        grid=(groups,),
        in_specs=[whole((width, rows)), pl.BlockSpec((1, rows, share), lambda j: (j, 0, 0))],
        out_specs=[
            pl.BlockSpec((2, 1, *pair), lambda j: (j % 2, j // 2, 0, 0)),
            pl.BlockSpec((1, 2, *pair), lambda j: (j // 2, j % 2, 0, 0)),
        ],
        out_shape=[jax.ShapeDtypeStruct((4, 4, *pair), BF16)] * 2,
        compiler_params=params(),
        name="weight_grad",
    )(turned, grad_whole)
    grad_weight = scattered_sum(first, second, cx, cy)

    grad_opened, head = pl.pallas_call(
        cotangent_kernel,
        grid=(blocks,),
        in_specs=[
            pl.BlockSpec((groups, CHUNK, share), lambda i: (0, i, 0)),
            whole(out_weight.shape),
            rows_of(width),
            rows_of(width),
            rows_of(HEAD),
            whole(table.shape),
        ],
        out_specs=[rows_of(width), whole(payload.shape)],
        out_shape=[jax.ShapeDtypeStruct((rows, width), F32), payload],
        scratch_shapes=[pltpu.VMEM((size, HEAD), F32)],
        compiler_params=params(),
        name="cotangent",
    )(grad_whole, out_weight, opened, queries, dcol, table)
    returned = exchanged(head, -1)

    far_a = turned_by(right[:2], "cy", -1)
    far_b = turned_by(left[2:], "cy", 1)

    grad_query = pl.pallas_call(
        query_kernel,
        grid=(blocks,),
        in_specs=[rows_of(width)] * 3
        + [rows_of(HEAD), row_block, whole(table.shape), state_block],
        out_specs=rows_of(width),
        out_shape=jax.ShapeDtypeStruct((rows, width), BF16),
        compiler_params=params(),
        name="grad_query",
    )(grad_opened, keys, values, dcol, drow, table, states)

    back_row = pl.BlockSpec((1, CHUNK), lambda i: (0, blocks - 1 - i))
    grad_key, grad_value = pl.pallas_call(
        key_value_kernel,
        grid=(blocks,),
        in_specs=[rows_of(width, blocks)] * 4
        + [rows_of(HEAD, blocks), back_row, whole(table.shape)]
        + [whole(payload.shape)] * len(returned),
        out_specs=[rows_of(width, blocks)] * 2,
        out_shape=[jax.ShapeDtypeStruct((rows, width), BF16)] * 2,
        scratch_shapes=[pltpu.VMEM((size, HEAD), F32)],
        compiler_params=params(),
        name="grad_key_value",
    )(grad_opened, queries, keys, values, dcol, drow, table, *returned)

    around = [2 * ((z + cy + s) % 4) + (core if o == 0 else 1 - core) for s in range(4) for o in range(2)]
    heads_at = [(cx - s) % 4 for s in range(4)]
    held = pl.BlockSpec(memory_space=pl.ANY)
    attended = pl.pallas_call(
        attended_kernel,
        grid_spec=pltpu.PrefetchScalarGridSpec(
            num_scalar_prefetch=1,
            grid=(blocks,),
            in_specs=[pl.BlockSpec((groups, CHUNK, width), lambda i, at: (0, i, 0))] + [held] * 5,
            out_specs=pl.BlockSpec((CHUNK, share), lambda i, at: (i, 0)),
            scratch_shapes=[
                pltpu.VMEM((groups, width, share), BF16),
                pltpu.SemaphoreType.DMA((32,)),
            ],
        ),
        out_shape=jax.ShapeDtypeStruct((rows, share), BF16),
        compiler_params=params(),
        name="attended",
    )(jnp.stack(around + heads_at), low_whole, own, right, left, far_a, far_b)
    return attended, grad_query, grad_key, grad_value, grad_weight


def solution(mesh):
    finer = Mesh(mesh.devices.reshape(4, 4, 4, 2), ("cx", "cy", "z", "core"))
    by_both = P(CTX, TENSOR)
    return jax.shard_map(
        body,
        mesh=finer,
        in_specs=(by_both, by_both, by_both, P(CTX), P(TENSOR, None), by_both),
        out_specs=(by_both, by_both, by_both, by_both, P(TENSOR, CTX)),
        check_vma=False,
    )
```

profile of v0, /device:TPU:2, one launch (start us, length us, event | category | flops | bytes accessed | tf_op | source)
XLA Modules:
  0.0 244.6 jit_solution(17432029340751823735)
XLA Ops:
  8.0 1.0 dynamic_slice.28
  9.0 0.7 collective-permute-start.5
  9.9 1.4 collective-permute-done.6
  11.9 2.5 %collective-permute-start.8 = (bf16[2,128,768]{2,1,0:T(8,128)(2,1)S(1)}, bf16[2,128,768]{2,1,0:T(8,128)(2,1)S(1)}, u32[]{:S(2)}, u32[]{:S(2)}) collective-permute-start(bf16[2,128,768]{2,1,0:T(8,128)(2,1)S(1)} %get-tuple-element.68), channel_id=1, source_target_pairs={{0,64},{32,96},{64,0},{96,32},{1,65},{33,97},{65,1},{97,33},{2,66}... | collective-permute-start | bytes 1179656 | tf_op jit(solution)/shard_map/ppermute | solution.py:277
  14.4 1.8 collective-permute-start.7
  16.5 1.0 broadcast_in_dim.8.dcol
  18.1 2.8 %tail.1.refs_0_ = bf16[528,128]{1,0:T(8,128)(2,1)} custom-call(bf16[1024,512]{1,0:T(8,128)(2,1)} %k.7, bf16[1024,512]{1,0:T(8,128)(2,1)} %v.7, f32[1024,128]{1,0:T(8,128)} %broadcast_in_dim.8.dcol, f32[16,128]{1,0:T(8,128)} %broadcast_in_dim.21.table), custom_call_target="tpu_custom_call" | custom-call | tf_op jit(solution)/shard_map/tail/pallas_call | solution.py:370
  21.0 15.3 %collective-permute-start = (bf16[528,128]{1,0:T(8,128)(2,1)}, bf16[528,128]{1,0:T(8,128)(2,1)S(1)}, u32[]{:S(2)}, u32[]{:S(2)}) collective-permute-start(bf16[528,128]{1,0:T(8,128)(2,1)} %tail.1.refs_0_), channel_id=1, source_target_pairs={{0,8},{8,16},{16,24},{24,0},{1,9},{9,17},{17,25},{25,1},{2,10},{10... | collective-permute-start | bytes 405512 | tf_op jit(solution)/shard_map/ppermute | solution.py:277
  36.3 3.8 %collective-permute-start.1 = (bf16[528,128]{1,0:T(8,128)(2,1)}, bf16[528,128]{1,0:T(8,128)(2,1)S(1)}, u32[]{:S(2)}, u32[]{:S(2)}) collective-permute-start(bf16[528,128]{1,0:T(8,128)(2,1)} %tail.1.refs_0_), channel_id=1, source_target_pairs={{0,16},{8,24},{16,0},{24,8},{1,17},{9,25},{17,1},{25,9},{2,18},{10... | collective-permute-start | bytes 405512 | tf_op jit(solution)/shard_map/ppermute | solution.py:277
  40.1 2.3 collective-permute-done.refs_1_.refs_0_
  42.4 2.6 %collective-permute-start.2 = (bf16[528,128]{1,0:T(8,128)(2,1)}, bf16[528,128]{1,0:T(8,128)(2,1)S(1)}, u32[]{:S(2)}, u32[]{:S(2)}) collective-permute-start(bf16[528,128]{1,0:T(8,128)(2,1)} %tail.1.refs_0_), channel_id=1, source_target_pairs={{0,24},{8,0},{16,8},{24,16},{1,25},{9,1},{17,9},{25,17},{2,26},{10... | collective-permute-start | bytes 405512 | tf_op jit(solution)/shard_map/ppermute | solution.py:277
  45.1 0.9 collective-permute-done.1.refs_2_.refs_1_
  46.0 2.0 collective-permute-done.2.refs_3_.refs_2_
  48.6 2.0 row_state.2
  50.6 2.2 collective-permute-start.3
  52.8 2.4 collective-permute-start.4
  55.4 3.6 %collective-permute-done.3.refs_3_ = bf16[528,128]{1,0:T(8,128)(2,1)S(1)} collective-permute-done((bf16[528,128]{1,0:T(8,128)(2,1)}, bf16[528,128]{1,0:T(8,128)(2,1)S(1)}, u32[]{:S(2)}, u32[]{:S(2)}) %collective-permute-start.3) | collective-permute-done | bytes 135200 | tf_op jit(solution)/shard_map/ppermute | solution.py:283
  59.8 6.8 %forward.1 = (f32[1024,512]{1,0:T(8,128)}, bf16[1024,512]{1,0:T(8,128)(2,1)}, bf16[512,1024]{1,0:T(8,128)(2,1)}, bf16[4,512,128]{2,1,0:T(8,128)(2,1)}) custom-call(bf16[1024,512]{1,0:T(8,128)(2,1)} %q.5, bf16[1024,512]{1,0:T(8,128)(2,1)} %k.7, bf16[1024,512]{1,0:T(8,128)(2,1)} %v.7, f32[1024,128]{1,0:T(8,128)} %broadcast_in_dim.8.dcol, f32[1,1024]{1,0:T(1,128)} %bitcast.45, ...), custom_call_target="tpu_custom_call" | custom-call | tf_op jit(solution)/shard_map/forward/pallas_call | solution.py:378
  66.6 2.9 %collective-permute-start.10 = (bf16[4,2,128,768]{3,2,1,0:T(8,128)(2,1)S(1)}, bf16[4,2,128,768]{3,2,1,0:T(8,128)(2,1)S(1)}, u32[]{:S(2)}, u32[]{:S(2)}) collective-permute-start(bf16[4,2,128,768]{3,2,1,0:T(8,128)(2,1)S(1)} %pad_maximum_fusion.own), channel_id=1, source_target_pairs={{0,24},{8,0},{16,8},{24,16},{1,25},{9,1},{17,9},{25,17},{2,26},{10... | collective-permute-start | bytes 4718600 | tf_op jit(solution)/shard_map/ppermute | solution.py:277
  69.5 29.2 %collective-permute-done.10.right = bf16[4,2,128,768]{3,2,1,0:T(8,128)(2,1)S(1)} collective-permute-done((bf16[4,2,128,768]{3,2,1,0:T(8,128)(2,1)S(1)}, bf16[4,2,128,768]{3,2,1,0:T(8,128)(2,1)S(1)}, u32[]{:S(2)}, u32[]{:S(2)}) %collective-permute-start.10) | collective-permute-done | bytes 1572896 | tf_op jit(solution)/shard_map/ppermute | solution.py:277
  98.7 3.5 %collective-permute-done.11.left = bf16[4,2,128,768]{3,2,1,0:T(8,128)(2,1)} collective-permute-done((bf16[4,2,128,768]{3,2,1,0:T(8,128)(2,1)S(1)}, bf16[4,2,128,768]{3,2,1,0:T(8,128)(2,1)}, u32[]{:S(2)}, u32[]{:S(2)}) %collective-permute-start.11) | collective-permute-done | bytes 1572896 | tf_op jit(solution)/shard_map/ppermute | solution.py:277
  102.2 13.2 %weight_grad.1 = (bf16[4,4,256,384]{3,2,1,0:T(8,128)(2,1)}, bf16[4,4,256,384]{3,2,1,0:T(8,128)(2,1)}) custom-call(bf16[512,1024]{1,0:T(8,128)(2,1)} %get-tuple-element.48.turned, bf16[8,1024,768]{2,1,0:T(8,128)(2,1)} %bitcast.38), custom_call_target="tpu_custom_call" | custom-call | tf_op jit(solution)/shard_map/weight_grad/pallas_call | solution.py:408
  115.4 3.2 %dynamic-slice_bitcast_fusion.3 = (bf16[4,256,384]{2,1,0:T(8,128)(2,1)}, bf16[4,256,384]{2,1,0:T(8,128)(2,1)}, bf16[4,256,384]{2,1,0:T(8,128)(2,1)}) fusion(bf16[4,4,256,384]{3,2,1,0:T(8,128)(2,1)} %get-tuple-element.49.a, s32[]{:T(128)S(6)} %select_n.120, s32[]{:T(128)S(6)} %select_n.118, s32[]{:T(128)S(6)} %select_n.116), kind=kLoop, calls=%fused_computation.4 | loop fusion | bytes 4718604 | tf_op jit(solution)/shard_map/jit(dynamic_index_in_dim)/squeeze | solution.py:291
  118.7 2.2 collective-permute-start.20
  120.8 1.1 collective-permute-start.21
  122.2 5.7 %collective-permute-start.22 = (bf16[4,256,384]{2,1,0:T(8,128)(2,1)S(1)}, bf16[4,256,384]{2,1,0:T(8,128)(2,1)S(1)}, u32[]{:S(2)}, u32[]{:S(2)}) collective-permute-start(bf16[4,256,384]{2,1,0:T(8,128)(2,1)S(1)} %get-tuple-element.63), channel_id=1, source_target_pairs={{0,32},{32,64},{64,96},{96,0},{1,33},{33,65},{65,97},{97,1},{2,34}... | collective-permute-start | bytes 2359304 | tf_op jit(solution)/shard_map/ppermute | solution.py:277
  128.1 22.4 %collective-permute-done.19.a1 = bf16[4,256,384]{2,1,0:T(8,128)(2,1)} collective-permute-done((bf16[4,256,384]{2,1,0:T(8,128)(2,1)}, bf16[4,256,384]{2,1,0:T(8,128)(2,1)}, u32[]{:S(2)}, u32[]{:S(2)}) %collective-permute-start.19) | collective-permute-done | bytes 786464 | tf_op jit(solution)/shard_map/ppermute | solution.py:277
  150.5 4.6 %collective-permute-start.24 = (bf16[4,256,384]{2,1,0:T(8,128)(2,1)S(1)}, bf16[4,256,384]{2,1,0:T(8,128)(2,1)S(1)}, u32[]{:S(2)}, u32[]{:S(2)}) collective-permute-start(bf16[4,256,384]{2,1,0:T(8,128)(2,1)S(1)} %get-tuple-element.61), channel_id=1, source_target_pairs={{0,96},{32,0},{64,32},{96,64},{1,97},{33,1},{65,33},{97,65},{2,98}... | collective-permute-start | bytes 2359304 | tf_op jit(solution)/shard_map/ppermute | solution.py:277
  155.3 1.2 slice.15
  156.5 2.3 collective-permute-start.13
  158.7 14.9 %cotangent.1 = (f32[1024,512]{1,0:T(8,128)}, bf16[528,128]{1,0:T(8,128)(2,1)}) custom-call(bf16[8,1024,768]{2,1,0:T(8,128)(2,1)} %bitcast.39, bf16[512,6144]{1,0:T(8,128)(2,1)} %weight.1, f32[1024,512]{1,0:T(8,128)} %get-tuple-element.42.opened, bf16[1024,512]{1,0:T(8,128)(2,1)} %q.5, f32[1024,128]{1,0:T(8,128)} %broadcast_in_dim.8.dcol, ...), custom_call_target="tpu_custom_call" | custom-call | tf_op jit(solution)/shard_map/cotangent/pallas_call | solution.py:422
  173.7 1.3 collective-permute-start.14
  175.0 0.9 collective-permute-start.15
  176.0 0.7 pad_add_fusion.places
  176.8 6.2 %middle_sum.1 = (f32[256,384]{1,0:T(8,128)}, bf16[256,384]{1,0:T(8,128)(2,1)}, bf16[256,384]{1,0:T(8,128)(2,1)}, bf16[256,384]{1,0:T(8,128)(2,1)}, f32[256,384]{...) custom-call(s32[2]{0:T(128)} %pad_add_fusion.places, ...), custom_call_target="tpu_custom_call" | custom-call | tf_op jit(solution)/shard_map/middle_sum/pallas_call | solution.py:329
  183.0 4.9 %collective-permute-start.25 = (bf16[256,384]{1,0:T(8,128)(2,1)}, bf16[256,384]{1,0:T(8,128)(2,1)}, u32[]{:S(2)}, u32[]{:S(2)}) collective-permute-start(bf16[256,384]{1,0:T(8,128)(2,1)} %get-tuple-element.52), channel_id=1, source_target_pairs={{0,32},{32,64},{64,96},{96,0},{1,33},{33,65},{65,97},{97,1},{2,34}... | collective-permute-start | bytes 589832 | tf_op jit(solution)/shard_map/ppermute | solution.py:277
  189.2 1.9 row_state.3
  191.1 1.9 collective-permute-start.17
  193.0 1.3 collective-permute-start.18
  194.3 4.2 %collective-permute-start.26 = (bf16[256,384]{1,0:T(8,128)(2,1)}, bf16[256,384]{1,0:T(8,128)(2,1)S(1)}, u32[]{:S(2)}, u32[]{:S(2)}) collective-permute-start(bf16[256,384]{1,0:T(8,128)(2,1)} %get-tuple-element.53), channel_id=1, source_target_pairs={{0,64},{32,96},{64,0},{96,32},{1,65},{33,97},{65,1},{97,33},{2,66}... | collective-permute-start | bytes 589832 | tf_op jit(solution)/shard_map/ppermute | solution.py:277
  198.5 3.5 %collective-permute-done.17.refs_3_ = bf16[528,128]{1,0:T(8,128)(2,1)S(1)} collective-permute-done((bf16[528,128]{1,0:T(8,128)(2,1)}, bf16[528,128]{1,0:T(8,128)(2,1)S(1)}, u32[]{:S(2)}, u32[]{:S(2)}) %collective-permute-start.17) | collective-permute-done | bytes 135200 | tf_op jit(solution)/shard_map/ppermute | solution.py:283
  202.1 1.0 collective-permute-done.18.refs_4_
  203.1 2.5 %collective-permute-start.29 = (bf16[256,384]{1,0:T(8,128)(2,1)}, bf16[256,384]{1,0:T(8,128)(2,1)S(1)}, u32[]{:S(2)}, u32[]{:S(2)}) collective-permute-start(bf16[256,384]{1,0:T(8,128)(2,1)} %get-tuple-element.57), channel_id=1, source_target_pairs={{0,16},{8,24},{16,0},{24,8},{1,17},{9,25},{17,1},{25,9},{2,18},{10... | collective-permute-start | bytes 589832 | tf_op jit(solution)/shard_map/ppermute | solution.py:277
  205.6 1.2 collective-permute-start.30
  207.4 13.4 %attended.1 = bf16[1024,768]{1,0:T(8,128)(2,1)} custom-call(s32[12]{0:T(128)} %stack.84.places, bf16[8,1024,512]{2,1,0:T(8,128)(2,1)} %bitcast.40, bf16[4,2,128,768]{3,2,1,0:T(8,128)(2,1)} %copy-done.1, bf16[4,2,128,768]{3,2,1,0:T(8,128)(2,1)} %copy-done.2, bf16[4,2,128,768]{3,2,1,0:T(8,128)(2,1)} %collective-permute-done.11.left, ...), custom_call_target="tpu_custom_call" | custom-call | tf_op jit(solution)/shard_map/attended/pallas_call | solution.py:472
  220.9 5.9 %grad_query.1 = bf16[1024,512]{1,0:T(8,128)(2,1)} custom-call(f32[1024,512]{1,0:T(8,128)} %get-tuple-element.43.go, bf16[1024,512]{1,0:T(8,128)(2,1)} %k.7, bf16[1024,512]{1,0:T(8,128)(2,1)} %v.7, f32[1024,128]{1,0:T(8,128)} %broadcast_in_dim.8.dcol, f32[1,1024]{1,0:T(1,128)} %bitcast.46, f32[16,128]{1,0:T(8,128)} %broadcast_in_dim.21.table, ...), custom_call_target="tpu_custom_call" | custom-call | tf_op jit(solution)/shard_map/grad_query/pallas_call | solution.py:444
  226.8 7.4 %grad_key_value.1 = (bf16[1024,512]{1,0:T(8,128)(2,1)}, bf16[1024,512]{1,0:T(8,128)(2,1)}) custom-call(f32[1024,512]{1,0:T(8,128)} %get-tuple-element.43.go, bf16[1024,512]{1,0:T(8,128)(2,1)} %q.5, bf16[1024,512]{1,0:T(8,128)(2,1)} %k.7, bf16[1024,512]{1,0:T(8,128)(2,1)} %v.7, f32[1024,128]{1,0:T(8,128)} %broadcast_in_dim.8.dcol, f32[1,1024]{1,0:T(1,128)} %bitcast.47, ...), custom_call_target="tpu_custom_call" | custom-call | tf_op jit(solution)/shard_map/grad_key_value/pallas_call | solution.py:456
  235.2 2.6 %last_sum.1 = f32[512,384]{1,0:T(8,128)} custom-call(f32[256,384]{1,0:T(8,128)} %get-tuple-element.51.a, bf16[256,384]{1,0:T(8,128)(2,1)} %collective-permute-done.25.a1, bf16[256,384]{1,0:T(8,128)(2,1)} %copy-done.15, bf16[256,384]{1,0:T(8,128)(2,1)} %copy-done.16, f32[256,384]{1,0:T(8,128)} %get-tuple-element.55.b, bf16[256,384]{1,0:T(8,128)(2,1)} %copy-done.17, ...), custom_call_target="tpu_custom_call" | custom-call | tf_op jit(solution)/shard_map/last_sum/pallas_call | solution.py:343
  (100 shorter events, 7.7 us)
Async XLA Ops:
  7.2 95.0 %all-gather.7.cloned.1.call-start = ((), (), s32[]{:S(2)}) async-start(), calls=%async_computation.1 | async-start | bytes 14155776 | tf_op jit(solution)/shard_map/all_gather | solution.py:360
  7.9 8.3 %copy-start.25 = (s32[1024]{0:T(1024)S(1)}, s32[1024]{0:T(1024)}, u32[]{:S(2)}) copy-start(s32[1024]{0:T(1024)} %param.9) | copy-start | bytes 12292
  7.9 199.5 %all-gather.5.cloned.1.call-start = ((), (), s32[]{:S(2)}) async-start(), calls=%async_computation | async-start | bytes 9437184 | tf_op jit(solution)/shard_map/all_gather | solution.py:401
  9.0 0.7 collective-permute-start.5
  9.8 1.5 collective-permute-start.6
  11.3 43.8 %collective-permute-start.9 = (bf16[2,128,768]{2,1,0:T(8,128)(2,1)S(1)}, bf16[2,128,768]{2,1,0:T(8,128)(2,1)S(1)}, u32[]{:S(2)}, u32[]{:S(2)}) collective-permute-start(bf16[2,128,768]{2,1,0:T(8,128)(2,1)S(1)} %get-tuple-element.68), channel_id=1, source_target_pairs={{0,96},{32,0},{64,32},{96,64},{1,97},{33,1},{65,33},{97,65},{2,98}... | collective-permute-start | bytes 1179656 | tf_op jit(solution)/shard_map/ppermute | solution.py:277
  11.9 43.3 %collective-permute-start.8 = (bf16[2,128,768]{2,1,0:T(8,128)(2,1)S(1)}, bf16[2,128,768]{2,1,0:T(8,128)(2,1)S(1)}, u32[]{:S(2)}, u32[]{:S(2)}) collective-permute-start(bf16[2,128,768]{2,1,0:T(8,128)(2,1)S(1)} %get-tuple-element.68), channel_id=1, source_target_pairs={{0,64},{32,96},{64,0},{96,32},{1,65},{33,97},{65,1},{97,33},{2,66}... | collective-permute-start | bytes 1179656 | tf_op jit(solution)/shard_map/ppermute | solution.py:277
  14.4 40.8 %collective-permute-start.7 = (bf16[2,128,768]{2,1,0:T(8,128)(2,1)S(1)}, bf16[2,128,768]{2,1,0:T(8,128)(2,1)S(1)}, u32[]{:S(2)}, u32[]{:S(2)}) collective-permute-start(bf16[2,128,768]{2,1,0:T(8,128)(2,1)S(1)} %get-tuple-element.68), channel_id=1, source_target_pairs={{0,32},{32,64},{64,96},{96,0},{1,33},{33,65},{65,97},{97,1},{2,34}... | collective-permute-start | bytes 1179656 | tf_op jit(solution)/shard_map/ppermute | solution.py:277
  16.2 4.8 %copy-start.20 = (f32[1024]{0:T(1024)}, f32[1024]{0:T(1024)S(1)}, u32[]{:S(2)}) copy-start(f32[1024]{0:T(1024)S(1)} %convert_element_type.6) | copy-start | bytes 12292
  21.0 21.5 %collective-permute-start = (bf16[528,128]{1,0:T(8,128)(2,1)}, bf16[528,128]{1,0:T(8,128)(2,1)S(1)}, u32[]{:S(2)}, u32[]{:S(2)}) collective-permute-start(bf16[528,128]{1,0:T(8,128)(2,1)} %tail.1.refs_0_), channel_id=1, source_target_pairs={{0,8},{8,16},{16,24},{24,0},{1,9},{9,17},{17,25},{25,1},{2,10},{10... | collective-permute-start | bytes 405512 | tf_op jit(solution)/shard_map/ppermute | solution.py:277
  36.3 9.7 %collective-permute-start.1 = (bf16[528,128]{1,0:T(8,128)(2,1)}, bf16[528,128]{1,0:T(8,128)(2,1)S(1)}, u32[]{:S(2)}, u32[]{:S(2)}) collective-permute-start(bf16[528,128]{1,0:T(8,128)(2,1)} %tail.1.refs_0_), channel_id=1, source_target_pairs={{0,16},{8,24},{16,0},{24,8},{1,17},{9,25},{17,1},{25,9},{2,18},{10... | collective-permute-start | bytes 405512 | tf_op jit(solution)/shard_map/ppermute | solution.py:277
  42.4 5.5 %copy-start.12 = (bf16[528,128]{1,0:T(8,128)(2,1)}, bf16[528,128]{1,0:T(8,128)(2,1)S(1)}, u32[]{:S(2)}) copy-start(bf16[528,128]{1,0:T(8,128)(2,1)S(1)} %collective-permute-done.refs_1_.refs_0_) | copy-start | bytes 405508
  42.4 5.5 %collective-permute-start.2 = (bf16[528,128]{1,0:T(8,128)(2,1)}, bf16[528,128]{1,0:T(8,128)(2,1)S(1)}, u32[]{:S(2)}, u32[]{:S(2)}) collective-permute-start(bf16[528,128]{1,0:T(8,128)(2,1)} %tail.1.refs_0_), channel_id=1, source_target_pairs={{0,24},{8,0},{16,8},{24,16},{1,25},{9,1},{17,9},{25,17},{2,26},{10... | collective-permute-start | bytes 405512 | tf_op jit(solution)/shard_map/ppermute | solution.py:277
  46.0 2.0 copy-start.13
  50.6 8.5 %collective-permute-start.3 = (bf16[528,128]{1,0:T(8,128)(2,1)}, bf16[528,128]{1,0:T(8,128)(2,1)S(1)}, u32[]{:S(2)}, u32[]{:S(2)}) collective-permute-start(bf16[528,128]{1,0:T(8,128)(2,1)} %row_state.2), channel_id=1, source_target_pairs={{0,32},{32,64},{64,96},{1,33},{33,65},{65,97},{2,34},{34,66},{66,9... | collective-permute-start | bytes 405512 | tf_op jit(solution)/shard_map/ppermute | solution.py:283
  52.8 6.3 %collective-permute-start.4 = (bf16[528,128]{1,0:T(8,128)(2,1)}, bf16[528,128]{1,0:T(8,128)(2,1)S(1)}, u32[]{:S(2)}, u32[]{:S(2)}) collective-permute-start(bf16[528,128]{1,0:T(8,128)(2,1)} %row_state.2), channel_id=1, source_target_pairs={{0,64},{32,96},{1,65},{33,97},{2,66},{34,98},{3,67},{35,99},{4,68}... | collective-permute-start | bytes 405512 | tf_op jit(solution)/shard_map/ppermute | solution.py:283
  55.4 14.1 %copy-start.1 = (bf16[4,2,128,768]{3,2,1,0:T(8,128)(2,1)}, bf16[4,2,128,768]{3,2,1,0:T(8,128)(2,1)S(1)}, u32[]{:S(2)}) copy-start(bf16[4,2,128,768]{3,2,1,0:T(8,128)(2,1)S(1)} %pad_maximum_fusion.own) | copy-start | bytes 4718596
  66.6 32.1 %collective-permute-start.10 = (bf16[4,2,128,768]{3,2,1,0:T(8,128)(2,1)S(1)}, bf16[4,2,128,768]{3,2,1,0:T(8,128)(2,1)S(1)}, u32[]{:S(2)}, u32[]{:S(2)}) collective-permute-start(bf16[4,2,128,768]{3,2,1,0:T(8,128)(2,1)S(1)} %pad_maximum_fusion.own), channel_id=1, source_target_pairs={{0,24},{8,0},{16,8},{24,16},{1,25},{9,1},{17,9},{25,17},{2,26},{10... | collective-permute-start | bytes 4718600 | tf_op jit(solution)/shard_map/ppermute | solution.py:277
  69.5 32.7 %collective-permute-start.11 = (bf16[4,2,128,768]{3,2,1,0:T(8,128)(2,1)S(1)}, bf16[4,2,128,768]{3,2,1,0:T(8,128)(2,1)}, u32[]{:S(2)}, u32[]{:S(2)}) collective-permute-start(bf16[4,2,128,768]{3,2,1,0:T(8,128)(2,1)S(1)} %pad_maximum_fusion.own), channel_id=1, source_target_pairs={{0,8},{8,16},{16,24},{24,0},{1,9},{9,17},{17,25},{25,1},{2,10},{10... | collective-permute-start | bytes 4718600 | tf_op jit(solution)/shard_map/ppermute | solution.py:277
  98.6 16.8 %copy-start.2 = (bf16[4,2,128,768]{3,2,1,0:T(8,128)(2,1)}, bf16[4,2,128,768]{3,2,1,0:T(8,128)(2,1)S(1)}, u32[]{:S(2)}) copy-start(bf16[4,2,128,768]{3,2,1,0:T(8,128)(2,1)S(1)} %collective-permute-done.10.right) | copy-start | bytes 4718596
  115.4 6.5 %copy-start = (bf16[4,4,256,384]{3,2,1,0:T(8,128)(2,1)S(1)}, bf16[4,4,256,384]{3,2,1,0:T(8,128)(2,1)}, u32[]{:S(2)}) copy-start(bf16[4,4,256,384]{3,2,1,0:T(8,128)(2,1)} %get-tuple-element.50.b) | copy-start | bytes 9437188
  118.7 31.9 %collective-permute-start.19 = (bf16[4,256,384]{2,1,0:T(8,128)(2,1)}, bf16[4,256,384]{2,1,0:T(8,128)(2,1)}, u32[]{:S(2)}, u32[]{:S(2)}) collective-permute-start(bf16[4,256,384]{2,1,0:T(8,128)(2,1)} %get-tuple-element.66), channel_id=1, source_target_pairs={{0,8},{8,16},{16,24},{24,0},{1,9},{9,17},{17,25},{25,1},{2,10},{10... | collective-permute-start | bytes 2359304 | tf_op jit(solution)/shard_map/ppermute | solution.py:277
  118.7 36.5 %collective-permute-start.20 = (bf16[4,256,384]{2,1,0:T(8,128)(2,1)}, bf16[4,256,384]{2,1,0:T(8,128)(2,1)}, u32[]{:S(2)}, u32[]{:S(2)}) collective-permute-start(bf16[4,256,384]{2,1,0:T(8,128)(2,1)} %get-tuple-element.65), channel_id=1, source_target_pairs={{0,16},{8,24},{16,0},{24,8},{1,17},{9,25},{17,1},{25,9},{2,18},{10... | collective-permute-start | bytes 2359304 | tf_op jit(solution)/shard_map/ppermute | solution.py:277
  120.8 35.7 %collective-permute-start.21 = (bf16[4,256,384]{2,1,0:T(8,128)(2,1)}, bf16[4,256,384]{2,1,0:T(8,128)(2,1)}, u32[]{:S(2)}, u32[]{:S(2)}) collective-permute-start(bf16[4,256,384]{2,1,0:T(8,128)(2,1)} %get-tuple-element.64), channel_id=1, source_target_pairs={{0,24},{8,0},{16,8},{24,16},{1,25},{9,1},{17,9},{25,17},{2,26},{10... | collective-permute-start | bytes 2359304 | tf_op jit(solution)/shard_map/ppermute | solution.py:277
  121.9 33.2 %copy-start.3 = (bf16[4,2,128,768]{3,2,1,0:T(8,128)(2,1)S(1)}, bf16[4,2,128,768]{3,2,1,0:T(8,128)(2,1)}, u32[]{:S(2)}) copy-start(bf16[4,2,128,768]{3,2,1,0:T(8,128)(2,1)} %copy-done.2) | copy-start | bytes 4718596
  122.2 51.5 %collective-permute-start.22 = (bf16[4,256,384]{2,1,0:T(8,128)(2,1)S(1)}, bf16[4,256,384]{2,1,0:T(8,128)(2,1)S(1)}, u32[]{:S(2)}, u32[]{:S(2)}) collective-permute-start(bf16[4,256,384]{2,1,0:T(8,128)(2,1)S(1)} %get-tuple-element.63), channel_id=1, source_target_pairs={{0,32},{32,64},{64,96},{96,0},{1,33},{33,65},{65,97},{97,1},{2,34}... | collective-permute-start | bytes 2359304 | tf_op jit(solution)/shard_map/ppermute | solution.py:277
  127.9 47.1 %collective-permute-start.23 = (bf16[4,256,384]{2,1,0:T(8,128)(2,1)S(1)}, bf16[4,256,384]{2,1,0:T(8,128)(2,1)S(1)}, u32[]{:S(2)}, u32[]{:S(2)}) collective-permute-start(bf16[4,256,384]{2,1,0:T(8,128)(2,1)S(1)} %get-tuple-element.62), channel_id=1, source_target_pairs={{0,64},{32,96},{64,0},{96,32},{1,65},{33,97},{65,1},{97,33},{2,66}... | collective-permute-start | bytes 2359304 | tf_op jit(solution)/shard_map/ppermute | solution.py:277
  150.5 25.4 %collective-permute-start.24 = (bf16[4,256,384]{2,1,0:T(8,128)(2,1)S(1)}, bf16[4,256,384]{2,1,0:T(8,128)(2,1)S(1)}, u32[]{:S(2)}, u32[]{:S(2)}) collective-permute-start(bf16[4,256,384]{2,1,0:T(8,128)(2,1)S(1)} %get-tuple-element.61), channel_id=1, source_target_pairs={{0,96},{32,0},{64,32},{96,64},{1,97},{33,1},{65,33},{97,65},{2,98}... | collective-permute-start | bytes 2359304 | tf_op jit(solution)/shard_map/ppermute | solution.py:277
  155.2 39.1 %collective-permute-start.12 = (bf16[2,2,128,768]{3,2,1,0:T(8,128)(2,1)S(1)}, bf16[2,2,128,768]{3,2,1,0:T(8,128)(2,1)S(1)}, u32[]{:S(2)}, u32[]{:S(2)}) collective-permute-start(bf16[2,2,128,768]{3,2,1,0:T(8,128)(2,1)S(1)} %slice.14), channel_id=1, source_target_pairs={{0,24},{8,0},{16,8},{24,16},{1,25},{9,1},{17,9},{25,17},{2,26},{10... | collective-permute-start | bytes 2359304 | tf_op jit(solution)/shard_map/ppermute | solution.py:277
  156.5 42.0 %collective-permute-start.13 = (bf16[2,2,128,768]{3,2,1,0:T(8,128)(2,1)S(1)}, bf16[2,2,128,768]{3,2,1,0:T(8,128)(2,1)S(1)}, u32[]{:S(2)}, u32[]{:S(2)}) collective-permute-start(bf16[2,2,128,768]{3,2,1,0:T(8,128)(2,1)S(1)} %slice.15), channel_id=1, source_target_pairs={{0,8},{8,16},{16,24},{24,0},{1,9},{9,17},{17,25},{25,1},{2,10},{10... | collective-permute-start | bytes 2359304 | tf_op jit(solution)/shard_map/ppermute | solution.py:277
  173.7 3.0 %copy-start.6 = (bf16[4,256,384]{2,1,0:T(8,128)(2,1)}, bf16[4,256,384]{2,1,0:T(8,128)(2,1)S(1)}, u32[]{:S(2)}) copy-start(bf16[4,256,384]{2,1,0:T(8,128)(2,1)S(1)} %collective-permute-done.22.b1) | copy-start | bytes 2359300
  173.7 9.3 %collective-permute-start.14 = (bf16[528,128]{1,0:T(8,128)(2,1)}, bf16[528,128]{1,0:T(8,128)(2,1)S(1)}, u32[]{:S(2)}, u32[]{:S(2)}) collective-permute-start(bf16[528,128]{1,0:T(8,128)(2,1)} %get-tuple-element.45.refs_0_), channel_id=1, source_target_pairs={{0,24},{8,0},{16,8},{24,16},{1,25},{9,1},{17,9},{25,17},{2,26},{10... | collective-permute-start | bytes 405512 | tf_op jit(solution)/shard_map/ppermute | solution.py:277
  175.0 1.7 copy-start.7
  175.0 12.9 %collective-permute-start.15 = (bf16[528,128]{1,0:T(8,128)(2,1)}, bf16[528,128]{1,0:T(8,128)(2,1)S(1)}, u32[]{:S(2)}, u32[]{:S(2)}) collective-permute-start(bf16[528,128]{1,0:T(8,128)(2,1)} %get-tuple-element.45.refs_0_), channel_id=1, source_target_pairs={{0,16},{8,24},{16,0},{24,8},{1,17},{9,25},{17,1},{25,9},{2,18},{10... | collective-permute-start | bytes 405512 | tf_op jit(solution)/shard_map/ppermute | solution.py:277
  175.9 12.0 %collective-permute-start.16 = (bf16[528,128]{1,0:T(8,128)(2,1)}, bf16[528,128]{1,0:T(8,128)(2,1)S(1)}, u32[]{:S(2)}, u32[]{:S(2)}) collective-permute-start(bf16[528,128]{1,0:T(8,128)(2,1)} %get-tuple-element.45.refs_0_), channel_id=1, source_target_pairs={{0,8},{8,16},{16,24},{24,0},{1,9},{9,17},{17,25},{25,1},{2,10},{10... | collective-permute-start | bytes 405512 | tf_op jit(solution)/shard_map/ppermute | solution.py:277
  183.0 4.9 %copy-start.9 = (bf16[528,128]{1,0:T(8,128)(2,1)}, bf16[528,128]{1,0:T(8,128)(2,1)S(1)}, u32[]{:S(2)}) copy-start(bf16[528,128]{1,0:T(8,128)(2,1)S(1)} %collective-permute-done.14.refs_1_.refs_0_) | copy-start | bytes 405508
  183.0 22.6 %collective-permute-start.25 = (bf16[256,384]{1,0:T(8,128)(2,1)}, bf16[256,384]{1,0:T(8,128)(2,1)}, u32[]{:S(2)}, u32[]{:S(2)}) collective-permute-start(bf16[256,384]{1,0:T(8,128)(2,1)} %get-tuple-element.52), channel_id=1, source_target_pairs={{0,32},{32,64},{64,96},{96,0},{1,33},{33,65},{65,97},{97,1},{2,34}... | collective-permute-start | bytes 589832 | tf_op jit(solution)/shard_map/ppermute | solution.py:277
  191.1 11.0 %collective-permute-start.17 = (bf16[528,128]{1,0:T(8,128)(2,1)}, bf16[528,128]{1,0:T(8,128)(2,1)S(1)}, u32[]{:S(2)}, u32[]{:S(2)}) collective-permute-start(bf16[528,128]{1,0:T(8,128)(2,1)} %row_state.3), channel_id=1, source_target_pairs={{32,0},{64,32},{96,64},{33,1},{65,33},{97,65},{34,2},{66,34},{98,6... | collective-permute-start | bytes 405512 | tf_op jit(solution)/shard_map/ppermute | solution.py:283
  193.0 10.1 %collective-permute-start.18 = (bf16[528,128]{1,0:T(8,128)(2,1)}, bf16[528,128]{1,0:T(8,128)(2,1)S(1)}, u32[]{:S(2)}, u32[]{:S(2)}) collective-permute-start(bf16[528,128]{1,0:T(8,128)(2,1)} %row_state.3), channel_id=1, source_target_pairs={{64,0},{96,32},{65,1},{97,33},{66,2},{98,34},{67,3},{99,35},{68,4}... | collective-permute-start | bytes 405512 | tf_op jit(solution)/shard_map/ppermute | solution.py:283
  194.3 13.1 %copy-start.4 = (bf16[2,2,128,768]{3,2,1,0:T(8,128)(2,1)}, bf16[2,2,128,768]{3,2,1,0:T(8,128)(2,1)S(1)}, u32[]{:S(2)}) copy-start(bf16[2,2,128,768]{3,2,1,0:T(8,128)(2,1)S(1)} %collective-permute-done.12.far_a) | copy-start | bytes 2359300
  194.3 39.9 %collective-permute-start.26 = (bf16[256,384]{1,0:T(8,128)(2,1)}, bf16[256,384]{1,0:T(8,128)(2,1)S(1)}, u32[]{:S(2)}, u32[]{:S(2)}) collective-permute-start(bf16[256,384]{1,0:T(8,128)(2,1)} %get-tuple-element.53), channel_id=1, source_target_pairs={{0,64},{32,96},{64,0},{96,32},{1,65},{33,97},{65,1},{97,33},{2,66}... | collective-permute-start | bytes 589832 | tf_op jit(solution)/shard_map/ppermute | solution.py:277
  198.5 8.9 %copy-start.5 = (bf16[2,2,128,768]{3,2,1,0:T(8,128)(2,1)}, bf16[2,2,128,768]{3,2,1,0:T(8,128)(2,1)S(1)}, u32[]{:S(2)}) copy-start(bf16[2,2,128,768]{3,2,1,0:T(8,128)(2,1)S(1)} %collective-permute-done.13.far_b) | copy-start | bytes 2359300
  198.5 35.7 %collective-permute-start.27 = (bf16[256,384]{1,0:T(8,128)(2,1)}, bf16[256,384]{1,0:T(8,128)(2,1)S(1)}, u32[]{:S(2)}, u32[]{:S(2)}) collective-permute-start(bf16[256,384]{1,0:T(8,128)(2,1)} %get-tuple-element.54), channel_id=1, source_target_pairs={{0,96},{32,0},{64,32},{96,64},{1,97},{33,1},{65,33},{97,65},{2,98}... | collective-permute-start | bytes 589832 | tf_op jit(solution)/shard_map/ppermute | solution.py:277
  202.1 18.8 %copy-start.21 = (bf16[528,128]{1,0:T(8,128)(2,1)}, bf16[528,128]{1,0:T(8,128)(2,1)S(1)}, u32[]{:S(2)}) copy-start(bf16[528,128]{1,0:T(8,128)(2,1)S(1)} %collective-permute-done.17.refs_3_) | copy-start | bytes 405508
  202.1 32.2 %collective-permute-start.28 = (bf16[256,384]{1,0:T(8,128)(2,1)}, bf16[256,384]{1,0:T(8,128)(2,1)S(1)}, u32[]{:S(2)}, u32[]{:S(2)}) collective-permute-start(bf16[256,384]{1,0:T(8,128)(2,1)} %get-tuple-element.56), channel_id=1, source_target_pairs={{0,8},{8,16},{16,24},{24,0},{1,9},{9,17},{17,25},{25,1},{2,10},{10... | collective-permute-start | bytes 589832 | tf_op jit(solution)/shard_map/ppermute | solution.py:277
  203.1 17.8 %copy-start.22 = (bf16[528,128]{1,0:T(8,128)(2,1)}, bf16[528,128]{1,0:T(8,128)(2,1)S(1)}, u32[]{:S(2)}) copy-start(bf16[528,128]{1,0:T(8,128)(2,1)S(1)} %collective-permute-done.18.refs_4_) | copy-start | bytes 405508
  203.1 31.2 %collective-permute-start.29 = (bf16[256,384]{1,0:T(8,128)(2,1)}, bf16[256,384]{1,0:T(8,128)(2,1)S(1)}, u32[]{:S(2)}, u32[]{:S(2)}) collective-permute-start(bf16[256,384]{1,0:T(8,128)(2,1)} %get-tuple-element.57), channel_id=1, source_target_pairs={{0,16},{8,24},{16,0},{24,8},{1,17},{9,25},{17,1},{25,9},{2,18},{10... | collective-permute-start | bytes 589832 | tf_op jit(solution)/shard_map/ppermute | solution.py:277
  205.6 28.7 %collective-permute-start.30 = (bf16[256,384]{1,0:T(8,128)(2,1)}, bf16[256,384]{1,0:T(8,128)(2,1)S(1)}, u32[]{:S(2)}, u32[]{:S(2)}) collective-permute-start(bf16[256,384]{1,0:T(8,128)(2,1)} %get-tuple-element.58), channel_id=1, source_target_pairs={{0,24},{8,0},{16,8},{24,16},{1,25},{9,1},{17,9},{25,17},{2,26},{10... | collective-permute-start | bytes 589832 | tf_op jit(solution)/shard_map/ppermute | solution.py:277
  (11 other events, 8.1 us)
Sparse Core Ops, SparseCore 0:
  9.7 69.9 all-gather.6
  81.9 50.1 all-gather.4
where the time goes:
time: 246 us; the launch traced here: 245 us
  Pallas kernels  77.2 us (31%)
  waiting for transfers between devices  70.6 us (29%)
  starting transfers between devices  69.4 us (28%)
  between operations  14.4 us (6%)
  local copies, waits for them, and re-layouts  12 us (5%)
    ppermute x25, starting transfers between devices, turned_by(): lax.ppermute(value, axis, [(i, (i + step) % size) for i in range(size)])  60.8 us
    ppermute x25, waiting for transfers between devices, turned_by(): lax.ppermute(value, axis, [(i, (i + step) % size) for i in range(size)])  60.3 us
    pallas_call x1, Pallas kernels, body(): pl.pallas_call(cotangent_kernel, grid=(blocks,), in_specs=[pl.BlockSpec((...  14.9 us
    pallas_call x1, Pallas kernels, body(): pl.pallas_call(attended_kernel, grid_spec=pltpu.PrefetchScalarGridSpec(nu...  13.4 us
    pallas_call x1, Pallas kernels, body(): pl.pallas_call(weight_kernel, grid=(groups,), in_specs=[whole((width, row...  13.2 us
    ppermute x4, waiting for transfers between devices, moved_by(): return lax.ppermute(value, axis, pairs)  8.14 us
    ppermute x4, starting transfers between devices, moved_by(): return lax.ppermute(value, axis, pairs)  7.74 us
    pallas_call x1, Pallas kernels, body(): pl.pallas_call(key_value_kernel, grid=(blocks,), in_specs=[rows_of(width,...  7.43 us
  transfers between devices with their start and end apart: 33, of which 10 were waited for; matrix products, arithmetic and copies ran while one was open for 4% of the time, Pallas kernels for 30%

commit v1 on v0

--- a/solution.py
+++ b/solution.py
@@ -116,13 +116,23 @@
         carry[c, :] = jnp.where(keep, state, 0.0) + dot(kept, vh, TN)
 
 
-def cotangent_kernel(grad, weight, opened, q, dcol, table, grad_opened, out, carry):
+def near_cotangent_kernel(places, *refs):
+    out = refs[-1]
+    count = (len(refs) - 1) // 2
+    total = dot(refs[0][...], refs[count][...], NT)
+    for p in range(1, count):
+        total = total + dot(refs[p][...], refs[count + p][...], NT)
+    out[...] = total
+
+
+def cotangent_kernel(
+    places, near, a0, b0, a1, b1, w0, w1, opened, q, dcol, table, grad_opened, out, carry
+):
     i = pl.program_id(0)
     heads = q.shape[1] // HEAD
-    width = grad.shape[2]
-    gn = dot(grad[0], weight[:, :width], NT)
-    for j in range(1, grad.shape[0]):
-        gn = gn + dot(grad[j], weight[:, j * width : (j + 1) * width], NT)
+    early = i < pl.num_programs(0) // 2
+    gn = near[...] + dot(jnp.where(early, a0[...], b0[...]), w0[...], NT)
+    gn = gn + dot(jnp.where(early, a1[...], b1[...]), w1[...], NT)
 
     @pl.when(i == 0)
     def _():
@@ -212,34 +222,47 @@
         carry[c, :] = jnp.where(keep, state, 0.0) + dot(kept, high, TN)
 
 
-def weight_kernel(turned, grad, first, second):
-    part = dot(turned[...], grad[0], NN).astype(BF16)
-    rows, cols = part.shape[0] // 2, part.shape[1] // 2
-    for h in range(2):
-        c = slice(h * cols, (h + 1) * cols)
-        first[h, 0] = part[:rows, c]
-        second[0, h] = part[rows:, c]
-
-
-def middle_sum_kernel(places, a, a1, a2, a3, b, b1, b2, b3, *outs):
-    for own, others, base in ((a, (a1, a2, a3), 0), (b, (b1, b2, b3), 4)):
-        total = own[0, 0].astype(F32)
-        for other in others:
-            total = total + other[0].astype(F32)
-        for s in range(4):
-
-            @pl.when(pl.program_id(0) == s)
-            def _():
-                outs[base + s][...] = total.astype(outs[base + s].dtype)
-
-
-def last_sum_kernel(a, a1, a2, a3, b, b1, b2, b3, out):
-    half = a.shape[0]
-    for parts, rows in (((a, a1, a2, a3), slice(0, half)), ((b, b1, b2, b3), slice(half, 2 * half))):
-        total = parts[0][...].astype(F32)
-        for part in parts[1:]:
-            total = total + part[...].astype(F32)
-        out[rows, :] = total
+def put_columns(part, out):
+    low = part.astype(BF16)
+    half = low.shape[1] // 2
+    out[0, 0] = low[:, :half]
+    out[0, 1] = low[:, half:]
+
+
+def near_weight_kernel(places, turned, *refs):
+    pieces, (out, held, sems) = refs[:-3], refs[-3:]
+    step = pl.program_id(0)
+
+    def fetch(p):
+        return pltpu.make_async_copy(pieces[p], held.at[p % 2], sems.at[p % 2])
+
+    for p in range(len(pieces)):
+
+        @pl.when(step == p)
+        def _():
+            if p == 0:
+                fetch(0).start()
+            if p + 1 < len(pieces):
+                fetch(p + 1).start()
+            fetch(p).wait()
+            put_columns(dot(turned[...], held[p % 2], NN), out)
+
+
+def far_weight_kernel(places, turned, a0, b0, a1, b1, started, out):
+    half = turned.shape[1] // 2
+    for p, (a, b) in enumerate(((a0, b0), (a1, b1))):
+
+        @pl.when(pl.program_id(0) == p)
+        def _():
+            part = dot(turned[:, :half], a[...], NN) + dot(turned[:, half:], b[...], NN)
+            put_columns(part, out)
+
+
+def sum_kernel(place, own, *refs):
+    total = own[0].astype(F32)
+    for ref in refs[:-1]:
+        total = total + ref[...].astype(F32)
+    refs[-1][...] = total
 
 
 def attended_kernel(places, low, own, right, left, far_a, far_b, out, columns, sems):
@@ -291,60 +314,49 @@
     return lax.dynamic_index_in_dim(value, index, axis, keepdims=False)
 
 
-def exchanged(state, step):
+def exchanged(state, step, extra=()):
     beside = [turned_by(state, "cy", step * s) for s in range(1, 4)]
+    beside, extra = lax.optimization_barrier((beside, extra))
     row = pl.pallas_call(
         lambda *refs: row_kernel(step > 0, *refs),
         out_shape=jax.ShapeDtypeStruct(state.shape, state.dtype),
         name="row_state",
     )(state, *beside)
-    return beside + [moved_by(row, "cx", step * s) for s in range(1, 3)]
-
-
-def column_pieces(out_weight, share, cx, core):
+    return beside + [moved_by(row, "cx", step * s) for s in range(1, 3)], extra
+
+
+def column_strip(out_weight, share, cx):
     cy, z = lax.axis_index("cy"), lax.axis_index("z")
     at = (cx * HEAD, (z - cy) % 4 * 2 * share)
     sent = lax.dynamic_slice(out_weight, at, (HEAD, 2 * share))
     pairs = [(4 * y + (i + y) % 4, 4 * y + i) for y in range(4) for i in range(4)]
-    held = lax.ppermute(sent, ("cy", "z"), pairs)
-    mine = lax.dynamic_slice(held, (0, core * share), (HEAD, share))
-    other = lax.dynamic_slice(held, (0, (1 - core) * share), (HEAD, share))
+    return lax.ppermute(sent, ("cy", "z"), pairs)
+
+
+def column_pieces(strip, share, core):
+    mine = lax.dynamic_slice(strip, (0, core * share), (HEAD, share))
+    other = lax.dynamic_slice(strip, (0, (1 - core) * share), (HEAD, share))
     both = jnp.stack([mine, swapped(other)])
     return jnp.stack([both] + [turned_by(both, "cx", s) for s in range(1, 4)])
 
 
-def scattered_sum(first, second, cx, cy):
-    half, part = first.shape[2:]
-    to_y = [turned_by(pick(first, (cy + s) % 4), "cy", s) for s in range(1, 4)]
-    to_x = [turned_by(pick(second, (cx + s) % 4), "cx", s) for s in range(1, 4)]
-
-    def own(line, start):
-        shape = (1, 1, half, part)
-        return pl.BlockSpec(shape, lambda i, p: (p[line], (p[start] + i) % 4, 0, 0))
-
-    def piece(start):
-        return pl.BlockSpec((1, half, part), lambda i, p: ((p[start] + i) % 4, 0, 0))
-
-    kinds = [F32, BF16, BF16, BF16] * 2
-    sums = pl.pallas_call(
-        middle_sum_kernel,
+def row_sum(mine, cy):
+    got = [turned_by(pick(mine, (cy + s) % 4), "cy", s) for s in range(1, 4)]
+    height, part = mine.shape[1:]
+    block = (CHUNK, part)
+    return pl.pallas_call(
+        sum_kernel,
         grid_spec=pltpu.PrefetchScalarGridSpec(
             num_scalar_prefetch=1,
-            grid=(4,),
-            in_specs=[own(1, 0)] + [piece(0)] * 3 + [own(0, 1)] + [piece(1)] * 3,
-            out_specs=[pl.BlockSpec((half, part), lambda i, p: (0, 0))] * 8,
+            grid=(height // CHUNK,),
+            in_specs=[pl.BlockSpec((1, *block), lambda i, p: (p[0], i, 0))]
+            + [pl.BlockSpec(block, lambda i, p: (i, 0))] * 3,
+            out_specs=pl.BlockSpec(block, lambda i, p: (i, 0)),
         ),
-        out_shape=[jax.ShapeDtypeStruct((half, part), kind) for kind in kinds],
-        compiler_params=params(),
-        name="middle_sum",
-    )(jnp.stack([cx, cy]), first, *to_y, second, *to_x)
-    to_x = [turned_by(sums[s], "cx", s) for s in range(1, 4)]
-    to_y = [turned_by(sums[4 + s], "cy", s) for s in range(1, 4)]
-    return pl.pallas_call(
-        last_sum_kernel,
-        out_shape=jax.ShapeDtypeStruct((2 * half, part), F32),
+        out_shape=jax.ShapeDtypeStruct((height, part), F32),
+        compiler_params=params(),
         name="last_sum",
-    )(sums[0], *to_x, sums[4], *to_y)
+    )(cy[None], mine, *got)
 
 
 def body(queries, keys, values, doc_ids, out_weight, grad_out):
@@ -357,7 +369,9 @@
     cx, cy = lax.axis_index("cx"), lax.axis_index("cy")
     z, core = lax.axis_index("z"), lax.axis_index("core")
 
-    grad_whole = lax.all_gather(grad_out, TENSOR, axis=0)
+    above = turned_by(grad_out, "z", -1)
+    below = turned_by(grad_out, "z", 1)
+    beside = swapped(grad_out)
 
     docs = doc_ids.astype(F32)
     dcol = jnp.broadcast_to(docs[:, None], (rows, HEAD))
@@ -368,10 +382,11 @@
     table = jnp.broadcast_to(table[:, None], (16, HEAD))
 
     tail = pl.pallas_call(tail_kernel, out_shape=payload, name="tail")(keys, values, dcol, table)
-    arrived = exchanged(tail, 1)
-
-    own = column_pieces(out_weight, share, cx, core)
-    arrived, own = lax.optimization_barrier((arrived, own))
+    strip = column_strip(out_weight, share, cx)
+    arrived, strip = exchanged(tail, 1, strip)
+    own = column_pieces(strip, share, core)
+    ready = (arrived, above, below, beside, own)
+    arrived, above, below, beside, own = lax.optimization_barrier(ready)
 
     row_block = pl.BlockSpec((1, CHUNK), lambda i: (0, i))
     state_block = pl.BlockSpec((1, size, HEAD), lambda i: (i, 0, 0))
@@ -400,46 +415,96 @@
 
     low_whole = lax.all_gather(low, TENSOR, axis=0)
 
+    half_rows = rows // 2
+    far_a = turned_by(above[:half_rows], "z", -1)
+    far_b = turned_by(below[half_rows:], "z", 1)
+    near = [grad_out, beside, above, swapped(above), below, swapped(below)]
+    lines = [(z + s) % 4 for s in (0, 0, 1, 1, 3, 3, 2, 2)]
+    sides = [core if p % 2 == 0 else 1 - core for p in range(8)]
+    places = jnp.stack([2 * a + b for a, b in zip(lines, sides)])
+
+    def weight_block(p):
+        return pl.BlockSpec((width, share), lambda i, at: (0, at[p]))
+
+    def some_rows(columns):
+        return pl.BlockSpec((CHUNK, columns), lambda i, at: (i, 0))
+
+    def column_block(first):
+        def index(g, at):
+            return (at[first + g] // 2, at[first + g] % 2, 0, 0)
+
+        return pl.BlockSpec((1, 2, width, share // 2), index)
+
+    held = pl.BlockSpec(memory_space=pl.ANY)
+    term = jax.ShapeDtypeStruct((4, 4, width, share // 2), BF16)
+    started = pl.pallas_call(
+        near_weight_kernel,
+        grid_spec=pltpu.PrefetchScalarGridSpec(
+            num_scalar_prefetch=1,
+            grid=(6,),
+            in_specs=[whole((width, rows))] + [held] * 6,
+            out_specs=column_block(0),
+            scratch_shapes=[pltpu.VMEM((2, rows, share), BF16), pltpu.SemaphoreType.DMA((2,))],
+        ),
+        out_shape=term,
+        compiler_params=params(),
+        name="near_weight",
+    )(places, turned, *near)
+    started, far_a, far_b, own = lax.optimization_barrier((started, far_a, far_b, own))
     right = turned_by(own, "cy", -1)
     left = turned_by(own, "cy", 1)
-    turned, right, left = lax.optimization_barrier((turned, right, left))
-
-    pair = (width // 2, share // 2)
-    first, second = pl.pallas_call(
-        weight_kernel,
-        grid=(groups,),
-        in_specs=[whole((width, rows)), pl.BlockSpec((1, rows, share), lambda j: (j, 0, 0))],
-        out_specs=[
-            pl.BlockSpec((2, 1, *pair), lambda j: (j % 2, j // 2, 0, 0)),
-            pl.BlockSpec((1, 2, *pair), lambda j: (j // 2, j % 2, 0, 0)),
-        ],
-        out_shape=[jax.ShapeDtypeStruct((4, 4, *pair), BF16)] * 2,
-        compiler_params=params(),
-        name="weight_grad",
-    )(turned, grad_whole)
-    grad_weight = scattered_sum(first, second, cx, cy)
-
+    far = [far_a, far_b, swapped(far_a), swapped(far_b)]
+    term = pl.pallas_call(
+        far_weight_kernel,
+        grid_spec=pltpu.PrefetchScalarGridSpec(
+            num_scalar_prefetch=1,
+            grid=(2,),
+            in_specs=[whole((width, rows))] + [whole((half_rows, share))] * 4 + [held],
+            out_specs=column_block(6),
+        ),
+        out_shape=term,
+        input_output_aliases={6: 0},
+        compiler_params=params(),
+        name="far_weight",
+    )(places, turned, *far, started)
+    grad_part = lax.psum_scatter(term, "cx", scatter_dimension=0, tiled=True)[0]
+
+    near_sum = pl.pallas_call(
+        near_cotangent_kernel,
+        grid_spec=pltpu.PrefetchScalarGridSpec(
+            num_scalar_prefetch=1,
+            grid=(blocks,),
+            in_specs=[some_rows(share)] * 6 + [weight_block(p) for p in range(6)],
+            out_specs=some_rows(width),
+        ),
+        out_shape=jax.ShapeDtypeStruct((rows, width), F32),
+        compiler_params=params(),
+        name="near_cotangent",
+    )(places, *near, *[out_weight] * 6)
+
+    upper = pl.BlockSpec((CHUNK, share), lambda i, at: (jnp.minimum(i, blocks // 2 - 1), 0))
+    lower = pl.BlockSpec((CHUNK, share), lambda i, at: (jnp.maximum(i - blocks // 2, 0), 0))
     grad_opened, head = pl.pallas_call(
         cotangent_kernel,
-        grid=(blocks,),
-        in_specs=[
-            pl.BlockSpec((groups, CHUNK, share), lambda i: (0, i, 0)),
-            whole(out_weight.shape),
-            rows_of(width),
-            rows_of(width),
-            rows_of(HEAD),
-            whole(table.shape),
-        ],
-        out_specs=[rows_of(width), whole(payload.shape)],
+        grid_spec=pltpu.PrefetchScalarGridSpec(
+            num_scalar_prefetch=1,
+            grid=(blocks,),
+            in_specs=[some_rows(width), upper, lower, upper, lower]
+            + [weight_block(6), weight_block(7)]
+            + [some_rows(width), some_rows(width), some_rows(HEAD), whole(table.shape)],
+            out_specs=[some_rows(width), whole(payload.shape)],
+            scratch_shapes=[pltpu.VMEM((size, HEAD), F32)],
+        ),
         out_shape=[jax.ShapeDtypeStruct((rows, width), F32), payload],
-        scratch_shapes=[pltpu.VMEM((size, HEAD), F32)],
         compiler_params=params(),
         name="cotangent",
-    )(grad_whole, out_weight, opened, queries, dcol, table)
-    returned = exchanged(head, -1)
-
-    far_a = turned_by(right[:2], "cy", -1)
-    far_b = turned_by(left[2:], "cy", 1)
+    )(places, near_sum, *far, out_weight, out_weight, opened, queries, dcol, table)
+
+    returned, _ = exchanged(head, -1)
+
+    returned, right, left = lax.optimization_barrier((returned, right, left))
+    across_a = turned_by(right[:2], "cy", -1)
+    across_b = turned_by(left[2:], "cy", 1)
 
     grad_query = pl.pallas_call(
         query_kernel,
@@ -468,7 +533,6 @@
 
     around = [2 * ((z + cy + s) % 4) + (core if o == 0 else 1 - core) for s in range(4) for o in range(2)]
     heads_at = [(cx - s) % 4 for s in range(4)]
-    held = pl.BlockSpec(memory_space=pl.ANY)
     attended = pl.pallas_call(
         attended_kernel,
         grid_spec=pltpu.PrefetchScalarGridSpec(
@@ -484,7 +548,9 @@
         out_shape=jax.ShapeDtypeStruct((rows, share), BF16),
         compiler_params=params(),
         name="attended",
-    )(jnp.stack(around + heads_at), low_whole, own, right, left, far_a, far_b)
+    )(jnp.stack(around + heads_at), low_whole, own, right, left, across_a, across_b)
+    grad_part, attended, grad_key = lax.optimization_barrier((grad_part, attended, grad_key))
+    grad_weight = row_sum(grad_part, cy)
     return attended, grad_query, grad_key, grad_value, grad_weight
 
 

time: 246 us -> 264 us (1.073)
  starting transfers between devices: 69.4 us -> 44.9 us
  waiting for transfers between devices: 70.6 us -> 94.6 us
  local copies, waits for them, and re-layouts: 12 us -> 19.7 us
  Pallas kernels: 77.2 us -> 81.8 us
  other arithmetic: 0.95 us -> 4.1 us
    ppermute x25 -> x20, starting transfers between devices: 60.8 us -> 30.7 us  [turned_by(): lax.ppermute(value, axis, [(i, (i + step) % size) for i in range(size)])]
    ppermute x25 -> x20, waiting for transfers between devices: 60.3 us -> 76 us  [turned_by(): lax.ppermute(value, axis, [(i, (i + step) % size) for i in range(size)])]
    ppermute x4, waiting for transfers between devices: 8.14 us -> 14 us  [moved_by(): return lax.ppermute(value, axis, pairs)]
    pallas_call x4 -> x5, Pallas kernels: 37 us -> 41.7 us  [the longest x1 12.2 us: body(): pl.pallas_call(near_weight_kernel, grid_spec=pltpu.PrefetchScalarGridSpec...]
    slice x2 -> x4, local copies, waits for them, and re-layouts: 1.24 us -> 5.46 us  [the longest x1 2.67 us: body(): across_a = turned_by(right[:2], 'cy', -1)]
    ppermute x1, starting transfers between devices: 0.69 us -> 4.47 us  [column_strip(): return lax.ppermute(sent, ('cy', 'z'), pairs)]
    another operation x2, other arithmetic: 0.25 us -> 3.41 us  [column_pieces(): return jnp.stack([both] + [turned_by(both, 'cx', s) for s in range(1, 4)])]
    unnamed x52 -> x40, local copies, waits for them, and re-layouts: 3.65 us -> 6.79 us
  transfers between devices with their start and end apart: 33 -> 33, of which waited for: 10 -> 17; matrix products, arithmetic and copies ran while one was open for 4% -> 5% of each run, Pallas kernels for 30% -> 28%
where the time goes in v1:
time: 264 us; the launch traced here: 261 us
  waiting for transfers between devices  94.6 us (36%)
  Pallas kernels  81.8 us (31%)
  starting transfers between devices  44.9 us (17%)
  local copies, waits for them, and re-layouts  19.7 us (7%)
  between operations  15.7 us (6%)
  other arithmetic  4.1 us (2%)
    ppermute x20, waiting for transfers between devices, turned_by(): lax.ppermute(value, axis, [(i, (i + step) % size) for i in range(size)])  76 us
    ppermute x20, starting transfers between devices, turned_by(): lax.ppermute(value, axis, [(i, (i + step) % size) for i in range(size)])  30.7 us
    ppermute x4, waiting for transfers between devices, moved_by(): return lax.ppermute(value, axis, pairs)  14 us
    pallas_call x1, Pallas kernels, body(): pl.pallas_call(attended_kernel, grid_spec=pltpu.PrefetchScalarGridSpec(nu...  13.4 us
    pallas_call x1, Pallas kernels, body(): pl.pallas_call(near_weight_kernel, grid_spec=pltpu.PrefetchScalarGridSpec...  12.2 us
    pallas_call x1, Pallas kernels, body(): pl.pallas_call(near_cotangent_kernel, grid_spec=pltpu.PrefetchScalarGridS...  11.4 us
    pallas_call x1, Pallas kernels, body(): pl.pallas_call(cotangent_kernel, grid_spec=pltpu.PrefetchScalarGridSpec(n...  9.89 us
    ppermute x4, starting transfers between devices, moved_by(): return lax.ppermute(value, axis, pairs)  8.43 us
  transfers between devices with their start and end apart: 33, of which 17 were waited for; matrix products, arithmetic and copies ran while one was open for 5% of the time, Pallas kernels for 28%

profile of v1, /device:TPU:2, one launch (start us, length us, event | category | flops | bytes accessed | tf_op | source)
XLA Modules:
  0.0 260.8 jit_solution(17287813783268427751)
XLA Ops:
  8.1 1.8 dynamic_slice.19
  9.8 4.5 %collective-permute-start.3 = (bf16[128,1536]{1,0:T(8,128)(2,1)}, bf16[128,1536]{1,0:T(8,128)(2,1)}, u32[]{:S(2)}, u32[]{:S(2)}) collective-permute-start(bf16[128,1536]{1,0:T(8,128)(2,1)} %dynamic_slice.19), channel_id=1, source_target_pairs={{0,0},{2,2},{4,4},{6,6},{10,8},{12,10},{14,12},{8,14},{20,16},{22,... | collective-permute-start | bytes 1179656 | tf_op jit(solution)/shard_map/ppermute | solution.py:333
  17.0 2.8 %tail.1.refs_0_ = bf16[528,128]{1,0:T(8,128)(2,1)} custom-call(bf16[1024,512]{1,0:T(8,128)(2,1)} %k.7, bf16[1024,512]{1,0:T(8,128)(2,1)} %v.7, f32[1024,128]{1,0:T(8,128)} %broadcast_in_dim.10.dcol, f32[16,128]{1,0:T(8,128)} %broadcast_in_dim.24.table), custom_call_target="tpu_custom_call" | custom-call | tf_op jit(solution)/shard_map/tail/pallas_call | solution.py:384
  19.8 2.4 collective-permute-start.2
  22.2 2.7 %collective-permute-start.1 = (bf16[528,128]{1,0:T(8,128)(2,1)}, bf16[528,128]{1,0:T(8,128)(2,1)}, u32[]{:S(2)}, u32[]{:S(2)}) collective-permute-start(bf16[528,128]{1,0:T(8,128)(2,1)} %tail.1.refs_0_), channel_id=1, source_target_pairs={{0,16},{8,24},{16,0},{24,8},{1,17},{9,25},{17,1},{25,9},{2,18},{10... | collective-permute-start | bytes 405512 | tf_op jit(solution)/shard_map/ppermute | solution.py:300
  25.3 1.7 collective-permute-done.2.refs_3_.refs_2_
  27.0 3.6 %collective-permute-start.6 = (bf16[1024,768]{1,0:T(8,128)(2,1)}, bf16[1024,768]{1,0:T(8,128)(2,1)S(1)}, u32[]{:S(2)}, u32[]{:S(2)}) collective-permute-start(bf16[1024,768]{1,0:T(8,128)(2,1)} %refs_0_.3), channel_id=1, source_target_pairs={{0,6},{2,0},{4,2},{6,4},{1,7},{3,1},{5,3},{7,5},{8,14},{10,8},{12,... | collective-permute-start | bytes 4718600 | tf_op jit(solution)/shard_map/ppermute | solution.py:300
  30.6 1.3 collective-permute-start
  32.0 5.1 %collective-permute-done.refs_1_.refs_0_ = bf16[528,128]{1,0:T(8,128)(2,1)S(1)} collective-permute-done((bf16[528,128]{1,0:T(8,128)(2,1)}, bf16[528,128]{1,0:T(8,128)(2,1)S(1)}, u32[]{:S(2)}, u32[]{:S(2)}) %collective-permute-start) | collective-permute-done | bytes 135200 | tf_op jit(solution)/shard_map/ppermute | solution.py:300
  38.3 1.4 collective-permute-done.9
  40.5 2.1 collective-permute-start.11
  42.6 10.9 %collective-permute-done.11 = bf16[2,128,768]{2,1,0:T(8,128)(2,1)} collective-permute-done((bf16[2,128,768]{2,1,0:T(8,128)(2,1)}, bf16[2,128,768]{2,1,0:T(8,128)(2,1)}, u32[]{:S(2)}, u32[]{:S(2)}) %collective-permute-start.11) | collective-permute-done | bytes 393248 | tf_op jit(solution)/shard_map/ppermute | solution.py:300
  53.5 1.4 collective-permute-start.12
  54.9 1.9 row_state.2
  56.7 5.3 %collective-permute-done.10 = bf16[2,128,768]{2,1,0:T(8,128)(2,1)} collective-permute-done((bf16[2,128,768]{2,1,0:T(8,128)(2,1)}, bf16[2,128,768]{2,1,0:T(8,128)(2,1)}, u32[]{:S(2)}, u32[]{:S(2)}) %collective-permute-start.10) | collective-permute-done | bytes 393248 | tf_op jit(solution)/shard_map/ppermute | solution.py:300
  62.0 1.8 collective-permute-start.5
  64.1 3.4 %collective-permute-start.4 = (bf16[528,128]{1,0:T(8,128)(2,1)}, bf16[528,128]{1,0:T(8,128)(2,1)S(1)}, u32[]{:S(2)}, u32[]{:S(2)}) collective-permute-start(bf16[528,128]{1,0:T(8,128)(2,1)} %row_state.2), channel_id=1, source_target_pairs={{0,32},{32,64},{64,96},{1,33},{33,65},{65,97},{2,34},{34,66},{66,9... | collective-permute-start | bytes 405512 | tf_op jit(solution)/shard_map/ppermute | solution.py:306
  67.6 2.6 %pad_maximum_fusion.own = bf16[4,2,128,768]{3,2,1,0:T(8,128)(2,1)} fusion(bf16[1,2,128,768]{3,2,1,0:T(8,128)(2,1)} %bitcast.15, bf16[1,2,128,768]{3,2,1,0:T(8,128)(2,1)} %bitcast.14, bf16[1,2,128,768]{3,2,1,0:T(8,128)(2,1)} %bitcast.13, bf16[1,2,128,768]{3,2,1,0:T(8,128)(2,1)S(1)} %get-tuple-element.86), kind=kLoop, calls=%fused_computation | loop fusion | flops 2359296 | bytes 3145728 | tf_op jit(solution)/shard_map/stack | solution.py:340
  70.2 2.3 collective-permute-done.4.refs_3_
  73.6 6.8 %forward.1 = (f32[1024,512]{1,0:T(8,128)}, bf16[1024,512]{1,0:T(8,128)(2,1)}, bf16[512,1024]{1,0:T(8,128)(2,1)}, bf16[4,512,128]{2,1,0:T(8,128)(2,1)}) custom-call(bf16[1024,512]{1,0:T(8,128)(2,1)} %q.5, bf16[1024,512]{1,0:T(8,128)(2,1)} %k.7, bf16[1024,512]{1,0:T(8,128)(2,1)} %v.7, f32[1024,128]{1,0:T(8,128)} %broadcast_in_dim.10.dcol, f32[1,1024]{1,0:T(1,128)} %bitcast.43, ...), custom_call_target="tpu_custom_call" | custom-call | tf_op jit(solution)/shard_map/forward/pallas_call | solution.py:393
  83.2 3.0 %collective-permute-start.15 = (bf16[512,768]{1,0:T(8,128)(2,1)}, bf16[512,768]{1,0:T(8,128)(2,1)}, u32[]{:S(2)}, u32[]{:S(2)}) collective-permute-start(bf16[512,768]{1,0:T(8,128)(2,1)} %slice.20), channel_id=1, source_target_pairs={{0,6},{2,0},{4,2},{6,4},{1,7},{3,1},{5,3},{7,5},{8,14},{10,8},{12,... | collective-permute-start | bytes 2359304 | tf_op jit(solution)/shard_map/ppermute | solution.py:300
  86.7 12.2 %near_weight.1.started = bf16[4,4,512,384]{3,2,1,0:T(8,128)(2,1)} custom-call(s32[8]{0:T(128)} %stack.98.places, bf16[512,1024]{1,0:T(8,128)(2,1)} %get-tuple-element.52.turned, bf16[1024,768]{1,0:T(8,128)(2,1)} %refs_0_.3, bf16[1024,768]{1,0:T(8,128)(2,1)} %collective-permute-done.8.refs_1_, bf16[1024,768]{1,0:T(8,128)(2,1)} %copy-done.1, ...), custom_call_target="tpu_custom_call" | custom-call | tf_op jit(solution)/shard_map/near_weight/pallas_call | solution.py:440
  99.0 15.8 %collective-permute-done.16.b0 = bf16[512,768]{1,0:T(8,128)(2,1)} collective-permute-done((bf16[512,768]{1,0:T(8,128)(2,1)}, bf16[512,768]{1,0:T(8,128)(2,1)}, u32[]{:S(2)}, u32[]{:S(2)}) %collective-permute-start.16) | collective-permute-done | bytes 786464 | tf_op jit(solution)/shard_map/ppermute | solution.py:300
  114.8 1.6 collective-permute-done.15.a0
  116.9 2.0 collective-permute-done.17.a1
  120.9 5.9 %far_weight.1 = bf16[4,4,512,384]{3,2,1,0:T(8,128)(2,1)} custom-call(s32[8]{0:T(128)} %stack.98.places, bf16[512,1024]{1,0:T(8,128)(2,1)} %get-tuple-element.52.turned, bf16[512,768]{1,0:T(8,128)(2,1)} %collective-permute-done.15.a0, bf16[512,768]{1,0:T(8,128)(2,1)} %collective-permute-done.16.b0, ...), custom_call_target="tpu_custom_call", output_to_operand_aliasing={{}: (6, {})} | custom-call | tf_op jit(solution)/shard_map/far_weight/pallas_call | solution.py:457
  126.8 1.5 copy-done.2
  128.3 3.2 %collective-permute-start.24 = (bf16[4,2,128,768]{3,2,1,0:T(8,128)(2,1)S(1)}, bf16[4,2,128,768]{3,2,1,0:T(8,128)(2,1)}, u32[]{:S(2)}, u32[]{:S(2)}) collective-permute-start(bf16[4,2,128,768]{3,2,1,0:T(8,128)(2,1)S(1)} %copy-done.2), channel_id=1, source_target_pairs={{0,24},{8,0},{16,8},{24,16},{1,25},{9,1},{17,9},{25,17},{2,26},{10... | collective-permute-start | bytes 4718600 | tf_op jit(solution)/shard_map/ppermute | solution.py:300
  131.5 11.4 %near_cotangent.1.near = f32[1024,512]{1,0:T(8,128)} custom-call(s32[8]{0:T(128)} %stack.98.places, bf16[1024,768]{1,0:T(8,128)(2,1)} %refs_0_.3, bf16[1024,768]{1,0:T(8,128)(2,1)} %collective-permute-done.8.refs_1_, bf16[1024,768]{1,0:T(8,128)(2,1)} %copy-done.1, bf16[1024,768]{1,0:T(8,128)(2,1)} %collective-permute-done.13.refs_3_, ...), custom_call_target="tpu_custom_call" | custom-call | tf_op jit(solution)/shard_map/near_cotangent/pallas_call | solution.py:472
  143.0 9.9 %cotangent.1 = (f32[1024,512]{1,0:T(8,128)}, bf16[528,128]{1,0:T(8,128)(2,1)}) custom-call(s32[8]{0:T(128)} %stack.98.places, f32[1024,512]{1,0:T(8,128)} %near_cotangent.1.near, bf16[512,768]{1,0:T(8,128)(2,1)} %collective-permute-done.15.a0, bf16[512,768]{1,0:T(8,128)(2,1)} %collective-permute-done.16.b0, bf16[512,768]{1,0:T(8,128)(2,1)} %copy-done.4, ...), custom_call_target="tpu_custom_call" | custom-call | tf_op jit(solution)/shard_map/cotangent/pallas_call | solution.py:487
  152.9 1.9 collective-permute-start.20
  154.8 1.3 collective-permute-start.19
  156.2 15.5 %collective-permute-done.21.refs_3_.refs_2_ = bf16[528,128]{1,0:T(8,128)(2,1)S(1)} collective-permute-done((bf16[528,128]{1,0:T(8,128)(2,1)}, bf16[528,128]{1,0:T(8,128)(2,1)S(1)}, u32[]{:S(2)}, u32[]{:S(2)}) %collective-permute-start.21) | collective-permute-done | bytes 135200 | tf_op jit(solution)/shard_map/ppermute | solution.py:300
  173.1 1.9 row_state.3
  176.2 1.9 collective-permute-start.22
  178.2 9.9 %collective-permute-done.23.refs_4_ = bf16[528,128]{1,0:T(8,128)(2,1)S(1)} collective-permute-done((bf16[528,128]{1,0:T(8,128)(2,1)}, bf16[528,128]{1,0:T(8,128)(2,1)S(1)}, u32[]{:S(2)}, u32[]{:S(2)}) %collective-permute-start.23) | collective-permute-done | bytes 135200 | tf_op jit(solution)/shard_map/ppermute | solution.py:306
  188.1 1.8 collective-permute-done.22.refs_3_
  189.9 2.7 %slice.22 = bf16[2,2,128,768]{3,2,1,0:T(8,128)(2,1)} slice(bf16[4,2,128,768]{3,2,1,0:T(8,128)(2,1)} %collective-permute-done.24.right), slice={[0:2], [0:2], [0:128], [0:768]} | slice | bytes 1572864 | tf_op jit(solution)/shard_map/slice | solution.py:506
  193.6 3.2 %collective-permute-start.26 = (bf16[2,2,128,768]{3,2,1,0:T(8,128)(2,1)}, bf16[2,2,128,768]{3,2,1,0:T(8,128)(2,1)S(1)}, u32[]{:S(2)}, u32[]{:S(2)}) collective-permute-start(bf16[2,2,128,768]{3,2,1,0:T(8,128)(2,1)} %slice.22), channel_id=1, source_target_pairs={{0,24},{8,0},{16,8},{24,16},{1,25},{9,1},{17,9},{25,17},{2,26},{10... | collective-permute-start | bytes 2359304 | tf_op jit(solution)/shard_map/ppermute | solution.py:300
  197.5 7.4 %grad_key_value.1 = (bf16[1024,512]{1,0:T(8,128)(2,1)}, bf16[1024,512]{1,0:T(8,128)(2,1)}) custom-call(f32[1024,512]{1,0:T(8,128)} %get-tuple-element.69.go, bf16[1024,512]{1,0:T(8,128)(2,1)} %q.5, bf16[1024,512]{1,0:T(8,128)(2,1)} %k.7, bf16[1024,512]{1,0:T(8,128)(2,1)} %v.7, f32[1024,128]{1,0:T(8,128)} %broadcast_in_dim.10.dcol, f32[1,1024]{1,0:T(1,128)} %bitcast.44, ...), custom_call_target="tpu_custom_call" | custom-call | tf_op jit(solution)/shard_map/grad_key_value/pallas_call | solution.py:521
  204.9 8.5 %collective-permute-done.27.far_b = bf16[2,2,128,768]{3,2,1,0:T(8,128)(2,1)S(1)} collective-permute-done((bf16[2,2,128,768]{3,2,1,0:T(8,128)(2,1)}, bf16[2,2,128,768]{3,2,1,0:T(8,128)(2,1)S(1)}, u32[]{:S(2)}, u32[]{:S(2)}) %collective-permute-start.27) | collective-permute-done | bytes 786464 | tf_op jit(solution)/shard_map/ppermute | solution.py:300
  214.5 13.4 %attended.1 = bf16[1024,768]{1,0:T(8,128)(2,1)} custom-call(s32[12]{0:T(128)} %stack.119.places, bf16[8,1024,512]{2,1,0:T(8,128)(2,1)} %bitcast.39, bf16[4,2,128,768]{3,2,1,0:T(8,128)(2,1)} %pad_maximum_fusion.own, bf16[4,2,128,768]{3,2,1,0:T(8,128)(2,1)} %collective-permute-done.24.right, bf16[4,2,128,768]{3,2,1,0:T(8,128)(2,1)} %copy-done.3, ...), custom_call_target="tpu_custom_call" | custom-call | tf_op jit(solution)/shard_map/attended/pallas_call | solution.py:536
  228.0 1.4 dynamic-slice_bitcast_fusion
  229.4 2.8 %collective-permute-start.30 = (bf16[512,384]{1,0:T(8,128)(2,1)S(1)}, bf16[512,384]{1,0:T(8,128)(2,1)S(1)}, u32[]{:S(2)}, u32[]{:S(2)}) collective-permute-start(bf16[512,384]{1,0:T(8,128)(2,1)S(1)} %get-tuple-element.83), channel_id=1, source_target_pairs={{0,24},{8,0},{16,8},{24,16},{1,25},{9,1},{17,9},{25,17},{2,26},{10... | collective-permute-start | bytes 1179656 | tf_op jit(solution)/shard_map/ppermute | solution.py:300
  233.1 5.9 %grad_query.1 = bf16[1024,512]{1,0:T(8,128)(2,1)} custom-call(f32[1024,512]{1,0:T(8,128)} %get-tuple-element.69.go, bf16[1024,512]{1,0:T(8,128)(2,1)} %k.7, bf16[1024,512]{1,0:T(8,128)(2,1)} %v.7, f32[1024,128]{1,0:T(8,128)} %broadcast_in_dim.10.dcol, f32[1,1024]{1,0:T(1,128)} %bitcast.45, f32[16,128]{1,0:T(8,128)} %broadcast_in_dim.24.table, ...), custom_call_target="tpu_custom_call" | custom-call | tf_op jit(solution)/shard_map/grad_query/pallas_call | solution.py:509
  239.0 7.9 %collective-permute-done.30.refs_2_ = bf16[512,384]{1,0:T(8,128)(2,1)S(1)} collective-permute-done((bf16[512,384]{1,0:T(8,128)(2,1)S(1)}, bf16[512,384]{1,0:T(8,128)(2,1)S(1)}, u32[]{:S(2)}, u32[]{:S(2)}) %collective-permute-start.30) | collective-permute-done | bytes 393248 | tf_op jit(solution)/shard_map/ppermute | solution.py:300
  246.9 3.4 %collective-permute-done.28.refs_0_ = bf16[512,384]{1,0:T(8,128)(2,1)S(1)} collective-permute-done((bf16[512,384]{1,0:T(8,128)(2,1)S(1)}, bf16[512,384]{1,0:T(8,128)(2,1)S(1)}, u32[]{:S(2)}, u32[]{:S(2)}) %collective-permute-start.28) | collective-permute-done | bytes 393248 | tf_op jit(solution)/shard_map/ppermute | solution.py:300
  251.0 2.3 last_sum.1
  (90 shorter events, 19.8 us)
Async XLA Ops:
  8.0 205.4 %all-gather.3.cloned.1.call-start = ((), (), s32[]{:S(2)}) async-start(), calls=%async_computation.2 | async-start | bytes 9437184 | tf_op jit(solution)/shard_map/all_gather | solution.py:416
  9.8 27.2 %collective-permute-start.3 = (bf16[128,1536]{1,0:T(8,128)(2,1)}, bf16[128,1536]{1,0:T(8,128)(2,1)}, u32[]{:S(2)}, u32[]{:S(2)}) collective-permute-start(bf16[128,1536]{1,0:T(8,128)(2,1)} %dynamic_slice.19), channel_id=1, source_target_pairs={{0,0},{2,2},{4,4},{6,6},{10,8},{12,10},{14,12},{8,14},{20,16},{22,... | collective-permute-start | bytes 1179656 | tf_op jit(solution)/shard_map/ppermute | solution.py:333
  15.0 4.8 %copy-start.15 = (f32[1024]{0:T(1024)}, f32[1024]{0:T(1024)S(1)}, u32[]{:S(2)}) copy-start(f32[1024]{0:T(1024)S(1)} %convert_element_type.6) | copy-start | bytes 12292
  19.8 7.2 %collective-permute-start.2 = (bf16[528,128]{1,0:T(8,128)(2,1)}, bf16[528,128]{1,0:T(8,128)(2,1)}, u32[]{:S(2)}, u32[]{:S(2)}) collective-permute-start(bf16[528,128]{1,0:T(8,128)(2,1)} %tail.1.refs_0_), channel_id=1, source_target_pairs={{0,24},{8,0},{16,8},{24,16},{1,25},{9,1},{17,9},{25,17},{2,26},{10... | collective-permute-start | bytes 405512 | tf_op jit(solution)/shard_map/ppermute | solution.py:300
  22.2 8.5 %collective-permute-start.1 = (bf16[528,128]{1,0:T(8,128)(2,1)}, bf16[528,128]{1,0:T(8,128)(2,1)}, u32[]{:S(2)}, u32[]{:S(2)}) collective-permute-start(bf16[528,128]{1,0:T(8,128)(2,1)} %tail.1.refs_0_), channel_id=1, source_target_pairs={{0,16},{8,24},{16,0},{24,8},{1,17},{9,25},{17,1},{25,9},{2,18},{10... | collective-permute-start | bytes 405512 | tf_op jit(solution)/shard_map/ppermute | solution.py:300
  24.9 47.5 %collective-permute-start.8 = (bf16[1024,768]{1,0:T(8,128)(2,1)}, bf16[1024,768]{1,0:T(8,128)(2,1)}, u32[]{:S(2)}, u32[]{:S(2)}) collective-permute-start(bf16[1024,768]{1,0:T(8,128)(2,1)} %refs_0_.3), channel_id=1, source_target_pairs={{0,1},{1,0},{2,3},{3,2},{4,5},{5,4},{6,7},{7,6},{8,9},{9,8},{10,11... | collective-permute-start | bytes 4718600 | tf_op jit(solution)/shard_map/ppermute | solution.py:310
  24.9 47.5 %collective-permute-start.7 = (bf16[1024,768]{1,0:T(8,128)(2,1)}, bf16[1024,768]{1,0:T(8,128)(2,1)S(1)}, u32[]{:S(2)}, u32[]{:S(2)}) collective-permute-start(bf16[1024,768]{1,0:T(8,128)(2,1)} %refs_0_.3), channel_id=1, source_target_pairs={{0,2},{2,4},{4,6},{6,0},{1,3},{3,5},{5,7},{7,1},{8,10},{10,12},{12... | collective-permute-start | bytes 4718600 | tf_op jit(solution)/shard_map/ppermute | solution.py:300
  27.0 45.4 %collective-permute-start.6 = (bf16[1024,768]{1,0:T(8,128)(2,1)}, bf16[1024,768]{1,0:T(8,128)(2,1)S(1)}, u32[]{:S(2)}, u32[]{:S(2)}) collective-permute-start(bf16[1024,768]{1,0:T(8,128)(2,1)} %refs_0_.3), channel_id=1, source_target_pairs={{0,6},{2,0},{4,2},{6,4},{1,7},{3,1},{5,3},{7,5},{8,14},{10,8},{12,... | collective-permute-start | bytes 4718600 | tf_op jit(solution)/shard_map/ppermute | solution.py:300
  30.6 6.4 %collective-permute-start = (bf16[528,128]{1,0:T(8,128)(2,1)}, bf16[528,128]{1,0:T(8,128)(2,1)S(1)}, u32[]{:S(2)}, u32[]{:S(2)}) collective-permute-start(bf16[528,128]{1,0:T(8,128)(2,1)} %tail.1.refs_0_), channel_id=1, source_target_pairs={{0,8},{8,16},{16,24},{24,0},{1,9},{9,17},{17,25},{25,1},{2,10},{10... | collective-permute-start | bytes 405512 | tf_op jit(solution)/shard_map/ppermute | solution.py:300
  37.1 2.6 %copy-start.11 = (bf16[528,128]{1,0:T(8,128)(2,1)}, bf16[528,128]{1,0:T(8,128)(2,1)S(1)}, u32[]{:S(2)}) copy-start(bf16[528,128]{1,0:T(8,128)(2,1)S(1)} %collective-permute-done.refs_1_.refs_0_) | copy-start | bytes 405508
  38.2 1.5 collective-permute-start.9
  40.5 13.0 %collective-permute-start.11 = (bf16[2,128,768]{2,1,0:T(8,128)(2,1)}, bf16[2,128,768]{2,1,0:T(8,128)(2,1)}, u32[]{:S(2)}, u32[]{:S(2)}) collective-permute-start(bf16[2,128,768]{2,1,0:T(8,128)(2,1)} %get-tuple-element.87), channel_id=1, source_target_pairs={{0,64},{32,96},{64,0},{96,32},{1,65},{33,97},{65,1},{97,33},{2,66}... | collective-permute-start | bytes 1179656 | tf_op jit(solution)/shard_map/ppermute | solution.py:300
  42.6 19.4 %collective-permute-start.10 = (bf16[2,128,768]{2,1,0:T(8,128)(2,1)}, bf16[2,128,768]{2,1,0:T(8,128)(2,1)}, u32[]{:S(2)}, u32[]{:S(2)}) collective-permute-start(bf16[2,128,768]{2,1,0:T(8,128)(2,1)} %get-tuple-element.87), channel_id=1, source_target_pairs={{0,32},{32,64},{64,96},{96,0},{1,33},{33,65},{65,97},{97,1},{2,34}... | collective-permute-start | bytes 1179656 | tf_op jit(solution)/shard_map/ppermute | solution.py:300
  53.5 10.6 %collective-permute-start.12 = (bf16[2,128,768]{2,1,0:T(8,128)(2,1)}, bf16[2,128,768]{2,1,0:T(8,128)(2,1)}, u32[]{:S(2)}, u32[]{:S(2)}) collective-permute-start(bf16[2,128,768]{2,1,0:T(8,128)(2,1)} %get-tuple-element.87), channel_id=1, source_target_pairs={{0,96},{32,0},{64,32},{96,64},{1,97},{33,1},{65,33},{97,65},{2,98}... | collective-permute-start | bytes 1179656 | tf_op jit(solution)/shard_map/ppermute | solution.py:300
  62.0 8.2 %collective-permute-start.5 = (bf16[528,128]{1,0:T(8,128)(2,1)}, bf16[528,128]{1,0:T(8,128)(2,1)S(1)}, u32[]{:S(2)}, u32[]{:S(2)}) collective-permute-start(bf16[528,128]{1,0:T(8,128)(2,1)} %row_state.2), channel_id=1, source_target_pairs={{0,64},{32,96},{1,65},{33,97},{2,66},{34,98},{3,67},{35,99},{4,68}... | collective-permute-start | bytes 405512 | tf_op jit(solution)/shard_map/ppermute | solution.py:306
  64.1 8.3 %collective-permute-start.4 = (bf16[528,128]{1,0:T(8,128)(2,1)}, bf16[528,128]{1,0:T(8,128)(2,1)S(1)}, u32[]{:S(2)}, u32[]{:S(2)}) collective-permute-start(bf16[528,128]{1,0:T(8,128)(2,1)} %row_state.2), channel_id=1, source_target_pairs={{0,32},{32,64},{64,96},{1,33},{33,65},{65,97},{2,34},{34,66},{66,9... | collective-permute-start | bytes 405512 | tf_op jit(solution)/shard_map/ppermute | solution.py:306
  70.2 2.3 copy-start.18
  72.4 1.2 copy-start.19
  72.4 9.5 %copy-start = (bf16[1024,768]{1,0:T(8,128)(2,1)}, bf16[1024,768]{1,0:T(8,128)(2,1)S(1)}, u32[]{:S(2)}) copy-start(bf16[1024,768]{1,0:T(8,128)(2,1)S(1)} %collective-permute-done.7.refs_4_) | copy-start | bytes 4718596
  72.5 8.6 %copy-start.1 = (bf16[1024,768]{1,0:T(8,128)(2,1)}, bf16[1024,768]{1,0:T(8,128)(2,1)S(1)}, u32[]{:S(2)}) copy-start(bf16[1024,768]{1,0:T(8,128)(2,1)S(1)} %collective-permute-done.6.refs_2_) | copy-start | bytes 4718596
  80.4 147.6 %reduce-scatter.2.cloned.1.call-start = ((), (), s32[]{:S(2)}) async-start(), calls=%async_computation.1 | async-start | bytes 7864320 | tf_op jit(solution)/shard_map/reduce_scatter | solution.py:470
  80.5 6.3 %collective-permute-start.13 = (bf16[1024,768]{1,0:T(8,128)(2,1)S(1)}, bf16[1024,768]{1,0:T(8,128)(2,1)}, u32[]{:S(2)}, u32[]{:S(2)}) collective-permute-start(bf16[1024,768]{1,0:T(8,128)(2,1)S(1)} %collective-permute-done.6.refs_2_), channel_id=1, source_target_pairs={{0,1},{1,0},{2,3},{3,2},{4,5},{5,4},{6,7},{7,6},{8,9},{9,8},{10,11... | collective-permute-start | bytes 4718600 | tf_op jit(solution)/shard_map/ppermute | solution.py:310
  80.5 6.2 %collective-permute-start.14 = (bf16[1024,768]{1,0:T(8,128)(2,1)S(1)}, bf16[1024,768]{1,0:T(8,128)(2,1)}, u32[]{:S(2)}, u32[]{:S(2)}) collective-permute-start(bf16[1024,768]{1,0:T(8,128)(2,1)S(1)} %collective-permute-done.7.refs_4_), channel_id=1, source_target_pairs={{0,1},{1,0},{2,3},{3,2},{4,5},{5,4},{6,7},{7,6},{8,9},{9,8},{10,11... | collective-permute-start | bytes 4718600 | tf_op jit(solution)/shard_map/ppermute | solution.py:310
  82.9 31.8 %collective-permute-start.16 = (bf16[512,768]{1,0:T(8,128)(2,1)}, bf16[512,768]{1,0:T(8,128)(2,1)}, u32[]{:S(2)}, u32[]{:S(2)}) collective-permute-start(bf16[512,768]{1,0:T(8,128)(2,1)} %slice.21), channel_id=1, source_target_pairs={{0,2},{2,4},{4,6},{6,0},{1,3},{3,5},{5,7},{7,1},{8,10},{10,12},{12... | collective-permute-start | bytes 2359304 | tf_op jit(solution)/shard_map/ppermute | solution.py:300
  83.2 33.2 %collective-permute-start.15 = (bf16[512,768]{1,0:T(8,128)(2,1)}, bf16[512,768]{1,0:T(8,128)(2,1)}, u32[]{:S(2)}, u32[]{:S(2)}) collective-permute-start(bf16[512,768]{1,0:T(8,128)(2,1)} %slice.20), channel_id=1, source_target_pairs={{0,6},{2,0},{4,2},{6,4},{1,7},{3,1},{5,3},{7,5},{8,14},{10,8},{12,... | collective-permute-start | bytes 2359304 | tf_op jit(solution)/shard_map/ppermute | solution.py:300
  116.4 2.5 collective-permute-start.17
  116.4 3.6 %collective-permute-start.18 = (bf16[512,768]{1,0:T(8,128)(2,1)}, bf16[512,768]{1,0:T(8,128)(2,1)S(1)}, u32[]{:S(2)}, u32[]{:S(2)}) collective-permute-start(bf16[512,768]{1,0:T(8,128)(2,1)} %collective-permute-done.16.b0), channel_id=1, source_target_pairs={{0,1},{1,0},{2,3},{3,2},{4,5},{5,4},{6,7},{7,6},{8,9},{9,8},{10,11... | collective-permute-start | bytes 2359304 | tf_op jit(solution)/shard_map/ppermute | solution.py:310
  118.9 1.1 copy-start.4
  126.8 1.5 copy-start.2
  128.3 61.6 %collective-permute-start.25 = (bf16[4,2,128,768]{3,2,1,0:T(8,128)(2,1)S(1)}, bf16[4,2,128,768]{3,2,1,0:T(8,128)(2,1)S(1)}, u32[]{:S(2)}, u32[]{:S(2)}) collective-permute-start(bf16[4,2,128,768]{3,2,1,0:T(8,128)(2,1)S(1)} %copy-done.2), channel_id=1, source_target_pairs={{0,8},{8,16},{16,24},{24,0},{1,9},{9,17},{17,25},{25,1},{2,10},{10... | collective-permute-start | bytes 4718600 | tf_op jit(solution)/shard_map/ppermute | solution.py:300
  128.3 61.6 %collective-permute-start.24 = (bf16[4,2,128,768]{3,2,1,0:T(8,128)(2,1)S(1)}, bf16[4,2,128,768]{3,2,1,0:T(8,128)(2,1)}, u32[]{:S(2)}, u32[]{:S(2)}) collective-permute-start(bf16[4,2,128,768]{3,2,1,0:T(8,128)(2,1)S(1)} %copy-done.2), channel_id=1, source_target_pairs={{0,24},{8,0},{16,8},{24,16},{1,25},{9,1},{17,9},{25,17},{2,26},{10... | collective-permute-start | bytes 4718600 | tf_op jit(solution)/shard_map/ppermute | solution.py:300
  152.9 18.8 %collective-permute-start.21 = (bf16[528,128]{1,0:T(8,128)(2,1)}, bf16[528,128]{1,0:T(8,128)(2,1)S(1)}, u32[]{:S(2)}, u32[]{:S(2)}) collective-permute-start(bf16[528,128]{1,0:T(8,128)(2,1)} %get-tuple-element.63.refs_0_), channel_id=1, source_target_pairs={{0,8},{8,16},{16,24},{24,0},{1,9},{9,17},{17,25},{25,1},{2,10},{10... | collective-permute-start | bytes 405512 | tf_op jit(solution)/shard_map/ppermute | solution.py:300
  152.9 18.8 %collective-permute-start.20 = (bf16[528,128]{1,0:T(8,128)(2,1)}, bf16[528,128]{1,0:T(8,128)(2,1)S(1)}, u32[]{:S(2)}, u32[]{:S(2)}) collective-permute-start(bf16[528,128]{1,0:T(8,128)(2,1)} %get-tuple-element.63.refs_0_), channel_id=1, source_target_pairs={{0,16},{8,24},{16,0},{24,8},{1,17},{9,25},{17,1},{25,9},{2,18},{10... | collective-permute-start | bytes 405512 | tf_op jit(solution)/shard_map/ppermute | solution.py:300
  154.8 16.9 %collective-permute-start.19 = (bf16[528,128]{1,0:T(8,128)(2,1)}, bf16[528,128]{1,0:T(8,128)(2,1)S(1)}, u32[]{:S(2)}, u32[]{:S(2)}) collective-permute-start(bf16[528,128]{1,0:T(8,128)(2,1)} %get-tuple-element.63.refs_0_), channel_id=1, source_target_pairs={{0,24},{8,0},{16,8},{24,16},{1,25},{9,1},{17,9},{25,17},{2,26},{10... | collective-permute-start | bytes 405512 | tf_op jit(solution)/shard_map/ppermute | solution.py:300
  175.0 13.1 %collective-permute-start.23 = (bf16[528,128]{1,0:T(8,128)(2,1)}, bf16[528,128]{1,0:T(8,128)(2,1)S(1)}, u32[]{:S(2)}, u32[]{:S(2)}) collective-permute-start(bf16[528,128]{1,0:T(8,128)(2,1)} %row_state.3), channel_id=1, source_target_pairs={{64,0},{96,32},{65,1},{97,33},{66,2},{98,34},{67,3},{99,35},{68,4}... | collective-permute-start | bytes 405512 | tf_op jit(solution)/shard_map/ppermute | solution.py:306
  176.2 13.7 %collective-permute-start.22 = (bf16[528,128]{1,0:T(8,128)(2,1)}, bf16[528,128]{1,0:T(8,128)(2,1)S(1)}, u32[]{:S(2)}, u32[]{:S(2)}) collective-permute-start(bf16[528,128]{1,0:T(8,128)(2,1)} %row_state.3), channel_id=1, source_target_pairs={{32,0},{64,32},{96,64},{33,1},{65,33},{97,65},{34,2},{66,34},{98,6... | collective-permute-start | bytes 405512 | tf_op jit(solution)/shard_map/ppermute | solution.py:306
  188.1 5.4 %copy-start.16 = (bf16[528,128]{1,0:T(8,128)(2,1)}, bf16[528,128]{1,0:T(8,128)(2,1)S(1)}, u32[]{:S(2)}) copy-start(bf16[528,128]{1,0:T(8,128)(2,1)S(1)} %collective-permute-done.23.refs_4_) | copy-start | bytes 405508
  189.9 3.6 %copy-start.17 = (bf16[528,128]{1,0:T(8,128)(2,1)}, bf16[528,128]{1,0:T(8,128)(2,1)S(1)}, u32[]{:S(2)}) copy-start(bf16[528,128]{1,0:T(8,128)(2,1)S(1)} %collective-permute-done.22.refs_3_) | copy-start | bytes 405508
  189.9 3.6 %copy-start.3 = (bf16[4,2,128,768]{3,2,1,0:T(8,128)(2,1)}, bf16[4,2,128,768]{3,2,1,0:T(8,128)(2,1)S(1)}, u32[]{:S(2)}) copy-start(bf16[4,2,128,768]{3,2,1,0:T(8,128)(2,1)S(1)} %collective-permute-done.25.left) | copy-start | bytes 4718596
  193.5 19.9 %collective-permute-start.27 = (bf16[2,2,128,768]{3,2,1,0:T(8,128)(2,1)}, bf16[2,2,128,768]{3,2,1,0:T(8,128)(2,1)S(1)}, u32[]{:S(2)}, u32[]{:S(2)}) collective-permute-start(bf16[2,2,128,768]{3,2,1,0:T(8,128)(2,1)} %slice.23), channel_id=1, source_target_pairs={{0,8},{8,16},{16,24},{24,0},{1,9},{9,17},{17,25},{25,1},{2,10},{10... | collective-permute-start | bytes 2359304 | tf_op jit(solution)/shard_map/ppermute | solution.py:300
  193.6 19.8 %collective-permute-start.26 = (bf16[2,2,128,768]{3,2,1,0:T(8,128)(2,1)}, bf16[2,2,128,768]{3,2,1,0:T(8,128)(2,1)S(1)}, u32[]{:S(2)}, u32[]{:S(2)}) collective-permute-start(bf16[2,2,128,768]{3,2,1,0:T(8,128)(2,1)} %slice.22), channel_id=1, source_target_pairs={{0,24},{8,0},{16,8},{24,16},{1,25},{9,1},{17,9},{25,17},{2,26},{10... | collective-permute-start | bytes 2359304 | tf_op jit(solution)/shard_map/ppermute | solution.py:300
  213.4 0.9 copy-start.6
  213.4 1.1 copy-start.7
  229.4 17.5 %collective-permute-start.30 = (bf16[512,384]{1,0:T(8,128)(2,1)S(1)}, bf16[512,384]{1,0:T(8,128)(2,1)S(1)}, u32[]{:S(2)}, u32[]{:S(2)}) collective-permute-start(bf16[512,384]{1,0:T(8,128)(2,1)S(1)} %get-tuple-element.83), channel_id=1, source_target_pairs={{0,24},{8,0},{16,8},{24,16},{1,25},{9,1},{17,9},{25,17},{2,26},{10... | collective-permute-start | bytes 1179656 | tf_op jit(solution)/shard_map/ppermute | solution.py:300
  232.1 14.7 %collective-permute-start.29 = (bf16[512,384]{1,0:T(8,128)(2,1)S(1)}, bf16[512,384]{1,0:T(8,128)(2,1)S(1)}, u32[]{:S(2)}, u32[]{:S(2)}) collective-permute-start(bf16[512,384]{1,0:T(8,128)(2,1)S(1)} %get-tuple-element.84), channel_id=1, source_target_pairs={{0,16},{8,24},{16,0},{24,8},{1,17},{9,25},{17,1},{25,9},{2,18},{10... | collective-permute-start | bytes 1179656 | tf_op jit(solution)/shard_map/ppermute | solution.py:300
  232.1 18.1 %collective-permute-start.28 = (bf16[512,384]{1,0:T(8,128)(2,1)S(1)}, bf16[512,384]{1,0:T(8,128)(2,1)S(1)}, u32[]{:S(2)}, u32[]{:S(2)}) collective-permute-start(bf16[512,384]{1,0:T(8,128)(2,1)S(1)} %get-tuple-element.85), channel_id=1, source_target_pairs={{0,8},{8,16},{16,24},{24,0},{1,9},{9,17},{17,25},{25,1},{2,10},{10... | collective-permute-start | bytes 1179656 | tf_op jit(solution)/shard_map/ppermute | solution.py:300
  246.9 3.4 %copy-start.12 = (bf16[512,384]{1,0:T(8,128)(2,1)}, bf16[512,384]{1,0:T(8,128)(2,1)S(1)}, u32[]{:S(2)}) copy-start(bf16[512,384]{1,0:T(8,128)(2,1)S(1)} %collective-permute-done.30.refs_2_) | copy-start | bytes 1179652
  246.9 3.4 %copy-start.13 = (bf16[512,384]{1,0:T(8,128)(2,1)}, bf16[512,384]{1,0:T(8,128)(2,1)S(1)}, u32[]{:S(2)}) copy-start(bf16[512,384]{1,0:T(8,128)(2,1)S(1)} %collective-permute-done.29.refs_1_) | copy-start | bytes 1179652
  (5 other events, 3.7 us)
Sparse Core Ops, SparseCore 0:
  80.5 58.8 all-gather.2
Sparse Core Ops, SparseCore 1:
  126.9 67.8 reduce-scatter.1

commit v2 on v0

--- a/solution.py
+++ b/solution.py
@@ -212,51 +212,38 @@
         carry[c, :] = jnp.where(keep, state, 0.0) + dot(kept, high, TN)
 
 
-def weight_kernel(turned, grad, first, second):
-    part = dot(turned[...], grad[0], NN).astype(BF16)
-    rows, cols = part.shape[0] // 2, part.shape[1] // 2
-    for h in range(2):
-        c = slice(h * cols, (h + 1) * cols)
-        first[h, 0] = part[:rows, c]
-        second[0, h] = part[rows:, c]
-
-
-def middle_sum_kernel(places, a, a1, a2, a3, b, b1, b2, b3, *outs):
-    for own, others, base in ((a, (a1, a2, a3), 0), (b, (b1, b2, b3), 4)):
-        total = own[0, 0].astype(F32)
-        for other in others:
-            total = total + other[0].astype(F32)
-        for s in range(4):
-
-            @pl.when(pl.program_id(0) == s)
-            def _():
-                outs[base + s][...] = total.astype(outs[base + s].dtype)
-
-
-def last_sum_kernel(a, a1, a2, a3, b, b1, b2, b3, out):
-    half = a.shape[0]
-    for parts, rows in (((a, a1, a2, a3), slice(0, half)), ((b, b1, b2, b3), slice(half, 2 * half))):
-        total = parts[0][...].astype(F32)
-        for part in parts[1:]:
-            total = total + part[...].astype(F32)
-        out[rows, :] = total
-
-
-def attended_kernel(places, low, own, right, left, far_a, far_b, out, columns, sems):
+def put_columns(part, out):
+    low = part.astype(BF16)
+    half = low.shape[1] // 2
+    out[0, 0] = low[:, :half]
+    out[0, 1] = low[:, half:]
+
+
+def weight_kernel(turned, grad, out):
+    put_columns(dot(turned[...], grad[0], NN), out)
+
+
+def sum_kernel(place, own, *refs):
+    total = own[0].astype(F32)
+    for ref in refs[:-1]:
+        total = total + ref[...].astype(F32)
+    refs[-1][...] = total
+
+
+def attended_kernel(places, *refs):
+    near, far, columns_of = refs[:6], refs[6:10], refs[10:18]
+    out, columns, sems = refs[18:]
     i = pl.program_id(0)
-    lines = 4
-    half = lines // 2
 
     def copies():
-        for y, pieces in enumerate(((own,), (right,), (far_a, far_b), (left,))):
-            for x in range(lines):
-                piece = pieces[0] if len(pieces) == 1 else pieces[x // half]
-                at = x if len(pieces) == 1 else x % half
+        for y in range(4):
+            for x in range(4):
                 for o in range(2):
                     group = places[2 * y + o]
                     row = pl.multiple_of(places[8 + x] * HEAD, HEAD)
                     to = columns.at[group, pl.ds(row, HEAD)]
-                    yield pltpu.make_async_copy(piece.at[at, o], to, sems.at[8 * y + 2 * x + o])
+                    piece = columns_of[2 * y + x // 2].at[x % 2, o]
+                    yield pltpu.make_async_copy(piece, to, sems.at[8 * y + 2 * x + o])
 
     @pl.when(i == 0)
     def _():
@@ -265,9 +252,12 @@
         for copy in copies():
             copy.wait()
 
+    early = i < pl.num_programs(0) // 2
+    pieces = [ref[...] for ref in near]
+    pieces += [jnp.where(early, far[p][...], far[p + 1][...]) for p in (0, 2)]
     total = None
-    for j in range(low.shape[0]):
-        part = dot(low[j], columns[j], NN)
+    for p, piece in enumerate(pieces):
+        part = dot(piece, columns[places[12 + p]], NN)
         total = part if total is None else total + part
     out[...] = total.astype(BF16)
 
@@ -291,60 +281,50 @@
     return lax.dynamic_index_in_dim(value, index, axis, keepdims=False)
 
 
-def exchanged(state, step):
+def exchanged(state, step, extra=()):
     beside = [turned_by(state, "cy", step * s) for s in range(1, 4)]
+    beside, extra = lax.optimization_barrier((beside, extra))
     row = pl.pallas_call(
         lambda *refs: row_kernel(step > 0, *refs),
         out_shape=jax.ShapeDtypeStruct(state.shape, state.dtype),
         name="row_state",
     )(state, *beside)
-    return beside + [moved_by(row, "cx", step * s) for s in range(1, 3)]
-
-
-def column_pieces(out_weight, share, cx, core):
+    return beside + [moved_by(row, "cx", step * s) for s in range(1, 3)], extra
+
+
+def column_strip(out_weight, share, cx):
     cy, z = lax.axis_index("cy"), lax.axis_index("z")
     at = (cx * HEAD, (z - cy) % 4 * 2 * share)
     sent = lax.dynamic_slice(out_weight, at, (HEAD, 2 * share))
     pairs = [(4 * y + (i + y) % 4, 4 * y + i) for y in range(4) for i in range(4)]
-    held = lax.ppermute(sent, ("cy", "z"), pairs)
-    mine = lax.dynamic_slice(held, (0, core * share), (HEAD, share))
-    other = lax.dynamic_slice(held, (0, (1 - core) * share), (HEAD, share))
+    return lax.ppermute(sent, ("cy", "z"), pairs)
+
+
+def column_pieces(strip, share, core):
+    mine = lax.dynamic_slice(strip, (0, core * share), (HEAD, share))
+    other = lax.dynamic_slice(strip, (0, (1 - core) * share), (HEAD, share))
     both = jnp.stack([mine, swapped(other)])
-    return jnp.stack([both] + [turned_by(both, "cx", s) for s in range(1, 4)])
-
-
-def scattered_sum(first, second, cx, cy):
-    half, part = first.shape[2:]
-    to_y = [turned_by(pick(first, (cy + s) % 4), "cy", s) for s in range(1, 4)]
-    to_x = [turned_by(pick(second, (cx + s) % 4), "cx", s) for s in range(1, 4)]
-
-    def own(line, start):
-        shape = (1, 1, half, part)
-        return pl.BlockSpec(shape, lambda i, p: (p[line], (p[start] + i) % 4, 0, 0))
-
-    def piece(start):
-        return pl.BlockSpec((1, half, part), lambda i, p: ((p[start] + i) % 4, 0, 0))
-
-    kinds = [F32, BF16, BF16, BF16] * 2
-    sums = pl.pallas_call(
-        middle_sum_kernel,
+    lines = [both] + [turned_by(both, "cx", s) for s in range(1, 4)]
+    return jnp.stack(lines[:2]), jnp.stack(lines[2:])
+
+
+def row_sum(mine, cy):
+    got = [turned_by(pick(mine, (cy + s) % 4), "cy", s) for s in range(1, 4)]
+    height, part = mine.shape[1:]
+    block = (CHUNK, part)
+    return pl.pallas_call(
+        sum_kernel,
         grid_spec=pltpu.PrefetchScalarGridSpec(
             num_scalar_prefetch=1,
-            grid=(4,),
-            in_specs=[own(1, 0)] + [piece(0)] * 3 + [own(0, 1)] + [piece(1)] * 3,
-            out_specs=[pl.BlockSpec((half, part), lambda i, p: (0, 0))] * 8,
+            grid=(height // CHUNK,),
+            in_specs=[pl.BlockSpec((1, *block), lambda i, p: (p[0], i, 0))]
+            + [pl.BlockSpec(block, lambda i, p: (i, 0))] * 3,
+            out_specs=pl.BlockSpec(block, lambda i, p: (i, 0)),
         ),
-        out_shape=[jax.ShapeDtypeStruct((half, part), kind) for kind in kinds],
-        compiler_params=params(),
-        name="middle_sum",
-    )(jnp.stack([cx, cy]), first, *to_y, second, *to_x)
-    to_x = [turned_by(sums[s], "cx", s) for s in range(1, 4)]
-    to_y = [turned_by(sums[4 + s], "cy", s) for s in range(1, 4)]
-    return pl.pallas_call(
-        last_sum_kernel,
-        out_shape=jax.ShapeDtypeStruct((2 * half, part), F32),
+        out_shape=jax.ShapeDtypeStruct((height, part), F32),
+        compiler_params=params(),
         name="last_sum",
-    )(sums[0], *to_x, sums[4], *to_y)
+    )(cy[None], mine, *got)
 
 
 def body(queries, keys, values, doc_ids, out_weight, grad_out):
@@ -368,9 +348,9 @@
     table = jnp.broadcast_to(table[:, None], (16, HEAD))
 
     tail = pl.pallas_call(tail_kernel, out_shape=payload, name="tail")(keys, values, dcol, table)
-    arrived = exchanged(tail, 1)
-
-    own = column_pieces(out_weight, share, cx, core)
+    strip = column_strip(out_weight, share, cx)
+    arrived, strip = exchanged(tail, 1, strip)
+    own = column_pieces(strip, share, core)
     arrived, own = lax.optimization_barrier((arrived, own))
 
     row_block = pl.BlockSpec((1, CHUNK), lambda i: (0, i))
@@ -398,26 +378,29 @@
         name="forward",
     )(queries, keys, values, dcol, drow, table, *arrived)
 
-    low_whole = lax.all_gather(low, TENSOR, axis=0)
-
-    right = turned_by(own, "cy", -1)
-    left = turned_by(own, "cy", 1)
-    turned, right, left = lax.optimization_barrier((turned, right, left))
-
-    pair = (width // 2, share // 2)
-    first, second = pl.pallas_call(
+    early = [turned_by(own[0], "cy", s) for s in (-1, 1)]
+    turned, early = lax.optimization_barrier((turned, early))
+    later = [turned_by(own[1], "cy", s) for s in (-1, 1)]
+
+    term = pl.pallas_call(
         weight_kernel,
         grid=(groups,),
         in_specs=[whole((width, rows)), pl.BlockSpec((1, rows, share), lambda j: (j, 0, 0))],
-        out_specs=[
-            pl.BlockSpec((2, 1, *pair), lambda j: (j % 2, j // 2, 0, 0)),
-            pl.BlockSpec((1, 2, *pair), lambda j: (j // 2, j % 2, 0, 0)),
-        ],
-        out_shape=[jax.ShapeDtypeStruct((4, 4, *pair), BF16)] * 2,
+        out_specs=pl.BlockSpec((1, 2, width, share // 2), lambda j: (j // 2, j % 2, 0, 0)),
+        out_shape=jax.ShapeDtypeStruct((4, 4, width, share // 2), BF16),
         compiler_params=params(),
         name="weight_grad",
     )(turned, grad_whole)
-    grad_weight = scattered_sum(first, second, cx, cy)
+    term, low = lax.optimization_barrier((term, low))
+    grad_part = lax.psum_scatter(term, "cx", scatter_dimension=0, tiled=True)[0]
+
+    half_rows = rows // 2
+    above = turned_by(low, "z", -1)
+    below = turned_by(low, "z", 1)
+    far_a = turned_by(above[:half_rows], "z", -1)
+    far_b = turned_by(below[half_rows:], "z", 1)
+    near = [low, swapped(low), above, swapped(above), below, swapped(below)]
+    far = [far_a, far_b, swapped(far_a), swapped(far_b)]
 
     grad_opened, head = pl.pallas_call(
         cotangent_kernel,
@@ -436,10 +419,12 @@
         compiler_params=params(),
         name="cotangent",
     )(grad_whole, out_weight, opened, queries, dcol, table)
-    returned = exchanged(head, -1)
-
-    far_a = turned_by(right[:2], "cy", -1)
-    far_b = turned_by(left[2:], "cy", 1)
+    head, later = lax.optimization_barrier((head, later))
+    returned, _ = exchanged(head, -1)
+
+    returned, early, later = lax.optimization_barrier((returned, early, later))
+    across = (turned_by(early[0], "cy", -1), turned_by(later[1], "cy", 1))
+    columns = [*own, early[0], later[0], *across, early[1], later[1]]
 
     grad_query = pl.pallas_call(
         query_kernel,
@@ -466,15 +451,20 @@
         name="grad_key_value",
     )(grad_opened, queries, keys, values, dcol, drow, table, *returned)
 
-    around = [2 * ((z + cy + s) % 4) + (core if o == 0 else 1 - core) for s in range(4) for o in range(2)]
+    sides = (core, 1 - core)
+    around = [2 * ((z + cy + s) % 4) + side for s in range(4) for side in sides]
     heads_at = [(cx - s) % 4 for s in range(4)]
+    groups_at = [2 * ((z + s) % 4) + side for s in (0, 1, 3, 2) for side in sides]
     held = pl.BlockSpec(memory_space=pl.ANY)
+    every = pl.BlockSpec((CHUNK, width), lambda i, at: (i, 0))
+    upper = pl.BlockSpec((CHUNK, width), lambda i, at: (jnp.minimum(i, blocks // 2 - 1), 0))
+    lower = pl.BlockSpec((CHUNK, width), lambda i, at: (jnp.maximum(i - blocks // 2, 0), 0))
     attended = pl.pallas_call(
         attended_kernel,
         grid_spec=pltpu.PrefetchScalarGridSpec(
             num_scalar_prefetch=1,
             grid=(blocks,),
-            in_specs=[pl.BlockSpec((groups, CHUNK, width), lambda i, at: (0, i, 0))] + [held] * 5,
+            in_specs=[every] * 6 + [upper, lower] * 2 + [held] * 8,
             out_specs=pl.BlockSpec((CHUNK, share), lambda i, at: (i, 0)),
             scratch_shapes=[
                 pltpu.VMEM((groups, width, share), BF16),
@@ -484,7 +474,9 @@
         out_shape=jax.ShapeDtypeStruct((rows, share), BF16),
         compiler_params=params(),
         name="attended",
-    )(jnp.stack(around + heads_at), low_whole, own, right, left, far_a, far_b)
+    )(jnp.stack(around + heads_at + groups_at), *near, *far, *columns)
+    grad_part, attended, grad_key = lax.optimization_barrier((grad_part, attended, grad_key))
+    grad_weight = row_sum(grad_part, cy)
     return attended, grad_query, grad_key, grad_value, grad_weight
 
 

time: 246 us -> 236 us (0.959)
  starting transfers between devices: 69.4 us -> 43.8 us
  waiting for transfers between devices: 70.6 us -> 91.7 us
  Pallas kernels: 77.2 us -> 71.6 us
    ppermute x25 -> x22, starting transfers between devices: 60.8 us -> 34.1 us  [turned_by(): lax.ppermute(value, axis, [(i, (i + step) % size) for i in range(size)])]
    ppermute x25 -> x22, waiting for transfers between devices: 60.3 us -> 74.3 us  [turned_by(): lax.ppermute(value, axis, [(i, (i + step) % size) for i in range(size)])]
    ppermute x4, waiting for transfers between devices: 8.14 us -> 15.2 us  [moved_by(): return lax.ppermute(value, axis, pairs)]
    pallas_call x2 -> x1, Pallas kernels: 8.8 us -> 2.3 us  [row_sum(): pl.pallas_call(sum_kernel, grid_spec=pltpu.PrefetchScalarGridSpec(num_sca...]
    unnamed x52 -> x54, local copies, waits for them, and re-layouts: 3.65 us -> 7.01 us
  transfers between devices with their start and end apart: 33 -> 35, of which waited for: 10 -> 19; matrix products, arithmetic and copies ran while one was open for 4% -> 2% of each run, Pallas kernels for 30% -> 24%
where the time goes in v2:
time: 236 us; the launch traced here: 235 us
  waiting for transfers between devices  91.7 us (39%)
  Pallas kernels  71.6 us (30%)
  starting transfers between devices  43.8 us (19%)
  between operations  14.4 us (6%)
  local copies, waits for them, and re-layouts  13.4 us (6%)
    ppermute x22, waiting for transfers between devices, turned_by(): lax.ppermute(value, axis, [(i, (i + step) % size) for i in range(size)])  74.3 us
    ppermute x22, starting transfers between devices, turned_by(): lax.ppermute(value, axis, [(i, (i + step) % size) for i in range(size)])  34.1 us
    pallas_call x1, Pallas kernels, body(): pl.pallas_call(cotangent_kernel, grid=(blocks,), in_specs=[pl.BlockSpec((...  15.8 us
    ppermute x4, waiting for transfers between devices, moved_by(): return lax.ppermute(value, axis, pairs)  15.2 us
    pallas_call x1, Pallas kernels, body(): pl.pallas_call(attended_kernel, grid_spec=pltpu.PrefetchScalarGridSpec(nu...  13.7 us
    pallas_call x1, Pallas kernels, body(): pl.pallas_call(weight_kernel, grid=(groups,), in_specs=[whole((width, row...  13 us
    ppermute x4, starting transfers between devices, moved_by(): return lax.ppermute(value, axis, pairs)  7.92 us
    pallas_call x1, Pallas kernels, body(): pl.pallas_call(key_value_kernel, grid=(blocks,), in_specs=[rows_of(width,...  7.43 us
  transfers between devices with their start and end apart: 35, of which 19 were waited for; matrix products, arithmetic and copies ran while one was open for 2% of the time, Pallas kernels for 24%

profile of v2, /device:TPU:2, one launch (start us, length us, event | category | flops | bytes accessed | tf_op | source)
XLA Modules:
  0.0 235.1 jit_solution(9617970166302929418)
XLA Ops:
  11.7 2.8 %tail.1.refs_0_ = bf16[528,128]{1,0:T(8,128)(2,1)} custom-call(bf16[1024,512]{1,0:T(8,128)(2,1)} %k.7, bf16[1024,512]{1,0:T(8,128)(2,1)} %v.7, f32[1024,128]{1,0:T(8,128)} %broadcast_in_dim.10.dcol, f32[16,128]{1,0:T(8,128)} %broadcast_in_dim.24.table), custom_call_target="tpu_custom_call" | custom-call | tf_op jit(solution)/shard_map/tail/pallas_call | solution.py:350
  14.6 6.2 %collective-permute-start.2 = (bf16[528,128]{1,0:T(8,128)(2,1)}, bf16[528,128]{1,0:T(8,128)(2,1)S(1)}, u32[]{:S(2)}, u32[]{:S(2)}) collective-permute-start(bf16[528,128]{1,0:T(8,128)(2,1)} %tail.1.refs_0_), channel_id=1, source_target_pairs={{0,24},{8,0},{16,8},{24,16},{1,25},{9,1},{17,9},{25,17},{2,26},{10... | collective-permute-start | bytes 405512 | tf_op jit(solution)/shard_map/ppermute | solution.py:267
  20.7 2.8 %collective-permute-start.1 = (bf16[528,128]{1,0:T(8,128)(2,1)}, bf16[528,128]{1,0:T(8,128)(2,1)S(1)}, u32[]{:S(2)}, u32[]{:S(2)}) collective-permute-start(bf16[528,128]{1,0:T(8,128)(2,1)} %tail.1.refs_0_), channel_id=1, source_target_pairs={{0,16},{8,24},{16,0},{24,8},{1,17},{9,25},{17,1},{25,9},{2,18},{10... | collective-permute-start | bytes 405512 | tf_op jit(solution)/shard_map/ppermute | solution.py:267
  24.3 1.2 collective-permute-done.2.refs_3_.refs_2_
  25.5 3.3 %collective-permute-done.1.refs_2_.refs_1_ = bf16[528,128]{1,0:T(8,128)(2,1)S(1)} collective-permute-done((bf16[528,128]{1,0:T(8,128)(2,1)}, bf16[528,128]{1,0:T(8,128)(2,1)S(1)}, u32[]{:S(2)}, u32[]{:S(2)}) %collective-permute-start.1) | collective-permute-done | bytes 135200 | tf_op jit(solution)/shard_map/ppermute | solution.py:267
  28.7 1.9 collective-permute-done.refs_1_.refs_0_
  30.7 1.4 collective-permute-done.6
  32.2 1.6 collective-permute-start.7
  33.8 1.1 collective-permute-start.8
  34.9 2.2 collective-permute-start.9
  37.1 1.9 row_state.2
  38.9 2.2 collective-permute-start.5
  41.1 1.9 collective-permute-start.4
  43.0 1.2 collective-permute-done.7
  44.3 2.9 %collective-permute-done.8 = bf16[2,128,768]{2,1,0:T(8,128)(2,1)S(1)} collective-permute-done((bf16[2,128,768]{2,1,0:T(8,128)(2,1)S(1)}, bf16[2,128,768]{2,1,0:T(8,128)(2,1)S(1)}, u32[]{:S(2)}, u32[]{:S(2)}) %collective-permute-start.8) | collective-permute-done | bytes 393248 | tf_op jit(solution)/shard_map/ppermute | solution.py:267
  47.3 6.6 %collective-permute-done.9 = bf16[2,128,768]{2,1,0:T(8,128)(2,1)S(1)} collective-permute-done((bf16[2,128,768]{2,1,0:T(8,128)(2,1)S(1)}, bf16[2,128,768]{2,1,0:T(8,128)(2,1)S(1)}, u32[]{:S(2)}, u32[]{:S(2)}) %collective-permute-start.9) | collective-permute-done | bytes 393248 | tf_op jit(solution)/shard_map/ppermute | solution.py:267
  54.8 2.9 %collective-permute-done.4.refs_3_ = bf16[528,128]{1,0:T(8,128)(2,1)S(1)} collective-permute-done((bf16[528,128]{1,0:T(8,128)(2,1)}, bf16[528,128]{1,0:T(8,128)(2,1)S(1)}, u32[]{:S(2)}, u32[]{:S(2)}) %collective-permute-start.4) | collective-permute-done | bytes 135200 | tf_op jit(solution)/shard_map/ppermute | solution.py:273
  58.5 2.5 %collective-permute-start.10 = (bf16[2,2,128,768]{3,2,1,0:T(8,128)(2,1)S(1)}, bf16[2,2,128,768]{3,2,1,0:T(8,128)(2,1)S(1)}, u32[]{:S(2)}, u32[]{:S(2)}) collective-permute-start(bf16[2,2,128,768]{3,2,1,0:T(8,128)(2,1)S(1)} %pad_maximum_fusion.refs_10_), channel_id=1, source_target_pairs={{0,24},{8,0},{16,8},{24,16},{1,25},{9,1},{17,9},{25,17},{2,26},{10... | collective-permute-start | bytes 2359304 | tf_op jit(solution)/shard_map/ppermute | solution.py:267
  61.0 6.9 %forward.1 = (f32[1024,512]{1,0:T(8,128)}, bf16[1024,512]{1,0:T(8,128)(2,1)}, bf16[512,1024]{1,0:T(8,128)(2,1)}, bf16[4,512,128]{2,1,0:T(8,128)(2,1)}) custom-call(bf16[1024,512]{1,0:T(8,128)(2,1)} %q.5, bf16[1024,512]{1,0:T(8,128)(2,1)} %k.7, bf16[1024,512]{1,0:T(8,128)(2,1)} %v.7, f32[1024,128]{1,0:T(8,128)} %broadcast_in_dim.10.dcol, f32[1,1024]{1,0:T(1,128)} %bitcast.47, ...), custom_call_target="tpu_custom_call" | custom-call | tf_op jit(solution)/shard_map/forward/pallas_call | solution.py:358
  67.9 9.9 %collective-permute-done.11.refs_16_ = bf16[2,2,128,768]{3,2,1,0:T(8,128)(2,1)S(1)} collective-permute-done((bf16[2,2,128,768]{3,2,1,0:T(8,128)(2,1)S(1)}, bf16[2,2,128,768]{3,2,1,0:T(8,128)(2,1)S(1)}, u32[]{:S(2)}, u32[]{:S(2)}) %collective-permute-start.11) | collective-permute-done | bytes 786464 | tf_op jit(solution)/shard_map/ppermute | solution.py:267
  79.7 13.0 %weight_grad.1 = bf16[4,4,512,384]{3,2,1,0:T(8,128)(2,1)} custom-call(bf16[512,1024]{1,0:T(8,128)(2,1)} %get-tuple-element.58.turned, bf16[8,1024,768]{2,1,0:T(8,128)(2,1)} %bitcast.39), custom_call_target="tpu_custom_call" | custom-call | tf_op jit(solution)/shard_map/weight_grad/pallas_call | solution.py:385
  92.7 1.6 collective-permute-start.22
  94.3 1.8 collective-permute-start.21
  96.0 1.6 collective-permute-start.15
  97.7 1.6 collective-permute-start.13
  99.2 15.8 %cotangent.1 = (f32[1024,512]{1,0:T(8,128)}, bf16[528,128]{1,0:T(8,128)(2,1)}) custom-call(bf16[8,1024,768]{2,1,0:T(8,128)(2,1)} %bitcast.40, bf16[512,6144]{1,0:T(8,128)(2,1)} %weight.1, f32[1024,512]{1,0:T(8,128)} %get-tuple-element.63.opened, bf16[1024,512]{1,0:T(8,128)(2,1)} %q.5, f32[1024,128]{1,0:T(8,128)} %broadcast_in_dim.10.dcol, ...), custom_call_target="tpu_custom_call" | custom-call | tf_op jit(solution)/shard_map/cotangent/pallas_call | solution.py:405
  116.9 2.2 collective-permute-start.24
  119.0 8.4 %collective-permute-done.25.refs_3_.refs_2_ = bf16[528,128]{1,0:T(8,128)(2,1)S(1)} collective-permute-done((bf16[528,128]{1,0:T(8,128)(2,1)}, bf16[528,128]{1,0:T(8,128)(2,1)S(1)}, u32[]{:S(2)}, u32[]{:S(2)}) %collective-permute-start.25) | collective-permute-done | bytes 135200 | tf_op jit(solution)/shard_map/ppermute | solution.py:267
  127.4 5.6 %collective-permute-done.23.refs_1_.refs_0_ = bf16[528,128]{1,0:T(8,128)(2,1)S(1)} collective-permute-done((bf16[528,128]{1,0:T(8,128)(2,1)}, bf16[528,128]{1,0:T(8,128)(2,1)S(1)}, u32[]{:S(2)}, u32[]{:S(2)}) %collective-permute-start.23) | collective-permute-done | bytes 135200 | tf_op jit(solution)/shard_map/ppermute | solution.py:267
  133.6 1.9 row_state.3
  135.5 1.3 collective-permute-start.27
  136.8 2.6 %collective-permute-start.26 = (bf16[528,128]{1,0:T(8,128)(2,1)}, bf16[528,128]{1,0:T(8,128)(2,1)S(1)}, u32[]{:S(2)}, u32[]{:S(2)}) collective-permute-start(bf16[528,128]{1,0:T(8,128)(2,1)} %row_state.3), channel_id=1, source_target_pairs={{32,0},{64,32},{96,64},{33,1},{65,33},{97,65},{34,2},{66,34},{98,6... | collective-permute-start | bytes 405512 | tf_op jit(solution)/shard_map/ppermute | solution.py:273
  139.4 9.3 %collective-permute-done.27.refs_4_ = bf16[528,128]{1,0:T(8,128)(2,1)S(1)} collective-permute-done((bf16[528,128]{1,0:T(8,128)(2,1)}, bf16[528,128]{1,0:T(8,128)(2,1)S(1)}, u32[]{:S(2)}, u32[]{:S(2)}) %collective-permute-start.27) | collective-permute-done | bytes 135200 | tf_op jit(solution)/shard_map/ppermute | solution.py:273
  148.6 2.2 collective-permute-done.26.refs_3_
  150.9 1.7 collective-permute-start.28
  152.7 1.3 slice.18
  154.0 3.0 %collective-permute-start.17 = (bf16[512,512]{1,0:T(8,128)(2,1)S(1)}, bf16[512,512]{1,0:T(8,128)(2,1)}, u32[]{:S(2)}, u32[]{:S(2)}) collective-permute-start(bf16[512,512]{1,0:T(8,128)(2,1)S(1)} %slice.18), channel_id=1, source_target_pairs={{0,6},{2,0},{4,2},{6,4},{1,7},{3,1},{5,3},{7,5},{8,14},{10,8},{12,... | collective-permute-start | bytes 1572872 | tf_op jit(solution)/shard_map/ppermute | solution.py:267
  157.6 12.2 %collective-permute-done.28.refs_14_ = bf16[2,2,128,768]{3,2,1,0:T(8,128)(2,1)S(1)} collective-permute-done((bf16[2,2,128,768]{3,2,1,0:T(8,128)(2,1)}, bf16[2,2,128,768]{3,2,1,0:T(8,128)(2,1)S(1)}, u32[]{:S(2)}, u32[]{:S(2)}) %collective-permute-start.28) | collective-permute-done | bytes 786464 | tf_op jit(solution)/shard_map/ppermute | solution.py:267
  171.8 7.4 %grad_key_value.1 = (bf16[1024,512]{1,0:T(8,128)(2,1)}, bf16[1024,512]{1,0:T(8,128)(2,1)}) custom-call(f32[1024,512]{1,0:T(8,128)} %get-tuple-element.77.go, bf16[1024,512]{1,0:T(8,128)(2,1)} %q.5, bf16[1024,512]{1,0:T(8,128)(2,1)} %k.7, bf16[1024,512]{1,0:T(8,128)(2,1)} %v.7, f32[1024,128]{1,0:T(8,128)} %broadcast_in_dim.10.dcol, f32[1,1024]{1,0:T(1,128)} %bitcast.48, ...), custom_call_target="tpu_custom_call" | custom-call | tf_op jit(solution)/shard_map/grad_key_value/pallas_call | solution.py:441
  179.3 10.0 %collective-permute-done.29.refs_15_ = bf16[2,2,128,768]{3,2,1,0:T(8,128)(2,1)} collective-permute-done((bf16[2,2,128,768]{3,2,1,0:T(8,128)(2,1)S(1)}, bf16[2,2,128,768]{3,2,1,0:T(8,128)(2,1)}, u32[]{:S(2)}, u32[]{:S(2)}) %collective-permute-start.29) | collective-permute-done | bytes 786464 | tf_op jit(solution)/shard_map/ppermute | solution.py:267
  190.3 13.7 %attended.1 = bf16[1024,768]{1,0:T(8,128)(2,1)} custom-call(s32[20]{0:T(128)} %stack.119.places, bf16[1024,512]{1,0:T(8,128)(2,1)} %get-tuple-element.61.refs_0_, bf16[1024,512]{1,0:T(8,128)(2,1)} %collective-permute-done.12.refs_1_, bf16[1024,512]{1,0:T(8,128)(2,1)} %collective-permute-done.13.refs_2_, bf16[1024,512]{1,0:T(8,128)(2,1)} %copy-done.4, ...), custom_call_target="tpu_custom_call" | custom-call | tf_op jit(solution)/shard_map/attended/pallas_call | solution.py:462
  204.0 1.4 dynamic-slice_bitcast_fusion
  205.4 1.8 collective-permute-start.32
  208.1 5.9 %grad_query.1 = bf16[1024,512]{1,0:T(8,128)(2,1)} custom-call(f32[1024,512]{1,0:T(8,128)} %get-tuple-element.77.go, bf16[1024,512]{1,0:T(8,128)(2,1)} %k.7, bf16[1024,512]{1,0:T(8,128)(2,1)} %v.7, f32[1024,128]{1,0:T(8,128)} %broadcast_in_dim.10.dcol, f32[1,1024]{1,0:T(1,128)} %bitcast.49, f32[16,128]{1,0:T(8,128)} %broadcast_in_dim.24.table, ...), custom_call_target="tpu_custom_call" | custom-call | tf_op jit(solution)/shard_map/grad_query/pallas_call | solution.py:429
  214.0 3.5 %collective-permute-done.32.refs_2_ = bf16[512,384]{1,0:T(8,128)(2,1)S(1)} collective-permute-done((bf16[512,384]{1,0:T(8,128)(2,1)S(1)}, bf16[512,384]{1,0:T(8,128)(2,1)S(1)}, u32[]{:S(2)}, u32[]{:S(2)}) %collective-permute-start.32) | collective-permute-done | bytes 393248 | tf_op jit(solution)/shard_map/ppermute | solution.py:267
  217.5 3.2 %collective-permute-done.31.refs_1_ = bf16[512,384]{1,0:T(8,128)(2,1)S(1)} collective-permute-done((bf16[512,384]{1,0:T(8,128)(2,1)S(1)}, bf16[512,384]{1,0:T(8,128)(2,1)S(1)}, u32[]{:S(2)}, u32[]{:S(2)}) %collective-permute-start.31) | collective-permute-done | bytes 393248 | tf_op jit(solution)/shard_map/ppermute | solution.py:267
  220.7 4.5 %collective-permute-done.30.refs_0_ = bf16[512,384]{1,0:T(8,128)(2,1)S(1)} collective-permute-done((bf16[512,384]{1,0:T(8,128)(2,1)S(1)}, bf16[512,384]{1,0:T(8,128)(2,1)S(1)}, u32[]{:S(2)}, u32[]{:S(2)}) %collective-permute-start.30) | collective-permute-done | bytes 393248 | tf_op jit(solution)/shard_map/ppermute | solution.py:267
  226.0 2.3 last_sum.1
  (104 shorter events, 16.9 us)
Async XLA Ops:
  7.2 72.5 %all-gather.3.cloned.1.call-start = ((), (), s32[]{:S(2)}) async-start(), calls=%async_computation.2 | async-start | bytes 14155776 | tf_op jit(solution)/shard_map/all_gather | solution.py:340
  7.9 196.1 %reduce-scatter.2.cloned.1.call-start = ((), (), s32[]{:S(2)}) async-start(), calls=%async_computation.1 | async-start | bytes 7864320 | tf_op jit(solution)/shard_map/reduce_scatter | solution.py:395
  9.0 21.6 %collective-permute-start.3 = (bf16[128,1536]{1,0:T(8,128)(2,1)S(1)}, bf16[128,1536]{1,0:T(8,128)(2,1)S(1)}, u32[]{:S(2)}, u32[]{:S(2)}) collective-permute-start(bf16[128,1536]{1,0:T(8,128)(2,1)S(1)} %dynamic_slice.19), channel_id=1, source_target_pairs={{0,0},{2,2},{4,4},{6,6},{10,8},{12,10},{14,12},{8,14},{20,16},{22,... | collective-permute-start | bytes 1179656 | tf_op jit(solution)/shard_map/ppermute | solution.py:300
  9.7 22.5 %copy-start.21 = (f32[1024]{0:T(1024)}, f32[1024]{0:T(1024)S(1)}, u32[]{:S(2)}) copy-start(f32[1024]{0:T(1024)S(1)} %convert_element_type.6) | copy-start | bytes 12292
  14.6 10.9 %collective-permute-start.2 = (bf16[528,128]{1,0:T(8,128)(2,1)}, bf16[528,128]{1,0:T(8,128)(2,1)S(1)}, u32[]{:S(2)}, u32[]{:S(2)}) collective-permute-start(bf16[528,128]{1,0:T(8,128)(2,1)} %tail.1.refs_0_), channel_id=1, source_target_pairs={{0,24},{8,0},{16,8},{24,16},{1,25},{9,1},{17,9},{25,17},{2,26},{10... | collective-permute-start | bytes 405512 | tf_op jit(solution)/shard_map/ppermute | solution.py:267
  20.7 8.0 %collective-permute-start.1 = (bf16[528,128]{1,0:T(8,128)(2,1)}, bf16[528,128]{1,0:T(8,128)(2,1)S(1)}, u32[]{:S(2)}, u32[]{:S(2)}) collective-permute-start(bf16[528,128]{1,0:T(8,128)(2,1)} %tail.1.refs_0_), channel_id=1, source_target_pairs={{0,16},{8,24},{16,0},{24,8},{1,17},{9,25},{17,1},{25,9},{2,18},{10... | collective-permute-start | bytes 405512 | tf_op jit(solution)/shard_map/ppermute | solution.py:267
  23.5 7.1 %collective-permute-start = (bf16[528,128]{1,0:T(8,128)(2,1)}, bf16[528,128]{1,0:T(8,128)(2,1)S(1)}, u32[]{:S(2)}, u32[]{:S(2)}) collective-permute-start(bf16[528,128]{1,0:T(8,128)(2,1)} %tail.1.refs_0_), channel_id=1, source_target_pairs={{0,8},{8,16},{16,24},{24,0},{1,9},{9,17},{17,25},{25,1},{2,10},{10... | collective-permute-start | bytes 405512 | tf_op jit(solution)/shard_map/ppermute | solution.py:267
  25.5 11.6 %copy-start.14 = (bf16[528,128]{1,0:T(8,128)(2,1)}, bf16[528,128]{1,0:T(8,128)(2,1)S(1)}, u32[]{:S(2)}) copy-start(bf16[528,128]{1,0:T(8,128)(2,1)S(1)} %collective-permute-done.2.refs_3_.refs_2_) | copy-start | bytes 405508
  28.7 8.3 %copy-start.15 = (bf16[528,128]{1,0:T(8,128)(2,1)}, bf16[528,128]{1,0:T(8,128)(2,1)S(1)}, u32[]{:S(2)}) copy-start(bf16[528,128]{1,0:T(8,128)(2,1)S(1)} %collective-permute-done.1.refs_2_.refs_1_) | copy-start | bytes 405508
  30.6 6.5 %copy-start.16 = (bf16[528,128]{1,0:T(8,128)(2,1)}, bf16[528,128]{1,0:T(8,128)(2,1)S(1)}, u32[]{:S(2)}) copy-start(bf16[528,128]{1,0:T(8,128)(2,1)S(1)} %collective-permute-done.refs_1_.refs_0_) | copy-start | bytes 405508
  30.6 1.5 collective-permute-start.6
  32.2 12.0 %collective-permute-start.7 = (bf16[2,128,768]{2,1,0:T(8,128)(2,1)S(1)}, bf16[2,128,768]{2,1,0:T(8,128)(2,1)S(1)}, u32[]{:S(2)}, u32[]{:S(2)}) collective-permute-start(bf16[2,128,768]{2,1,0:T(8,128)(2,1)S(1)} %get-tuple-element.95), channel_id=1, source_target_pairs={{0,32},{32,64},{64,96},{96,0},{1,33},{33,65},{65,97},{97,1},{2,34}... | collective-permute-start | bytes 1179656 | tf_op jit(solution)/shard_map/ppermute | solution.py:267
  33.8 13.5 %collective-permute-start.8 = (bf16[2,128,768]{2,1,0:T(8,128)(2,1)S(1)}, bf16[2,128,768]{2,1,0:T(8,128)(2,1)S(1)}, u32[]{:S(2)}, u32[]{:S(2)}) collective-permute-start(bf16[2,128,768]{2,1,0:T(8,128)(2,1)S(1)} %get-tuple-element.95), channel_id=1, source_target_pairs={{0,64},{32,96},{64,0},{96,32},{1,65},{33,97},{65,1},{97,33},{2,66}... | collective-permute-start | bytes 1179656 | tf_op jit(solution)/shard_map/ppermute | solution.py:267
  34.9 19.0 %collective-permute-start.9 = (bf16[2,128,768]{2,1,0:T(8,128)(2,1)S(1)}, bf16[2,128,768]{2,1,0:T(8,128)(2,1)S(1)}, u32[]{:S(2)}, u32[]{:S(2)}) collective-permute-start(bf16[2,128,768]{2,1,0:T(8,128)(2,1)S(1)} %get-tuple-element.95), channel_id=1, source_target_pairs={{0,96},{32,0},{64,32},{96,64},{1,97},{33,1},{65,33},{97,65},{2,98}... | collective-permute-start | bytes 1179656 | tf_op jit(solution)/shard_map/ppermute | solution.py:267
  38.9 15.8 %collective-permute-start.5 = (bf16[528,128]{1,0:T(8,128)(2,1)}, bf16[528,128]{1,0:T(8,128)(2,1)S(1)}, u32[]{:S(2)}, u32[]{:S(2)}) collective-permute-start(bf16[528,128]{1,0:T(8,128)(2,1)} %row_state.2), channel_id=1, source_target_pairs={{0,64},{32,96},{1,65},{33,97},{2,66},{34,98},{3,67},{35,99},{4,68}... | collective-permute-start | bytes 405512 | tf_op jit(solution)/shard_map/ppermute | solution.py:273
  41.1 16.6 %collective-permute-start.4 = (bf16[528,128]{1,0:T(8,128)(2,1)}, bf16[528,128]{1,0:T(8,128)(2,1)S(1)}, u32[]{:S(2)}, u32[]{:S(2)}) collective-permute-start(bf16[528,128]{1,0:T(8,128)(2,1)} %row_state.2), channel_id=1, source_target_pairs={{0,32},{32,64},{64,96},{1,33},{33,65},{65,97},{2,34},{34,66},{66,9... | collective-permute-start | bytes 405512 | tf_op jit(solution)/shard_map/ppermute | solution.py:273
  44.3 23.5 %copy-start = (bf16[2,2,128,768]{3,2,1,0:T(8,128)(2,1)}, bf16[2,2,128,768]{3,2,1,0:T(8,128)(2,1)S(1)}, u32[]{:S(2)}) copy-start(bf16[2,2,128,768]{3,2,1,0:T(8,128)(2,1)S(1)} %pad_maximum_fusion.refs_10_) | copy-start | bytes 2359300
  54.0 40.2 %copy-start.1 = (bf16[2,2,128,768]{3,2,1,0:T(8,128)(2,1)}, bf16[2,2,128,768]{3,2,1,0:T(8,128)(2,1)S(1)}, u32[]{:S(2)}) copy-start(bf16[2,2,128,768]{3,2,1,0:T(8,128)(2,1)S(1)} %pad_maximum_fusion.1.refs_11_) | copy-start | bytes 2359300
  54.8 6.2 %copy-start.24 = (bf16[528,128]{1,0:T(8,128)(2,1)}, bf16[528,128]{1,0:T(8,128)(2,1)S(1)}, u32[]{:S(2)}) copy-start(bf16[528,128]{1,0:T(8,128)(2,1)S(1)} %collective-permute-done.5.refs_4_) | copy-start | bytes 405508
  57.7 20.1 %collective-permute-start.11 = (bf16[2,2,128,768]{3,2,1,0:T(8,128)(2,1)S(1)}, bf16[2,2,128,768]{3,2,1,0:T(8,128)(2,1)S(1)}, u32[]{:S(2)}, u32[]{:S(2)}) collective-permute-start(bf16[2,2,128,768]{3,2,1,0:T(8,128)(2,1)S(1)} %pad_maximum_fusion.refs_10_), channel_id=1, source_target_pairs={{0,8},{8,16},{16,24},{24,0},{1,9},{9,17},{17,25},{25,1},{2,10},{10... | collective-permute-start | bytes 2359304 | tf_op jit(solution)/shard_map/ppermute | solution.py:267
  58.5 19.3 %collective-permute-start.10 = (bf16[2,2,128,768]{3,2,1,0:T(8,128)(2,1)S(1)}, bf16[2,2,128,768]{3,2,1,0:T(8,128)(2,1)S(1)}, u32[]{:S(2)}, u32[]{:S(2)}) collective-permute-start(bf16[2,2,128,768]{3,2,1,0:T(8,128)(2,1)S(1)} %pad_maximum_fusion.refs_10_), channel_id=1, source_target_pairs={{0,24},{8,0},{16,8},{24,16},{1,25},{9,1},{17,9},{25,17},{2,26},{10... | collective-permute-start | bytes 2359304 | tf_op jit(solution)/shard_map/ppermute | solution.py:267
  92.7 22.3 %collective-permute-start.22 = (bf16[2,2,128,768]{3,2,1,0:T(8,128)(2,1)S(1)}, bf16[2,2,128,768]{3,2,1,0:T(8,128)(2,1)S(1)}, u32[]{:S(2)}, u32[]{:S(2)}) collective-permute-start(bf16[2,2,128,768]{3,2,1,0:T(8,128)(2,1)S(1)} %pad_maximum_fusion.1.refs_11_), channel_id=1, source_target_pairs={{0,8},{8,16},{16,24},{24,0},{1,9},{9,17},{17,25},{25,1},{2,10},{10... | collective-permute-start | bytes 2359304 | tf_op jit(solution)/shard_map/ppermute | solution.py:267
  94.3 20.8 %collective-permute-start.21 = (bf16[2,2,128,768]{3,2,1,0:T(8,128)(2,1)S(1)}, bf16[2,2,128,768]{3,2,1,0:T(8,128)(2,1)S(1)}, u32[]{:S(2)}, u32[]{:S(2)}) collective-permute-start(bf16[2,2,128,768]{3,2,1,0:T(8,128)(2,1)S(1)} %pad_maximum_fusion.1.refs_11_), channel_id=1, source_target_pairs={{0,24},{8,0},{16,8},{24,16},{1,25},{9,1},{17,9},{25,17},{2,26},{10... | collective-permute-start | bytes 2359304 | tf_op jit(solution)/shard_map/ppermute | solution.py:267
  96.0 56.5 %collective-permute-start.15 = (bf16[1024,512]{1,0:T(8,128)(2,1)S(1)}, bf16[1024,512]{1,0:T(8,128)(2,1)S(1)}, u32[]{:S(2)}, u32[]{:S(2)}) collective-permute-start(bf16[1024,512]{1,0:T(8,128)(2,1)S(1)} %copy-done.3), channel_id=1, source_target_pairs={{0,2},{2,4},{4,6},{6,0},{1,3},{3,5},{5,7},{7,1},{8,10},{10,12},{12... | collective-permute-start | bytes 3145736 | tf_op jit(solution)/shard_map/ppermute | solution.py:267
  97.7 55.0 %collective-permute-start.13 = (bf16[1024,512]{1,0:T(8,128)(2,1)S(1)}, bf16[1024,512]{1,0:T(8,128)(2,1)}, u32[]{:S(2)}, u32[]{:S(2)}) collective-permute-start(bf16[1024,512]{1,0:T(8,128)(2,1)S(1)} %copy-done.3), channel_id=1, source_target_pairs={{0,6},{2,0},{4,2},{6,4},{1,7},{3,1},{5,3},{7,5},{8,14},{10,8},{12,... | collective-permute-start | bytes 3145736 | tf_op jit(solution)/shard_map/ppermute | solution.py:267
  99.2 57.8 %collective-permute-start.12 = (bf16[1024,512]{1,0:T(8,128)(2,1)S(1)}, bf16[1024,512]{1,0:T(8,128)(2,1)}, u32[]{:S(2)}, u32[]{:S(2)}) collective-permute-start(bf16[1024,512]{1,0:T(8,128)(2,1)S(1)} %copy-done.3), channel_id=1, source_target_pairs={{0,1},{1,0},{2,3},{3,2},{4,5},{5,4},{6,7},{7,6},{8,9},{9,8},{10,11... | collective-permute-start | bytes 3145736 | tf_op jit(solution)/shard_map/ppermute | solution.py:277
  116.9 52.9 %copy-start.8 = (bf16[2,2,128,768]{3,2,1,0:T(8,128)(2,1)S(1)}, bf16[2,2,128,768]{3,2,1,0:T(8,128)(2,1)}, u32[]{:S(2)}) copy-start(bf16[2,2,128,768]{3,2,1,0:T(8,128)(2,1)} %copy-done.7) | copy-start | bytes 2359300
  116.9 10.5 %collective-permute-start.25 = (bf16[528,128]{1,0:T(8,128)(2,1)}, bf16[528,128]{1,0:T(8,128)(2,1)S(1)}, u32[]{:S(2)}, u32[]{:S(2)}) collective-permute-start(bf16[528,128]{1,0:T(8,128)(2,1)} %get-tuple-element.65.refs_0_), channel_id=1, source_target_pairs={{0,8},{8,16},{16,24},{24,0},{1,9},{9,17},{17,25},{25,1},{2,10},{10... | collective-permute-start | bytes 405512 | tf_op jit(solution)/shard_map/ppermute | solution.py:267
  116.9 10.6 %collective-permute-start.24 = (bf16[528,128]{1,0:T(8,128)(2,1)}, bf16[528,128]{1,0:T(8,128)(2,1)S(1)}, u32[]{:S(2)}, u32[]{:S(2)}) collective-permute-start(bf16[528,128]{1,0:T(8,128)(2,1)} %get-tuple-element.65.refs_0_), channel_id=1, source_target_pairs={{0,16},{8,24},{16,0},{24,8},{1,17},{9,25},{17,1},{25,9},{2,18},{10... | collective-permute-start | bytes 405512 | tf_op jit(solution)/shard_map/ppermute | solution.py:267
  127.4 5.6 %copy-start.11 = (bf16[528,128]{1,0:T(8,128)(2,1)}, bf16[528,128]{1,0:T(8,128)(2,1)S(1)}, u32[]{:S(2)}) copy-start(bf16[528,128]{1,0:T(8,128)(2,1)S(1)} %collective-permute-done.25.refs_3_.refs_2_) | copy-start | bytes 405508
  127.4 5.6 %collective-permute-start.23 = (bf16[528,128]{1,0:T(8,128)(2,1)}, bf16[528,128]{1,0:T(8,128)(2,1)S(1)}, u32[]{:S(2)}, u32[]{:S(2)}) collective-permute-start(bf16[528,128]{1,0:T(8,128)(2,1)} %get-tuple-element.65.refs_0_), channel_id=1, source_target_pairs={{0,24},{8,0},{16,8},{24,16},{1,25},{9,1},{17,9},{25,17},{2,26},{10... | collective-permute-start | bytes 405512 | tf_op jit(solution)/shard_map/ppermute | solution.py:267
  135.5 13.1 %collective-permute-start.27 = (bf16[528,128]{1,0:T(8,128)(2,1)}, bf16[528,128]{1,0:T(8,128)(2,1)S(1)}, u32[]{:S(2)}, u32[]{:S(2)}) collective-permute-start(bf16[528,128]{1,0:T(8,128)(2,1)} %row_state.3), channel_id=1, source_target_pairs={{64,0},{96,32},{65,1},{97,33},{66,2},{98,34},{67,3},{99,35},{68,4}... | collective-permute-start | bytes 405512 | tf_op jit(solution)/shard_map/ppermute | solution.py:273
  136.8 14.1 %collective-permute-start.26 = (bf16[528,128]{1,0:T(8,128)(2,1)}, bf16[528,128]{1,0:T(8,128)(2,1)S(1)}, u32[]{:S(2)}, u32[]{:S(2)}) collective-permute-start(bf16[528,128]{1,0:T(8,128)(2,1)} %row_state.3), channel_id=1, source_target_pairs={{32,0},{64,32},{96,64},{33,1},{65,33},{97,65},{34,2},{66,34},{98,6... | collective-permute-start | bytes 405512 | tf_op jit(solution)/shard_map/ppermute | solution.py:273
  148.6 23.2 %copy-start.22 = (bf16[528,128]{1,0:T(8,128)(2,1)}, bf16[528,128]{1,0:T(8,128)(2,1)S(1)}, u32[]{:S(2)}) copy-start(bf16[528,128]{1,0:T(8,128)(2,1)S(1)} %collective-permute-done.27.refs_4_) | copy-start | bytes 405508
  150.9 18.9 %collective-permute-start.28 = (bf16[2,2,128,768]{3,2,1,0:T(8,128)(2,1)}, bf16[2,2,128,768]{3,2,1,0:T(8,128)(2,1)S(1)}, u32[]{:S(2)}, u32[]{:S(2)}) collective-permute-start(bf16[2,2,128,768]{3,2,1,0:T(8,128)(2,1)} %copy-done.6), channel_id=1, source_target_pairs={{0,24},{8,0},{16,8},{24,16},{1,25},{9,1},{17,9},{25,17},{2,26},{10... | collective-permute-start | bytes 2359304 | tf_op jit(solution)/shard_map/ppermute | solution.py:267
  152.5 26.7 %copy-start.2 = (bf16[1024,512]{1,0:T(8,128)(2,1)}, bf16[1024,512]{1,0:T(8,128)(2,1)S(1)}, u32[]{:S(2)}) copy-start(bf16[1024,512]{1,0:T(8,128)(2,1)S(1)} %collective-permute-done.15.refs_4_) | copy-start | bytes 3145732
  152.6 18.1 %collective-permute-start.18 = (bf16[512,512]{1,0:T(8,128)(2,1)S(1)}, bf16[512,512]{1,0:T(8,128)(2,1)S(1)}, u32[]{:S(2)}, u32[]{:S(2)}) collective-permute-start(bf16[512,512]{1,0:T(8,128)(2,1)S(1)} %slice.19), channel_id=1, source_target_pairs={{0,2},{2,4},{4,6},{6,0},{1,3},{3,5},{5,7},{7,1},{8,10},{10,12},{12... | collective-permute-start | bytes 1572872 | tf_op jit(solution)/shard_map/ppermute | solution.py:267
  154.0 16.7 %collective-permute-start.17 = (bf16[512,512]{1,0:T(8,128)(2,1)S(1)}, bf16[512,512]{1,0:T(8,128)(2,1)}, u32[]{:S(2)}, u32[]{:S(2)}) collective-permute-start(bf16[512,512]{1,0:T(8,128)(2,1)S(1)} %slice.18), channel_id=1, source_target_pairs={{0,6},{2,0},{4,2},{6,4},{1,7},{3,1},{5,3},{7,5},{8,14},{10,8},{12,... | collective-permute-start | bytes 1572872 | tf_op jit(solution)/shard_map/ppermute | solution.py:267
  157.1 32.2 %collective-permute-start.16 = (bf16[1024,512]{1,0:T(8,128)(2,1)S(1)}, bf16[1024,512]{1,0:T(8,128)(2,1)}, u32[]{:S(2)}, u32[]{:S(2)}) collective-permute-start(bf16[1024,512]{1,0:T(8,128)(2,1)S(1)} %collective-permute-done.15.refs_4_), channel_id=1, source_target_pairs={{0,1},{1,0},{2,3},{3,2},{4,5},{5,4},{6,7},{7,6},{8,9},{9,8},{10,11... | collective-permute-start | bytes 3145736 | tf_op jit(solution)/shard_map/ppermute | solution.py:277
  157.1 32.2 %collective-permute-start.14 = (bf16[1024,512]{1,0:T(8,128)(2,1)}, bf16[1024,512]{1,0:T(8,128)(2,1)S(1)}, u32[]{:S(2)}, u32[]{:S(2)}) collective-permute-start(bf16[1024,512]{1,0:T(8,128)(2,1)} %collective-permute-done.13.refs_2_), channel_id=1, source_target_pairs={{0,1},{1,0},{2,3},{3,2},{4,5},{5,4},{6,7},{7,6},{8,9},{9,8},{10,11... | collective-permute-start | bytes 3145736 | tf_op jit(solution)/shard_map/ppermute | solution.py:277
  169.8 19.5 %collective-permute-start.29 = (bf16[2,2,128,768]{3,2,1,0:T(8,128)(2,1)S(1)}, bf16[2,2,128,768]{3,2,1,0:T(8,128)(2,1)}, u32[]{:S(2)}, u32[]{:S(2)}) collective-permute-start(bf16[2,2,128,768]{3,2,1,0:T(8,128)(2,1)S(1)} %copy-done.8), channel_id=1, source_target_pairs={{0,8},{8,16},{16,24},{24,0},{1,9},{9,17},{17,25},{25,1},{2,10},{10... | collective-permute-start | bytes 2359304 | tf_op jit(solution)/shard_map/ppermute | solution.py:267
  170.7 8.6 %copy-start.17 = (bf16[512,512]{1,0:T(8,128)(2,1)}, bf16[512,512]{1,0:T(8,128)(2,1)S(1)}, u32[]{:S(2)}) copy-start(bf16[512,512]{1,0:T(8,128)(2,1)S(1)} %collective-permute-done.18.refs_7_) | copy-start | bytes 1572868
  170.7 18.6 %collective-permute-start.20 = (bf16[512,512]{1,0:T(8,128)(2,1)S(1)}, bf16[512,512]{1,0:T(8,128)(2,1)}, u32[]{:S(2)}, u32[]{:S(2)}) collective-permute-start(bf16[512,512]{1,0:T(8,128)(2,1)S(1)} %collective-permute-done.18.refs_7_), channel_id=1, source_target_pairs={{0,1},{1,0},{2,3},{3,2},{4,5},{5,4},{6,7},{7,6},{8,9},{9,8},{10,11... | collective-permute-start | bytes 1572872 | tf_op jit(solution)/shard_map/ppermute | solution.py:277
  170.7 18.6 %collective-permute-start.19 = (bf16[512,512]{1,0:T(8,128)(2,1)}, bf16[512,512]{1,0:T(8,128)(2,1)}, u32[]{:S(2)}, u32[]{:S(2)}) collective-permute-start(bf16[512,512]{1,0:T(8,128)(2,1)} %collective-permute-done.17.refs_6_), channel_id=1, source_target_pairs={{0,1},{1,0},{2,3},{3,2},{4,5},{5,4},{6,7},{7,6},{8,9},{9,8},{10,11... | collective-permute-start | bytes 1572872 | tf_op jit(solution)/shard_map/ppermute | solution.py:277
  205.4 12.1 %collective-permute-start.32 = (bf16[512,384]{1,0:T(8,128)(2,1)S(1)}, bf16[512,384]{1,0:T(8,128)(2,1)S(1)}, u32[]{:S(2)}, u32[]{:S(2)}) collective-permute-start(bf16[512,384]{1,0:T(8,128)(2,1)S(1)} %get-tuple-element.91), channel_id=1, source_target_pairs={{0,24},{8,0},{16,8},{24,16},{1,25},{9,1},{17,9},{25,17},{2,26},{10... | collective-permute-start | bytes 1179656 | tf_op jit(solution)/shard_map/ppermute | solution.py:267
  207.2 13.6 %collective-permute-start.31 = (bf16[512,384]{1,0:T(8,128)(2,1)S(1)}, bf16[512,384]{1,0:T(8,128)(2,1)S(1)}, u32[]{:S(2)}, u32[]{:S(2)}) collective-permute-start(bf16[512,384]{1,0:T(8,128)(2,1)S(1)} %get-tuple-element.92), channel_id=1, source_target_pairs={{0,16},{8,24},{16,0},{24,8},{1,17},{9,25},{17,1},{25,9},{2,18},{10... | collective-permute-start | bytes 1179656 | tf_op jit(solution)/shard_map/ppermute | solution.py:267
  207.2 18.0 %collective-permute-start.30 = (bf16[512,384]{1,0:T(8,128)(2,1)S(1)}, bf16[512,384]{1,0:T(8,128)(2,1)S(1)}, u32[]{:S(2)}, u32[]{:S(2)}) collective-permute-start(bf16[512,384]{1,0:T(8,128)(2,1)S(1)} %get-tuple-element.93), channel_id=1, source_target_pairs={{0,8},{8,16},{16,24},{24,0},{1,9},{9,17},{17,25},{25,1},{2,10},{10... | collective-permute-start | bytes 1179656 | tf_op jit(solution)/shard_map/ppermute | solution.py:267
  217.5 7.7 %copy-start.18 = (bf16[512,384]{1,0:T(8,128)(2,1)}, bf16[512,384]{1,0:T(8,128)(2,1)S(1)}, u32[]{:S(2)}) copy-start(bf16[512,384]{1,0:T(8,128)(2,1)S(1)} %collective-permute-done.32.refs_2_) | copy-start | bytes 1179652
  (14 other events, 27.8 us)
Sparse Core Ops, SparseCore 0:
  9.7 69.9 all-gather.2
  92.8 69.2 reduce-scatter.1

commit v3 on v2

--- a/solution.py
+++ b/solution.py
@@ -348,10 +348,11 @@
     table = jnp.broadcast_to(table[:, None], (16, HEAD))
 
     tail = pl.pallas_call(tail_kernel, out_shape=payload, name="tail")(keys, values, dcol, table)
-    strip = column_strip(out_weight, share, cx)
-    arrived, strip = exchanged(tail, 1, strip)
-    own = column_pieces(strip, share, core)
-    arrived, own = lax.optimization_barrier((arrived, own))
+    own = column_pieces(column_strip(out_weight, share, cx), share, core)
+    arrived, own = exchanged(tail, 1, own)
+    early = [turned_by(own[0], "cy", -1), turned_by(own[1], "cy", 1)]
+    arrived, early = lax.optimization_barrier((arrived, early))
+    later = [turned_by(own[1], "cy", -1), turned_by(own[0], "cy", 1)]
 
     row_block = pl.BlockSpec((1, CHUNK), lambda i: (0, i))
     state_block = pl.BlockSpec((1, size, HEAD), lambda i: (i, 0, 0))
@@ -378,9 +379,8 @@
         name="forward",
     )(queries, keys, values, dcol, drow, table, *arrived)
 
-    early = [turned_by(own[0], "cy", s) for s in (-1, 1)]
-    turned, early = lax.optimization_barrier((turned, early))
-    later = [turned_by(own[1], "cy", s) for s in (-1, 1)]
+    turned, later = lax.optimization_barrier((turned, later))
+    across = [turned_by(early[0], "cy", -1), turned_by(early[1], "cy", 1)]
 
     term = pl.pallas_call(
         weight_kernel,
@@ -397,10 +397,6 @@
     half_rows = rows // 2
     above = turned_by(low, "z", -1)
     below = turned_by(low, "z", 1)
-    far_a = turned_by(above[:half_rows], "z", -1)
-    far_b = turned_by(below[half_rows:], "z", 1)
-    near = [low, swapped(low), above, swapped(above), below, swapped(below)]
-    far = [far_a, far_b, swapped(far_a), swapped(far_b)]
 
     grad_opened, head = pl.pallas_call(
         cotangent_kernel,
@@ -419,12 +415,13 @@
         compiler_params=params(),
         name="cotangent",
     )(grad_whole, out_weight, opened, queries, dcol, table)
-    head, later = lax.optimization_barrier((head, later))
-    returned, _ = exchanged(head, -1)
-
-    returned, early, later = lax.optimization_barrier((returned, early, later))
-    across = (turned_by(early[0], "cy", -1), turned_by(later[1], "cy", 1))
-    columns = [*own, early[0], later[0], *across, early[1], later[1]]
+    head, across, above, below = lax.optimization_barrier((head, across, above, below))
+    far_a = turned_by(above[:half_rows], "z", -1)
+    far_b = turned_by(below[half_rows:], "z", 1)
+    returned, (far_a, far_b, low) = exchanged(head, -1, (far_a, far_b, low))
+    near = [low, swapped(low), above, swapped(above), below, swapped(below)]
+    far = [far_a, far_b, swapped(far_a), swapped(far_b)]
+    columns = [*own, early[0], later[0], *across, later[1], early[1]]
 
     grad_query = pl.pallas_call(
         query_kernel,
@@ -436,20 +433,6 @@
         compiler_params=params(),
         name="grad_query",
     )(grad_opened, keys, values, dcol, drow, table, states)
-
-    back_row = pl.BlockSpec((1, CHUNK), lambda i: (0, blocks - 1 - i))
-    grad_key, grad_value = pl.pallas_call(
-        key_value_kernel,
-        grid=(blocks,),
-        in_specs=[rows_of(width, blocks)] * 4
-        + [rows_of(HEAD, blocks), back_row, whole(table.shape)]
-        + [whole(payload.shape)] * len(returned),
-        out_specs=[rows_of(width, blocks)] * 2,
-        out_shape=[jax.ShapeDtypeStruct((rows, width), BF16)] * 2,
-        scratch_shapes=[pltpu.VMEM((size, HEAD), F32)],
-        compiler_params=params(),
-        name="grad_key_value",
-    )(grad_opened, queries, keys, values, dcol, drow, table, *returned)
 
     sides = (core, 1 - core)
     around = [2 * ((z + cy + s) % 4) + side for s in range(4) for side in sides]
@@ -475,7 +458,23 @@
         compiler_params=params(),
         name="attended",
     )(jnp.stack(around + heads_at + groups_at), *near, *far, *columns)
-    grad_part, attended, grad_key = lax.optimization_barrier((grad_part, attended, grad_key))
+    returned, attended = lax.optimization_barrier((returned, attended))
+
+    back_row = pl.BlockSpec((1, CHUNK), lambda i: (0, blocks - 1 - i))
+    grad_key, grad_value = pl.pallas_call(
+        key_value_kernel,
+        grid=(blocks,),
+        in_specs=[rows_of(width, blocks)] * 4
+        + [rows_of(HEAD, blocks), back_row, whole(table.shape)]
+        + [whole(payload.shape)] * len(returned),
+        out_specs=[rows_of(width, blocks)] * 2,
+        out_shape=[jax.ShapeDtypeStruct((rows, width), BF16)] * 2,
+        scratch_shapes=[pltpu.VMEM((size, HEAD), F32)],
+        compiler_params=params(),
+        name="grad_key_value",
+    )(grad_opened, queries, keys, values, dcol, drow, table, *returned)
+
+    grad_part, grad_key = lax.optimization_barrier((grad_part, grad_key))
     grad_weight = row_sum(grad_part, cy)
     return attended, grad_query, grad_key, grad_value, grad_weight
 

time: 236 us -> 205 us (0.87)
  waiting for transfers between devices: 91.7 us -> 49.9 us
  starting transfers between devices: 43.8 us -> 59 us
  local copies, waits for them, and re-layouts: 13.4 us -> 7.85 us
    ppermute x22, waiting for transfers between devices: 74.3 us -> 39.8 us  [turned_by(): lax.ppermute(value, axis, [(i, (i + step) % size) for i in range(size)])]
    ppermute x22, starting transfers between devices: 34.1 us -> 44.5 us  [turned_by(): lax.ppermute(value, axis, [(i, (i + step) % size) for i in range(size)])]
    ppermute x4, waiting for transfers between devices: 15.2 us -> 5.71 us  [moved_by(): return lax.ppermute(value, axis, pairs)]
    ppermute x4, starting transfers between devices: 7.92 us -> 12.6 us  [moved_by(): return lax.ppermute(value, axis, pairs)]
    unnamed x54 -> x48, local copies, waits for them, and re-layouts: 7.01 us -> 2.7 us
  transfers between devices with their start and end apart: 35 -> 35, of which waited for: 19 -> 18; matrix products, arithmetic and copies ran while one was open for 2% -> 2% of each run, Pallas kernels for 24% -> 28%
where the time goes in v3:
time: 205 us; the launch traced here: 203 us
  Pallas kernels  71.5 us (35%)
  starting transfers between devices  59 us (29%)
  waiting for transfers between devices  49.9 us (24%)
  between operations  14.6 us (7%)
  local copies, waits for them, and re-layouts  7.85 us (4%)
    ppermute x22, starting transfers between devices, turned_by(): lax.ppermute(value, axis, [(i, (i + step) % size) for i in range(size)])  44.5 us
    ppermute x22, waiting for transfers between devices, turned_by(): lax.ppermute(value, axis, [(i, (i + step) % size) for i in range(size)])  39.8 us
    pallas_call x1, Pallas kernels, body(): pl.pallas_call(cotangent_kernel, grid=(blocks,), in_specs=[pl.BlockSpec((...  15.8 us
    pallas_call x1, Pallas kernels, body(): pl.pallas_call(attended_kernel, grid_spec=pltpu.PrefetchScalarGridSpec(nu...  13.7 us
    pallas_call x1, Pallas kernels, body(): pl.pallas_call(weight_kernel, grid=(groups,), in_specs=[whole((width, row...  13 us
    ppermute x4, starting transfers between devices, moved_by(): return lax.ppermute(value, axis, pairs)  12.6 us
    pallas_call x1, Pallas kernels, body(): pl.pallas_call(key_value_kernel, grid=(blocks,), in_specs=[rows_of(width,...  7.51 us
    pallas_call x1, Pallas kernels, body(): pl.pallas_call(forward_kernel, grid=(blocks,), in_specs=[rows_of(width)]...  6.76 us
  transfers between devices with their start and end apart: 35, of which 18 were waited for; matrix products, arithmetic and copies ran while one was open for 2% of the time, Pallas kernels for 28%

profile of v3, /device:TPU:2, one launch (start us, length us, event | category | flops | bytes accessed | tf_op | source)
XLA Modules:
  0.0 203.2 jit_solution(2196850595251651407)
XLA Ops:
  8.0 1.0 dynamic_slice.19
  9.9 1.4 collective-permute-done.4
  11.3 1.6 collective-permute-start.5
  12.9 1.0 collective-permute-start.6
  13.9 2.2 %collective-permute-start.7 = (bf16[2,128,768]{2,1,0:T(8,128)(2,1)S(1)}, bf16[2,128,768]{2,1,0:T(8,128)(2,1)S(1)}, u32[]{:S(2)}, u32[]{:S(2)}) collective-permute-start(bf16[2,128,768]{2,1,0:T(8,128)(2,1)S(1)} %get-tuple-element.99), channel_id=1, source_target_pairs={{0,96},{32,0},{64,32},{96,64},{1,97},{33,1},{65,33},{97,65},{2,98}... | collective-permute-start | bytes 1179656 | tf_op jit(solution)/shard_map/ppermute | solution.py:267
  17.1 1.0 broadcast_in_dim.10.dcol
  18.2 2.8 %tail.1.refs_0_ = bf16[528,128]{1,0:T(8,128)(2,1)} custom-call(bf16[1024,512]{1,0:T(8,128)(2,1)} %k.7, bf16[1024,512]{1,0:T(8,128)(2,1)} %v.7, f32[1024,128]{1,0:T(8,128)} %broadcast_in_dim.10.dcol, f32[16,128]{1,0:T(8,128)} %broadcast_in_dim.24.table), custom_call_target="tpu_custom_call" | custom-call | tf_op jit(solution)/shard_map/tail/pallas_call | solution.py:350
  21.0 17.7 %collective-permute-start.2 = (bf16[528,128]{1,0:T(8,128)(2,1)}, bf16[528,128]{1,0:T(8,128)(2,1)S(1)}, u32[]{:S(2)}, u32[]{:S(2)}) collective-permute-start(bf16[528,128]{1,0:T(8,128)(2,1)} %tail.1.refs_0_), channel_id=1, source_target_pairs={{0,24},{8,0},{16,8},{24,16},{1,25},{9,1},{17,9},{25,17},{2,26},{10... | collective-permute-start | bytes 405512 | tf_op jit(solution)/shard_map/ppermute | solution.py:267
  38.7 1.4 collective-permute-start
  40.3 3.9 %collective-permute-done.2.refs_3_.refs_2_ = bf16[528,128]{1,0:T(8,128)(2,1)S(1)} collective-permute-done((bf16[528,128]{1,0:T(8,128)(2,1)}, bf16[528,128]{1,0:T(8,128)(2,1)S(1)}, u32[]{:S(2)}, u32[]{:S(2)}) %collective-permute-start.2) | collective-permute-done | bytes 135200 | tf_op jit(solution)/shard_map/ppermute | solution.py:267
  44.2 2.3 %collective-permute-done.1.refs_2_.refs_1_ = bf16[528,128]{1,0:T(8,128)(2,1)S(1)} collective-permute-done((bf16[528,128]{1,0:T(8,128)(2,1)}, bf16[528,128]{1,0:T(8,128)(2,1)S(1)}, u32[]{:S(2)}, u32[]{:S(2)}) %collective-permute-start.1) | collective-permute-done | bytes 135200 | tf_op jit(solution)/shard_map/ppermute | solution.py:267
  46.5 1.1 collective-permute-done.refs_1_.refs_0_
  47.5 3.4 %collective-permute-start.10 = (bf16[2,2,128,768]{3,2,1,0:T(8,128)(2,1)S(1)}, bf16[2,2,128,768]{3,2,1,0:T(8,128)(2,1)S(1)}, u32[]{:S(2)}, u32[]{:S(2)}) collective-permute-start(bf16[2,2,128,768]{3,2,1,0:T(8,128)(2,1)S(1)} %pad_maximum_fusion.refs_10_), channel_id=1, source_target_pairs={{0,24},{8,0},{16,8},{24,16},{1,25},{9,1},{17,9},{25,17},{2,26},{10... | collective-permute-start | bytes 2359304 | tf_op jit(solution)/shard_map/ppermute | solution.py:267
  51.0 3.2 %collective-permute-start.14 = (bf16[2,2,128,768]{3,2,1,0:T(8,128)(2,1)S(1)}, bf16[2,2,128,768]{3,2,1,0:T(8,128)(2,1)}, u32[]{:S(2)}, u32[]{:S(2)}) collective-permute-start(bf16[2,2,128,768]{3,2,1,0:T(8,128)(2,1)S(1)} %pad_maximum_fusion.1.refs_11_), channel_id=1, source_target_pairs={{0,24},{8,0},{16,8},{24,16},{1,25},{9,1},{17,9},{25,17},{2,26},{10... | collective-permute-start | bytes 2359304 | tf_op jit(solution)/shard_map/ppermute | solution.py:267
  54.2 1.9 row_state.2
  56.0 3.7 %collective-permute-start.9 = (bf16[528,128]{1,0:T(8,128)(2,1)}, bf16[528,128]{1,0:T(8,128)(2,1)S(1)}, u32[]{:S(2)}, u32[]{:S(2)}) collective-permute-start(bf16[528,128]{1,0:T(8,128)(2,1)} %row_state.2), channel_id=1, source_target_pairs={{0,64},{32,96},{1,65},{33,97},{2,66},{34,98},{3,67},{35,99},{4,68}... | collective-permute-start | bytes 405512 | tf_op jit(solution)/shard_map/ppermute | solution.py:273
  59.7 2.9 %collective-permute-done.9.refs_4_ = bf16[528,128]{1,0:T(8,128)(2,1)S(1)} collective-permute-done((bf16[528,128]{1,0:T(8,128)(2,1)}, bf16[528,128]{1,0:T(8,128)(2,1)S(1)}, u32[]{:S(2)}, u32[]{:S(2)}) %collective-permute-start.9) | collective-permute-done | bytes 135200 | tf_op jit(solution)/shard_map/ppermute | solution.py:273
  62.6 5.2 %collective-permute-start.8 = (bf16[528,128]{1,0:T(8,128)(2,1)}, bf16[528,128]{1,0:T(8,128)(2,1)S(1)}, u32[]{:S(2)}, u32[]{:S(2)}) collective-permute-start(bf16[528,128]{1,0:T(8,128)(2,1)} %row_state.2), channel_id=1, source_target_pairs={{0,32},{32,64},{64,96},{1,33},{33,65},{65,97},{2,34},{34,66},{66,9... | collective-permute-start | bytes 405512 | tf_op jit(solution)/shard_map/ppermute | solution.py:273
  67.8 2.9 %collective-permute-done.8.refs_3_ = bf16[528,128]{1,0:T(8,128)(2,1)S(1)} collective-permute-done((bf16[528,128]{1,0:T(8,128)(2,1)}, bf16[528,128]{1,0:T(8,128)(2,1)S(1)}, u32[]{:S(2)}, u32[]{:S(2)}) %collective-permute-start.8) | collective-permute-done | bytes 135200 | tf_op jit(solution)/shard_map/ppermute | solution.py:273
  70.7 2.0 collective-permute-done.11.refs_17_
  72.7 6.8 %forward.1 = (f32[1024,512]{1,0:T(8,128)}, bf16[1024,512]{1,0:T(8,128)(2,1)}, bf16[512,1024]{1,0:T(8,128)(2,1)}, bf16[4,512,128]{2,1,0:T(8,128)(2,1)}) custom-call(bf16[1024,512]{1,0:T(8,128)(2,1)} %q.5, bf16[1024,512]{1,0:T(8,128)(2,1)} %k.7, bf16[1024,512]{1,0:T(8,128)(2,1)} %v.7, f32[1024,128]{1,0:T(8,128)} %broadcast_in_dim.10.dcol, f32[1,1024]{1,0:T(1,128)} %bitcast.47, ...), custom_call_target="tpu_custom_call" | custom-call | tf_op jit(solution)/shard_map/forward/pallas_call | solution.py:359
  79.5 8.1 %collective-permute-done.15.refs_16_ = bf16[2,2,128,768]{3,2,1,0:T(8,128)(2,1)} collective-permute-done((bf16[2,2,128,768]{3,2,1,0:T(8,128)(2,1)S(1)}, bf16[2,2,128,768]{3,2,1,0:T(8,128)(2,1)}, u32[]{:S(2)}, u32[]{:S(2)}) %collective-permute-start.15) | collective-permute-done | bytes 786464 | tf_op jit(solution)/shard_map/ppermute | solution.py:267
  87.6 13.0 %weight_grad.1 = bf16[4,4,512,384]{3,2,1,0:T(8,128)(2,1)} custom-call(bf16[512,1024]{1,0:T(8,128)(2,1)} %get-tuple-element.64.turned, bf16[8,1024,768]{2,1,0:T(8,128)(2,1)} %bitcast.39), custom_call_target="tpu_custom_call" | custom-call | tf_op jit(solution)/shard_map/weight_grad/pallas_call | solution.py:385
  100.7 1.2 copy-done.4
  101.9 3.2 %collective-permute-start.16 = (bf16[1024,512]{1,0:T(8,128)(2,1)S(1)}, bf16[1024,512]{1,0:T(8,128)(2,1)S(1)}, u32[]{:S(2)}, u32[]{:S(2)}) collective-permute-start(bf16[1024,512]{1,0:T(8,128)(2,1)S(1)} %copy-done.4), channel_id=1, source_target_pairs={{0,6},{2,0},{4,2},{6,4},{1,7},{3,1},{5,3},{7,5},{8,14},{10,8},{12,... | collective-permute-start | bytes 3145736 | tf_op jit(solution)/shard_map/ppermute | solution.py:267
  105.4 1.8 collective-permute-start.13
  107.1 15.8 %cotangent.1 = (f32[1024,512]{1,0:T(8,128)}, bf16[528,128]{1,0:T(8,128)(2,1)}) custom-call(bf16[8,1024,768]{2,1,0:T(8,128)(2,1)} %bitcast.40, bf16[512,6144]{1,0:T(8,128)(2,1)} %weight.1, f32[1024,512]{1,0:T(8,128)} %get-tuple-element.59.opened, bf16[1024,512]{1,0:T(8,128)(2,1)} %q.5, f32[1024,128]{1,0:T(8,128)} %broadcast_in_dim.10.dcol, ...), custom_call_target="tpu_custom_call" | custom-call | tf_op jit(solution)/shard_map/cotangent/pallas_call | solution.py:401
  123.0 0.9 collective-permute-done.13.refs_15_
  123.9 2.5 %collective-permute-done.17.refs_4_ = bf16[1024,512]{1,0:T(8,128)(2,1)S(1)} collective-permute-done((bf16[1024,512]{1,0:T(8,128)(2,1)S(1)}, bf16[1024,512]{1,0:T(8,128)(2,1)S(1)}, u32[]{:S(2)}, u32[]{:S(2)}) %collective-permute-start.17) | collective-permute-done | bytes 1048608 | tf_op jit(solution)/shard_map/ppermute | solution.py:267
  126.5 3.2 %collective-permute-start.21 = (bf16[512,512]{1,0:T(8,128)(2,1)S(1)}, bf16[512,512]{1,0:T(8,128)(2,1)}, u32[]{:S(2)}, u32[]{:S(2)}) collective-permute-start(bf16[512,512]{1,0:T(8,128)(2,1)S(1)} %slice.14), channel_id=1, source_target_pairs={{0,6},{2,0},{4,2},{6,4},{1,7},{3,1},{5,3},{7,5},{8,14},{10,8},{12,... | collective-permute-start | bytes 1572872 | tf_op jit(solution)/shard_map/ppermute | solution.py:267
  129.8 2.0 collective-permute-start.19
  131.8 1.2 collective-permute-start.18
  133.0 4.4 %collective-permute-done.20.refs_3_.refs_2_ = bf16[528,128]{1,0:T(8,128)(2,1)S(1)} collective-permute-done((bf16[528,128]{1,0:T(8,128)(2,1)S(1)}, bf16[528,128]{1,0:T(8,128)(2,1)S(1)}, u32[]{:S(2)}, u32[]{:S(2)}) %collective-permute-start.20) | collective-permute-done | bytes 135200 | tf_op jit(solution)/shard_map/ppermute | solution.py:267
  139.5 1.9 row_state.3
  141.4 2.0 %collective-permute-done.28.refs_8_ = bf16[512,512]{1,0:T(8,128)(2,1)} collective-permute-done((bf16[512,512]{1,0:T(8,128)(2,1)}, bf16[512,512]{1,0:T(8,128)(2,1)}, u32[]{:S(2)}, u32[]{:S(2)}) %collective-permute-start.28) | collective-permute-done | bytes 524320 | tf_op jit(solution)/shard_map/ppermute | solution.py:277
  143.4 1.3 collective-permute-start.24
  144.9 2.4 %collective-permute-start.23 = (bf16[528,128]{1,0:T(8,128)(2,1)}, bf16[528,128]{1,0:T(8,128)(2,1)S(1)}, u32[]{:S(2)}, u32[]{:S(2)}) collective-permute-start(bf16[528,128]{1,0:T(8,128)(2,1)} %row_state.3), channel_id=1, source_target_pairs={{32,0},{64,32},{96,64},{33,1},{65,33},{97,65},{34,2},{66,34},{98,6... | collective-permute-start | bytes 405512 | tf_op jit(solution)/shard_map/ppermute | solution.py:273
  148.3 13.7 %attended.1 = bf16[1024,768]{1,0:T(8,128)(2,1)} custom-call(s32[20]{0:T(128)} %stack.119.places, bf16[1024,512]{1,0:T(8,128)(2,1)} %get-tuple-element.73.refs_0_, bf16[1024,512]{1,0:T(8,128)(2,1)} %collective-permute-done.25.refs_1_, bf16[1024,512]{1,0:T(8,128)(2,1)} %copy-done.3, bf16[1024,512]{1,0:T(8,128)(2,1)} %collective-permute-done.26.refs_3_, ...), custom_call_target="tpu_custom_call" | custom-call | tf_op jit(solution)/shard_map/attended/pallas_call | solution.py:445
  162.7 7.5 %grad_key_value.1 = (bf16[1024,512]{1,0:T(8,128)(2,1)}, bf16[1024,512]{1,0:T(8,128)(2,1)}) custom-call(f32[1024,512]{1,0:T(8,128)} %get-tuple-element.81.go, bf16[1024,512]{1,0:T(8,128)(2,1)} %q.5, bf16[1024,512]{1,0:T(8,128)(2,1)} %k.7, bf16[1024,512]{1,0:T(8,128)(2,1)} %v.7, f32[1024,128]{1,0:T(8,128)} %broadcast_in_dim.10.dcol, f32[1,1024]{1,0:T(1,128)} %bitcast.48, ...), custom_call_target="tpu_custom_call" | custom-call | tf_op jit(solution)/shard_map/grad_key_value/pallas_call | solution.py:464
  170.2 1.4 dynamic-slice_bitcast_fusion
  171.6 0.9 collective-permute-start.32
  172.8 0.9 collective-permute-start.30
  173.7 5.9 %grad_query.1 = bf16[1024,512]{1,0:T(8,128)(2,1)} custom-call(f32[1024,512]{1,0:T(8,128)} %get-tuple-element.81.go, bf16[1024,512]{1,0:T(8,128)(2,1)} %k.7, bf16[1024,512]{1,0:T(8,128)(2,1)} %v.7, f32[1024,128]{1,0:T(8,128)} %broadcast_in_dim.10.dcol, f32[1,1024]{1,0:T(1,128)} %bitcast.49, f32[16,128]{1,0:T(8,128)} %broadcast_in_dim.24.table, ...), custom_call_target="tpu_custom_call" | custom-call | tf_op jit(solution)/shard_map/grad_query/pallas_call | solution.py:426
  179.6 4.1 %collective-permute-done.32.refs_2_ = bf16[512,384]{1,0:T(8,128)(2,1)S(1)} collective-permute-done((bf16[512,384]{1,0:T(8,128)(2,1)S(1)}, bf16[512,384]{1,0:T(8,128)(2,1)S(1)}, u32[]{:S(2)}, u32[]{:S(2)}) %collective-permute-start.32) | collective-permute-done | bytes 393248 | tf_op jit(solution)/shard_map/ppermute | solution.py:267
  183.7 2.4 %collective-permute-done.31.refs_1_ = bf16[512,384]{1,0:T(8,128)(2,1)S(1)} collective-permute-done((bf16[512,384]{1,0:T(8,128)(2,1)S(1)}, bf16[512,384]{1,0:T(8,128)(2,1)S(1)}, u32[]{:S(2)}, u32[]{:S(2)}) %collective-permute-start.31) | collective-permute-done | bytes 393248 | tf_op jit(solution)/shard_map/ppermute | solution.py:267
  186.0 7.2 %collective-permute-done.30.refs_0_ = bf16[512,384]{1,0:T(8,128)(2,1)S(1)} collective-permute-done((bf16[512,384]{1,0:T(8,128)(2,1)S(1)}, bf16[512,384]{1,0:T(8,128)(2,1)S(1)}, u32[]{:S(2)}, u32[]{:S(2)}) %collective-permute-start.30) | collective-permute-done | bytes 393248 | tf_op jit(solution)/shard_map/ppermute | solution.py:267
  193.3 0.7 copy-done.16
  194.0 2.3 %last_sum.1 = f32[512,384]{1,0:T(8,128)} custom-call(s32[1]{0:T(128)} %bitcast.30.place, bf16[4,512,384]{2,1,0:T(8,128)(2,1)} %bitcast.42, bf16[512,384]{1,0:T(8,128)(2,1)} %copy-done.16, bf16[512,384]{1,0:T(8,128)(2,1)} %copy-done.15, bf16[512,384]{1,0:T(8,128)(2,1)} %copy-done.14), custom_call_target="tpu_custom_call" | custom-call | tf_op jit(solution)/shard_map/last_sum/pallas_call | solution.py:315
  (98 shorter events, 7.3 us)
Async XLA Ops:
  7.2 9.0 %copy-start.23 = (s32[1024]{0:T(1024)S(1)}, s32[1024]{0:T(1024)}, u32[]{:S(2)}) copy-start(s32[1024]{0:T(1024)} %param.9) | copy-start | bytes 12292
  7.2 80.5 %all-gather.3.cloned.1.call-start = ((), (), s32[]{:S(2)}) async-start(), calls=%async_computation.2 | async-start | bytes 14155776 | tf_op jit(solution)/shard_map/all_gather | solution.py:340
  7.9 162.3 %reduce-scatter.2.cloned.1.call-start = ((), (), s32[]{:S(2)}) async-start(), calls=%async_computation.1 | async-start | bytes 7864320 | tf_op jit(solution)/shard_map/reduce_scatter | solution.py:395
  9.0 0.7 collective-permute-start.3
  9.8 1.5 collective-permute-start.4
  11.3 27.3 %collective-permute-start.5 = (bf16[2,128,768]{2,1,0:T(8,128)(2,1)S(1)}, bf16[2,128,768]{2,1,0:T(8,128)(2,1)S(1)}, u32[]{:S(2)}, u32[]{:S(2)}) collective-permute-start(bf16[2,128,768]{2,1,0:T(8,128)(2,1)S(1)} %get-tuple-element.99), channel_id=1, source_target_pairs={{0,32},{32,64},{64,96},{96,0},{1,33},{33,65},{65,97},{97,1},{2,34}... | collective-permute-start | bytes 1179656 | tf_op jit(solution)/shard_map/ppermute | solution.py:267
  12.9 27.3 %collective-permute-start.6 = (bf16[2,128,768]{2,1,0:T(8,128)(2,1)S(1)}, bf16[2,128,768]{2,1,0:T(8,128)(2,1)S(1)}, u32[]{:S(2)}, u32[]{:S(2)}) collective-permute-start(bf16[2,128,768]{2,1,0:T(8,128)(2,1)S(1)} %get-tuple-element.99), channel_id=1, source_target_pairs={{0,64},{32,96},{64,0},{96,32},{1,65},{33,97},{65,1},{97,33},{2,66}... | collective-permute-start | bytes 1179656 | tf_op jit(solution)/shard_map/ppermute | solution.py:267
  13.9 26.3 %collective-permute-start.7 = (bf16[2,128,768]{2,1,0:T(8,128)(2,1)S(1)}, bf16[2,128,768]{2,1,0:T(8,128)(2,1)S(1)}, u32[]{:S(2)}, u32[]{:S(2)}) collective-permute-start(bf16[2,128,768]{2,1,0:T(8,128)(2,1)S(1)} %get-tuple-element.99), channel_id=1, source_target_pairs={{0,96},{32,0},{64,32},{96,64},{1,97},{33,1},{65,33},{97,65},{2,98}... | collective-permute-start | bytes 1179656 | tf_op jit(solution)/shard_map/ppermute | solution.py:267
  16.2 24.0 %copy-start.17 = (f32[1024]{0:T(1024)}, f32[1024]{0:T(1024)S(1)}, u32[]{:S(2)}) copy-start(f32[1024]{0:T(1024)S(1)} %convert_element_type.6) | copy-start | bytes 12292
  21.0 23.2 %collective-permute-start.2 = (bf16[528,128]{1,0:T(8,128)(2,1)}, bf16[528,128]{1,0:T(8,128)(2,1)S(1)}, u32[]{:S(2)}, u32[]{:S(2)}) collective-permute-start(bf16[528,128]{1,0:T(8,128)(2,1)} %tail.1.refs_0_), channel_id=1, source_target_pairs={{0,24},{8,0},{16,8},{24,16},{1,25},{9,1},{17,9},{25,17},{2,26},{10... | collective-permute-start | bytes 405512 | tf_op jit(solution)/shard_map/ppermute | solution.py:267
  38.7 7.8 %collective-permute-start.1 = (bf16[528,128]{1,0:T(8,128)(2,1)}, bf16[528,128]{1,0:T(8,128)(2,1)S(1)}, u32[]{:S(2)}, u32[]{:S(2)}) collective-permute-start(bf16[528,128]{1,0:T(8,128)(2,1)} %tail.1.refs_0_), channel_id=1, source_target_pairs={{0,16},{8,24},{16,0},{24,8},{1,17},{9,25},{17,1},{25,9},{2,18},{10... | collective-permute-start | bytes 405512 | tf_op jit(solution)/shard_map/ppermute | solution.py:267
  38.7 8.8 %collective-permute-start = (bf16[528,128]{1,0:T(8,128)(2,1)}, bf16[528,128]{1,0:T(8,128)(2,1)S(1)}, u32[]{:S(2)}, u32[]{:S(2)}) collective-permute-start(bf16[528,128]{1,0:T(8,128)(2,1)} %tail.1.refs_0_), channel_id=1, source_target_pairs={{0,8},{8,16},{16,24},{24,0},{1,9},{9,17},{17,25},{25,1},{2,10},{10... | collective-permute-start | bytes 405512 | tf_op jit(solution)/shard_map/ppermute | solution.py:267
  40.2 39.3 %copy-start = (bf16[2,2,128,768]{3,2,1,0:T(8,128)(2,1)}, bf16[2,2,128,768]{3,2,1,0:T(8,128)(2,1)S(1)}, u32[]{:S(2)}) copy-start(bf16[2,2,128,768]{3,2,1,0:T(8,128)(2,1)S(1)} %pad_maximum_fusion.refs_10_) | copy-start | bytes 2359300
  40.3 39.2 %copy-start.1 = (bf16[2,2,128,768]{3,2,1,0:T(8,128)(2,1)}, bf16[2,2,128,768]{3,2,1,0:T(8,128)(2,1)S(1)}, u32[]{:S(2)}) copy-start(bf16[2,2,128,768]{3,2,1,0:T(8,128)(2,1)S(1)} %pad_maximum_fusion.1.refs_11_) | copy-start | bytes 2359300
  44.2 10.0 %copy-start.11 = (bf16[528,128]{1,0:T(8,128)(2,1)}, bf16[528,128]{1,0:T(8,128)(2,1)S(1)}, u32[]{:S(2)}) copy-start(bf16[528,128]{1,0:T(8,128)(2,1)S(1)} %collective-permute-done.2.refs_3_.refs_2_) | copy-start | bytes 405508
  46.5 7.7 %copy-start.12 = (bf16[528,128]{1,0:T(8,128)(2,1)}, bf16[528,128]{1,0:T(8,128)(2,1)S(1)}, u32[]{:S(2)}) copy-start(bf16[528,128]{1,0:T(8,128)(2,1)S(1)} %collective-permute-done.1.refs_2_.refs_1_) | copy-start | bytes 405508
  47.5 23.2 %collective-permute-start.10 = (bf16[2,2,128,768]{3,2,1,0:T(8,128)(2,1)S(1)}, bf16[2,2,128,768]{3,2,1,0:T(8,128)(2,1)S(1)}, u32[]{:S(2)}, u32[]{:S(2)}) collective-permute-start(bf16[2,2,128,768]{3,2,1,0:T(8,128)(2,1)S(1)} %pad_maximum_fusion.refs_10_), channel_id=1, source_target_pairs={{0,24},{8,0},{16,8},{24,16},{1,25},{9,1},{17,9},{25,17},{2,26},{10... | collective-permute-start | bytes 2359304 | tf_op jit(solution)/shard_map/ppermute | solution.py:267
  50.9 21.8 %collective-permute-start.11 = (bf16[2,2,128,768]{3,2,1,0:T(8,128)(2,1)S(1)}, bf16[2,2,128,768]{3,2,1,0:T(8,128)(2,1)}, u32[]{:S(2)}, u32[]{:S(2)}) collective-permute-start(bf16[2,2,128,768]{3,2,1,0:T(8,128)(2,1)S(1)} %pad_maximum_fusion.1.refs_11_), channel_id=1, source_target_pairs={{0,8},{8,16},{16,24},{24,0},{1,9},{9,17},{17,25},{25,1},{2,10},{10... | collective-permute-start | bytes 2359304 | tf_op jit(solution)/shard_map/ppermute | solution.py:267
  50.9 36.7 %collective-permute-start.15 = (bf16[2,2,128,768]{3,2,1,0:T(8,128)(2,1)S(1)}, bf16[2,2,128,768]{3,2,1,0:T(8,128)(2,1)}, u32[]{:S(2)}, u32[]{:S(2)}) collective-permute-start(bf16[2,2,128,768]{3,2,1,0:T(8,128)(2,1)S(1)} %pad_maximum_fusion.refs_10_), channel_id=1, source_target_pairs={{0,8},{8,16},{16,24},{24,0},{1,9},{9,17},{17,25},{25,1},{2,10},{10... | collective-permute-start | bytes 2359304 | tf_op jit(solution)/shard_map/ppermute | solution.py:267
  51.0 36.7 %collective-permute-start.14 = (bf16[2,2,128,768]{3,2,1,0:T(8,128)(2,1)S(1)}, bf16[2,2,128,768]{3,2,1,0:T(8,128)(2,1)}, u32[]{:S(2)}, u32[]{:S(2)}) collective-permute-start(bf16[2,2,128,768]{3,2,1,0:T(8,128)(2,1)S(1)} %pad_maximum_fusion.1.refs_11_), channel_id=1, source_target_pairs={{0,24},{8,0},{16,8},{24,16},{1,25},{9,1},{17,9},{25,17},{2,26},{10... | collective-permute-start | bytes 2359304 | tf_op jit(solution)/shard_map/ppermute | solution.py:267
  56.0 6.5 %collective-permute-start.9 = (bf16[528,128]{1,0:T(8,128)(2,1)}, bf16[528,128]{1,0:T(8,128)(2,1)S(1)}, u32[]{:S(2)}, u32[]{:S(2)}) collective-permute-start(bf16[528,128]{1,0:T(8,128)(2,1)} %row_state.2), channel_id=1, source_target_pairs={{0,64},{32,96},{1,65},{33,97},{2,66},{34,98},{3,67},{35,99},{4,68}... | collective-permute-start | bytes 405512 | tf_op jit(solution)/shard_map/ppermute | solution.py:273
  62.6 10.1 %copy-start.20 = (bf16[528,128]{1,0:T(8,128)(2,1)}, bf16[528,128]{1,0:T(8,128)(2,1)S(1)}, u32[]{:S(2)}) copy-start(bf16[528,128]{1,0:T(8,128)(2,1)S(1)} %collective-permute-done.9.refs_4_) | copy-start | bytes 405508
  62.6 8.1 %collective-permute-start.8 = (bf16[528,128]{1,0:T(8,128)(2,1)}, bf16[528,128]{1,0:T(8,128)(2,1)S(1)}, u32[]{:S(2)}, u32[]{:S(2)}) collective-permute-start(bf16[528,128]{1,0:T(8,128)(2,1)} %row_state.2), channel_id=1, source_target_pairs={{0,32},{32,64},{64,96},{1,33},{33,65},{65,97},{2,34},{34,66},{66,9... | collective-permute-start | bytes 405512 | tf_op jit(solution)/shard_map/ppermute | solution.py:273
  70.7 8.8 %copy-start.5 = (bf16[2,2,128,768]{3,2,1,0:T(8,128)(2,1)}, bf16[2,2,128,768]{3,2,1,0:T(8,128)(2,1)S(1)}, u32[]{:S(2)}) copy-start(bf16[2,2,128,768]{3,2,1,0:T(8,128)(2,1)S(1)} %collective-permute-done.10.refs_12_) | copy-start | bytes 2359300
  101.9 24.5 %collective-permute-start.17 = (bf16[1024,512]{1,0:T(8,128)(2,1)S(1)}, bf16[1024,512]{1,0:T(8,128)(2,1)S(1)}, u32[]{:S(2)}, u32[]{:S(2)}) collective-permute-start(bf16[1024,512]{1,0:T(8,128)(2,1)S(1)} %copy-done.4), channel_id=1, source_target_pairs={{0,2},{2,4},{4,6},{6,0},{1,3},{3,5},{5,7},{7,1},{8,10},{10,12},{12... | collective-permute-start | bytes 3145736 | tf_op jit(solution)/shard_map/ppermute | solution.py:267
  101.9 24.5 %collective-permute-start.16 = (bf16[1024,512]{1,0:T(8,128)(2,1)S(1)}, bf16[1024,512]{1,0:T(8,128)(2,1)S(1)}, u32[]{:S(2)}, u32[]{:S(2)}) collective-permute-start(bf16[1024,512]{1,0:T(8,128)(2,1)S(1)} %copy-done.4), channel_id=1, source_target_pairs={{0,6},{2,0},{4,2},{6,4},{1,7},{3,1},{5,3},{7,5},{8,14},{10,8},{12,... | collective-permute-start | bytes 3145736 | tf_op jit(solution)/shard_map/ppermute | solution.py:267
  105.1 17.8 %collective-permute-start.12 = (bf16[2,2,128,768]{3,2,1,0:T(8,128)(2,1)}, bf16[2,2,128,768]{3,2,1,0:T(8,128)(2,1)S(1)}, u32[]{:S(2)}, u32[]{:S(2)}) collective-permute-start(bf16[2,2,128,768]{3,2,1,0:T(8,128)(2,1)} %copy-done.5), channel_id=1, source_target_pairs={{0,24},{8,0},{16,8},{24,16},{1,25},{9,1},{17,9},{25,17},{2,26},{10... | collective-permute-start | bytes 2359304 | tf_op jit(solution)/shard_map/ppermute | solution.py:267
  105.4 18.5 %collective-permute-start.13 = (bf16[2,2,128,768]{3,2,1,0:T(8,128)(2,1)}, bf16[2,2,128,768]{3,2,1,0:T(8,128)(2,1)S(1)}, u32[]{:S(2)}, u32[]{:S(2)}) collective-permute-start(bf16[2,2,128,768]{3,2,1,0:T(8,128)(2,1)} %collective-permute-done.11.refs_17_), channel_id=1, source_target_pairs={{0,8},{8,16},{16,24},{24,0},{1,9},{9,17},{17,25},{25,1},{2,10},{10... | collective-permute-start | bytes 2359304 | tf_op jit(solution)/shard_map/ppermute | solution.py:267
  123.0 16.0 %copy-start.6 = (bf16[2,2,128,768]{3,2,1,0:T(8,128)(2,1)}, bf16[2,2,128,768]{3,2,1,0:T(8,128)(2,1)S(1)}, u32[]{:S(2)}) copy-start(bf16[2,2,128,768]{3,2,1,0:T(8,128)(2,1)S(1)} %collective-permute-done.12.refs_14_) | copy-start | bytes 2359300
  123.9 15.6 %copy-start.7 = (bf16[2,2,128,768]{3,2,1,0:T(8,128)(2,1)}, bf16[2,2,128,768]{3,2,1,0:T(8,128)(2,1)S(1)}, u32[]{:S(2)}) copy-start(bf16[2,2,128,768]{3,2,1,0:T(8,128)(2,1)S(1)} %collective-permute-done.13.refs_15_) | copy-start | bytes 2359300
  126.3 21.9 %copy-start.2 = (bf16[1024,512]{1,0:T(8,128)(2,1)}, bf16[1024,512]{1,0:T(8,128)(2,1)S(1)}, u32[]{:S(2)}) copy-start(bf16[1024,512]{1,0:T(8,128)(2,1)S(1)} %collective-permute-done.17.refs_4_) | copy-start | bytes 3145732
  126.4 21.9 %copy-start.3 = (bf16[1024,512]{1,0:T(8,128)(2,1)}, bf16[1024,512]{1,0:T(8,128)(2,1)S(1)}, u32[]{:S(2)}) copy-start(bf16[1024,512]{1,0:T(8,128)(2,1)S(1)} %collective-permute-done.16.refs_2_) | copy-start | bytes 3145732
  126.4 12.5 %collective-permute-start.22 = (bf16[512,512]{1,0:T(8,128)(2,1)S(1)}, bf16[512,512]{1,0:T(8,128)(2,1)}, u32[]{:S(2)}, u32[]{:S(2)}) collective-permute-start(bf16[512,512]{1,0:T(8,128)(2,1)S(1)} %slice.15), channel_id=1, source_target_pairs={{0,2},{2,4},{4,6},{6,0},{1,3},{3,5},{5,7},{7,1},{8,10},{10,12},{12... | collective-permute-start | bytes 1572872 | tf_op jit(solution)/shard_map/ppermute | solution.py:267
  126.5 12.4 %collective-permute-start.21 = (bf16[512,512]{1,0:T(8,128)(2,1)S(1)}, bf16[512,512]{1,0:T(8,128)(2,1)}, u32[]{:S(2)}, u32[]{:S(2)}) collective-permute-start(bf16[512,512]{1,0:T(8,128)(2,1)S(1)} %slice.14), channel_id=1, source_target_pairs={{0,6},{2,0},{4,2},{6,4},{1,7},{3,1},{5,3},{7,5},{8,14},{10,8},{12,... | collective-permute-start | bytes 1572872 | tf_op jit(solution)/shard_map/ppermute | solution.py:267
  129.7 7.7 %collective-permute-start.20 = (bf16[528,128]{1,0:T(8,128)(2,1)S(1)}, bf16[528,128]{1,0:T(8,128)(2,1)S(1)}, u32[]{:S(2)}, u32[]{:S(2)}) collective-permute-start(bf16[528,128]{1,0:T(8,128)(2,1)S(1)} %copy-done.22), channel_id=1, source_target_pairs={{0,8},{8,16},{16,24},{24,0},{1,9},{9,17},{17,25},{25,1},{2,10},{10... | collective-permute-start | bytes 405512 | tf_op jit(solution)/shard_map/ppermute | solution.py:267
  129.8 7.7 %collective-permute-start.19 = (bf16[528,128]{1,0:T(8,128)(2,1)S(1)}, bf16[528,128]{1,0:T(8,128)(2,1)S(1)}, u32[]{:S(2)}, u32[]{:S(2)}) collective-permute-start(bf16[528,128]{1,0:T(8,128)(2,1)S(1)} %copy-done.22), channel_id=1, source_target_pairs={{0,16},{8,24},{16,0},{24,8},{1,17},{9,25},{17,1},{25,9},{2,18},{10... | collective-permute-start | bytes 405512 | tf_op jit(solution)/shard_map/ppermute | solution.py:267
  131.8 6.6 %collective-permute-start.18 = (bf16[528,128]{1,0:T(8,128)(2,1)S(1)}, bf16[528,128]{1,0:T(8,128)(2,1)S(1)}, u32[]{:S(2)}, u32[]{:S(2)}) collective-permute-start(bf16[528,128]{1,0:T(8,128)(2,1)S(1)} %copy-done.22), channel_id=1, source_target_pairs={{0,24},{8,0},{16,8},{24,16},{1,25},{9,1},{17,9},{25,17},{2,26},{10... | collective-permute-start | bytes 405512 | tf_op jit(solution)/shard_map/ppermute | solution.py:267
  137.4 10.8 %collective-permute-start.26 = (bf16[1024,512]{1,0:T(8,128)(2,1)S(1)}, bf16[1024,512]{1,0:T(8,128)(2,1)}, u32[]{:S(2)}, u32[]{:S(2)}) collective-permute-start(bf16[1024,512]{1,0:T(8,128)(2,1)S(1)} %collective-permute-done.16.refs_2_), channel_id=1, source_target_pairs={{0,1},{1,0},{2,3},{3,2},{4,5},{5,4},{6,7},{7,6},{8,9},{9,8},{10,11... | collective-permute-start | bytes 3145736 | tf_op jit(solution)/shard_map/ppermute | solution.py:277
  137.4 10.8 %collective-permute-start.27 = (bf16[1024,512]{1,0:T(8,128)(2,1)S(1)}, bf16[1024,512]{1,0:T(8,128)(2,1)}, u32[]{:S(2)}, u32[]{:S(2)}) collective-permute-start(bf16[1024,512]{1,0:T(8,128)(2,1)S(1)} %collective-permute-done.17.refs_4_), channel_id=1, source_target_pairs={{0,1},{1,0},{2,3},{3,2},{4,5},{5,4},{6,7},{7,6},{8,9},{9,8},{10,11... | collective-permute-start | bytes 3145736 | tf_op jit(solution)/shard_map/ppermute | solution.py:277
  138.9 9.3 %collective-permute-start.25 = (bf16[1024,512]{1,0:T(8,128)(2,1)S(1)}, bf16[1024,512]{1,0:T(8,128)(2,1)}, u32[]{:S(2)}, u32[]{:S(2)}) collective-permute-start(bf16[1024,512]{1,0:T(8,128)(2,1)S(1)} %copy-done.4), channel_id=1, source_target_pairs={{0,1},{1,0},{2,3},{3,2},{4,5},{5,4},{6,7},{7,6},{8,9},{9,8},{10,11... | collective-permute-start | bytes 3145736 | tf_op jit(solution)/shard_map/ppermute | solution.py:277
  138.9 4.5 %collective-permute-start.28 = (bf16[512,512]{1,0:T(8,128)(2,1)}, bf16[512,512]{1,0:T(8,128)(2,1)}, u32[]{:S(2)}, u32[]{:S(2)}) collective-permute-start(bf16[512,512]{1,0:T(8,128)(2,1)} %collective-permute-done.21.refs_6_), channel_id=1, source_target_pairs={{0,1},{1,0},{2,3},{3,2},{4,5},{5,4},{6,7},{7,6},{8,9},{9,8},{10,11... | collective-permute-start | bytes 1572872 | tf_op jit(solution)/shard_map/ppermute | solution.py:277
  139.4 5.5 %collective-permute-start.29 = (bf16[512,512]{1,0:T(8,128)(2,1)}, bf16[512,512]{1,0:T(8,128)(2,1)}, u32[]{:S(2)}, u32[]{:S(2)}) collective-permute-start(bf16[512,512]{1,0:T(8,128)(2,1)} %collective-permute-done.22.refs_7_), channel_id=1, source_target_pairs={{0,1},{1,0},{2,3},{3,2},{4,5},{5,4},{6,7},{7,6},{8,9},{9,8},{10,11... | collective-permute-start | bytes 1572872 | tf_op jit(solution)/shard_map/ppermute | solution.py:277
  143.4 18.5 %collective-permute-start.24 = (bf16[528,128]{1,0:T(8,128)(2,1)}, bf16[528,128]{1,0:T(8,128)(2,1)S(1)}, u32[]{:S(2)}, u32[]{:S(2)}) collective-permute-start(bf16[528,128]{1,0:T(8,128)(2,1)} %row_state.3), channel_id=1, source_target_pairs={{64,0},{96,32},{65,1},{97,33},{66,2},{98,34},{67,3},{99,35},{68,4}... | collective-permute-start | bytes 405512 | tf_op jit(solution)/shard_map/ppermute | solution.py:273
  144.9 17.1 %collective-permute-start.23 = (bf16[528,128]{1,0:T(8,128)(2,1)}, bf16[528,128]{1,0:T(8,128)(2,1)S(1)}, u32[]{:S(2)}, u32[]{:S(2)}) collective-permute-start(bf16[528,128]{1,0:T(8,128)(2,1)} %row_state.3), channel_id=1, source_target_pairs={{32,0},{64,32},{96,64},{33,1},{65,33},{97,65},{34,2},{66,34},{98,6... | collective-permute-start | bytes 405512 | tf_op jit(solution)/shard_map/ppermute | solution.py:273
  171.6 12.1 %collective-permute-start.32 = (bf16[512,384]{1,0:T(8,128)(2,1)S(1)}, bf16[512,384]{1,0:T(8,128)(2,1)S(1)}, u32[]{:S(2)}, u32[]{:S(2)}) collective-permute-start(bf16[512,384]{1,0:T(8,128)(2,1)S(1)} %get-tuple-element.95), channel_id=1, source_target_pairs={{0,24},{8,0},{16,8},{24,16},{1,25},{9,1},{17,9},{25,17},{2,26},{10... | collective-permute-start | bytes 1179656 | tf_op jit(solution)/shard_map/ppermute | solution.py:267
  172.5 13.6 %collective-permute-start.31 = (bf16[512,384]{1,0:T(8,128)(2,1)S(1)}, bf16[512,384]{1,0:T(8,128)(2,1)S(1)}, u32[]{:S(2)}, u32[]{:S(2)}) collective-permute-start(bf16[512,384]{1,0:T(8,128)(2,1)S(1)} %get-tuple-element.96), channel_id=1, source_target_pairs={{0,16},{8,24},{16,0},{24,8},{1,17},{9,25},{17,1},{25,9},{2,18},{10... | collective-permute-start | bytes 1179656 | tf_op jit(solution)/shard_map/ppermute | solution.py:267
  172.8 20.4 %collective-permute-start.30 = (bf16[512,384]{1,0:T(8,128)(2,1)S(1)}, bf16[512,384]{1,0:T(8,128)(2,1)S(1)}, u32[]{:S(2)}, u32[]{:S(2)}) collective-permute-start(bf16[512,384]{1,0:T(8,128)(2,1)S(1)} %get-tuple-element.97), channel_id=1, source_target_pairs={{0,8},{8,16},{16,24},{24,0},{1,9},{9,17},{17,25},{25,1},{2,10},{10... | collective-permute-start | bytes 1179656 | tf_op jit(solution)/shard_map/ppermute | solution.py:267
  183.7 9.6 %copy-start.14 = (bf16[512,384]{1,0:T(8,128)(2,1)}, bf16[512,384]{1,0:T(8,128)(2,1)S(1)}, u32[]{:S(2)}) copy-start(bf16[512,384]{1,0:T(8,128)(2,1)S(1)} %collective-permute-done.32.refs_2_) | copy-start | bytes 1179652
  (11 other events, 31.4 us)
Sparse Core Ops, SparseCore 0:
  9.7 69.9 all-gather.2
  100.8 66.4 reduce-scatter.1

commit v4 on v2

--- a/solution.py
+++ b/solution.py
@@ -348,10 +348,10 @@
     table = jnp.broadcast_to(table[:, None], (16, HEAD))
 
     tail = pl.pallas_call(tail_kernel, out_shape=payload, name="tail")(keys, values, dcol, table)
-    strip = column_strip(out_weight, share, cx)
-    arrived, strip = exchanged(tail, 1, strip)
+    arrived, strip = exchanged(tail, 1, column_strip(out_weight, share, cx))
     own = column_pieces(strip, share, core)
     arrived, own = lax.optimization_barrier((arrived, own))
+    early = [turned_by(own[0], "cy", -1), turned_by(own[1], "cy", 1)]
 
     row_block = pl.BlockSpec((1, CHUNK), lambda i: (0, i))
     state_block = pl.BlockSpec((1, size, HEAD), lambda i: (i, 0, 0))
@@ -378,10 +378,7 @@
         name="forward",
     )(queries, keys, values, dcol, drow, table, *arrived)
 
-    early = [turned_by(own[0], "cy", s) for s in (-1, 1)]
     turned, early = lax.optimization_barrier((turned, early))
-    later = [turned_by(own[1], "cy", s) for s in (-1, 1)]
-
     term = pl.pallas_call(
         weight_kernel,
         grid=(groups,),
@@ -391,16 +388,13 @@
         compiler_params=params(),
         name="weight_grad",
     )(turned, grad_whole)
-    term, low = lax.optimization_barrier((term, low))
+    term, low, own = lax.optimization_barrier((term, low, own))
+    later = [turned_by(own[1], "cy", -1), turned_by(own[0], "cy", 1)]
     grad_part = lax.psum_scatter(term, "cx", scatter_dimension=0, tiled=True)[0]
 
     half_rows = rows // 2
     above = turned_by(low, "z", -1)
     below = turned_by(low, "z", 1)
-    far_a = turned_by(above[:half_rows], "z", -1)
-    far_b = turned_by(below[half_rows:], "z", 1)
-    near = [low, swapped(low), above, swapped(above), below, swapped(below)]
-    far = [far_a, far_b, swapped(far_a), swapped(far_b)]
 
     grad_opened, head = pl.pallas_call(
         cotangent_kernel,
@@ -419,12 +413,15 @@
         compiler_params=params(),
         name="cotangent",
     )(grad_whole, out_weight, opened, queries, dcol, table)
-    head, later = lax.optimization_barrier((head, later))
-    returned, _ = exchanged(head, -1)
-
-    returned, early, later = lax.optimization_barrier((returned, early, later))
-    across = (turned_by(early[0], "cy", -1), turned_by(later[1], "cy", 1))
-    columns = [*own, early[0], later[0], *across, early[1], later[1]]
+    head, later, above, below = lax.optimization_barrier((head, later, above, below))
+    far_a = turned_by(above[:half_rows], "z", -1)
+    far_b = turned_by(below[half_rows:], "z", 1)
+    moved = (far_a, far_b, low, above, below, early)
+    returned, (far_a, far_b, low, above, below, early) = exchanged(head, -1, moved)
+    across = [turned_by(early[0], "cy", -1), turned_by(early[1], "cy", 1)]
+    near = [low, swapped(low), above, swapped(above), below, swapped(below)]
+    far = [far_a, far_b, swapped(far_a), swapped(far_b)]
+    columns = [*own, early[0], later[0], *across, later[1], early[1]]
 
     grad_query = pl.pallas_call(
         query_kernel,
@@ -436,6 +433,9 @@
         compiler_params=params(),
         name="grad_query",
     )(grad_opened, keys, values, dcol, drow, table, states)
+
+    ready = (returned, grad_query, near, far)
+    returned, grad_query, near, far = lax.optimization_barrier(ready)
 
     back_row = pl.BlockSpec((1, CHUNK), lambda i: (0, blocks - 1 - i))
     grad_key, grad_value = pl.pallas_call(
@@ -451,6 +451,8 @@
         name="grad_key_value",
     )(grad_opened, queries, keys, values, dcol, drow, table, *returned)
 
+    ready = (grad_part, grad_key, columns)
+    grad_part, grad_key, columns = lax.optimization_barrier(ready)
     sides = (core, 1 - core)
     around = [2 * ((z + cy + s) % 4) + side for s in range(4) for side in sides]
     heads_at = [(cx - s) % 4 for s in range(4)]
@@ -475,7 +477,6 @@
         compiler_params=params(),
         name="attended",
     )(jnp.stack(around + heads_at + groups_at), *near, *far, *columns)
-    grad_part, attended, grad_key = lax.optimization_barrier((grad_part, attended, grad_key))
     grad_weight = row_sum(grad_part, cy)
     return attended, grad_query, grad_key, grad_value, grad_weight
 

time: 236 us -> 213 us (0.903)
  waiting for transfers between devices: 91.7 us -> 70.7 us
  local copies, waits for them, and re-layouts: 13.4 us -> 8.6 us
    ppermute x22, waiting for transfers between devices: 74.3 us -> 52.4 us  [turned_by(): lax.ppermute(value, axis, [(i, (i + step) % size) for i in range(size)])]
    unnamed x54 -> x58, local copies, waits for them, and re-layouts: 7.01 us -> 3.58 us
  transfers between devices with their start and end apart: 35 -> 35, of which waited for: 19 -> 22; matrix products, arithmetic and copies ran while one was open for 2% -> 3% of each run, Pallas kernels for 24% -> 26%
where the time goes in v4:
time: 213 us; the launch traced here: 212 us
  Pallas kernels  70.8 us (33%)
  waiting for transfers between devices  70.7 us (33%)
  starting transfers between devices  44.9 us (21%)
  between operations  14.4 us (7%)
  local copies, waits for them, and re-layouts  8.6 us (4%)
  other arithmetic  2.29 us (1%)
    ppermute x22, waiting for transfers between devices, turned_by(): lax.ppermute(value, axis, [(i, (i + step) % size) for i in range(size)])  52.4 us
    ppermute x22, starting transfers between devices, turned_by(): lax.ppermute(value, axis, [(i, (i + step) % size) for i in range(size)])  35.2 us
    pallas_call x1, Pallas kernels, body(): pl.pallas_call(cotangent_kernel, grid=(blocks,), in_specs=[pl.BlockSpec((...  14.9 us
    ppermute x4, waiting for transfers between devices, moved_by(): return lax.ppermute(value, axis, pairs)  14 us
    pallas_call x1, Pallas kernels, body(): pl.pallas_call(attended_kernel, grid_spec=pltpu.PrefetchScalarGridSpec(nu...  13.7 us
    pallas_call x1, Pallas kernels, body(): pl.pallas_call(weight_kernel, grid=(groups,), in_specs=[whole((width, row...  13 us
    ppermute x4, starting transfers between devices, moved_by(): return lax.ppermute(value, axis, pairs)  8.28 us
    pallas_call x1, Pallas kernels, body(): pl.pallas_call(key_value_kernel, grid=(blocks,), in_specs=[rows_of(width,...  7.45 us
  transfers between devices with their start and end apart: 35, of which 22 were waited for; matrix products, arithmetic and copies ran while one was open for 3% of the time, Pallas kernels for 26%

profile of v4, /device:TPU:2, one launch (start us, length us, event | category | flops | bytes accessed | tf_op | source)
XLA Modules:
  0.0 211.7 jit_solution(9458592390515658368)
XLA Ops:
  11.7 2.8 %tail.1.refs_0_ = bf16[528,128]{1,0:T(8,128)(2,1)} custom-call(bf16[1024,512]{1,0:T(8,128)(2,1)} %k.7, bf16[1024,512]{1,0:T(8,128)(2,1)} %v.7, f32[1024,128]{1,0:T(8,128)} %broadcast_in_dim.10.dcol, f32[16,128]{1,0:T(8,128)} %broadcast_in_dim.24.table), custom_call_target="tpu_custom_call" | custom-call | tf_op jit(solution)/shard_map/tail/pallas_call | solution.py:350
  14.5 6.8 %collective-permute-start = (bf16[528,128]{1,0:T(8,128)(2,1)}, bf16[528,128]{1,0:T(8,128)(2,1)S(1)}, u32[]{:S(2)}, u32[]{:S(2)}) collective-permute-start(bf16[528,128]{1,0:T(8,128)(2,1)} %tail.1.refs_0_), channel_id=1, source_target_pairs={{0,8},{8,16},{16,24},{24,0},{1,9},{9,17},{17,25},{25,1},{2,10},{10... | collective-permute-start | bytes 405512 | tf_op jit(solution)/shard_map/ppermute | solution.py:267
  21.4 1.5 collective-permute-start.1
  22.8 2.6 %collective-permute-start.2 = (bf16[528,128]{1,0:T(8,128)(2,1)}, bf16[528,128]{1,0:T(8,128)(2,1)S(1)}, u32[]{:S(2)}, u32[]{:S(2)}) collective-permute-start(bf16[528,128]{1,0:T(8,128)(2,1)} %tail.1.refs_0_), channel_id=1, source_target_pairs={{0,24},{8,0},{16,8},{24,16},{1,25},{9,1},{17,9},{25,17},{2,26},{10... | collective-permute-start | bytes 405512 | tf_op jit(solution)/shard_map/ppermute | solution.py:267
  25.7 3.6 %collective-permute-done.1.refs_2_.refs_1_ = bf16[528,128]{1,0:T(8,128)(2,1)S(1)} collective-permute-done((bf16[528,128]{1,0:T(8,128)(2,1)}, bf16[528,128]{1,0:T(8,128)(2,1)S(1)}, u32[]{:S(2)}, u32[]{:S(2)}) %collective-permute-start.1) | collective-permute-done | bytes 135200 | tf_op jit(solution)/shard_map/ppermute | solution.py:267
  29.4 1.4 collective-permute-done.6
  30.9 1.6 collective-permute-start.7
  33.0 2.1 %collective-permute-start.8 = (bf16[2,128,768]{2,1,0:T(8,128)(2,1)S(1)}, bf16[2,128,768]{2,1,0:T(8,128)(2,1)S(1)}, u32[]{:S(2)}, u32[]{:S(2)}) collective-permute-start(bf16[2,128,768]{2,1,0:T(8,128)(2,1)S(1)} %get-tuple-element.145), channel_id=1, source_target_pairs={{0,64},{32,96},{64,0},{96,32},{1,65},{33,97},{65,1},{97,33},{2,66}... | collective-permute-start | bytes 1179656 | tf_op jit(solution)/shard_map/ppermute | solution.py:267
  35.1 1.9 row_state.2
  37.0 3.0 %collective-permute-start.4 = (bf16[528,128]{1,0:T(8,128)(2,1)}, bf16[528,128]{1,0:T(8,128)(2,1)S(1)}, u32[]{:S(2)}, u32[]{:S(2)}) collective-permute-start(bf16[528,128]{1,0:T(8,128)(2,1)} %row_state.2), channel_id=1, source_target_pairs={{0,32},{32,64},{64,96},{1,33},{33,65},{65,97},{2,34},{34,66},{66,9... | collective-permute-start | bytes 405512 | tf_op jit(solution)/shard_map/ppermute | solution.py:273
  40.0 1.6 collective-permute-start.5
  41.6 8.2 %collective-permute-done.7 = bf16[2,128,768]{2,1,0:T(8,128)(2,1)S(1)} collective-permute-done((bf16[2,128,768]{2,1,0:T(8,128)(2,1)S(1)}, bf16[2,128,768]{2,1,0:T(8,128)(2,1)S(1)}, u32[]{:S(2)}, u32[]{:S(2)}) %collective-permute-start.7) | collective-permute-done | bytes 393248 | tf_op jit(solution)/shard_map/ppermute | solution.py:267
  50.6 1.1 pad_maximum_fusion.refs_10_
  53.1 1.2 pad_maximum_fusion.1.refs_11_
  54.3 2.8 %collective-permute-start.10 = (bf16[2,2,128,768]{3,2,1,0:T(8,128)(2,1)S(1)}, bf16[2,2,128,768]{3,2,1,0:T(8,128)(2,1)S(1)}, u32[]{:S(2)}, u32[]{:S(2)}) collective-permute-start(bf16[2,2,128,768]{3,2,1,0:T(8,128)(2,1)S(1)} %pad_maximum_fusion.refs_10_), channel_id=1, source_target_pairs={{0,24},{8,0},{16,8},{24,16},{1,25},{9,1},{17,9},{25,17},{2,26},{10... | collective-permute-start | bytes 2359304 | tf_op jit(solution)/shard_map/ppermute | solution.py:267
  57.2 6.9 %forward.1 = (f32[1024,512]{1,0:T(8,128)}, bf16[1024,512]{1,0:T(8,128)(2,1)}, bf16[512,1024]{1,0:T(8,128)(2,1)}, bf16[4,512,128]{2,1,0:T(8,128)(2,1)}) custom-call(bf16[1024,512]{1,0:T(8,128)(2,1)} %q.5, bf16[1024,512]{1,0:T(8,128)(2,1)} %k.7, bf16[1024,512]{1,0:T(8,128)(2,1)} %v.7, f32[1024,128]{1,0:T(8,128)} %broadcast_in_dim.10.dcol, f32[1,1024]{1,0:T(1,128)} %bitcast.47, ...), custom_call_target="tpu_custom_call" | custom-call | tf_op jit(solution)/shard_map/forward/pallas_call | solution.py:358
  64.1 9.0 %collective-permute-done.10.refs_12_ = bf16[2,2,128,768]{3,2,1,0:T(8,128)(2,1)S(1)} collective-permute-done((bf16[2,2,128,768]{3,2,1,0:T(8,128)(2,1)S(1)}, bf16[2,2,128,768]{3,2,1,0:T(8,128)(2,1)S(1)}, u32[]{:S(2)}, u32[]{:S(2)}) %collective-permute-start.10) | collective-permute-done | bytes 786464 | tf_op jit(solution)/shard_map/ppermute | solution.py:267
  73.2 3.4 %collective-permute-done.11.refs_17_ = bf16[2,2,128,768]{3,2,1,0:T(8,128)(2,1)S(1)} collective-permute-done((bf16[2,2,128,768]{3,2,1,0:T(8,128)(2,1)S(1)}, bf16[2,2,128,768]{3,2,1,0:T(8,128)(2,1)S(1)}, u32[]{:S(2)}, u32[]{:S(2)}) %collective-permute-start.11) | collective-permute-done | bytes 786464 | tf_op jit(solution)/shard_map/ppermute | solution.py:267
  77.5 2.2 %all-gather.3.cloned.1.call-done = bf16[8192,768]{1,0:T(8,128)(2,1)} async-done(((bf16[1024,768]{1,0:T(8,128)(2,1)}), bf16[8192,768]{1,0:T(8,128)(2,1)}) %all-gather.3.cloned.1.call-update) | async-done | bytes 12582928 | tf_op jit(solution)/shard_map/all_gather | solution.py:340
  79.7 13.0 %weight_grad.1 = bf16[4,4,512,384]{3,2,1,0:T(8,128)(2,1)} custom-call(bf16[512,1024]{1,0:T(8,128)(2,1)} %get-tuple-element.86.turned, bf16[8,1024,768]{2,1,0:T(8,128)(2,1)} %bitcast.39), custom_call_target="tpu_custom_call" | custom-call | tf_op jit(solution)/shard_map/weight_grad/pallas_call | solution.py:382
  93.7 1.1 collective-permute-start.15
  94.8 2.7 %collective-permute-start.12 = (bf16[2,2,128,768]{3,2,1,0:T(8,128)(2,1)S(1)}, bf16[2,2,128,768]{3,2,1,0:T(8,128)(2,1)S(1)}, u32[]{:S(2)}, u32[]{:S(2)}) collective-permute-start(bf16[2,2,128,768]{3,2,1,0:T(8,128)(2,1)S(1)} %pad_maximum_fusion.1.refs_11_), channel_id=1, source_target_pairs={{0,24},{8,0},{16,8},{24,16},{1,25},{9,1},{17,9},{25,17},{2,26},{10... | collective-permute-start | bytes 2359304 | tf_op jit(solution)/shard_map/ppermute | solution.py:267
  97.5 14.9 %cotangent.1 = (f32[1024,512]{1,0:T(8,128)}, bf16[528,128]{1,0:T(8,128)(2,1)}) custom-call(bf16[8,1024,768]{2,1,0:T(8,128)(2,1)} %bitcast.40, bf16[512,6144]{1,0:T(8,128)(2,1)} %weight.1, f32[1024,512]{1,0:T(8,128)} %get-tuple-element.81.opened, bf16[1024,512]{1,0:T(8,128)(2,1)} %q.5, f32[1024,128]{1,0:T(8,128)} %broadcast_in_dim.10.dcol, ...), custom_call_target="tpu_custom_call" | custom-call | tf_op jit(solution)/shard_map/cotangent/pallas_call | solution.py:399
  112.5 1.7 collective-permute-done.12.refs_13_
  114.2 3.4 %collective-permute-done.13.refs_16_ = bf16[2,2,128,768]{3,2,1,0:T(8,128)(2,1)S(1)} collective-permute-done((bf16[2,2,128,768]{3,2,1,0:T(8,128)(2,1)S(1)}, bf16[2,2,128,768]{3,2,1,0:T(8,128)(2,1)S(1)}, u32[]{:S(2)}, u32[]{:S(2)}) %collective-permute-start.13) | collective-permute-done | bytes 786464 | tf_op jit(solution)/shard_map/ppermute | solution.py:267
  118.3 1.9 collective-permute-done.15.refs_4_
  121.2 1.2 collective-permute-start.20
  122.4 2.7 %collective-permute-start.16 = (bf16[528,128]{1,0:T(8,128)(2,1)S(1)}, bf16[528,128]{1,0:T(8,128)(2,1)S(1)}, u32[]{:S(2)}, u32[]{:S(2)}) collective-permute-start(bf16[528,128]{1,0:T(8,128)(2,1)S(1)} %copy-done.27), channel_id=1, source_target_pairs={{0,24},{8,0},{16,8},{24,16},{1,25},{9,1},{17,9},{25,17},{2,26},{10... | collective-permute-start | bytes 405512 | tf_op jit(solution)/shard_map/ppermute | solution.py:267
  126.9 2.9 %collective-permute-done.16.refs_1_.refs_0_ = bf16[528,128]{1,0:T(8,128)(2,1)S(1)} collective-permute-done((bf16[528,128]{1,0:T(8,128)(2,1)S(1)}, bf16[528,128]{1,0:T(8,128)(2,1)S(1)}, u32[]{:S(2)}, u32[]{:S(2)}) %collective-permute-start.16) | collective-permute-done | bytes 135200 | tf_op jit(solution)/shard_map/ppermute | solution.py:267
  129.7 2.3 %collective-permute-done.17.refs_2_.refs_1_ = bf16[528,128]{1,0:T(8,128)(2,1)S(1)} collective-permute-done((bf16[528,128]{1,0:T(8,128)(2,1)S(1)}, bf16[528,128]{1,0:T(8,128)(2,1)S(1)}, u32[]{:S(2)}, u32[]{:S(2)}) %collective-permute-start.17) | collective-permute-done | bytes 135200 | tf_op jit(solution)/shard_map/ppermute | solution.py:267
  132.0 1.3 collective-permute-done.18.refs_3_.refs_2_
  133.4 2.2 %collective-permute-done.20.refs_7_ = bf16[512,512]{1,0:T(8,128)(2,1)} collective-permute-done((bf16[512,512]{1,0:T(8,128)(2,1)S(1)}, bf16[512,512]{1,0:T(8,128)(2,1)}, u32[]{:S(2)}, u32[]{:S(2)}) %collective-permute-start.20) | collective-permute-done | bytes 524320 | tf_op jit(solution)/shard_map/ppermute | solution.py:267
  136.1 1.9 row_state.3
  138.0 2.4 %collective-permute-start.21 = (bf16[528,128]{1,0:T(8,128)(2,1)}, bf16[528,128]{1,0:T(8,128)(2,1)S(1)}, u32[]{:S(2)}, u32[]{:S(2)}) collective-permute-start(bf16[528,128]{1,0:T(8,128)(2,1)} %row_state.3), channel_id=1, source_target_pairs={{32,0},{64,32},{96,64},{33,1},{65,33},{97,65},{34,2},{66,34},{98,6... | collective-permute-start | bytes 405512 | tf_op jit(solution)/shard_map/ppermute | solution.py:273
  140.4 1.3 collective-permute-start.22
  141.8 7.4 %collective-permute-done.21.refs_3_ = bf16[528,128]{1,0:T(8,128)(2,1)S(1)} collective-permute-done((bf16[528,128]{1,0:T(8,128)(2,1)}, bf16[528,128]{1,0:T(8,128)(2,1)S(1)}, u32[]{:S(2)}, u32[]{:S(2)}) %collective-permute-start.21) | collective-permute-done | bytes 135200 | tf_op jit(solution)/shard_map/ppermute | solution.py:273
  149.2 6.6 %collective-permute-done.22.refs_4_ = bf16[528,128]{1,0:T(8,128)(2,1)S(1)} collective-permute-done((bf16[528,128]{1,0:T(8,128)(2,1)}, bf16[528,128]{1,0:T(8,128)(2,1)S(1)}, u32[]{:S(2)}, u32[]{:S(2)}) %collective-permute-start.22) | collective-permute-done | bytes 135200 | tf_op jit(solution)/shard_map/ppermute | solution.py:273
  155.8 2.8 %collective-permute-start.28 = (bf16[2,2,128,768]{3,2,1,0:T(8,128)(2,1)}, bf16[2,2,128,768]{3,2,1,0:T(8,128)(2,1)S(1)}, u32[]{:S(2)}, u32[]{:S(2)}) collective-permute-start(bf16[2,2,128,768]{3,2,1,0:T(8,128)(2,1)} %copy-done.5), channel_id=1, source_target_pairs={{0,24},{8,0},{16,8},{24,16},{1,25},{9,1},{17,9},{25,17},{2,26},{10... | collective-permute-start | bytes 2359304 | tf_op jit(solution)/shard_map/ppermute | solution.py:267
  158.7 5.9 %grad_query.1 = bf16[1024,512]{1,0:T(8,128)(2,1)} custom-call(f32[1024,512]{1,0:T(8,128)} %get-tuple-element.99.go, bf16[1024,512]{1,0:T(8,128)(2,1)} %k.7, bf16[1024,512]{1,0:T(8,128)(2,1)} %v.7, f32[1024,128]{1,0:T(8,128)} %broadcast_in_dim.10.dcol, f32[1,1024]{1,0:T(1,128)} %bitcast.48, f32[16,128]{1,0:T(8,128)} %broadcast_in_dim.24.table, ...), custom_call_target="tpu_custom_call" | custom-call | tf_op jit(solution)/shard_map/grad_query/pallas_call | solution.py:426
  164.6 7.4 %grad_key_value.1 = (bf16[1024,512]{1,0:T(8,128)(2,1)}, bf16[1024,512]{1,0:T(8,128)(2,1)}) custom-call(f32[1024,512]{1,0:T(8,128)} %get-tuple-element.99.go, bf16[1024,512]{1,0:T(8,128)(2,1)} %q.5, bf16[1024,512]{1,0:T(8,128)(2,1)} %k.7, bf16[1024,512]{1,0:T(8,128)(2,1)} %v.7, f32[1024,128]{1,0:T(8,128)} %broadcast_in_dim.10.dcol, f32[1,1024]{1,0:T(1,128)} %bitcast.49, ...), custom_call_target="tpu_custom_call" | custom-call | tf_op jit(solution)/shard_map/grad_key_value/pallas_call | solution.py:441
  172.1 4.3 %collective-permute-done.28.refs_14_ = bf16[2,2,128,768]{3,2,1,0:T(8,128)(2,1)S(1)} collective-permute-done((bf16[2,2,128,768]{3,2,1,0:T(8,128)(2,1)}, bf16[2,2,128,768]{3,2,1,0:T(8,128)(2,1)S(1)}, u32[]{:S(2)}, u32[]{:S(2)}) %collective-permute-start.28) | collective-permute-done | bytes 786464 | tf_op jit(solution)/shard_map/ppermute | solution.py:267
  176.4 3.4 %collective-permute-done.29.refs_15_ = bf16[2,2,128,768]{3,2,1,0:T(8,128)(2,1)} collective-permute-done((bf16[2,2,128,768]{3,2,1,0:T(8,128)(2,1)}, bf16[2,2,128,768]{3,2,1,0:T(8,128)(2,1)}, u32[]{:S(2)}, u32[]{:S(2)}) %collective-permute-start.29) | collective-permute-done | bytes 786464 | tf_op jit(solution)/shard_map/ppermute | solution.py:267
  179.8 1.4 dynamic-slice_bitcast_fusion
  181.3 1.9 collective-permute-start.31
  183.2 1.3 collective-permute-start.32
  185.1 13.7 %attended.1 = bf16[1024,768]{1,0:T(8,128)(2,1)} custom-call(s32[20]{0:T(128)} %stack.110.places, bf16[1024,512]{1,0:T(8,128)(2,1)} %get-tuple-element.106.refs_0_, bf16[1024,512]{1,0:T(8,128)(2,1)} %collective-permute-done.23.refs_1_, bf16[1024,512]{1,0:T(8,128)(2,1)} %copy-done.2, bf16[1024,512]{1,0:T(8,128)(2,1)} %collective-permute-done.24.refs_3_, ...), custom_call_target="tpu_custom_call" | custom-call | tf_op jit(solution)/shard_map/attended/pallas_call | solution.py:464
  198.7 2.5 %collective-permute-done.30.refs_0_ = bf16[512,384]{1,0:T(8,128)(2,1)S(1)} collective-permute-done((bf16[512,384]{1,0:T(8,128)(2,1)S(1)}, bf16[512,384]{1,0:T(8,128)(2,1)S(1)}, u32[]{:S(2)}, u32[]{:S(2)}) %collective-permute-start.30) | collective-permute-done | bytes 393248 | tf_op jit(solution)/shard_map/ppermute | solution.py:267
  202.6 2.3 %last_sum.1 = f32[512,384]{1,0:T(8,128)} custom-call(s32[1]{0:T(128)} %bitcast.30.place, bf16[4,512,384]{2,1,0:T(8,128)(2,1)} %bitcast.42, bf16[512,384]{1,0:T(8,128)(2,1)} %copy-done.19, bf16[512,384]{1,0:T(8,128)(2,1)} %copy-done.20, bf16[512,384]{1,0:T(8,128)(2,1)} %copy-done.21), custom_call_target="tpu_custom_call" | custom-call | tf_op jit(solution)/shard_map/last_sum/pallas_call | solution.py:315
  (108 shorter events, 15.6 us)
Async XLA Ops:
  7.2 72.5 %all-gather.3.cloned.1.call-start = ((), (), s32[]{:S(2)}) async-start(), calls=%async_computation.2 | async-start | bytes 14155776 | tf_op jit(solution)/shard_map/all_gather | solution.py:340
  7.9 171.9 %reduce-scatter.2.cloned.1.call-start = ((), (), s32[]{:S(2)}) async-start(), calls=%async_computation.1 | async-start | bytes 7864320 | tf_op jit(solution)/shard_map/reduce_scatter | solution.py:393
  9.0 20.2 %collective-permute-start.3 = (bf16[128,1536]{1,0:T(8,128)(2,1)S(1)}, bf16[128,1536]{1,0:T(8,128)(2,1)S(1)}, u32[]{:S(2)}, u32[]{:S(2)}) collective-permute-start(bf16[128,1536]{1,0:T(8,128)(2,1)S(1)} %dynamic_slice.19), channel_id=1, source_target_pairs={{0,0},{2,2},{4,4},{6,6},{10,8},{12,10},{14,12},{8,14},{20,16},{22,... | collective-permute-start | bytes 1179656 | tf_op jit(solution)/shard_map/ppermute | solution.py:300
  9.7 21.1 %copy-start.22 = (f32[1024]{0:T(1024)}, f32[1024]{0:T(1024)S(1)}, u32[]{:S(2)}) copy-start(f32[1024]{0:T(1024)S(1)} %convert_element_type.6) | copy-start | bytes 12292
  14.5 11.1 %collective-permute-start = (bf16[528,128]{1,0:T(8,128)(2,1)}, bf16[528,128]{1,0:T(8,128)(2,1)S(1)}, u32[]{:S(2)}, u32[]{:S(2)}) collective-permute-start(bf16[528,128]{1,0:T(8,128)(2,1)} %tail.1.refs_0_), channel_id=1, source_target_pairs={{0,8},{8,16},{16,24},{24,0},{1,9},{9,17},{17,25},{25,1},{2,10},{10... | collective-permute-start | bytes 405512 | tf_op jit(solution)/shard_map/ppermute | solution.py:267
  21.4 7.9 %collective-permute-start.1 = (bf16[528,128]{1,0:T(8,128)(2,1)}, bf16[528,128]{1,0:T(8,128)(2,1)S(1)}, u32[]{:S(2)}, u32[]{:S(2)}) collective-permute-start(bf16[528,128]{1,0:T(8,128)(2,1)} %tail.1.refs_0_), channel_id=1, source_target_pairs={{0,16},{8,24},{16,0},{24,8},{1,17},{9,25},{17,1},{25,9},{2,18},{10... | collective-permute-start | bytes 405512 | tf_op jit(solution)/shard_map/ppermute | solution.py:267
  22.8 6.4 %collective-permute-start.2 = (bf16[528,128]{1,0:T(8,128)(2,1)}, bf16[528,128]{1,0:T(8,128)(2,1)S(1)}, u32[]{:S(2)}, u32[]{:S(2)}) collective-permute-start(bf16[528,128]{1,0:T(8,128)(2,1)} %tail.1.refs_0_), channel_id=1, source_target_pairs={{0,24},{8,0},{16,8},{24,16},{1,25},{9,1},{17,9},{25,17},{2,26},{10... | collective-permute-start | bytes 405512 | tf_op jit(solution)/shard_map/ppermute | solution.py:267
  25.7 9.4 %copy-start.13 = (bf16[528,128]{1,0:T(8,128)(2,1)}, bf16[528,128]{1,0:T(8,128)(2,1)S(1)}, u32[]{:S(2)}) copy-start(bf16[528,128]{1,0:T(8,128)(2,1)S(1)} %collective-permute-done.refs_1_.refs_0_) | copy-start | bytes 405508
  29.3 1.5 collective-permute-start.6
  30.9 18.9 %collective-permute-start.7 = (bf16[2,128,768]{2,1,0:T(8,128)(2,1)S(1)}, bf16[2,128,768]{2,1,0:T(8,128)(2,1)S(1)}, u32[]{:S(2)}, u32[]{:S(2)}) collective-permute-start(bf16[2,128,768]{2,1,0:T(8,128)(2,1)S(1)} %get-tuple-element.145), channel_id=1, source_target_pairs={{0,32},{32,64},{64,96},{96,0},{1,33},{33,65},{65,97},{97,1},{2,34}... | collective-permute-start | bytes 1179656 | tf_op jit(solution)/shard_map/ppermute | solution.py:267
  32.4 19.2 %collective-permute-start.9 = (bf16[2,128,768]{2,1,0:T(8,128)(2,1)S(1)}, bf16[2,128,768]{2,1,0:T(8,128)(2,1)S(1)}, u32[]{:S(2)}, u32[]{:S(2)}) collective-permute-start(bf16[2,128,768]{2,1,0:T(8,128)(2,1)S(1)} %get-tuple-element.145), channel_id=1, source_target_pairs={{0,96},{32,0},{64,32},{96,64},{1,97},{33,1},{65,33},{97,65},{2,98}... | collective-permute-start | bytes 1179656 | tf_op jit(solution)/shard_map/ppermute | solution.py:267
  33.0 19.4 %collective-permute-start.8 = (bf16[2,128,768]{2,1,0:T(8,128)(2,1)S(1)}, bf16[2,128,768]{2,1,0:T(8,128)(2,1)S(1)}, u32[]{:S(2)}, u32[]{:S(2)}) collective-permute-start(bf16[2,128,768]{2,1,0:T(8,128)(2,1)S(1)} %get-tuple-element.145), channel_id=1, source_target_pairs={{0,64},{32,96},{64,0},{96,32},{1,65},{33,97},{65,1},{97,33},{2,66}... | collective-permute-start | bytes 1179656 | tf_op jit(solution)/shard_map/ppermute | solution.py:267
  37.0 17.3 %collective-permute-start.4 = (bf16[528,128]{1,0:T(8,128)(2,1)}, bf16[528,128]{1,0:T(8,128)(2,1)S(1)}, u32[]{:S(2)}, u32[]{:S(2)}) collective-permute-start(bf16[528,128]{1,0:T(8,128)(2,1)} %row_state.2), channel_id=1, source_target_pairs={{0,32},{32,64},{64,96},{1,33},{33,65},{65,97},{2,34},{34,66},{66,9... | collective-permute-start | bytes 405512 | tf_op jit(solution)/shard_map/ppermute | solution.py:273
  40.0 14.4 %collective-permute-start.5 = (bf16[528,128]{1,0:T(8,128)(2,1)}, bf16[528,128]{1,0:T(8,128)(2,1)S(1)}, u32[]{:S(2)}, u32[]{:S(2)}) collective-permute-start(bf16[528,128]{1,0:T(8,128)(2,1)} %row_state.2), channel_id=1, source_target_pairs={{0,64},{32,96},{1,65},{33,97},{2,66},{34,98},{3,67},{35,99},{4,68}... | collective-permute-start | bytes 405512 | tf_op jit(solution)/shard_map/ppermute | solution.py:273
  51.6 45.9 %copy-start = (bf16[2,2,128,768]{3,2,1,0:T(8,128)(2,1)}, bf16[2,2,128,768]{3,2,1,0:T(8,128)(2,1)S(1)}, u32[]{:S(2)}) copy-start(bf16[2,2,128,768]{3,2,1,0:T(8,128)(2,1)S(1)} %pad_maximum_fusion.refs_10_) | copy-start | bytes 2359300
  54.3 40.5 %copy-start.1 = (bf16[2,2,128,768]{3,2,1,0:T(8,128)(2,1)}, bf16[2,2,128,768]{3,2,1,0:T(8,128)(2,1)S(1)}, u32[]{:S(2)}) copy-start(bf16[2,2,128,768]{3,2,1,0:T(8,128)(2,1)S(1)} %pad_maximum_fusion.1.refs_11_) | copy-start | bytes 2359300
  54.3 18.9 %collective-permute-start.10 = (bf16[2,2,128,768]{3,2,1,0:T(8,128)(2,1)S(1)}, bf16[2,2,128,768]{3,2,1,0:T(8,128)(2,1)S(1)}, u32[]{:S(2)}, u32[]{:S(2)}) collective-permute-start(bf16[2,2,128,768]{3,2,1,0:T(8,128)(2,1)S(1)} %pad_maximum_fusion.refs_10_), channel_id=1, source_target_pairs={{0,24},{8,0},{16,8},{24,16},{1,25},{9,1},{17,9},{25,17},{2,26},{10... | collective-permute-start | bytes 2359304 | tf_op jit(solution)/shard_map/ppermute | solution.py:267
  57.2 19.4 %collective-permute-start.11 = (bf16[2,2,128,768]{3,2,1,0:T(8,128)(2,1)S(1)}, bf16[2,2,128,768]{3,2,1,0:T(8,128)(2,1)S(1)}, u32[]{:S(2)}, u32[]{:S(2)}) collective-permute-start(bf16[2,2,128,768]{3,2,1,0:T(8,128)(2,1)S(1)} %pad_maximum_fusion.1.refs_11_), channel_id=1, source_target_pairs={{0,8},{8,16},{16,24},{24,0},{1,9},{9,17},{17,25},{25,1},{2,10},{10... | collective-permute-start | bytes 2359304 | tf_op jit(solution)/shard_map/ppermute | solution.py:267
  92.7 25.6 %collective-permute-start.14 = (bf16[1024,512]{1,0:T(8,128)(2,1)}, bf16[1024,512]{1,0:T(8,128)(2,1)S(1)}, u32[]{:S(2)}, u32[]{:S(2)}) collective-permute-start(bf16[1024,512]{1,0:T(8,128)(2,1)} %get-tuple-element.106.refs_0_), channel_id=1, source_target_pairs={{0,6},{2,0},{4,2},{6,4},{1,7},{3,1},{5,3},{7,5},{8,14},{10,8},{12,... | collective-permute-start | bytes 3145736 | tf_op jit(solution)/shard_map/ppermute | solution.py:267
  93.7 26.5 %collective-permute-start.15 = (bf16[1024,512]{1,0:T(8,128)(2,1)}, bf16[1024,512]{1,0:T(8,128)(2,1)S(1)}, u32[]{:S(2)}, u32[]{:S(2)}) collective-permute-start(bf16[1024,512]{1,0:T(8,128)(2,1)} %get-tuple-element.106.refs_0_), channel_id=1, source_target_pairs={{0,2},{2,4},{4,6},{6,0},{1,3},{3,5},{5,7},{7,1},{8,10},{10,12},{12... | collective-permute-start | bytes 3145736 | tf_op jit(solution)/shard_map/ppermute | solution.py:267
  94.8 19.4 %collective-permute-start.12 = (bf16[2,2,128,768]{3,2,1,0:T(8,128)(2,1)S(1)}, bf16[2,2,128,768]{3,2,1,0:T(8,128)(2,1)S(1)}, u32[]{:S(2)}, u32[]{:S(2)}) collective-permute-start(bf16[2,2,128,768]{3,2,1,0:T(8,128)(2,1)S(1)} %pad_maximum_fusion.1.refs_11_), channel_id=1, source_target_pairs={{0,24},{8,0},{16,8},{24,16},{1,25},{9,1},{17,9},{25,17},{2,26},{10... | collective-permute-start | bytes 2359304 | tf_op jit(solution)/shard_map/ppermute | solution.py:267
  97.5 20.1 %collective-permute-start.13 = (bf16[2,2,128,768]{3,2,1,0:T(8,128)(2,1)S(1)}, bf16[2,2,128,768]{3,2,1,0:T(8,128)(2,1)S(1)}, u32[]{:S(2)}, u32[]{:S(2)}) collective-permute-start(bf16[2,2,128,768]{3,2,1,0:T(8,128)(2,1)S(1)} %pad_maximum_fusion.refs_10_), channel_id=1, source_target_pairs={{0,8},{8,16},{16,24},{24,0},{1,9},{9,17},{17,25},{25,1},{2,10},{10... | collective-permute-start | bytes 2359304 | tf_op jit(solution)/shard_map/ppermute | solution.py:267
  112.5 10.0 %copy-start.27 = (bf16[528,128]{1,0:T(8,128)(2,1)S(1)}, bf16[528,128]{1,0:T(8,128)(2,1)}, u32[]{:S(2)}) copy-start(bf16[528,128]{1,0:T(8,128)(2,1)} %get-tuple-element.91.refs_0_) | copy-start | bytes 405508
  114.2 7.0 %copy-start.7 = (bf16[2,2,128,768]{3,2,1,0:T(8,128)(2,1)}, bf16[2,2,128,768]{3,2,1,0:T(8,128)(2,1)S(1)}, u32[]{:S(2)}) copy-start(bf16[2,2,128,768]{3,2,1,0:T(8,128)(2,1)S(1)} %collective-permute-done.12.refs_13_) | copy-start | bytes 2359300
  114.2 27.5 %copy-start.4 = (bf16[1024,512]{1,0:T(8,128)(2,1)S(1)}, bf16[1024,512]{1,0:T(8,128)(2,1)}, u32[]{:S(2)}) copy-start(bf16[1024,512]{1,0:T(8,128)(2,1)} %get-tuple-element.106.refs_0_) | copy-start | bytes 3145732
  118.3 46.3 %copy-start.2 = (bf16[1024,512]{1,0:T(8,128)(2,1)}, bf16[1024,512]{1,0:T(8,128)(2,1)S(1)}, u32[]{:S(2)}) copy-start(bf16[1024,512]{1,0:T(8,128)(2,1)S(1)} %collective-permute-done.14.refs_2_) | copy-start | bytes 3145732
  120.2 13.1 %collective-permute-start.19 = (bf16[512,512]{1,0:T(8,128)(2,1)S(1)}, bf16[512,512]{1,0:T(8,128)(2,1)S(1)}, u32[]{:S(2)}, u32[]{:S(2)}) collective-permute-start(bf16[512,512]{1,0:T(8,128)(2,1)S(1)} %slice.14), channel_id=1, source_target_pairs={{0,6},{2,0},{4,2},{6,4},{1,7},{3,1},{5,3},{7,5},{8,14},{10,8},{12,... | collective-permute-start | bytes 1572872 | tf_op jit(solution)/shard_map/ppermute | solution.py:267
  121.2 14.3 %collective-permute-start.20 = (bf16[512,512]{1,0:T(8,128)(2,1)S(1)}, bf16[512,512]{1,0:T(8,128)(2,1)}, u32[]{:S(2)}, u32[]{:S(2)}) collective-permute-start(bf16[512,512]{1,0:T(8,128)(2,1)S(1)} %slice.15), channel_id=1, source_target_pairs={{0,2},{2,4},{4,6},{6,0},{1,3},{3,5},{5,7},{7,1},{8,10},{10,12},{12... | collective-permute-start | bytes 1572872 | tf_op jit(solution)/shard_map/ppermute | solution.py:267
  122.4 7.3 %collective-permute-start.16 = (bf16[528,128]{1,0:T(8,128)(2,1)S(1)}, bf16[528,128]{1,0:T(8,128)(2,1)S(1)}, u32[]{:S(2)}, u32[]{:S(2)}) collective-permute-start(bf16[528,128]{1,0:T(8,128)(2,1)S(1)} %copy-done.27), channel_id=1, source_target_pairs={{0,24},{8,0},{16,8},{24,16},{1,25},{9,1},{17,9},{25,17},{2,26},{10... | collective-permute-start | bytes 405512 | tf_op jit(solution)/shard_map/ppermute | solution.py:267
  125.2 6.8 %collective-permute-start.17 = (bf16[528,128]{1,0:T(8,128)(2,1)S(1)}, bf16[528,128]{1,0:T(8,128)(2,1)S(1)}, u32[]{:S(2)}, u32[]{:S(2)}) collective-permute-start(bf16[528,128]{1,0:T(8,128)(2,1)S(1)} %copy-done.27), channel_id=1, source_target_pairs={{0,16},{8,24},{16,0},{24,8},{1,17},{9,25},{17,1},{25,9},{2,18},{10... | collective-permute-start | bytes 405512 | tf_op jit(solution)/shard_map/ppermute | solution.py:267
  126.0 7.4 %collective-permute-start.18 = (bf16[528,128]{1,0:T(8,128)(2,1)S(1)}, bf16[528,128]{1,0:T(8,128)(2,1)S(1)}, u32[]{:S(2)}, u32[]{:S(2)}) collective-permute-start(bf16[528,128]{1,0:T(8,128)(2,1)S(1)} %copy-done.27), channel_id=1, source_target_pairs={{0,8},{8,16},{16,24},{24,0},{1,9},{9,17},{17,25},{25,1},{2,10},{10... | collective-permute-start | bytes 405512 | tf_op jit(solution)/shard_map/ppermute | solution.py:267
  129.7 6.3 %copy-start.10 = (bf16[528,128]{1,0:T(8,128)(2,1)}, bf16[528,128]{1,0:T(8,128)(2,1)S(1)}, u32[]{:S(2)}) copy-start(bf16[528,128]{1,0:T(8,128)(2,1)S(1)} %collective-permute-done.16.refs_1_.refs_0_) | copy-start | bytes 405508
  133.4 22.5 %copy-start.16 = (bf16[512,512]{1,0:T(8,128)(2,1)}, bf16[512,512]{1,0:T(8,128)(2,1)S(1)}, u32[]{:S(2)}) copy-start(bf16[512,512]{1,0:T(8,128)(2,1)S(1)} %collective-permute-done.19.refs_6_) | copy-start | bytes 1572868
  135.6 20.3 %collective-permute-start.26 = (bf16[512,512]{1,0:T(8,128)(2,1)S(1)}, bf16[512,512]{1,0:T(8,128)(2,1)}, u32[]{:S(2)}, u32[]{:S(2)}) collective-permute-start(bf16[512,512]{1,0:T(8,128)(2,1)S(1)} %collective-permute-done.19.refs_6_), channel_id=1, source_target_pairs={{0,1},{1,0},{2,3},{3,2},{4,5},{5,4},{6,7},{7,6},{8,9},{9,8},{10,11... | collective-permute-start | bytes 1572872 | tf_op jit(solution)/shard_map/ppermute | solution.py:277
  135.6 23.1 %collective-permute-start.27 = (bf16[512,512]{1,0:T(8,128)(2,1)}, bf16[512,512]{1,0:T(8,128)(2,1)}, u32[]{:S(2)}, u32[]{:S(2)}) collective-permute-start(bf16[512,512]{1,0:T(8,128)(2,1)} %collective-permute-done.20.refs_7_), channel_id=1, source_target_pairs={{0,1},{1,0},{2,3},{3,2},{4,5},{5,4},{6,7},{7,6},{8,9},{9,8},{10,11... | collective-permute-start | bytes 1572872 | tf_op jit(solution)/shard_map/ppermute | solution.py:277
  138.0 11.2 %collective-permute-start.21 = (bf16[528,128]{1,0:T(8,128)(2,1)}, bf16[528,128]{1,0:T(8,128)(2,1)S(1)}, u32[]{:S(2)}, u32[]{:S(2)}) collective-permute-start(bf16[528,128]{1,0:T(8,128)(2,1)} %row_state.3), channel_id=1, source_target_pairs={{32,0},{64,32},{96,64},{33,1},{65,33},{97,65},{34,2},{66,34},{98,6... | collective-permute-start | bytes 405512 | tf_op jit(solution)/shard_map/ppermute | solution.py:273
  140.4 15.4 %collective-permute-start.22 = (bf16[528,128]{1,0:T(8,128)(2,1)}, bf16[528,128]{1,0:T(8,128)(2,1)S(1)}, u32[]{:S(2)}, u32[]{:S(2)}) collective-permute-start(bf16[528,128]{1,0:T(8,128)(2,1)} %row_state.3), channel_id=1, source_target_pairs={{64,0},{96,32},{65,1},{97,33},{66,2},{98,34},{67,3},{99,35},{68,4}... | collective-permute-start | bytes 405512 | tf_op jit(solution)/shard_map/ppermute | solution.py:273
  141.7 22.9 %collective-permute-start.23 = (bf16[1024,512]{1,0:T(8,128)(2,1)S(1)}, bf16[1024,512]{1,0:T(8,128)(2,1)}, u32[]{:S(2)}, u32[]{:S(2)}) collective-permute-start(bf16[1024,512]{1,0:T(8,128)(2,1)S(1)} %copy-done.4), channel_id=1, source_target_pairs={{0,1},{1,0},{2,3},{3,2},{4,5},{5,4},{6,7},{7,6},{8,9},{9,8},{10,11... | collective-permute-start | bytes 3145736 | tf_op jit(solution)/shard_map/ppermute | solution.py:277
  149.2 15.4 %copy-start.23 = (bf16[528,128]{1,0:T(8,128)(2,1)}, bf16[528,128]{1,0:T(8,128)(2,1)S(1)}, u32[]{:S(2)}) copy-start(bf16[528,128]{1,0:T(8,128)(2,1)S(1)} %collective-permute-done.21.refs_3_) | copy-start | bytes 405508
  149.2 15.5 %collective-permute-start.24 = (bf16[1024,512]{1,0:T(8,128)(2,1)S(1)}, bf16[1024,512]{1,0:T(8,128)(2,1)}, u32[]{:S(2)}, u32[]{:S(2)}) collective-permute-start(bf16[1024,512]{1,0:T(8,128)(2,1)S(1)} %collective-permute-done.14.refs_2_), channel_id=1, source_target_pairs={{0,1},{1,0},{2,3},{3,2},{4,5},{5,4},{6,7},{7,6},{8,9},{9,8},{10,11... | collective-permute-start | bytes 3145736 | tf_op jit(solution)/shard_map/ppermute | solution.py:277
  155.8 8.8 %copy-start.24 = (bf16[528,128]{1,0:T(8,128)(2,1)}, bf16[528,128]{1,0:T(8,128)(2,1)S(1)}, u32[]{:S(2)}) copy-start(bf16[528,128]{1,0:T(8,128)(2,1)S(1)} %collective-permute-done.22.refs_4_) | copy-start | bytes 405508
  155.8 8.8 %collective-permute-start.25 = (bf16[1024,512]{1,0:T(8,128)(2,1)}, bf16[1024,512]{1,0:T(8,128)(2,1)}, u32[]{:S(2)}, u32[]{:S(2)}) collective-permute-start(bf16[1024,512]{1,0:T(8,128)(2,1)} %copy-done.3), channel_id=1, source_target_pairs={{0,1},{1,0},{2,3},{3,2},{4,5},{5,4},{6,7},{7,6},{8,9},{9,8},{10,11... | collective-permute-start | bytes 3145736 | tf_op jit(solution)/shard_map/ppermute | solution.py:277
  155.8 20.6 %collective-permute-start.28 = (bf16[2,2,128,768]{3,2,1,0:T(8,128)(2,1)}, bf16[2,2,128,768]{3,2,1,0:T(8,128)(2,1)S(1)}, u32[]{:S(2)}, u32[]{:S(2)}) collective-permute-start(bf16[2,2,128,768]{3,2,1,0:T(8,128)(2,1)} %copy-done.5), channel_id=1, source_target_pairs={{0,24},{8,0},{16,8},{24,16},{1,25},{9,1},{17,9},{25,17},{2,26},{10... | collective-permute-start | bytes 2359304 | tf_op jit(solution)/shard_map/ppermute | solution.py:267
  158.7 21.1 %collective-permute-start.29 = (bf16[2,2,128,768]{3,2,1,0:T(8,128)(2,1)}, bf16[2,2,128,768]{3,2,1,0:T(8,128)(2,1)}, u32[]{:S(2)}, u32[]{:S(2)}) collective-permute-start(bf16[2,2,128,768]{3,2,1,0:T(8,128)(2,1)} %copy-done.6), channel_id=1, source_target_pairs={{0,8},{8,16},{16,24},{24,0},{1,9},{9,17},{17,25},{25,1},{2,10},{10... | collective-permute-start | bytes 2359304 | tf_op jit(solution)/shard_map/ppermute | solution.py:267
  176.4 8.7 %copy-start.9 = (bf16[2,2,128,768]{3,2,1,0:T(8,128)(2,1)}, bf16[2,2,128,768]{3,2,1,0:T(8,128)(2,1)S(1)}, u32[]{:S(2)}) copy-start(bf16[2,2,128,768]{3,2,1,0:T(8,128)(2,1)S(1)} %collective-permute-done.28.refs_14_) | copy-start | bytes 2359300
  181.2 20.1 %collective-permute-start.30 = (bf16[512,384]{1,0:T(8,128)(2,1)S(1)}, bf16[512,384]{1,0:T(8,128)(2,1)S(1)}, u32[]{:S(2)}, u32[]{:S(2)}) collective-permute-start(bf16[512,384]{1,0:T(8,128)(2,1)S(1)} %get-tuple-element.143), channel_id=1, source_target_pairs={{0,8},{8,16},{16,24},{24,0},{1,9},{9,17},{17,25},{25,1},{2,10},{10... | collective-permute-start | bytes 1179656 | tf_op jit(solution)/shard_map/ppermute | solution.py:267
  181.3 20.0 %collective-permute-start.31 = (bf16[512,384]{1,0:T(8,128)(2,1)S(1)}, bf16[512,384]{1,0:T(8,128)(2,1)S(1)}, u32[]{:S(2)}, u32[]{:S(2)}) collective-permute-start(bf16[512,384]{1,0:T(8,128)(2,1)S(1)} %get-tuple-element.142), channel_id=1, source_target_pairs={{0,16},{8,24},{16,0},{24,8},{1,17},{9,25},{17,1},{25,9},{2,18},{10... | collective-permute-start | bytes 1179656 | tf_op jit(solution)/shard_map/ppermute | solution.py:267
  183.2 18.7 %collective-permute-start.32 = (bf16[512,384]{1,0:T(8,128)(2,1)S(1)}, bf16[512,384]{1,0:T(8,128)(2,1)S(1)}, u32[]{:S(2)}, u32[]{:S(2)}) collective-permute-start(bf16[512,384]{1,0:T(8,128)(2,1)S(1)} %get-tuple-element.141), channel_id=1, source_target_pairs={{0,24},{8,0},{16,8},{24,16},{1,25},{9,1},{17,9},{25,17},{2,26},{10... | collective-permute-start | bytes 1179656 | tf_op jit(solution)/shard_map/ppermute | solution.py:267
  (16 other events, 40.9 us)
Sparse Core Ops, SparseCore 0:
  9.7 69.9 all-gather.2
  92.8 68.7 reduce-scatter.1

commit v5 on v3

--- a/solution.py
+++ b/solution.py
@@ -348,10 +348,10 @@
     table = jnp.broadcast_to(table[:, None], (16, HEAD))
 
     tail = pl.pallas_call(tail_kernel, out_shape=payload, name="tail")(keys, values, dcol, table)
-    own = column_pieces(column_strip(out_weight, share, cx), share, core)
-    arrived, own = exchanged(tail, 1, own)
+    arrived, strip = exchanged(tail, 1, column_strip(out_weight, share, cx))
+    own = column_pieces(strip, share, core)
+    arrived, own = lax.optimization_barrier((arrived, own))
     early = [turned_by(own[0], "cy", -1), turned_by(own[1], "cy", 1)]
-    arrived, early = lax.optimization_barrier((arrived, early))
     later = [turned_by(own[1], "cy", -1), turned_by(own[0], "cy", 1)]
 
     row_block = pl.BlockSpec((1, CHUNK), lambda i: (0, i))
@@ -379,9 +379,6 @@
         name="forward",
     )(queries, keys, values, dcol, drow, table, *arrived)
 
-    turned, later = lax.optimization_barrier((turned, later))
-    across = [turned_by(early[0], "cy", -1), turned_by(early[1], "cy", 1)]
-
     term = pl.pallas_call(
         weight_kernel,
         grid=(groups,),
@@ -391,7 +388,8 @@
         compiler_params=params(),
         name="weight_grad",
     )(turned, grad_whole)
-    term, low = lax.optimization_barrier((term, low))
+    term, low, early, later = lax.optimization_barrier((term, low, early, later))
+    across = [turned_by(early[0], "cy", -1), turned_by(early[1], "cy", 1)]
     grad_part = lax.psum_scatter(term, "cx", scatter_dimension=0, tiled=True)[0]
 
     half_rows = rows // 2
@@ -418,21 +416,11 @@
     head, across, above, below = lax.optimization_barrier((head, across, above, below))
     far_a = turned_by(above[:half_rows], "z", -1)
     far_b = turned_by(below[half_rows:], "z", 1)
-    returned, (far_a, far_b, low) = exchanged(head, -1, (far_a, far_b, low))
+    moved = (far_a, far_b, low, above, below)
+    returned, (far_a, far_b, low, above, below) = exchanged(head, -1, moved)
     near = [low, swapped(low), above, swapped(above), below, swapped(below)]
     far = [far_a, far_b, swapped(far_a), swapped(far_b)]
     columns = [*own, early[0], later[0], *across, later[1], early[1]]
-
-    grad_query = pl.pallas_call(
-        query_kernel,
-        grid=(blocks,),
-        in_specs=[rows_of(width)] * 3
-        + [rows_of(HEAD), row_block, whole(table.shape), state_block],
-        out_specs=rows_of(width),
-        out_shape=jax.ShapeDtypeStruct((rows, width), BF16),
-        compiler_params=params(),
-        name="grad_query",
-    )(grad_opened, keys, values, dcol, drow, table, states)
 
     sides = (core, 1 - core)
     around = [2 * ((z + cy + s) % 4) + side for s in range(4) for side in sides]
@@ -458,7 +446,20 @@
         compiler_params=params(),
         name="attended",
     )(jnp.stack(around + heads_at + groups_at), *near, *far, *columns)
-    returned, attended = lax.optimization_barrier((returned, attended))
+    ready = (returned, grad_opened, grad_part, attended)
+    returned, grad_opened, grad_part, attended = lax.optimization_barrier(ready)
+
+    grad_query = pl.pallas_call(
+        query_kernel,
+        grid=(blocks,),
+        in_specs=[rows_of(width)] * 3
+        + [rows_of(HEAD), row_block, whole(table.shape), state_block],
+        out_specs=rows_of(width),
+        out_shape=jax.ShapeDtypeStruct((rows, width), BF16),
+        compiler_params=params(),
+        name="grad_query",
+    )(grad_opened, keys, values, dcol, drow, table, states)
+
 
     back_row = pl.BlockSpec((1, CHUNK), lambda i: (0, blocks - 1 - i))
     grad_key, grad_value = pl.pallas_call(
@@ -474,7 +475,6 @@
         name="grad_key_value",
     )(grad_opened, queries, keys, values, dcol, drow, table, *returned)
 
-    grad_part, grad_key = lax.optimization_barrier((grad_part, grad_key))
     grad_weight = row_sum(grad_part, cy)
     return attended, grad_query, grad_key, grad_value, grad_weight
 

time: 205 us -> 196 us (0.956)
  starting transfers between devices: 59 us -> 48.1 us
  waiting for transfers between devices: 49.9 us -> 54.3 us
    all_gather x1, waiting for transfers between devices: 0.01 us -> 12.4 us  [body(): grad_whole = lax.all_gather(grad_out, TENSOR, axis=0)]
    ppermute x22, waiting for transfers between devices: 39.8 us -> 32.9 us  [turned_by(): lax.ppermute(value, axis, [(i, (i + step) % size) for i in range(size)])]
    ppermute x22, starting transfers between devices: 44.5 us -> 38.3 us  [turned_by(): lax.ppermute(value, axis, [(i, (i + step) % size) for i in range(size)])]
    ppermute x4, starting transfers between devices: 12.6 us -> 7.8 us  [moved_by(): return lax.ppermute(value, axis, pairs)]
    ppermute x4, waiting for transfers between devices: 5.71 us -> 1.82 us  [moved_by(): return lax.ppermute(value, axis, pairs)]
    reduce_scatter x1, waiting for transfers between devices: 0.02 us -> 3.52 us  [body(): grad_part = lax.psum_scatter(term, 'cx', scatter_dimension=0, tiled=True)[0]]
  transfers between devices with their start and end apart: 35 -> 35, of which waited for: 18 -> 19; matrix products, arithmetic and copies ran while one was open for 2% -> 2% of each run, Pallas kernels for 28% -> 35%
where the time goes in v5:
time: 196 us; the launch traced here: 195 us
  Pallas kernels  70.9 us (36%)
  waiting for transfers between devices  54.3 us (28%)
  starting transfers between devices  48.1 us (25%)
  between operations  14.6 us (7%)
  local copies, waits for them, and re-layouts  7.31 us (4%)
    ppermute x22, starting transfers between devices, turned_by(): lax.ppermute(value, axis, [(i, (i + step) % size) for i in range(size)])  38.3 us
    ppermute x22, waiting for transfers between devices, turned_by(): lax.ppermute(value, axis, [(i, (i + step) % size) for i in range(size)])  32.9 us
    pallas_call x1, Pallas kernels, body(): pl.pallas_call(cotangent_kernel, grid=(blocks,), in_specs=[pl.BlockSpec((...  15.1 us
    pallas_call x1, Pallas kernels, body(): pl.pallas_call(attended_kernel, grid_spec=pltpu.PrefetchScalarGridSpec(nu...  13.8 us
    pallas_call x1, Pallas kernels, body(): pl.pallas_call(weight_kernel, grid=(groups,), in_specs=[whole((width, row...  13 us
    all_gather x1, waiting for transfers between devices, body(): grad_whole = lax.all_gather(grad_out, TENSOR, axis=0)  12.4 us
    ppermute x4, starting transfers between devices, moved_by(): return lax.ppermute(value, axis, pairs)  7.8 us
    pallas_call x1, Pallas kernels, body(): pl.pallas_call(key_value_kernel, grid=(blocks,), in_specs=[rows_of(width,...  7.43 us
  transfers between devices with their start and end apart: 35, of which 19 were waited for; matrix products, arithmetic and copies ran while one was open for 2% of the time, Pallas kernels for 35%

profile of v5, /device:TPU:2, one launch (start us, length us, event | category | flops | bytes accessed | tf_op | source)
XLA Modules:
  0.0 195.4 jit_solution(8917116109553791854)
XLA Ops:
  8.0 1.0 dynamic_slice.19
  10.0 1.0 broadcast_in_dim.10.dcol
  11.7 2.8 %tail.1.refs_0_ = bf16[528,128]{1,0:T(8,128)(2,1)} custom-call(bf16[1024,512]{1,0:T(8,128)(2,1)} %k.7, bf16[1024,512]{1,0:T(8,128)(2,1)} %v.7, f32[1024,128]{1,0:T(8,128)} %broadcast_in_dim.10.dcol, f32[16,128]{1,0:T(8,128)} %broadcast_in_dim.24.table), custom_call_target="tpu_custom_call" | custom-call | tf_op jit(solution)/shard_map/tail/pallas_call | solution.py:350
  14.6 6.8 %collective-permute-start = (bf16[528,128]{1,0:T(8,128)(2,1)}, bf16[528,128]{1,0:T(8,128)(2,1)S(1)}, u32[]{:S(2)}, u32[]{:S(2)}) collective-permute-start(bf16[528,128]{1,0:T(8,128)(2,1)} %tail.1.refs_0_), channel_id=1, source_target_pairs={{0,8},{8,16},{16,24},{24,0},{1,9},{9,17},{17,25},{25,1},{2,10},{10... | collective-permute-start | bytes 405512 | tf_op jit(solution)/shard_map/ppermute | solution.py:267
  21.4 1.5 collective-permute-start.1
  22.9 2.6 %collective-permute-start.2 = (bf16[528,128]{1,0:T(8,128)(2,1)}, bf16[528,128]{1,0:T(8,128)(2,1)S(1)}, u32[]{:S(2)}, u32[]{:S(2)}) collective-permute-start(bf16[528,128]{1,0:T(8,128)(2,1)} %tail.1.refs_0_), channel_id=1, source_target_pairs={{0,24},{8,0},{16,8},{24,16},{1,25},{9,1},{17,9},{25,17},{2,26},{10... | collective-permute-start | bytes 405512 | tf_op jit(solution)/shard_map/ppermute | solution.py:267
  25.7 3.6 %collective-permute-done.1.refs_2_.refs_1_ = bf16[528,128]{1,0:T(8,128)(2,1)S(1)} collective-permute-done((bf16[528,128]{1,0:T(8,128)(2,1)}, bf16[528,128]{1,0:T(8,128)(2,1)S(1)}, u32[]{:S(2)}, u32[]{:S(2)}) %collective-permute-start.1) | collective-permute-done | bytes 135200 | tf_op jit(solution)/shard_map/ppermute | solution.py:267
  29.4 1.4 collective-permute-done.6
  30.9 1.6 collective-permute-start.7
  33.0 2.1 %collective-permute-start.8 = (bf16[2,128,768]{2,1,0:T(8,128)(2,1)S(1)}, bf16[2,128,768]{2,1,0:T(8,128)(2,1)S(1)}, u32[]{:S(2)}, u32[]{:S(2)}) collective-permute-start(bf16[2,128,768]{2,1,0:T(8,128)(2,1)S(1)} %get-tuple-element.103), channel_id=1, source_target_pairs={{0,64},{32,96},{64,0},{96,32},{1,65},{33,97},{65,1},{97,33},{2,66}... | collective-permute-start | bytes 1179656 | tf_op jit(solution)/shard_map/ppermute | solution.py:267
  35.1 1.9 row_state.2
  37.0 3.0 %collective-permute-start.4 = (bf16[528,128]{1,0:T(8,128)(2,1)}, bf16[528,128]{1,0:T(8,128)(2,1)S(1)}, u32[]{:S(2)}, u32[]{:S(2)}) collective-permute-start(bf16[528,128]{1,0:T(8,128)(2,1)} %row_state.2), channel_id=1, source_target_pairs={{0,32},{32,64},{64,96},{1,33},{33,65},{65,97},{2,34},{34,66},{66,9... | collective-permute-start | bytes 405512 | tf_op jit(solution)/shard_map/ppermute | solution.py:273
  40.0 1.6 collective-permute-start.5
  41.6 8.2 %collective-permute-done.7 = bf16[2,128,768]{2,1,0:T(8,128)(2,1)S(1)} collective-permute-done((bf16[2,128,768]{2,1,0:T(8,128)(2,1)S(1)}, bf16[2,128,768]{2,1,0:T(8,128)(2,1)S(1)}, u32[]{:S(2)}, u32[]{:S(2)}) %collective-permute-start.7) | collective-permute-done | bytes 393248 | tf_op jit(solution)/shard_map/ppermute | solution.py:267
  50.0 2.5 %collective-permute-done.8 = bf16[2,128,768]{2,1,0:T(8,128)(2,1)S(1)} collective-permute-done((bf16[2,128,768]{2,1,0:T(8,128)(2,1)S(1)}, bf16[2,128,768]{2,1,0:T(8,128)(2,1)S(1)}, u32[]{:S(2)}, u32[]{:S(2)}) %collective-permute-start.8) | collective-permute-done | bytes 393248 | tf_op jit(solution)/shard_map/ppermute | solution.py:267
  52.5 1.8 collective-permute-done.4.refs_3_
  54.3 2.9 %collective-permute-start.10 = (bf16[2,2,128,768]{3,2,1,0:T(8,128)(2,1)S(1)}, bf16[2,2,128,768]{3,2,1,0:T(8,128)(2,1)S(1)}, u32[]{:S(2)}, u32[]{:S(2)}) collective-permute-start(bf16[2,2,128,768]{3,2,1,0:T(8,128)(2,1)S(1)} %pad_maximum_fusion.refs_10_), channel_id=1, source_target_pairs={{0,24},{8,0},{16,8},{24,16},{1,25},{9,1},{17,9},{25,17},{2,26},{10... | collective-permute-start | bytes 2359304 | tf_op jit(solution)/shard_map/ppermute | solution.py:267
  57.2 3.2 %collective-permute-start.12 = (bf16[2,2,128,768]{3,2,1,0:T(8,128)(2,1)S(1)}, bf16[2,2,128,768]{3,2,1,0:T(8,128)(2,1)}, u32[]{:S(2)}, u32[]{:S(2)}) collective-permute-start(bf16[2,2,128,768]{3,2,1,0:T(8,128)(2,1)S(1)} %pad_maximum_fusion.1.refs_11_), channel_id=1, source_target_pairs={{0,24},{8,0},{16,8},{24,16},{1,25},{9,1},{17,9},{25,17},{2,26},{10... | collective-permute-start | bytes 2359304 | tf_op jit(solution)/shard_map/ppermute | solution.py:267
  60.4 6.8 %forward.1 = (f32[1024,512]{1,0:T(8,128)}, bf16[1024,512]{1,0:T(8,128)(2,1)}, bf16[512,1024]{1,0:T(8,128)(2,1)}, bf16[4,512,128]{2,1,0:T(8,128)(2,1)}) custom-call(bf16[1024,512]{1,0:T(8,128)(2,1)} %q.5, bf16[1024,512]{1,0:T(8,128)(2,1)} %k.7, bf16[1024,512]{1,0:T(8,128)(2,1)} %v.7, f32[1024,128]{1,0:T(8,128)} %broadcast_in_dim.10.dcol, f32[1,1024]{1,0:T(1,128)} %bitcast.47, ...), custom_call_target="tpu_custom_call" | custom-call | tf_op jit(solution)/shard_map/forward/pallas_call | solution.py:359
  67.2 12.4 %all-gather.3.cloned.1.call-done = bf16[8192,768]{1,0:T(8,128)(2,1)} async-done(((bf16[1024,768]{1,0:T(8,128)(2,1)}), bf16[8192,768]{1,0:T(8,128)(2,1)}) %all-gather.3.cloned.1.call-update) | async-done | bytes 12582928 | tf_op jit(solution)/shard_map/all_gather | solution.py:340
  79.7 13.0 %weight_grad.1 = bf16[4,4,512,384]{3,2,1,0:T(8,128)(2,1)} custom-call(bf16[512,1024]{1,0:T(8,128)(2,1)} %get-tuple-element.62.turned, bf16[8,1024,768]{2,1,0:T(8,128)(2,1)} %bitcast.39), custom_call_target="tpu_custom_call" | custom-call | tf_op jit(solution)/shard_map/weight_grad/pallas_call | solution.py:382
  95.1 1.3 collective-permute-start.17
  96.4 2.6 %collective-permute-start.14 = (bf16[2,2,128,768]{3,2,1,0:T(8,128)(2,1)}, bf16[2,2,128,768]{3,2,1,0:T(8,128)(2,1)S(1)}, u32[]{:S(2)}, u32[]{:S(2)}) collective-permute-start(bf16[2,2,128,768]{3,2,1,0:T(8,128)(2,1)} %copy-done.5), channel_id=1, source_target_pairs={{0,24},{8,0},{16,8},{24,16},{1,25},{9,1},{17,9},{25,17},{2,26},{10... | collective-permute-start | bytes 2359304 | tf_op jit(solution)/shard_map/ppermute | solution.py:267
  99.0 15.1 %cotangent.1 = (f32[1024,512]{1,0:T(8,128)}, bf16[528,128]{1,0:T(8,128)(2,1)}) custom-call(bf16[8,1024,768]{2,1,0:T(8,128)(2,1)} %bitcast.40, bf16[512,6144]{1,0:T(8,128)(2,1)} %weight.1, f32[1024,512]{1,0:T(8,128)} %get-tuple-element.60.opened, bf16[1024,512]{1,0:T(8,128)(2,1)} %q.5, f32[1024,128]{1,0:T(8,128)} %broadcast_in_dim.10.dcol, ...), custom_call_target="tpu_custom_call" | custom-call | tf_op jit(solution)/shard_map/cotangent/pallas_call | solution.py:399
  114.1 1.8 collective-permute-done.14.refs_14_
  115.9 3.3 %collective-permute-done.15.refs_15_ = bf16[2,2,128,768]{3,2,1,0:T(8,128)(2,1)S(1)} collective-permute-done((bf16[2,2,128,768]{3,2,1,0:T(8,128)(2,1)}, bf16[2,2,128,768]{3,2,1,0:T(8,128)(2,1)S(1)}, u32[]{:S(2)}, u32[]{:S(2)}) %collective-permute-start.15) | collective-permute-done | bytes 786464 | tf_op jit(solution)/shard_map/ppermute | solution.py:267
  119.5 1.9 collective-permute-done.17.refs_4_
  122.1 1.8 collective-permute-start.22
  123.8 2.7 %collective-permute-start.18 = (bf16[528,128]{1,0:T(8,128)(2,1)S(1)}, bf16[528,128]{1,0:T(8,128)(2,1)S(1)}, u32[]{:S(2)}, u32[]{:S(2)}) collective-permute-start(bf16[528,128]{1,0:T(8,128)(2,1)S(1)} %copy-done.22), channel_id=1, source_target_pairs={{0,24},{8,0},{16,8},{24,16},{1,25},{9,1},{17,9},{25,17},{2,26},{10... | collective-permute-start | bytes 405512 | tf_op jit(solution)/shard_map/ppermute | solution.py:267
  127.4 0.9 collective-permute-start.20
  128.2 2.8 %collective-permute-done.18.refs_1_.refs_0_ = bf16[528,128]{1,0:T(8,128)(2,1)S(1)} collective-permute-done((bf16[528,128]{1,0:T(8,128)(2,1)S(1)}, bf16[528,128]{1,0:T(8,128)(2,1)S(1)}, u32[]{:S(2)}, u32[]{:S(2)}) %collective-permute-start.18) | collective-permute-done | bytes 135200 | tf_op jit(solution)/shard_map/ppermute | solution.py:267
  131.1 2.3 %collective-permute-done.19.refs_2_.refs_1_ = bf16[528,128]{1,0:T(8,128)(2,1)S(1)} collective-permute-done((bf16[528,128]{1,0:T(8,128)(2,1)S(1)}, bf16[528,128]{1,0:T(8,128)(2,1)S(1)}, u32[]{:S(2)}, u32[]{:S(2)}) %collective-permute-start.19) | collective-permute-done | bytes 135200 | tf_op jit(solution)/shard_map/ppermute | solution.py:267
  133.4 1.3 collective-permute-done.20.refs_3_.refs_2_
  134.7 1.7 collective-permute-done.22.refs_7_
  137.5 1.9 row_state.3
  139.4 1.5 collective-permute-done.28.refs_8_
  140.9 1.9 collective-permute-start.23
  142.9 1.3 collective-permute-start.24
  145.1 13.8 %attended.1 = bf16[1024,768]{1,0:T(8,128)(2,1)} custom-call(s32[20]{0:T(128)} %stack.119.places, bf16[1024,512]{1,0:T(8,128)(2,1)} %get-tuple-element.77.refs_0_, bf16[1024,512]{1,0:T(8,128)(2,1)} %collective-permute-done.25.refs_1_, bf16[1024,512]{1,0:T(8,128)(2,1)} %copy-done.2, bf16[1024,512]{1,0:T(8,128)(2,1)} %collective-permute-done.26.refs_3_, ...), custom_call_target="tpu_custom_call" | custom-call | tf_op jit(solution)/shard_map/attended/pallas_call | solution.py:433
  158.9 3.5 %reduce-scatter.2.cloned.1.call-done = bf16[1,4,512,384]{3,2,1,0:T(8,128)(2,1)} async-done(((bf16[4,4,512,384]{3,2,1,0:T(8,128)(2,1)}), bf16[1,4,512,384]{3,2,1,0:T(8,128)(2,1)}) %reduce-scatter.2.cloned.1.call-update) | async-done | bytes 1572880 | tf_op jit(solution)/shard_map/reduce_scatter | solution.py:393
  162.5 1.4 dynamic-slice_bitcast_fusion
  163.8 1.5 collective-permute-start.30
  165.4 2.7 %collective-permute-start.31 = (bf16[512,384]{1,0:T(8,128)(2,1)S(1)}, bf16[512,384]{1,0:T(8,128)(2,1)S(1)}, u32[]{:S(2)}, u32[]{:S(2)}) collective-permute-start(bf16[512,384]{1,0:T(8,128)(2,1)S(1)} %get-tuple-element.100), channel_id=1, source_target_pairs={{0,16},{8,24},{16,0},{24,8},{1,17},{9,25},{17,1},{25,9},{2,18},{10... | collective-permute-start | bytes 1179656 | tf_op jit(solution)/shard_map/ppermute | solution.py:267
  168.1 1.4 collective-permute-start.32
  169.5 5.9 %grad_query.1 = bf16[1024,512]{1,0:T(8,128)(2,1)} custom-call(f32[1024,512]{1,0:T(8,128)} %get-tuple-element.87.go, bf16[1024,512]{1,0:T(8,128)(2,1)} %k.7, bf16[1024,512]{1,0:T(8,128)(2,1)} %v.7, f32[1024,128]{1,0:T(8,128)} %broadcast_in_dim.10.dcol, f32[1,1024]{1,0:T(1,128)} %bitcast.48, f32[16,128]{1,0:T(8,128)} %broadcast_in_dim.24.table, ...), custom_call_target="tpu_custom_call" | custom-call | tf_op jit(solution)/shard_map/grad_query/pallas_call | solution.py:452
  175.4 7.4 %grad_key_value.1 = (bf16[1024,512]{1,0:T(8,128)(2,1)}, bf16[1024,512]{1,0:T(8,128)(2,1)}) custom-call(f32[1024,512]{1,0:T(8,128)} %get-tuple-element.87.go, bf16[1024,512]{1,0:T(8,128)(2,1)} %q.5, bf16[1024,512]{1,0:T(8,128)(2,1)} %k.7, bf16[1024,512]{1,0:T(8,128)(2,1)} %v.7, f32[1024,128]{1,0:T(8,128)} %broadcast_in_dim.10.dcol, f32[1,1024]{1,0:T(1,128)} %bitcast.49, ...), custom_call_target="tpu_custom_call" | custom-call | tf_op jit(solution)/shard_map/grad_key_value/pallas_call | solution.py:465
  182.9 2.5 %collective-permute-done.31.refs_1_ = bf16[512,384]{1,0:T(8,128)(2,1)S(1)} collective-permute-done((bf16[512,384]{1,0:T(8,128)(2,1)S(1)}, bf16[512,384]{1,0:T(8,128)(2,1)S(1)}, u32[]{:S(2)}, u32[]{:S(2)}) %collective-permute-start.31) | collective-permute-done | bytes 393248 | tf_op jit(solution)/shard_map/ppermute | solution.py:267
  186.3 2.3 %last_sum.1 = f32[512,384]{1,0:T(8,128)} custom-call(s32[1]{0:T(128)} %bitcast.30.place, bf16[4,512,384]{2,1,0:T(8,128)(2,1)} %bitcast.42, bf16[512,384]{1,0:T(8,128)(2,1)} %copy-done.14, bf16[512,384]{1,0:T(8,128)(2,1)} %copy-done.15, bf16[512,384]{1,0:T(8,128)(2,1)} %copy-done.16), custom_call_target="tpu_custom_call" | custom-call | tf_op jit(solution)/shard_map/last_sum/pallas_call | solution.py:315
  (98 shorter events, 10.5 us)
Async XLA Ops:
  7.2 72.5 %all-gather.3.cloned.1.call-start = ((), (), s32[]{:S(2)}) async-start(), calls=%async_computation.2 | async-start | bytes 14155776 | tf_op jit(solution)/shard_map/all_gather | solution.py:340
  7.9 154.6 %reduce-scatter.2.cloned.1.call-start = ((), (), s32[]{:S(2)}) async-start(), calls=%async_computation.1 | async-start | bytes 7864320 | tf_op jit(solution)/shard_map/reduce_scatter | solution.py:393
  9.0 20.3 %collective-permute-start.3 = (bf16[128,1536]{1,0:T(8,128)(2,1)S(1)}, bf16[128,1536]{1,0:T(8,128)(2,1)S(1)}, u32[]{:S(2)}, u32[]{:S(2)}) collective-permute-start(bf16[128,1536]{1,0:T(8,128)(2,1)S(1)} %dynamic_slice.19), channel_id=1, source_target_pairs={{0,0},{2,2},{4,4},{6,6},{10,8},{12,10},{14,12},{8,14},{20,16},{22,... | collective-permute-start | bytes 1179656 | tf_op jit(solution)/shard_map/ppermute | solution.py:300
  9.7 21.2 %copy-start.17 = (f32[1024]{0:T(1024)}, f32[1024]{0:T(1024)S(1)}, u32[]{:S(2)}) copy-start(f32[1024]{0:T(1024)S(1)} %convert_element_type.6) | copy-start | bytes 12292
  14.6 11.1 %collective-permute-start = (bf16[528,128]{1,0:T(8,128)(2,1)}, bf16[528,128]{1,0:T(8,128)(2,1)S(1)}, u32[]{:S(2)}, u32[]{:S(2)}) collective-permute-start(bf16[528,128]{1,0:T(8,128)(2,1)} %tail.1.refs_0_), channel_id=1, source_target_pairs={{0,8},{8,16},{16,24},{24,0},{1,9},{9,17},{17,25},{25,1},{2,10},{10... | collective-permute-start | bytes 405512 | tf_op jit(solution)/shard_map/ppermute | solution.py:267
  21.4 7.9 %collective-permute-start.1 = (bf16[528,128]{1,0:T(8,128)(2,1)}, bf16[528,128]{1,0:T(8,128)(2,1)S(1)}, u32[]{:S(2)}, u32[]{:S(2)}) collective-permute-start(bf16[528,128]{1,0:T(8,128)(2,1)} %tail.1.refs_0_), channel_id=1, source_target_pairs={{0,16},{8,24},{16,0},{24,8},{1,17},{9,25},{17,1},{25,9},{2,18},{10... | collective-permute-start | bytes 405512 | tf_op jit(solution)/shard_map/ppermute | solution.py:267
  22.9 6.4 %collective-permute-start.2 = (bf16[528,128]{1,0:T(8,128)(2,1)}, bf16[528,128]{1,0:T(8,128)(2,1)S(1)}, u32[]{:S(2)}, u32[]{:S(2)}) collective-permute-start(bf16[528,128]{1,0:T(8,128)(2,1)} %tail.1.refs_0_), channel_id=1, source_target_pairs={{0,24},{8,0},{16,8},{24,16},{1,25},{9,1},{17,9},{25,17},{2,26},{10... | collective-permute-start | bytes 405512 | tf_op jit(solution)/shard_map/ppermute | solution.py:267
  25.7 9.4 %copy-start.11 = (bf16[528,128]{1,0:T(8,128)(2,1)}, bf16[528,128]{1,0:T(8,128)(2,1)S(1)}, u32[]{:S(2)}) copy-start(bf16[528,128]{1,0:T(8,128)(2,1)S(1)} %collective-permute-done.refs_1_.refs_0_) | copy-start | bytes 405508
  29.3 1.5 collective-permute-start.6
  30.9 18.9 %collective-permute-start.7 = (bf16[2,128,768]{2,1,0:T(8,128)(2,1)S(1)}, bf16[2,128,768]{2,1,0:T(8,128)(2,1)S(1)}, u32[]{:S(2)}, u32[]{:S(2)}) collective-permute-start(bf16[2,128,768]{2,1,0:T(8,128)(2,1)S(1)} %get-tuple-element.103), channel_id=1, source_target_pairs={{0,32},{32,64},{64,96},{96,0},{1,33},{33,65},{65,97},{97,1},{2,34}... | collective-permute-start | bytes 1179656 | tf_op jit(solution)/shard_map/ppermute | solution.py:267
  32.5 17.5 %collective-permute-start.9 = (bf16[2,128,768]{2,1,0:T(8,128)(2,1)S(1)}, bf16[2,128,768]{2,1,0:T(8,128)(2,1)S(1)}, u32[]{:S(2)}, u32[]{:S(2)}) collective-permute-start(bf16[2,128,768]{2,1,0:T(8,128)(2,1)S(1)} %get-tuple-element.103), channel_id=1, source_target_pairs={{0,96},{32,0},{64,32},{96,64},{1,97},{33,1},{65,33},{97,65},{2,98}... | collective-permute-start | bytes 1179656 | tf_op jit(solution)/shard_map/ppermute | solution.py:267
  33.0 19.4 %collective-permute-start.8 = (bf16[2,128,768]{2,1,0:T(8,128)(2,1)S(1)}, bf16[2,128,768]{2,1,0:T(8,128)(2,1)S(1)}, u32[]{:S(2)}, u32[]{:S(2)}) collective-permute-start(bf16[2,128,768]{2,1,0:T(8,128)(2,1)S(1)} %get-tuple-element.103), channel_id=1, source_target_pairs={{0,64},{32,96},{64,0},{96,32},{1,65},{33,97},{65,1},{97,33},{2,66}... | collective-permute-start | bytes 1179656 | tf_op jit(solution)/shard_map/ppermute | solution.py:267
  37.0 17.3 %collective-permute-start.4 = (bf16[528,128]{1,0:T(8,128)(2,1)}, bf16[528,128]{1,0:T(8,128)(2,1)S(1)}, u32[]{:S(2)}, u32[]{:S(2)}) collective-permute-start(bf16[528,128]{1,0:T(8,128)(2,1)} %row_state.2), channel_id=1, source_target_pairs={{0,32},{32,64},{64,96},{1,33},{33,65},{65,97},{2,34},{34,66},{66,9... | collective-permute-start | bytes 405512 | tf_op jit(solution)/shard_map/ppermute | solution.py:273
  40.0 14.3 %collective-permute-start.5 = (bf16[528,128]{1,0:T(8,128)(2,1)}, bf16[528,128]{1,0:T(8,128)(2,1)S(1)}, u32[]{:S(2)}, u32[]{:S(2)}) collective-permute-start(bf16[528,128]{1,0:T(8,128)(2,1)} %row_state.2), channel_id=1, source_target_pairs={{0,64},{32,96},{1,65},{33,97},{2,66},{34,98},{3,67},{35,99},{4,68}... | collective-permute-start | bytes 405512 | tf_op jit(solution)/shard_map/ppermute | solution.py:273
  49.9 17.3 %copy-start = (bf16[2,2,128,768]{3,2,1,0:T(8,128)(2,1)}, bf16[2,2,128,768]{3,2,1,0:T(8,128)(2,1)S(1)}, u32[]{:S(2)}) copy-start(bf16[2,2,128,768]{3,2,1,0:T(8,128)(2,1)S(1)} %pad_maximum_fusion.refs_10_) | copy-start | bytes 2359300
  52.5 14.7 %copy-start.1 = (bf16[2,2,128,768]{3,2,1,0:T(8,128)(2,1)}, bf16[2,2,128,768]{3,2,1,0:T(8,128)(2,1)S(1)}, u32[]{:S(2)}) copy-start(bf16[2,2,128,768]{3,2,1,0:T(8,128)(2,1)S(1)} %pad_maximum_fusion.1.refs_11_) | copy-start | bytes 2359300
  54.3 6.1 %copy-start.20 = (bf16[528,128]{1,0:T(8,128)(2,1)}, bf16[528,128]{1,0:T(8,128)(2,1)S(1)}, u32[]{:S(2)}) copy-start(bf16[528,128]{1,0:T(8,128)(2,1)S(1)} %collective-permute-done.4.refs_3_) | copy-start | bytes 405508
  54.3 38.4 %collective-permute-start.10 = (bf16[2,2,128,768]{3,2,1,0:T(8,128)(2,1)S(1)}, bf16[2,2,128,768]{3,2,1,0:T(8,128)(2,1)S(1)}, u32[]{:S(2)}, u32[]{:S(2)}) collective-permute-start(bf16[2,2,128,768]{3,2,1,0:T(8,128)(2,1)S(1)} %pad_maximum_fusion.refs_10_), channel_id=1, source_target_pairs={{0,24},{8,0},{16,8},{24,16},{1,25},{9,1},{17,9},{25,17},{2,26},{10... | collective-permute-start | bytes 2359304 | tf_op jit(solution)/shard_map/ppermute | solution.py:267
  57.2 35.5 %collective-permute-start.11 = (bf16[2,2,128,768]{3,2,1,0:T(8,128)(2,1)S(1)}, bf16[2,2,128,768]{3,2,1,0:T(8,128)(2,1)}, u32[]{:S(2)}, u32[]{:S(2)}) collective-permute-start(bf16[2,2,128,768]{3,2,1,0:T(8,128)(2,1)S(1)} %pad_maximum_fusion.1.refs_11_), channel_id=1, source_target_pairs={{0,8},{8,16},{16,24},{24,0},{1,9},{9,17},{17,25},{25,1},{2,10},{10... | collective-permute-start | bytes 2359304 | tf_op jit(solution)/shard_map/ppermute | solution.py:267
  57.2 35.5 %collective-permute-start.12 = (bf16[2,2,128,768]{3,2,1,0:T(8,128)(2,1)S(1)}, bf16[2,2,128,768]{3,2,1,0:T(8,128)(2,1)}, u32[]{:S(2)}, u32[]{:S(2)}) collective-permute-start(bf16[2,2,128,768]{3,2,1,0:T(8,128)(2,1)S(1)} %pad_maximum_fusion.1.refs_11_), channel_id=1, source_target_pairs={{0,24},{8,0},{16,8},{24,16},{1,25},{9,1},{17,9},{25,17},{2,26},{10... | collective-permute-start | bytes 2359304 | tf_op jit(solution)/shard_map/ppermute | solution.py:267
  60.4 32.7 %collective-permute-start.13 = (bf16[2,2,128,768]{3,2,1,0:T(8,128)(2,1)S(1)}, bf16[2,2,128,768]{3,2,1,0:T(8,128)(2,1)}, u32[]{:S(2)}, u32[]{:S(2)}) collective-permute-start(bf16[2,2,128,768]{3,2,1,0:T(8,128)(2,1)S(1)} %pad_maximum_fusion.refs_10_), channel_id=1, source_target_pairs={{0,8},{8,16},{16,24},{24,0},{1,9},{9,17},{17,25},{25,1},{2,10},{10... | collective-permute-start | bytes 2359304 | tf_op jit(solution)/shard_map/ppermute | solution.py:267
  94.4 25.2 %collective-permute-start.16 = (bf16[1024,512]{1,0:T(8,128)(2,1)S(1)}, bf16[1024,512]{1,0:T(8,128)(2,1)S(1)}, u32[]{:S(2)}, u32[]{:S(2)}) collective-permute-start(bf16[1024,512]{1,0:T(8,128)(2,1)S(1)} %copy-done.4), channel_id=1, source_target_pairs={{0,6},{2,0},{4,2},{6,4},{1,7},{3,1},{5,3},{7,5},{8,14},{10,8},{12,... | collective-permute-start | bytes 3145736 | tf_op jit(solution)/shard_map/ppermute | solution.py:267
  95.1 26.3 %collective-permute-start.17 = (bf16[1024,512]{1,0:T(8,128)(2,1)S(1)}, bf16[1024,512]{1,0:T(8,128)(2,1)S(1)}, u32[]{:S(2)}, u32[]{:S(2)}) collective-permute-start(bf16[1024,512]{1,0:T(8,128)(2,1)S(1)} %copy-done.4), channel_id=1, source_target_pairs={{0,2},{2,4},{4,6},{6,0},{1,3},{3,5},{5,7},{7,1},{8,10},{10,12},{12... | collective-permute-start | bytes 3145736 | tf_op jit(solution)/shard_map/ppermute | solution.py:267
  96.4 19.6 %collective-permute-start.14 = (bf16[2,2,128,768]{3,2,1,0:T(8,128)(2,1)}, bf16[2,2,128,768]{3,2,1,0:T(8,128)(2,1)S(1)}, u32[]{:S(2)}, u32[]{:S(2)}) collective-permute-start(bf16[2,2,128,768]{3,2,1,0:T(8,128)(2,1)} %copy-done.5), channel_id=1, source_target_pairs={{0,24},{8,0},{16,8},{24,16},{1,25},{9,1},{17,9},{25,17},{2,26},{10... | collective-permute-start | bytes 2359304 | tf_op jit(solution)/shard_map/ppermute | solution.py:267
  99.0 20.3 %collective-permute-start.15 = (bf16[2,2,128,768]{3,2,1,0:T(8,128)(2,1)}, bf16[2,2,128,768]{3,2,1,0:T(8,128)(2,1)S(1)}, u32[]{:S(2)}, u32[]{:S(2)}) collective-permute-start(bf16[2,2,128,768]{3,2,1,0:T(8,128)(2,1)} %collective-permute-done.11.refs_17_), channel_id=1, source_target_pairs={{0,8},{8,16},{16,24},{24,0},{1,9},{9,17},{17,25},{25,1},{2,10},{10... | collective-permute-start | bytes 2359304 | tf_op jit(solution)/shard_map/ppermute | solution.py:267
  114.1 9.7 %copy-start.22 = (bf16[528,128]{1,0:T(8,128)(2,1)S(1)}, bf16[528,128]{1,0:T(8,128)(2,1)}, u32[]{:S(2)}) copy-start(bf16[528,128]{1,0:T(8,128)(2,1)} %get-tuple-element.69.refs_0_) | copy-start | bytes 405508
  115.9 20.5 %copy-start.6 = (bf16[2,2,128,768]{3,2,1,0:T(8,128)(2,1)}, bf16[2,2,128,768]{3,2,1,0:T(8,128)(2,1)S(1)}, u32[]{:S(2)}) copy-start(bf16[2,2,128,768]{3,2,1,0:T(8,128)(2,1)S(1)} %collective-permute-done.14.refs_14_) | copy-start | bytes 2359300
  119.2 17.7 %copy-start.7 = (bf16[2,2,128,768]{3,2,1,0:T(8,128)(2,1)}, bf16[2,2,128,768]{3,2,1,0:T(8,128)(2,1)S(1)}, u32[]{:S(2)}) copy-start(bf16[2,2,128,768]{3,2,1,0:T(8,128)(2,1)S(1)} %collective-permute-done.15.refs_15_) | copy-start | bytes 2359300
  119.5 25.5 %copy-start.2 = (bf16[1024,512]{1,0:T(8,128)(2,1)}, bf16[1024,512]{1,0:T(8,128)(2,1)S(1)}, u32[]{:S(2)}) copy-start(bf16[1024,512]{1,0:T(8,128)(2,1)S(1)} %collective-permute-done.16.refs_2_) | copy-start | bytes 3145732
  121.4 23.7 %copy-start.3 = (bf16[1024,512]{1,0:T(8,128)(2,1)}, bf16[1024,512]{1,0:T(8,128)(2,1)S(1)}, u32[]{:S(2)}) copy-start(bf16[1024,512]{1,0:T(8,128)(2,1)S(1)} %collective-permute-done.17.refs_4_) | copy-start | bytes 3145732
  121.4 13.3 %collective-permute-start.21 = (bf16[512,512]{1,0:T(8,128)(2,1)S(1)}, bf16[512,512]{1,0:T(8,128)(2,1)}, u32[]{:S(2)}, u32[]{:S(2)}) collective-permute-start(bf16[512,512]{1,0:T(8,128)(2,1)S(1)} %slice.14), channel_id=1, source_target_pairs={{0,6},{2,0},{4,2},{6,4},{1,7},{3,1},{5,3},{7,5},{8,14},{10,8},{12,... | collective-permute-start | bytes 1572872 | tf_op jit(solution)/shard_map/ppermute | solution.py:267
  122.1 14.4 %collective-permute-start.22 = (bf16[512,512]{1,0:T(8,128)(2,1)S(1)}, bf16[512,512]{1,0:T(8,128)(2,1)}, u32[]{:S(2)}, u32[]{:S(2)}) collective-permute-start(bf16[512,512]{1,0:T(8,128)(2,1)S(1)} %slice.15), channel_id=1, source_target_pairs={{0,2},{2,4},{4,6},{6,0},{1,3},{3,5},{5,7},{7,1},{8,10},{10,12},{12... | collective-permute-start | bytes 1572872 | tf_op jit(solution)/shard_map/ppermute | solution.py:267
  123.8 7.3 %collective-permute-start.18 = (bf16[528,128]{1,0:T(8,128)(2,1)S(1)}, bf16[528,128]{1,0:T(8,128)(2,1)S(1)}, u32[]{:S(2)}, u32[]{:S(2)}) collective-permute-start(bf16[528,128]{1,0:T(8,128)(2,1)S(1)} %copy-done.22), channel_id=1, source_target_pairs={{0,24},{8,0},{16,8},{24,16},{1,25},{9,1},{17,9},{25,17},{2,26},{10... | collective-permute-start | bytes 405512 | tf_op jit(solution)/shard_map/ppermute | solution.py:267
  126.6 6.8 %collective-permute-start.19 = (bf16[528,128]{1,0:T(8,128)(2,1)S(1)}, bf16[528,128]{1,0:T(8,128)(2,1)S(1)}, u32[]{:S(2)}, u32[]{:S(2)}) collective-permute-start(bf16[528,128]{1,0:T(8,128)(2,1)S(1)} %copy-done.22), channel_id=1, source_target_pairs={{0,16},{8,24},{16,0},{24,8},{1,17},{9,25},{17,1},{25,9},{2,18},{10... | collective-permute-start | bytes 405512 | tf_op jit(solution)/shard_map/ppermute | solution.py:267
  127.4 7.3 %collective-permute-start.20 = (bf16[528,128]{1,0:T(8,128)(2,1)S(1)}, bf16[528,128]{1,0:T(8,128)(2,1)S(1)}, u32[]{:S(2)}, u32[]{:S(2)}) collective-permute-start(bf16[528,128]{1,0:T(8,128)(2,1)S(1)} %copy-done.22), channel_id=1, source_target_pairs={{0,8},{8,16},{16,24},{24,0},{1,9},{9,17},{17,25},{25,1},{2,10},{10... | collective-permute-start | bytes 405512 | tf_op jit(solution)/shard_map/ppermute | solution.py:267
  131.1 6.4 %copy-start.8 = (bf16[528,128]{1,0:T(8,128)(2,1)}, bf16[528,128]{1,0:T(8,128)(2,1)S(1)}, u32[]{:S(2)}) copy-start(bf16[528,128]{1,0:T(8,128)(2,1)S(1)} %collective-permute-done.18.refs_1_.refs_0_) | copy-start | bytes 405508
  136.4 8.6 %collective-permute-start.25 = (bf16[1024,512]{1,0:T(8,128)(2,1)S(1)}, bf16[1024,512]{1,0:T(8,128)(2,1)}, u32[]{:S(2)}, u32[]{:S(2)}) collective-permute-start(bf16[1024,512]{1,0:T(8,128)(2,1)S(1)} %copy-done.4), channel_id=1, source_target_pairs={{0,1},{1,0},{2,3},{3,2},{4,5},{5,4},{6,7},{7,6},{8,9},{9,8},{10,11... | collective-permute-start | bytes 3145736 | tf_op jit(solution)/shard_map/ppermute | solution.py:277
  136.4 8.6 %collective-permute-start.26 = (bf16[1024,512]{1,0:T(8,128)(2,1)S(1)}, bf16[1024,512]{1,0:T(8,128)(2,1)}, u32[]{:S(2)}, u32[]{:S(2)}) collective-permute-start(bf16[1024,512]{1,0:T(8,128)(2,1)S(1)} %collective-permute-done.16.refs_2_), channel_id=1, source_target_pairs={{0,1},{1,0},{2,3},{3,2},{4,5},{5,4},{6,7},{7,6},{8,9},{9,8},{10,11... | collective-permute-start | bytes 3145736 | tf_op jit(solution)/shard_map/ppermute | solution.py:277
  136.9 8.1 %collective-permute-start.27 = (bf16[1024,512]{1,0:T(8,128)(2,1)S(1)}, bf16[1024,512]{1,0:T(8,128)(2,1)}, u32[]{:S(2)}, u32[]{:S(2)}) collective-permute-start(bf16[1024,512]{1,0:T(8,128)(2,1)S(1)} %collective-permute-done.17.refs_4_), channel_id=1, source_target_pairs={{0,1},{1,0},{2,3},{3,2},{4,5},{5,4},{6,7},{7,6},{8,9},{9,8},{10,11... | collective-permute-start | bytes 3145736 | tf_op jit(solution)/shard_map/ppermute | solution.py:277
  137.0 3.9 %collective-permute-start.28 = (bf16[512,512]{1,0:T(8,128)(2,1)}, bf16[512,512]{1,0:T(8,128)(2,1)}, u32[]{:S(2)}, u32[]{:S(2)}) collective-permute-start(bf16[512,512]{1,0:T(8,128)(2,1)} %collective-permute-done.21.refs_6_), channel_id=1, source_target_pairs={{0,1},{1,0},{2,3},{3,2},{4,5},{5,4},{6,7},{7,6},{8,9},{9,8},{10,11... | collective-permute-start | bytes 1572872 | tf_op jit(solution)/shard_map/ppermute | solution.py:277
  137.5 5.4 %collective-permute-start.29 = (bf16[512,512]{1,0:T(8,128)(2,1)}, bf16[512,512]{1,0:T(8,128)(2,1)}, u32[]{:S(2)}, u32[]{:S(2)}) collective-permute-start(bf16[512,512]{1,0:T(8,128)(2,1)} %collective-permute-done.22.refs_7_), channel_id=1, source_target_pairs={{0,1},{1,0},{2,3},{3,2},{4,5},{5,4},{6,7},{7,6},{8,9},{9,8},{10,11... | collective-permute-start | bytes 1572872 | tf_op jit(solution)/shard_map/ppermute | solution.py:277
  140.9 18.0 %collective-permute-start.23 = (bf16[528,128]{1,0:T(8,128)(2,1)}, bf16[528,128]{1,0:T(8,128)(2,1)S(1)}, u32[]{:S(2)}, u32[]{:S(2)}) collective-permute-start(bf16[528,128]{1,0:T(8,128)(2,1)} %row_state.3), channel_id=1, source_target_pairs={{32,0},{64,32},{96,64},{33,1},{65,33},{97,65},{34,2},{66,34},{98,6... | collective-permute-start | bytes 405512 | tf_op jit(solution)/shard_map/ppermute | solution.py:273
  142.9 16.1 %collective-permute-start.24 = (bf16[528,128]{1,0:T(8,128)(2,1)}, bf16[528,128]{1,0:T(8,128)(2,1)S(1)}, u32[]{:S(2)}, u32[]{:S(2)}) collective-permute-start(bf16[528,128]{1,0:T(8,128)(2,1)} %row_state.3), channel_id=1, source_target_pairs={{64,0},{96,32},{65,1},{97,33},{66,2},{98,34},{67,3},{99,35},{68,4}... | collective-permute-start | bytes 405512 | tf_op jit(solution)/shard_map/ppermute | solution.py:273
  158.9 16.5 %copy-start.18 = (bf16[528,128]{1,0:T(8,128)(2,1)}, bf16[528,128]{1,0:T(8,128)(2,1)S(1)}, u32[]{:S(2)}) copy-start(bf16[528,128]{1,0:T(8,128)(2,1)S(1)} %collective-permute-done.23.refs_3_) | copy-start | bytes 405508
  158.9 16.5 %copy-start.19 = (bf16[528,128]{1,0:T(8,128)(2,1)}, bf16[528,128]{1,0:T(8,128)(2,1)S(1)}, u32[]{:S(2)}) copy-start(bf16[528,128]{1,0:T(8,128)(2,1)S(1)} %collective-permute-done.24.refs_4_) | copy-start | bytes 405508
  163.8 19.0 %collective-permute-start.30 = (bf16[512,384]{1,0:T(8,128)(2,1)S(1)}, bf16[512,384]{1,0:T(8,128)(2,1)S(1)}, u32[]{:S(2)}, u32[]{:S(2)}) collective-permute-start(bf16[512,384]{1,0:T(8,128)(2,1)S(1)} %get-tuple-element.101), channel_id=1, source_target_pairs={{0,8},{8,16},{16,24},{24,0},{1,9},{9,17},{17,25},{25,1},{2,10},{10... | collective-permute-start | bytes 1179656 | tf_op jit(solution)/shard_map/ppermute | solution.py:267
  165.4 20.0 %collective-permute-start.31 = (bf16[512,384]{1,0:T(8,128)(2,1)S(1)}, bf16[512,384]{1,0:T(8,128)(2,1)S(1)}, u32[]{:S(2)}, u32[]{:S(2)}) collective-permute-start(bf16[512,384]{1,0:T(8,128)(2,1)S(1)} %get-tuple-element.100), channel_id=1, source_target_pairs={{0,16},{8,24},{16,0},{24,8},{1,17},{9,25},{17,1},{25,9},{2,18},{10... | collective-permute-start | bytes 1179656 | tf_op jit(solution)/shard_map/ppermute | solution.py:267
  168.1 17.3 %collective-permute-start.32 = (bf16[512,384]{1,0:T(8,128)(2,1)S(1)}, bf16[512,384]{1,0:T(8,128)(2,1)S(1)}, u32[]{:S(2)}, u32[]{:S(2)}) collective-permute-start(bf16[512,384]{1,0:T(8,128)(2,1)S(1)} %get-tuple-element.99), channel_id=1, source_target_pairs={{0,24},{8,0},{16,8},{24,16},{1,25},{9,1},{17,9},{25,17},{2,26},{10... | collective-permute-start | bytes 1179656 | tf_op jit(solution)/shard_map/ppermute | solution.py:267
  (11 other events, 33.7 us)
Sparse Core Ops, SparseCore 0:
  9.7 69.9 all-gather.2
  93.7 68.7 reduce-scatter.1

commit v6 on v5

--- a/solution.py
+++ b/solution.py
@@ -116,13 +116,18 @@
         carry[c, :] = jnp.where(keep, state, 0.0) + dot(kept, vh, TN)
 
 
-def cotangent_kernel(grad, weight, opened, q, dcol, table, grad_opened, out, carry):
+def near_cotangent_kernel(places, own, beside, first, second, out):
+    out[...] = dot(own[...], first[...], NT) + dot(beside[...], second[...], NT)
+
+
+def cotangent_kernel(places, near, *refs):
+    grads, weights = refs[:6], refs[6:12]
+    opened, q, dcol, table, grad_opened, out, carry = refs[12:]
     i = pl.program_id(0)
     heads = q.shape[1] // HEAD
-    width = grad.shape[2]
-    gn = dot(grad[0], weight[:, :width], NT)
-    for j in range(1, grad.shape[0]):
-        gn = gn + dot(grad[j], weight[:, j * width : (j + 1) * width], NT)
+    gn = near[...]
+    for grad, weight in zip(grads, weights):
+        gn = gn + dot(grad[0], weight[...], NT)
 
     @pl.when(i == 0)
     def _():
@@ -215,19 +220,20 @@
 def put_columns(part, out):
     low = part.astype(BF16)
     half = low.shape[1] // 2
-    out[0, 0] = low[:, :half]
-    out[0, 1] = low[:, half:]
-
-
-def weight_kernel(turned, grad, out):
+    out[0] = low[:, :half]
+    out[1] = low[:, half:]
+
+
+def near_weight_kernel(places, turned, own, beside, out):
+    for p, piece in enumerate((own, beside)):
+
+        @pl.when(pl.program_id(0) == p)
+        def _():
+            put_columns(dot(turned[...], piece[...], NN), out)
+
+
+def weight_kernel(places, turned, grad, started, out):
     put_columns(dot(turned[...], grad[0], NN), out)
-
-
-def sum_kernel(place, own, *refs):
-    total = own[0].astype(F32)
-    for ref in refs[:-1]:
-        total = total + ref[...].astype(F32)
-    refs[-1][...] = total
 
 
 def attended_kernel(places, *refs):
@@ -308,25 +314,6 @@
     return jnp.stack(lines[:2]), jnp.stack(lines[2:])
 
 
-def row_sum(mine, cy):
-    got = [turned_by(pick(mine, (cy + s) % 4), "cy", s) for s in range(1, 4)]
-    height, part = mine.shape[1:]
-    block = (CHUNK, part)
-    return pl.pallas_call(
-        sum_kernel,
-        grid_spec=pltpu.PrefetchScalarGridSpec(
-            num_scalar_prefetch=1,
-            grid=(height // CHUNK,),
-            in_specs=[pl.BlockSpec((1, *block), lambda i, p: (p[0], i, 0))]
-            + [pl.BlockSpec(block, lambda i, p: (i, 0))] * 3,
-            out_specs=pl.BlockSpec(block, lambda i, p: (i, 0)),
-        ),
-        out_shape=jax.ShapeDtypeStruct((height, part), F32),
-        compiler_params=params(),
-        name="last_sum",
-    )(cy[None], mine, *got)
-
-
 def body(queries, keys, values, doc_ids, out_weight, grad_out):
     rows, width = queries.shape
     blocks = rows // CHUNK
@@ -338,6 +325,7 @@
     z, core = lax.axis_index("z"), lax.axis_index("core")
 
     grad_whole = lax.all_gather(grad_out, TENSOR, axis=0)
+    beside = swapped(grad_out)
 
     docs = doc_ids.astype(F32)
     dcol = jnp.broadcast_to(docs[:, None], (rows, HEAD))
@@ -348,7 +336,8 @@
     table = jnp.broadcast_to(table[:, None], (16, HEAD))
 
     tail = pl.pallas_call(tail_kernel, out_shape=payload, name="tail")(keys, values, dcol, table)
-    arrived, strip = exchanged(tail, 1, column_strip(out_weight, share, cx))
+    strip = column_strip(out_weight, share, cx)
+    arrived, (strip, beside) = exchanged(tail, 1, (strip, beside))
     own = column_pieces(strip, share, core)
     arrived, own = lax.optimization_barrier((arrived, own))
     early = [turned_by(own[0], "cy", -1), turned_by(own[1], "cy", 1)]
@@ -379,18 +368,69 @@
         name="forward",
     )(queries, keys, values, dcol, drow, table, *arrived)
 
+    sides = (core, 1 - core)
+    places = jnp.stack([2 * ((z + s) % 4) + side for s in range(4) for side in sides])
+
+    def weight_block(p):
+        return pl.BlockSpec((width, share), lambda i, at: (0, at[p]))
+
+    def some_rows(columns):
+        return pl.BlockSpec((CHUNK, columns), lambda i, at: (i, 0))
+
+    def grad_block(p):
+        return pl.BlockSpec((1, CHUNK, share), lambda i, at: (at[p], i, 0))
+
+    near_sum = pl.pallas_call(
+        near_cotangent_kernel,
+        grid_spec=pltpu.PrefetchScalarGridSpec(
+            num_scalar_prefetch=1,
+            grid=(blocks,),
+            in_specs=[some_rows(share)] * 2 + [weight_block(0), weight_block(1)],
+            out_specs=some_rows(width),
+        ),
+        out_shape=jax.ShapeDtypeStruct((rows, width), F32),
+        compiler_params=params(),
+        name="near_cotangent",
+    )(places, grad_out, beside, out_weight, out_weight)
+
+    def column_block(base):
+        return pl.BlockSpec((2, width, share // 2), lambda j, at: (at[base + j], 0, 0))
+
+    held = pl.BlockSpec(memory_space=pl.ANY)
+    term_shape = jax.ShapeDtypeStruct((2 * groups, width, share // 2), BF16)
+    started = pl.pallas_call(
+        near_weight_kernel,
+        grid_spec=pltpu.PrefetchScalarGridSpec(
+            num_scalar_prefetch=1,
+            grid=(2,),
+            in_specs=[whole((width, rows))] + [whole((rows, share))] * 2,
+            out_specs=column_block(0),
+        ),
+        out_shape=term_shape,
+        compiler_params=params(),
+        name="near_weight",
+    )(places, turned, grad_out, beside)
+    started, near_sum = lax.optimization_barrier((started, near_sum))
     term = pl.pallas_call(
         weight_kernel,
-        grid=(groups,),
-        in_specs=[whole((width, rows)), pl.BlockSpec((1, rows, share), lambda j: (j, 0, 0))],
-        out_specs=pl.BlockSpec((1, 2, width, share // 2), lambda j: (j // 2, j % 2, 0, 0)),
-        out_shape=jax.ShapeDtypeStruct((4, 4, width, share // 2), BF16),
+        grid_spec=pltpu.PrefetchScalarGridSpec(
+            num_scalar_prefetch=1,
+            grid=(groups - 2,),
+            in_specs=[
+                whole((width, rows)),
+                pl.BlockSpec((1, rows, share), lambda j, at: (at[2 + j], 0, 0)),
+                held,
+            ],
+            out_specs=column_block(2),
+        ),
+        out_shape=term_shape,
+        input_output_aliases={3: 0},
         compiler_params=params(),
         name="weight_grad",
-    )(turned, grad_whole)
+    )(places, turned, grad_whole, started)
     term, low, early, later = lax.optimization_barrier((term, low, early, later))
     across = [turned_by(early[0], "cy", -1), turned_by(early[1], "cy", 1)]
-    grad_part = lax.psum_scatter(term, "cx", scatter_dimension=0, tiled=True)[0]
+    grad_part = lax.psum_scatter(term, CTX, scatter_dimension=0, tiled=True)
 
     half_rows = rows // 2
     above = turned_by(low, "z", -1)
@@ -398,21 +438,20 @@
 
     grad_opened, head = pl.pallas_call(
         cotangent_kernel,
-        grid=(blocks,),
-        in_specs=[
-            pl.BlockSpec((groups, CHUNK, share), lambda i: (0, i, 0)),
-            whole(out_weight.shape),
-            rows_of(width),
-            rows_of(width),
-            rows_of(HEAD),
-            whole(table.shape),
-        ],
-        out_specs=[rows_of(width), whole(payload.shape)],
+        grid_spec=pltpu.PrefetchScalarGridSpec(
+            num_scalar_prefetch=1,
+            grid=(blocks,),
+            in_specs=[some_rows(width)]
+            + [grad_block(p) for p in range(2, 8)]
+            + [weight_block(p) for p in range(2, 8)]
+            + [some_rows(width), some_rows(width), some_rows(HEAD), whole(table.shape)],
+            out_specs=[some_rows(width), whole(payload.shape)],
+            scratch_shapes=[pltpu.VMEM((size, HEAD), F32)],
+        ),
         out_shape=[jax.ShapeDtypeStruct((rows, width), F32), payload],
-        scratch_shapes=[pltpu.VMEM((size, HEAD), F32)],
         compiler_params=params(),
         name="cotangent",
-    )(grad_whole, out_weight, opened, queries, dcol, table)
+    )(places, near_sum, *[grad_whole] * 6, *[out_weight] * 6, opened, queries, dcol, table)
     head, across, above, below = lax.optimization_barrier((head, across, above, below))
     far_a = turned_by(above[:half_rows], "z", -1)
     far_b = turned_by(below[half_rows:], "z", 1)
@@ -422,7 +461,6 @@
     far = [far_a, far_b, swapped(far_a), swapped(far_b)]
     columns = [*own, early[0], later[0], *across, later[1], early[1]]
 
-    sides = (core, 1 - core)
     around = [2 * ((z + cy + s) % 4) + side for s in range(4) for side in sides]
     heads_at = [(cx - s) % 4 for s in range(4)]
     groups_at = [2 * ((z + s) % 4) + side for s in (0, 1, 3, 2) for side in sides]
@@ -446,8 +484,8 @@
         compiler_params=params(),
         name="attended",
     )(jnp.stack(around + heads_at + groups_at), *near, *far, *columns)
-    ready = (returned, grad_opened, grad_part, attended)
-    returned, grad_opened, grad_part, attended = lax.optimization_barrier(ready)
+    ready = (returned, grad_opened, attended)
+    returned, grad_opened, attended = lax.optimization_barrier(ready)
 
     grad_query = pl.pallas_call(
         query_kernel,
@@ -475,7 +513,9 @@
         name="grad_key_value",
     )(grad_opened, queries, keys, values, dcol, drow, table, *returned)
 
-    grad_weight = row_sum(grad_part, cy)
+    ready = (grad_part, grad_query, grad_key)
+    grad_part, grad_query, grad_key = lax.optimization_barrier(ready)
+    grad_weight = grad_part.reshape(width, share // 2).astype(F32)
     return attended, grad_query, grad_key, grad_value, grad_weight
 
 

time: 196 us -> 196 us (level); the launches traced: 195 us -> 193 us
  waiting for transfers between devices: 54.3 us -> 45.8 us
  Pallas kernels: 70.9 us -> 78.4 us
  starting transfers between devices: 48.1 us -> 42.1 us
  other arithmetic: 0.2 us -> 5 us
    all_gather x1, waiting for transfers between devices: 12.4 us -> 0.01 us  [body(): grad_whole = lax.all_gather(grad_out, TENSOR, axis=0)]
    ppermute x22 -> x19, starting transfers between devices: 38.3 us -> 29.2 us  [turned_by(): lax.ppermute(value, axis, [(i, (i + step) % size) for i in range(size)])]
    ppermute x22 -> x19, waiting for transfers between devices: 32.9 us -> 40.5 us  [turned_by(): lax.ppermute(value, axis, [(i, (i + step) % size) for i in range(size)])]
    pallas_call x3 -> x4, Pallas kernels: 30.4 us -> 37.5 us  [the longest x1 14.4 us: body(): pl.pallas_call(cotangent_kernel, grid_spec=pltpu.PrefetchScalarGridSpec(n...]
    reduce_scatter x1 -> x0, waiting for transfers between devices: 3.52 us -> none  [body(): grad_part = lax.psum_scatter(term, 'cx', scatter_dimension=0, tiled=True)[0]]
    ppermute x4, starting transfers between devices: 7.8 us -> 10.8 us  [moved_by(): return lax.ppermute(value, axis, pairs)]
    another operation x3, other arithmetic: 0.2 us -> 3.07 us  [column_pieces(): return (jnp.stack(lines[:2]), jnp.stack(lines[2:]))]
  transfers between devices with their start and end apart: 35 -> 33, of which waited for: 19 -> 14; matrix products, arithmetic and copies ran while one was open for 2% -> 4% of each run, Pallas kernels for 35% -> 41%
where the time goes in v6:
time: 196 us; the launch traced here: 193 us
  Pallas kernels  78.4 us (40%)
  waiting for transfers between devices  45.8 us (23%)
  starting transfers between devices  42.1 us (21%)
  between operations  14.6 us (7%)
  local copies, waits for them, and re-layouts  7.16 us (4%)
  other arithmetic  5 us (3%)
    ppermute x19, waiting for transfers between devices, turned_by(): lax.ppermute(value, axis, [(i, (i + step) % size) for i in range(size)])  40.5 us
    ppermute x19, starting transfers between devices, turned_by(): lax.ppermute(value, axis, [(i, (i + step) % size) for i in range(size)])  29.2 us
    pallas_call x1, Pallas kernels, body(): pl.pallas_call(cotangent_kernel, grid_spec=pltpu.PrefetchScalarGridSpec(n...  14.4 us
    pallas_call x1, Pallas kernels, body(): pl.pallas_call(attended_kernel, grid_spec=pltpu.PrefetchScalarGridSpec(nu...  13.8 us
    pallas_call x1, Pallas kernels, body(): pl.pallas_call(weight_kernel, grid_spec=pltpu.PrefetchScalarGridSpec(num_...  10.9 us
    ppermute x4, starting transfers between devices, moved_by(): return lax.ppermute(value, axis, pairs)  10.8 us
    pallas_call x1, Pallas kernels, body(): pl.pallas_call(key_value_kernel, grid=(blocks,), in_specs=[rows_of(width,...  7.5 us
    pallas_call x1, Pallas kernels, body(): pl.pallas_call(forward_kernel, grid=(blocks,), in_specs=[rows_of(width)]...  6.9 us
  transfers between devices with their start and end apart: 33, of which 14 were waited for; matrix products, arithmetic and copies ran while one was open for 4% of the time, Pallas kernels for 41%

profile of v6, /device:TPU:2, one launch (start us, length us, event | category | flops | bytes accessed | tf_op | source)
XLA Modules:
  0.0 193.0 jit_solution(4964088587514447432)
XLA Ops:
  8.1 1.0 dynamic_slice.9
  10.1 1.0 broadcast_in_dim.8.dcol.refs_14_
  11.8 2.8 %tail.1.refs_0_ = bf16[528,128]{1,0:T(8,128)(2,1)} custom-call(bf16[1024,512]{1,0:T(8,128)(2,1)} %k.7, bf16[1024,512]{1,0:T(8,128)(2,1)} %v.7, f32[1024,128]{1,0:T(8,128)} %broadcast_in_dim.8.dcol.refs_14_, f32[16,128]{1,0:T(8,128)} %broadcast_in_dim.21.table.refs_15_), custom_call_target="tpu_custom_call" | custom-call | tf_op jit(solution)/shard_map/tail/pallas_call | solution.py:338
  14.7 6.8 %collective-permute-start = (bf16[528,128]{1,0:T(8,128)(2,1)}, bf16[528,128]{1,0:T(8,128)(2,1)S(1)}, u32[]{:S(2)}, u32[]{:S(2)}) collective-permute-start(bf16[528,128]{1,0:T(8,128)(2,1)} %tail.1.refs_0_), channel_id=1, source_target_pairs={{0,8},{8,16},{16,24},{24,0},{1,9},{9,17},{17,25},{25,1},{2,10},{10... | collective-permute-start | bytes 405512 | tf_op jit(solution)/shard_map/ppermute | solution.py:273
  21.5 1.5 collective-permute-start.1
  23.0 2.6 %collective-permute-start.2 = (bf16[528,128]{1,0:T(8,128)(2,1)}, bf16[528,128]{1,0:T(8,128)(2,1)S(1)}, u32[]{:S(2)}, u32[]{:S(2)}) collective-permute-start(bf16[528,128]{1,0:T(8,128)(2,1)} %tail.1.refs_0_), channel_id=1, source_target_pairs={{0,24},{8,0},{16,8},{24,16},{1,25},{9,1},{17,9},{25,17},{2,26},{10... | collective-permute-start | bytes 405512 | tf_op jit(solution)/shard_map/ppermute | solution.py:273
  25.8 4.2 %collective-permute-done.1.refs_2_.refs_1_ = bf16[528,128]{1,0:T(8,128)(2,1)S(1)} collective-permute-done((bf16[528,128]{1,0:T(8,128)(2,1)}, bf16[528,128]{1,0:T(8,128)(2,1)S(1)}, u32[]{:S(2)}, u32[]{:S(2)}) %collective-permute-start.1) | collective-permute-done | bytes 135200 | tf_op jit(solution)/shard_map/ppermute | solution.py:273
  30.2 1.4 collective-permute-done.7
  31.6 0.8 fusion
  32.4 1.5 collective-permute-start.8
  34.4 2.1 %collective-permute-start.9 = (bf16[2,128,768]{2,1,0:T(8,128)(2,1)}, bf16[2,128,768]{2,1,0:T(8,128)(2,1)}, u32[]{:S(2)}, u32[]{:S(2)}) collective-permute-start(bf16[2,128,768]{2,1,0:T(8,128)(2,1)} %get-tuple-element.110), channel_id=1, source_target_pairs={{0,64},{32,96},{64,0},{96,32},{1,65},{33,97},{65,1},{97,33},{2,66}... | collective-permute-start | bytes 1179656 | tf_op jit(solution)/shard_map/ppermute | solution.py:273
  36.6 1.9 row_state.2
  38.4 3.1 %collective-permute-start.5 = (bf16[528,128]{1,0:T(8,128)(2,1)}, bf16[528,128]{1,0:T(8,128)(2,1)S(1)}, u32[]{:S(2)}, u32[]{:S(2)}) collective-permute-start(bf16[528,128]{1,0:T(8,128)(2,1)} %row_state.2), channel_id=1, source_target_pairs={{0,32},{32,64},{64,96},{1,33},{33,65},{65,97},{2,34},{34,66},{66,9... | collective-permute-start | bytes 405512 | tf_op jit(solution)/shard_map/ppermute | solution.py:279
  41.5 1.5 collective-permute-start.6
  43.0 8.6 %collective-permute-done.8 = bf16[2,128,768]{2,1,0:T(8,128)(2,1)S(1)} collective-permute-done((bf16[2,128,768]{2,1,0:T(8,128)(2,1)}, bf16[2,128,768]{2,1,0:T(8,128)(2,1)S(1)}, u32[]{:S(2)}, u32[]{:S(2)}) %collective-permute-start.8) | collective-permute-done | bytes 393248 | tf_op jit(solution)/shard_map/ppermute | solution.py:273
  51.6 0.7 copy-done.16
  52.3 1.1 pad_maximum_fusion.refs_10_
  53.4 0.7 collective-permute-done.9
  54.1 1.2 pad_maximum_fusion.1.refs_11_
  55.9 0.7 copy-done.21
  56.6 2.6 %collective-permute-start.11 = (bf16[2,2,128,768]{3,2,1,0:T(8,128)(2,1)S(1)}, bf16[2,2,128,768]{3,2,1,0:T(8,128)(2,1)S(1)}, u32[]{:S(2)}, u32[]{:S(2)}) collective-permute-start(bf16[2,2,128,768]{3,2,1,0:T(8,128)(2,1)S(1)} %pad_maximum_fusion.refs_10_), channel_id=1, source_target_pairs={{0,24},{8,0},{16,8},{24,16},{1,25},{9,1},{17,9},{25,17},{2,26},{10... | collective-permute-start | bytes 2359304 | tf_op jit(solution)/shard_map/ppermute | solution.py:273
  59.3 3.2 %collective-permute-start.13 = (bf16[2,2,128,768]{3,2,1,0:T(8,128)(2,1)S(1)}, bf16[2,2,128,768]{3,2,1,0:T(8,128)(2,1)}, u32[]{:S(2)}, u32[]{:S(2)}) collective-permute-start(bf16[2,2,128,768]{3,2,1,0:T(8,128)(2,1)S(1)} %pad_maximum_fusion.1.refs_11_), channel_id=1, source_target_pairs={{0,24},{8,0},{16,8},{24,16},{1,25},{9,1},{17,9},{25,17},{2,26},{10... | collective-permute-start | bytes 2359304 | tf_op jit(solution)/shard_map/ppermute | solution.py:273
  63.2 6.4 %near_cotangent.1.near = f32[1024,512]{1,0:T(8,128)} custom-call(s32[8]{0:T(128)} %stack.109.places, bf16[1024,768]{1,0:T(8,128)(2,1)} %own.3, bf16[1024,768]{1,0:T(8,128)(2,1)} %copy-done, bf16[512,6144]{1,0:T(8,128)(2,1)} %refs_11_.1, bf16[512,6144]{1,0:T(8,128)(2,1)} %refs_11_.1), custom_call_target="tpu_custom_call" | custom-call | tf_op jit(solution)/shard_map/near_cotangent/pallas_call | solution.py:383
  69.6 6.9 %forward.1 = (f32[1024,512]{1,0:T(8,128)}, bf16[1024,512]{1,0:T(8,128)(2,1)}, bf16[512,1024]{1,0:T(8,128)(2,1)}, bf16[4,512,128]{2,1,0:T(8,128)(2,1)}) custom-call(bf16[1024,512]{1,0:T(8,128)(2,1)} %q.3, bf16[1024,512]{1,0:T(8,128)(2,1)} %k.7, bf16[1024,512]{1,0:T(8,128)(2,1)} %v.7, f32[1024,128]{1,0:T(8,128)} %broadcast_in_dim.8.dcol.refs_14_, ...), custom_call_target="tpu_custom_call" | custom-call | tf_op jit(solution)/shard_map/forward/pallas_call | solution.py:348
  76.5 5.9 %near_weight.1.started = bf16[16,512,384]{2,1,0:T(8,128)(2,1)} custom-call(s32[8]{0:T(128)} %stack.109.places, bf16[512,1024]{1,0:T(8,128)(2,1)} %get-tuple-element.65.turned, bf16[1024,768]{1,0:T(8,128)(2,1)} %own.3, bf16[1024,768]{1,0:T(8,128)(2,1)} %copy-done), custom_call_target="tpu_custom_call" | custom-call | tf_op jit(solution)/shard_map/near_weight/pallas_call | solution.py:401
  82.4 10.9 %weight_grad.1 = bf16[16,512,384]{2,1,0:T(8,128)(2,1)} custom-call(s32[8]{0:T(128)} %stack.109.places, bf16[512,1024]{1,0:T(8,128)(2,1)} %get-tuple-element.65.turned, bf16[8,1024,768]{2,1,0:T(8,128)(2,1)} %bitcast.35, bf16[16,512,384]{2,1,0:T(8,128)(2,1)} %near_weight.1.started), custom_call_target="tpu_custom_call", output_to_operand_aliasing={{}: (3, {})} | custom-call | tf_op jit(solution)/shard_map/weight_grad/pallas_call | solution.py:414
  93.3 2.0 %collective-permute-done.14.refs_16_ = bf16[2,2,128,768]{3,2,1,0:T(8,128)(2,1)} collective-permute-done((bf16[2,2,128,768]{3,2,1,0:T(8,128)(2,1)S(1)}, bf16[2,2,128,768]{3,2,1,0:T(8,128)(2,1)}, u32[]{:S(2)}, u32[]{:S(2)}) %collective-permute-start.14) | collective-permute-done | bytes 786464 | tf_op jit(solution)/shard_map/ppermute | solution.py:273
  95.3 1.2 copy-done.5
  96.5 0.9 collective-permute-start.17
  97.5 1.1 collective-permute-start.18
  98.5 1.7 collective-permute-start.15
  100.6 14.4 %cotangent.1 = (f32[1024,512]{1,0:T(8,128)}, bf16[528,128]{1,0:T(8,128)(2,1)}) custom-call(s32[8]{0:T(128)} %stack.109.places, f32[1024,512]{1,0:T(8,128)} %near_cotangent.1.near, bf16[8,1024,768]{2,1,0:T(8,128)(2,1)} %bitcast.36, bf16[8,1024,768]{2,1,0:T(8,128)(2,1)} %bitcast.37, bf16[8,1024,768]{2,1,0:T(8,128)(2,1)} %bitcast.38, ...), custom_call_target="tpu_custom_call" | custom-call | tf_op jit(solution)/shard_map/cotangent/pallas_call | solution.py:439
  115.0 8.8 %collective-permute-done.15.refs_14_ = bf16[2,2,128,768]{3,2,1,0:T(8,128)(2,1)S(1)} collective-permute-done((bf16[2,2,128,768]{3,2,1,0:T(8,128)(2,1)}, bf16[2,2,128,768]{3,2,1,0:T(8,128)(2,1)S(1)}, u32[]{:S(2)}, u32[]{:S(2)}) %collective-permute-start.15) | collective-permute-done | bytes 786464 | tf_op jit(solution)/shard_map/ppermute | solution.py:273
  123.8 6.9 %collective-permute-done.16.refs_15_ = bf16[2,2,128,768]{3,2,1,0:T(8,128)(2,1)S(1)} collective-permute-done((bf16[2,2,128,768]{3,2,1,0:T(8,128)(2,1)}, bf16[2,2,128,768]{3,2,1,0:T(8,128)(2,1)S(1)}, u32[]{:S(2)}, u32[]{:S(2)}) %collective-permute-start.16) | collective-permute-done | bytes 786464 | tf_op jit(solution)/shard_map/ppermute | solution.py:273
  130.8 1.4 collective-permute-start.22
  132.2 0.8 collective-permute-start.23
  133.0 2.0 %collective-permute-start.21 = (bf16[528,128]{1,0:T(8,128)(2,1)S(1)}, bf16[528,128]{1,0:T(8,128)(2,1)S(1)}, u32[]{:S(2)}, u32[]{:S(2)}) collective-permute-start(bf16[528,128]{1,0:T(8,128)(2,1)S(1)} %copy-done.22), channel_id=1, source_target_pairs={{0,8},{8,16},{16,24},{24,0},{1,9},{9,17},{17,25},{25,1},{2,10},{10... | collective-permute-start | bytes 405512 | tf_op jit(solution)/shard_map/ppermute | solution.py:273
  135.0 5.1 %collective-permute-done.19.refs_1_.refs_0_ = bf16[528,128]{1,0:T(8,128)(2,1)S(1)} collective-permute-done((bf16[528,128]{1,0:T(8,128)(2,1)S(1)}, bf16[528,128]{1,0:T(8,128)(2,1)S(1)}, u32[]{:S(2)}, u32[]{:S(2)}) %collective-permute-start.19) | collective-permute-done | bytes 135200 | tf_op jit(solution)/shard_map/ppermute | solution.py:273
  140.8 3.3 %collective-permute-done.21.refs_3_.refs_2_ = bf16[528,128]{1,0:T(8,128)(2,1)S(1)} collective-permute-done((bf16[528,128]{1,0:T(8,128)(2,1)S(1)}, bf16[528,128]{1,0:T(8,128)(2,1)S(1)}, u32[]{:S(2)}, u32[]{:S(2)}) %collective-permute-start.21) | collective-permute-done | bytes 135200 | tf_op jit(solution)/shard_map/ppermute | solution.py:273
  145.3 1.9 row_state.3
  147.3 1.4 collective-permute-done.29.refs_8_
  148.7 5.0 %collective-permute-start.24 = (bf16[528,128]{1,0:T(8,128)(2,1)}, bf16[528,128]{1,0:T(8,128)(2,1)S(1)}, u32[]{:S(2)}, u32[]{:S(2)}) collective-permute-start(bf16[528,128]{1,0:T(8,128)(2,1)} %row_state.3), channel_id=1, source_target_pairs={{32,0},{64,32},{96,64},{33,1},{65,33},{97,65},{34,2},{66,34},{98,6... | collective-permute-start | bytes 405512 | tf_op jit(solution)/shard_map/ppermute | solution.py:279
  153.7 1.3 collective-permute-start.25
  155.8 13.8 %attended.1 = bf16[1024,768]{1,0:T(8,128)(2,1)} custom-call(s32[20]{0:T(128)} %stack.131.places, bf16[1024,512]{1,0:T(8,128)(2,1)} %get-tuple-element.84.refs_0_, bf16[1024,512]{1,0:T(8,128)(2,1)} %collective-permute-done.26.refs_1_, bf16[1024,512]{1,0:T(8,128)(2,1)} %copy-done.3, bf16[1024,512]{1,0:T(8,128)(2,1)} %collective-permute-done.27.refs_3_, ...), custom_call_target="tpu_custom_call" | custom-call | tf_op jit(solution)/shard_map/attended/pallas_call | solution.py:471
  169.6 6.1 %grad_query.1 = bf16[1024,512]{1,0:T(8,128)(2,1)} custom-call(f32[1024,512]{1,0:T(8,128)} %get-tuple-element.95.go, bf16[1024,512]{1,0:T(8,128)(2,1)} %k.7, bf16[1024,512]{1,0:T(8,128)(2,1)} %v.7, f32[1024,128]{1,0:T(8,128)} %broadcast_in_dim.8.dcol.refs_14_, f32[1,1024]{1,0:T(1,128)} %bitcast.45, f32[16,128]{1,0:T(8,128)} %broadcast_in_dim.21.table.refs_15_, ...), custom_call_target="tpu_custom_call" | custom-call | tf_op jit(solution)/shard_map/grad_query/pallas_call | solution.py:490
  175.7 7.5 %grad_key_value.1 = (bf16[1024,512]{1,0:T(8,128)(2,1)}, bf16[1024,512]{1,0:T(8,128)(2,1)}) custom-call(f32[1024,512]{1,0:T(8,128)} %get-tuple-element.95.go, bf16[1024,512]{1,0:T(8,128)(2,1)} %q.3, bf16[1024,512]{1,0:T(8,128)(2,1)} %k.7, bf16[1024,512]{1,0:T(8,128)(2,1)} %v.7, f32[1024,128]{1,0:T(8,128)} %broadcast_in_dim.8.dcol.refs_14_, ...), custom_call_target="tpu_custom_call" | custom-call | tf_op jit(solution)/shard_map/grad_key_value/pallas_call | solution.py:503
  183.2 1.1 reduce-scatter.4.cloned.1.call-done
  184.2 1.9 bitcast_convert_fusion
  (96 shorter events, 7.6 us)
Async XLA Ops:
  7.2 75.2 %all-gather.3.cloned.1.call-start = ((), (), s32[]{:S(2)}) async-start(), calls=%async_computation.1 | async-start | bytes 14155776 | tf_op jit(solution)/shard_map/all_gather | solution.py:327
  7.9 176.3 %reduce-scatter.4.cloned.1.call-start = ((), (), s32[]{:S(2)}) async-start(), calls=%async_computation.2 | async-start | bytes 6684672
  8.0 22.1 %collective-permute-start.4 = (bf16[1024,768]{1,0:T(8,128)(2,1)}, bf16[1024,768]{1,0:T(8,128)(2,1)S(1)}, u32[]{:S(2)}, u32[]{:S(2)}) collective-permute-start(bf16[1024,768]{1,0:T(8,128)(2,1)} %own.3), channel_id=1, source_target_pairs={{0,1},{1,0},{2,3},{3,2},{4,5},{5,4},{6,7},{7,6},{8,9},{9,8},{10,11... | collective-permute-start | bytes 4718600 | tf_op jit(solution)/shard_map/ppermute | solution.py:283
  9.1 20.9 %collective-permute-start.3 = (bf16[128,1536]{1,0:T(8,128)(2,1)S(1)}, bf16[128,1536]{1,0:T(8,128)(2,1)S(1)}, u32[]{:S(2)}, u32[]{:S(2)}) collective-permute-start(bf16[128,1536]{1,0:T(8,128)(2,1)S(1)} %dynamic_slice.9), channel_id=1, source_target_pairs={{0,0},{2,2},{4,4},{6,6},{10,8},{12,10},{14,12},{8,14},{20,16},{22,... | collective-permute-start | bytes 1179656 | tf_op jit(solution)/shard_map/ppermute | solution.py:306
  9.8 22.6 %copy-start.17 = (f32[1024]{0:T(1024)}, f32[1024]{0:T(1024)S(1)}, u32[]{:S(2)}) copy-start(f32[1024]{0:T(1024)S(1)} %convert_element_type.12) | copy-start | bytes 12292
  14.7 11.1 %collective-permute-start = (bf16[528,128]{1,0:T(8,128)(2,1)}, bf16[528,128]{1,0:T(8,128)(2,1)S(1)}, u32[]{:S(2)}, u32[]{:S(2)}) collective-permute-start(bf16[528,128]{1,0:T(8,128)(2,1)} %tail.1.refs_0_), channel_id=1, source_target_pairs={{0,8},{8,16},{16,24},{24,0},{1,9},{9,17},{17,25},{25,1},{2,10},{10... | collective-permute-start | bytes 405512 | tf_op jit(solution)/shard_map/ppermute | solution.py:273
  21.5 8.5 %collective-permute-start.1 = (bf16[528,128]{1,0:T(8,128)(2,1)}, bf16[528,128]{1,0:T(8,128)(2,1)S(1)}, u32[]{:S(2)}, u32[]{:S(2)}) collective-permute-start(bf16[528,128]{1,0:T(8,128)(2,1)} %tail.1.refs_0_), channel_id=1, source_target_pairs={{0,16},{8,24},{16,0},{24,8},{1,17},{9,25},{17,1},{25,9},{2,18},{10... | collective-permute-start | bytes 405512 | tf_op jit(solution)/shard_map/ppermute | solution.py:273
  23.0 7.0 %collective-permute-start.2 = (bf16[528,128]{1,0:T(8,128)(2,1)}, bf16[528,128]{1,0:T(8,128)(2,1)S(1)}, u32[]{:S(2)}, u32[]{:S(2)}) collective-permute-start(bf16[528,128]{1,0:T(8,128)(2,1)} %tail.1.refs_0_), channel_id=1, source_target_pairs={{0,24},{8,0},{16,8},{24,16},{1,25},{9,1},{17,9},{25,17},{2,26},{10... | collective-permute-start | bytes 405512 | tf_op jit(solution)/shard_map/ppermute | solution.py:273
  25.8 10.8 %copy-start.13 = (bf16[528,128]{1,0:T(8,128)(2,1)}, bf16[528,128]{1,0:T(8,128)(2,1)S(1)}, u32[]{:S(2)}) copy-start(bf16[528,128]{1,0:T(8,128)(2,1)S(1)} %collective-permute-done.refs_1_.refs_0_) | copy-start | bytes 405508
  30.0 6.6 %copy-start.14 = (bf16[528,128]{1,0:T(8,128)(2,1)}, bf16[528,128]{1,0:T(8,128)(2,1)S(1)}, u32[]{:S(2)}) copy-start(bf16[528,128]{1,0:T(8,128)(2,1)S(1)} %collective-permute-done.1.refs_2_.refs_1_) | copy-start | bytes 405508
  30.0 6.6 %copy-start.15 = (bf16[528,128]{1,0:T(8,128)(2,1)}, bf16[528,128]{1,0:T(8,128)(2,1)S(1)}, u32[]{:S(2)}) copy-start(bf16[528,128]{1,0:T(8,128)(2,1)S(1)} %collective-permute-done.2.refs_3_.refs_2_) | copy-start | bytes 405508
  30.0 23.4 %copy-start = (bf16[1024,768]{1,0:T(8,128)(2,1)}, bf16[1024,768]{1,0:T(8,128)(2,1)S(1)}, u32[]{:S(2)}) copy-start(bf16[1024,768]{1,0:T(8,128)(2,1)S(1)} %collective-permute-done.4.beside) | copy-start | bytes 4718596
  30.1 1.5 collective-permute-start.7
  32.4 19.2 %collective-permute-start.8 = (bf16[2,128,768]{2,1,0:T(8,128)(2,1)}, bf16[2,128,768]{2,1,0:T(8,128)(2,1)S(1)}, u32[]{:S(2)}, u32[]{:S(2)}) collective-permute-start(bf16[2,128,768]{2,1,0:T(8,128)(2,1)} %get-tuple-element.110), channel_id=1, source_target_pairs={{0,32},{32,64},{64,96},{96,0},{1,33},{33,65},{65,97},{97,1},{2,34}... | collective-permute-start | bytes 1179656 | tf_op jit(solution)/shard_map/ppermute | solution.py:273
  33.9 19.5 %collective-permute-start.10 = (bf16[2,128,768]{2,1,0:T(8,128)(2,1)}, bf16[2,128,768]{2,1,0:T(8,128)(2,1)}, u32[]{:S(2)}, u32[]{:S(2)}) collective-permute-start(bf16[2,128,768]{2,1,0:T(8,128)(2,1)} %get-tuple-element.110), channel_id=1, source_target_pairs={{0,96},{32,0},{64,32},{96,64},{1,97},{33,1},{65,33},{97,65},{2,98}... | collective-permute-start | bytes 1179656 | tf_op jit(solution)/shard_map/ppermute | solution.py:273
  34.4 19.7 %collective-permute-start.9 = (bf16[2,128,768]{2,1,0:T(8,128)(2,1)}, bf16[2,128,768]{2,1,0:T(8,128)(2,1)}, u32[]{:S(2)}, u32[]{:S(2)}) collective-permute-start(bf16[2,128,768]{2,1,0:T(8,128)(2,1)} %get-tuple-element.110), channel_id=1, source_target_pairs={{0,64},{32,96},{64,0},{96,32},{1,65},{33,97},{65,1},{97,33},{2,66}... | collective-permute-start | bytes 1179656 | tf_op jit(solution)/shard_map/ppermute | solution.py:273
  38.4 17.5 %collective-permute-start.5 = (bf16[528,128]{1,0:T(8,128)(2,1)}, bf16[528,128]{1,0:T(8,128)(2,1)S(1)}, u32[]{:S(2)}, u32[]{:S(2)}) collective-permute-start(bf16[528,128]{1,0:T(8,128)(2,1)} %row_state.2), channel_id=1, source_target_pairs={{0,32},{32,64},{64,96},{1,33},{33,65},{65,97},{2,34},{34,66},{66,9... | collective-permute-start | bytes 405512 | tf_op jit(solution)/shard_map/ppermute | solution.py:279
  41.5 14.4 %collective-permute-start.6 = (bf16[528,128]{1,0:T(8,128)(2,1)}, bf16[528,128]{1,0:T(8,128)(2,1)S(1)}, u32[]{:S(2)}, u32[]{:S(2)}) collective-permute-start(bf16[528,128]{1,0:T(8,128)(2,1)} %row_state.2), channel_id=1, source_target_pairs={{0,64},{32,96},{1,65},{33,97},{2,66},{34,98},{3,67},{35,99},{4,68}... | collective-permute-start | bytes 405512 | tf_op jit(solution)/shard_map/ppermute | solution.py:279
  53.4 16.1 %copy-start.1 = (bf16[2,2,128,768]{3,2,1,0:T(8,128)(2,1)}, bf16[2,2,128,768]{3,2,1,0:T(8,128)(2,1)S(1)}, u32[]{:S(2)}) copy-start(bf16[2,2,128,768]{3,2,1,0:T(8,128)(2,1)S(1)} %pad_maximum_fusion.refs_10_) | copy-start | bytes 2359300
  55.3 14.2 %copy-start.2 = (bf16[2,2,128,768]{3,2,1,0:T(8,128)(2,1)}, bf16[2,2,128,768]{3,2,1,0:T(8,128)(2,1)S(1)}, u32[]{:S(2)}) copy-start(bf16[2,2,128,768]{3,2,1,0:T(8,128)(2,1)S(1)} %pad_maximum_fusion.1.refs_11_) | copy-start | bytes 2359300
  55.9 13.6 %copy-start.20 = (bf16[528,128]{1,0:T(8,128)(2,1)}, bf16[528,128]{1,0:T(8,128)(2,1)S(1)}, u32[]{:S(2)}) copy-start(bf16[528,128]{1,0:T(8,128)(2,1)S(1)} %collective-permute-done.5.refs_3_) | copy-start | bytes 405508
  56.6 36.6 %collective-permute-start.11 = (bf16[2,2,128,768]{3,2,1,0:T(8,128)(2,1)S(1)}, bf16[2,2,128,768]{3,2,1,0:T(8,128)(2,1)S(1)}, u32[]{:S(2)}, u32[]{:S(2)}) collective-permute-start(bf16[2,2,128,768]{3,2,1,0:T(8,128)(2,1)S(1)} %pad_maximum_fusion.refs_10_), channel_id=1, source_target_pairs={{0,24},{8,0},{16,8},{24,16},{1,25},{9,1},{17,9},{25,17},{2,26},{10... | collective-permute-start | bytes 2359304 | tf_op jit(solution)/shard_map/ppermute | solution.py:273
  59.3 34.0 %collective-permute-start.12 = (bf16[2,2,128,768]{3,2,1,0:T(8,128)(2,1)S(1)}, bf16[2,2,128,768]{3,2,1,0:T(8,128)(2,1)S(1)}, u32[]{:S(2)}, u32[]{:S(2)}) collective-permute-start(bf16[2,2,128,768]{3,2,1,0:T(8,128)(2,1)S(1)} %pad_maximum_fusion.1.refs_11_), channel_id=1, source_target_pairs={{0,8},{8,16},{16,24},{24,0},{1,9},{9,17},{17,25},{25,1},{2,10},{10... | collective-permute-start | bytes 2359304 | tf_op jit(solution)/shard_map/ppermute | solution.py:273
  59.3 34.0 %collective-permute-start.13 = (bf16[2,2,128,768]{3,2,1,0:T(8,128)(2,1)S(1)}, bf16[2,2,128,768]{3,2,1,0:T(8,128)(2,1)}, u32[]{:S(2)}, u32[]{:S(2)}) collective-permute-start(bf16[2,2,128,768]{3,2,1,0:T(8,128)(2,1)S(1)} %pad_maximum_fusion.1.refs_11_), channel_id=1, source_target_pairs={{0,24},{8,0},{16,8},{24,16},{1,25},{9,1},{17,9},{25,17},{2,26},{10... | collective-permute-start | bytes 2359304 | tf_op jit(solution)/shard_map/ppermute | solution.py:273
  62.5 32.8 %collective-permute-start.14 = (bf16[2,2,128,768]{3,2,1,0:T(8,128)(2,1)S(1)}, bf16[2,2,128,768]{3,2,1,0:T(8,128)(2,1)}, u32[]{:S(2)}, u32[]{:S(2)}) collective-permute-start(bf16[2,2,128,768]{3,2,1,0:T(8,128)(2,1)S(1)} %pad_maximum_fusion.refs_10_), channel_id=1, source_target_pairs={{0,8},{8,16},{16,24},{24,0},{1,9},{9,17},{17,25},{25,1},{2,10},{10... | collective-permute-start | bytes 2359304 | tf_op jit(solution)/shard_map/ppermute | solution.py:273
  96.5 34.2 %collective-permute-start.17 = (bf16[1024,512]{1,0:T(8,128)(2,1)S(1)}, bf16[1024,512]{1,0:T(8,128)(2,1)S(1)}, u32[]{:S(2)}, u32[]{:S(2)}) collective-permute-start(bf16[1024,512]{1,0:T(8,128)(2,1)S(1)} %copy-done.5), channel_id=1, source_target_pairs={{0,6},{2,0},{4,2},{6,4},{1,7},{3,1},{5,3},{7,5},{8,14},{10,8},{12,... | collective-permute-start | bytes 3145736 | tf_op jit(solution)/shard_map/ppermute | solution.py:273
  97.5 33.3 %collective-permute-start.18 = (bf16[1024,512]{1,0:T(8,128)(2,1)S(1)}, bf16[1024,512]{1,0:T(8,128)(2,1)S(1)}, u32[]{:S(2)}, u32[]{:S(2)}) collective-permute-start(bf16[1024,512]{1,0:T(8,128)(2,1)S(1)} %copy-done.5), channel_id=1, source_target_pairs={{0,2},{2,4},{4,6},{6,0},{1,3},{3,5},{5,7},{7,1},{8,10},{10,12},{12... | collective-permute-start | bytes 3145736 | tf_op jit(solution)/shard_map/ppermute | solution.py:273
  98.5 25.2 %collective-permute-start.15 = (bf16[2,2,128,768]{3,2,1,0:T(8,128)(2,1)}, bf16[2,2,128,768]{3,2,1,0:T(8,128)(2,1)S(1)}, u32[]{:S(2)}, u32[]{:S(2)}) collective-permute-start(bf16[2,2,128,768]{3,2,1,0:T(8,128)(2,1)} %copy-done.6), channel_id=1, source_target_pairs={{0,24},{8,0},{16,8},{24,16},{1,25},{9,1},{17,9},{25,17},{2,26},{10... | collective-permute-start | bytes 2359304 | tf_op jit(solution)/shard_map/ppermute | solution.py:273
  100.3 30.4 %collective-permute-start.16 = (bf16[2,2,128,768]{3,2,1,0:T(8,128)(2,1)}, bf16[2,2,128,768]{3,2,1,0:T(8,128)(2,1)S(1)}, u32[]{:S(2)}, u32[]{:S(2)}) collective-permute-start(bf16[2,2,128,768]{3,2,1,0:T(8,128)(2,1)} %copy-done.7), channel_id=1, source_target_pairs={{0,8},{8,16},{16,24},{24,0},{1,9},{9,17},{17,25},{25,1},{2,10},{10... | collective-permute-start | bytes 2359304 | tf_op jit(solution)/shard_map/ppermute | solution.py:273
  114.9 18.1 %copy-start.22 = (bf16[528,128]{1,0:T(8,128)(2,1)S(1)}, bf16[528,128]{1,0:T(8,128)(2,1)}, u32[]{:S(2)}) copy-start(bf16[528,128]{1,0:T(8,128)(2,1)} %get-tuple-element.77.refs_0_) | copy-start | bytes 405508
  123.8 20.4 %copy-start.8 = (bf16[2,2,128,768]{3,2,1,0:T(8,128)(2,1)}, bf16[2,2,128,768]{3,2,1,0:T(8,128)(2,1)S(1)}, u32[]{:S(2)}) copy-start(bf16[2,2,128,768]{3,2,1,0:T(8,128)(2,1)S(1)} %collective-permute-done.15.refs_14_) | copy-start | bytes 2359300
  130.7 14.0 %copy-start.9 = (bf16[2,2,128,768]{3,2,1,0:T(8,128)(2,1)}, bf16[2,2,128,768]{3,2,1,0:T(8,128)(2,1)S(1)}, u32[]{:S(2)}) copy-start(bf16[2,2,128,768]{3,2,1,0:T(8,128)(2,1)S(1)} %collective-permute-done.16.refs_15_) | copy-start | bytes 2359300
  130.7 25.0 %copy-start.3 = (bf16[1024,512]{1,0:T(8,128)(2,1)}, bf16[1024,512]{1,0:T(8,128)(2,1)S(1)}, u32[]{:S(2)}) copy-start(bf16[1024,512]{1,0:T(8,128)(2,1)S(1)} %collective-permute-done.17.refs_2_) | copy-start | bytes 3145732
  130.7 25.0 %copy-start.4 = (bf16[1024,512]{1,0:T(8,128)(2,1)}, bf16[1024,512]{1,0:T(8,128)(2,1)S(1)}, u32[]{:S(2)}) copy-start(bf16[1024,512]{1,0:T(8,128)(2,1)S(1)} %collective-permute-done.18.refs_4_) | copy-start | bytes 3145732
  130.8 13.3 %collective-permute-start.22 = (bf16[512,512]{1,0:T(8,128)(2,1)S(1)}, bf16[512,512]{1,0:T(8,128)(2,1)}, u32[]{:S(2)}, u32[]{:S(2)}) collective-permute-start(bf16[512,512]{1,0:T(8,128)(2,1)S(1)} %slice.14), channel_id=1, source_target_pairs={{0,6},{2,0},{4,2},{6,4},{1,7},{3,1},{5,3},{7,5},{8,14},{10,8},{12,... | collective-permute-start | bytes 1572872 | tf_op jit(solution)/shard_map/ppermute | solution.py:273
  132.2 11.9 %collective-permute-start.23 = (bf16[512,512]{1,0:T(8,128)(2,1)S(1)}, bf16[512,512]{1,0:T(8,128)(2,1)}, u32[]{:S(2)}, u32[]{:S(2)}) collective-permute-start(bf16[512,512]{1,0:T(8,128)(2,1)S(1)} %slice.15), channel_id=1, source_target_pairs={{0,2},{2,4},{4,6},{6,0},{1,3},{3,5},{5,7},{7,1},{8,10},{10,12},{12... | collective-permute-start | bytes 1572872 | tf_op jit(solution)/shard_map/ppermute | solution.py:273
  133.0 7.1 %collective-permute-start.19 = (bf16[528,128]{1,0:T(8,128)(2,1)S(1)}, bf16[528,128]{1,0:T(8,128)(2,1)S(1)}, u32[]{:S(2)}, u32[]{:S(2)}) collective-permute-start(bf16[528,128]{1,0:T(8,128)(2,1)S(1)} %copy-done.22), channel_id=1, source_target_pairs={{0,24},{8,0},{16,8},{24,16},{1,25},{9,1},{17,9},{25,17},{2,26},{10... | collective-permute-start | bytes 405512 | tf_op jit(solution)/shard_map/ppermute | solution.py:273
  133.0 7.8 %collective-permute-start.20 = (bf16[528,128]{1,0:T(8,128)(2,1)S(1)}, bf16[528,128]{1,0:T(8,128)(2,1)S(1)}, u32[]{:S(2)}, u32[]{:S(2)}) collective-permute-start(bf16[528,128]{1,0:T(8,128)(2,1)S(1)} %copy-done.22), channel_id=1, source_target_pairs={{0,16},{8,24},{16,0},{24,8},{1,17},{9,25},{17,1},{25,9},{2,18},{10... | collective-permute-start | bytes 405512 | tf_op jit(solution)/shard_map/ppermute | solution.py:273
  133.0 11.1 %collective-permute-start.21 = (bf16[528,128]{1,0:T(8,128)(2,1)S(1)}, bf16[528,128]{1,0:T(8,128)(2,1)S(1)}, u32[]{:S(2)}, u32[]{:S(2)}) collective-permute-start(bf16[528,128]{1,0:T(8,128)(2,1)S(1)} %copy-done.22), channel_id=1, source_target_pairs={{0,8},{8,16},{16,24},{24,0},{1,9},{9,17},{17,25},{25,1},{2,10},{10... | collective-permute-start | bytes 405512 | tf_op jit(solution)/shard_map/ppermute | solution.py:273
  144.1 11.6 %collective-permute-start.26 = (bf16[1024,512]{1,0:T(8,128)(2,1)S(1)}, bf16[1024,512]{1,0:T(8,128)(2,1)}, u32[]{:S(2)}, u32[]{:S(2)}) collective-permute-start(bf16[1024,512]{1,0:T(8,128)(2,1)S(1)} %copy-done.5), channel_id=1, source_target_pairs={{0,1},{1,0},{2,3},{3,2},{4,5},{5,4},{6,7},{7,6},{8,9},{9,8},{10,11... | collective-permute-start | bytes 3145736 | tf_op jit(solution)/shard_map/ppermute | solution.py:283
  144.2 11.5 %collective-permute-start.27 = (bf16[1024,512]{1,0:T(8,128)(2,1)S(1)}, bf16[1024,512]{1,0:T(8,128)(2,1)}, u32[]{:S(2)}, u32[]{:S(2)}) collective-permute-start(bf16[1024,512]{1,0:T(8,128)(2,1)S(1)} %collective-permute-done.17.refs_2_), channel_id=1, source_target_pairs={{0,1},{1,0},{2,3},{3,2},{4,5},{5,4},{6,7},{7,6},{8,9},{9,8},{10,11... | collective-permute-start | bytes 3145736 | tf_op jit(solution)/shard_map/ppermute | solution.py:283
  144.7 11.0 %collective-permute-start.28 = (bf16[1024,512]{1,0:T(8,128)(2,1)S(1)}, bf16[1024,512]{1,0:T(8,128)(2,1)}, u32[]{:S(2)}, u32[]{:S(2)}) collective-permute-start(bf16[1024,512]{1,0:T(8,128)(2,1)S(1)} %collective-permute-done.18.refs_4_), channel_id=1, source_target_pairs={{0,1},{1,0},{2,3},{3,2},{4,5},{5,4},{6,7},{7,6},{8,9},{9,8},{10,11... | collective-permute-start | bytes 3145736 | tf_op jit(solution)/shard_map/ppermute | solution.py:283
  144.8 3.9 %collective-permute-start.29 = (bf16[512,512]{1,0:T(8,128)(2,1)}, bf16[512,512]{1,0:T(8,128)(2,1)}, u32[]{:S(2)}, u32[]{:S(2)}) collective-permute-start(bf16[512,512]{1,0:T(8,128)(2,1)} %collective-permute-done.22.refs_6_), channel_id=1, source_target_pairs={{0,1},{1,0},{2,3},{3,2},{4,5},{5,4},{6,7},{7,6},{8,9},{9,8},{10,11... | collective-permute-start | bytes 1572872 | tf_op jit(solution)/shard_map/ppermute | solution.py:283
  145.2 8.4 %collective-permute-start.30 = (bf16[512,512]{1,0:T(8,128)(2,1)}, bf16[512,512]{1,0:T(8,128)(2,1)}, u32[]{:S(2)}, u32[]{:S(2)}) collective-permute-start(bf16[512,512]{1,0:T(8,128)(2,1)} %collective-permute-done.23.refs_7_), channel_id=1, source_target_pairs={{0,1},{1,0},{2,3},{3,2},{4,5},{5,4},{6,7},{7,6},{8,9},{9,8},{10,11... | collective-permute-start | bytes 1572872 | tf_op jit(solution)/shard_map/ppermute | solution.py:283
  148.7 20.9 %collective-permute-start.24 = (bf16[528,128]{1,0:T(8,128)(2,1)}, bf16[528,128]{1,0:T(8,128)(2,1)S(1)}, u32[]{:S(2)}, u32[]{:S(2)}) collective-permute-start(bf16[528,128]{1,0:T(8,128)(2,1)} %row_state.3), channel_id=1, source_target_pairs={{32,0},{64,32},{96,64},{33,1},{65,33},{97,65},{34,2},{66,34},{98,6... | collective-permute-start | bytes 405512 | tf_op jit(solution)/shard_map/ppermute | solution.py:279
  153.7 15.9 %collective-permute-start.25 = (bf16[528,128]{1,0:T(8,128)(2,1)}, bf16[528,128]{1,0:T(8,128)(2,1)S(1)}, u32[]{:S(2)}, u32[]{:S(2)}) collective-permute-start(bf16[528,128]{1,0:T(8,128)(2,1)} %row_state.3), channel_id=1, source_target_pairs={{64,0},{96,32},{65,1},{97,33},{66,2},{98,34},{67,3},{99,35},{68,4}... | collective-permute-start | bytes 405512 | tf_op jit(solution)/shard_map/ppermute | solution.py:279
  169.6 6.1 %copy-start.18 = (bf16[528,128]{1,0:T(8,128)(2,1)}, bf16[528,128]{1,0:T(8,128)(2,1)S(1)}, u32[]{:S(2)}) copy-start(bf16[528,128]{1,0:T(8,128)(2,1)S(1)} %collective-permute-done.24.refs_3_) | copy-start | bytes 405508
  169.6 6.1 %copy-start.19 = (bf16[528,128]{1,0:T(8,128)(2,1)}, bf16[528,128]{1,0:T(8,128)(2,1)S(1)}, u32[]{:S(2)}) copy-start(bf16[528,128]{1,0:T(8,128)(2,1)S(1)} %collective-permute-done.25.refs_4_) | copy-start | bytes 405508
  (9 other events, 20.3 us)
Sparse Core Ops, SparseCore 0:
  9.7 69.9 all-gather.2
  95.4 88.7 reduce-scatter.3

commit v7 on v4

--- a/solution.py
+++ b/solution.py
@@ -212,22 +212,11 @@
         carry[c, :] = jnp.where(keep, state, 0.0) + dot(kept, high, TN)
 
 
-def put_columns(part, out):
-    low = part.astype(BF16)
+def weight_kernel(turned, grad, out):
+    low = dot(turned[...], grad[0], NN).astype(BF16)
     half = low.shape[1] // 2
-    out[0, 0] = low[:, :half]
-    out[0, 1] = low[:, half:]
-
-
-def weight_kernel(turned, grad, out):
-    put_columns(dot(turned[...], grad[0], NN), out)
-
-
-def sum_kernel(place, own, *refs):
-    total = own[0].astype(F32)
-    for ref in refs[:-1]:
-        total = total + ref[...].astype(F32)
-    refs[-1][...] = total
+    out[0] = low[:, :half]
+    out[1] = low[:, half:]
 
 
 def attended_kernel(places, *refs):
@@ -308,25 +297,6 @@
     return jnp.stack(lines[:2]), jnp.stack(lines[2:])
 
 
-def row_sum(mine, cy):
-    got = [turned_by(pick(mine, (cy + s) % 4), "cy", s) for s in range(1, 4)]
-    height, part = mine.shape[1:]
-    block = (CHUNK, part)
-    return pl.pallas_call(
-        sum_kernel,
-        grid_spec=pltpu.PrefetchScalarGridSpec(
-            num_scalar_prefetch=1,
-            grid=(height // CHUNK,),
-            in_specs=[pl.BlockSpec((1, *block), lambda i, p: (p[0], i, 0))]
-            + [pl.BlockSpec(block, lambda i, p: (i, 0))] * 3,
-            out_specs=pl.BlockSpec(block, lambda i, p: (i, 0)),
-        ),
-        out_shape=jax.ShapeDtypeStruct((height, part), F32),
-        compiler_params=params(),
-        name="last_sum",
-    )(cy[None], mine, *got)
-
-
 def body(queries, keys, values, doc_ids, out_weight, grad_out):
     rows, width = queries.shape
     blocks = rows // CHUNK
@@ -352,6 +322,7 @@
     own = column_pieces(strip, share, core)
     arrived, own = lax.optimization_barrier((arrived, own))
     early = [turned_by(own[0], "cy", -1), turned_by(own[1], "cy", 1)]
+    later = [turned_by(own[1], "cy", -1), turned_by(own[0], "cy", 1)]
 
     row_block = pl.BlockSpec((1, CHUNK), lambda i: (0, i))
     state_block = pl.BlockSpec((1, size, HEAD), lambda i: (i, 0, 0))
@@ -378,19 +349,18 @@
         name="forward",
     )(queries, keys, values, dcol, drow, table, *arrived)
 
-    turned, early = lax.optimization_barrier((turned, early))
     term = pl.pallas_call(
         weight_kernel,
         grid=(groups,),
         in_specs=[whole((width, rows)), pl.BlockSpec((1, rows, share), lambda j: (j, 0, 0))],
-        out_specs=pl.BlockSpec((1, 2, width, share // 2), lambda j: (j // 2, j % 2, 0, 0)),
-        out_shape=jax.ShapeDtypeStruct((4, 4, width, share // 2), BF16),
+        out_specs=pl.BlockSpec((2, width, share // 2), lambda j: (j, 0, 0)),
+        out_shape=jax.ShapeDtypeStruct((2 * groups, width, share // 2), BF16),
         compiler_params=params(),
         name="weight_grad",
     )(turned, grad_whole)
-    term, low, own = lax.optimization_barrier((term, low, own))
-    later = [turned_by(own[1], "cy", -1), turned_by(own[0], "cy", 1)]
-    grad_part = lax.psum_scatter(term, "cx", scatter_dimension=0, tiled=True)[0]
+    term, low, early, later = lax.optimization_barrier((term, low, early, later))
+    across = [turned_by(early[0], "cy", -1), turned_by(early[1], "cy", 1)]
+    grad_part = lax.psum_scatter(term, CTX, scatter_dimension=0, tiled=True)
 
     half_rows = rows // 2
     above = turned_by(low, "z", -1)
@@ -413,16 +383,12 @@
         compiler_params=params(),
         name="cotangent",
     )(grad_whole, out_weight, opened, queries, dcol, table)
-    head, later, above, below = lax.optimization_barrier((head, later, above, below))
+    head, above, below = lax.optimization_barrier((head, above, below))
+    returned, (low, above, below) = exchanged(head, -1, (low, above, below))
     far_a = turned_by(above[:half_rows], "z", -1)
     far_b = turned_by(below[half_rows:], "z", 1)
-    moved = (far_a, far_b, low, above, below, early)
-    returned, (far_a, far_b, low, above, below, early) = exchanged(head, -1, moved)
-    across = [turned_by(early[0], "cy", -1), turned_by(early[1], "cy", 1)]
     near = [low, swapped(low), above, swapped(above), below, swapped(below)]
-    far = [far_a, far_b, swapped(far_a), swapped(far_b)]
-    columns = [*own, early[0], later[0], *across, later[1], early[1]]
-
+    grad_opened, across = lax.optimization_barrier((grad_opened, across))
     grad_query = pl.pallas_call(
         query_kernel,
         grid=(blocks,),
@@ -434,9 +400,10 @@
         name="grad_query",
     )(grad_opened, keys, values, dcol, drow, table, states)
 
-    ready = (returned, grad_query, near, far)
-    returned, grad_query, near, far = lax.optimization_barrier(ready)
-
+
+    ready = (returned, grad_query, far_a, far_b)
+    returned, grad_query, far_a, far_b = lax.optimization_barrier(ready)
+    far = [far_a, far_b, swapped(far_a), swapped(far_b)]
     back_row = pl.BlockSpec((1, CHUNK), lambda i: (0, blocks - 1 - i))
     grad_key, grad_value = pl.pallas_call(
         key_value_kernel,
@@ -451,8 +418,8 @@
         name="grad_key_value",
     )(grad_opened, queries, keys, values, dcol, drow, table, *returned)
 
-    ready = (grad_part, grad_key, columns)
-    grad_part, grad_key, columns = lax.optimization_barrier(ready)
+    near, grad_key = lax.optimization_barrier((near, grad_key))
+    columns = [*own, early[0], later[0], *across, later[1], early[1]]
     sides = (core, 1 - core)
     around = [2 * ((z + cy + s) % 4) + side for s in range(4) for side in sides]
     heads_at = [(cx - s) % 4 for s in range(4)]
@@ -477,7 +444,9 @@
         compiler_params=params(),
         name="attended",
     )(jnp.stack(around + heads_at + groups_at), *near, *far, *columns)
-    grad_weight = row_sum(grad_part, cy)
+    ready = (grad_part, attended)
+    grad_part, attended = lax.optimization_barrier(ready)
+    grad_weight = grad_part.reshape(width, share // 2).astype(F32)
     return attended, grad_query, grad_key, grad_value, grad_weight
 
 

time: 213 us -> 199 us (0.934)
  waiting for transfers between devices: 70.7 us -> 63.8 us
  starting transfers between devices: 44.9 us -> 41.6 us
  local copies, waits for them, and re-layouts: 8.6 us -> 5.61 us
  Pallas kernels: 70.8 us -> 68.5 us
    ppermute x22 -> x19, waiting for transfers between devices: 52.4 us -> 40.1 us  [turned_by(): lax.ppermute(value, axis, [(i, (i + step) % size) for i in range(size)])]
    all_gather x1, waiting for transfers between devices: 2.17 us -> 12.4 us  [body(): grad_whole = lax.all_gather(grad_out, TENSOR, axis=0)]
    ppermute x4, waiting for transfers between devices: 14 us -> 9.14 us  [moved_by(): return lax.ppermute(value, axis, pairs)]
    ppermute x22 -> x19, starting transfers between devices: 35.2 us -> 31.5 us  [turned_by(): lax.ppermute(value, axis, [(i, (i + step) % size) for i in range(size)])]
    pallas_call x1 -> x0, Pallas kernels: 2.3 us -> none  [row_sum(): pl.pallas_call(sum_kernel, grid_spec=pltpu.PrefetchScalarGridSpec(num_sca...]
  transfers between devices with their start and end apart: 35 -> 32, of which waited for: 22 -> 16; matrix products, arithmetic and copies ran while one was open for 3% -> 2% of each run, Pallas kernels for 26% -> 35%
where the time goes in v7:
time: 199 us; the launch traced here: 196 us
  Pallas kernels  68.5 us (34%)
  waiting for transfers between devices  63.8 us (32%)
  starting transfers between devices  41.6 us (21%)
  between operations  14.4 us (7%)
  local copies, waits for them, and re-layouts  5.61 us (3%)
  other arithmetic  2.13 us (1%)
    ppermute x19, waiting for transfers between devices, turned_by(): lax.ppermute(value, axis, [(i, (i + step) % size) for i in range(size)])  40.1 us
    ppermute x19, starting transfers between devices, turned_by(): lax.ppermute(value, axis, [(i, (i + step) % size) for i in range(size)])  31.5 us
    pallas_call x1, Pallas kernels, body(): pl.pallas_call(cotangent_kernel, grid=(blocks,), in_specs=[pl.BlockSpec((...  14.9 us
    pallas_call x1, Pallas kernels, body(): pl.pallas_call(attended_kernel, grid_spec=pltpu.PrefetchScalarGridSpec(nu...  13.8 us
    pallas_call x1, Pallas kernels, body(): pl.pallas_call(weight_kernel, grid=(groups,), in_specs=[whole((width, row...  13 us
    all_gather x1, waiting for transfers between devices, body(): grad_whole = lax.all_gather(grad_out, TENSOR, axis=0)  12.4 us
    ppermute x4, waiting for transfers between devices, moved_by(): return lax.ppermute(value, axis, pairs)  9.14 us
    ppermute x4, starting transfers between devices, moved_by(): return lax.ppermute(value, axis, pairs)  8.04 us
  transfers between devices with their start and end apart: 32, of which 16 were waited for; matrix products, arithmetic and copies ran while one was open for 2% of the time, Pallas kernels for 35%

profile of v7, /device:TPU:2, one launch (start us, length us, event | category | flops | bytes accessed | tf_op | source)
XLA Modules:
  0.0 196.0 jit_solution(16994005045675030883)
XLA Ops:
  7.2 0.7 all-gather.3.cloned.1.call-update
  8.0 1.0 dynamic_slice.9
  9.0 0.7 collective-permute-start.3
  10.0 1.0 broadcast_in_dim.8.dcol
  11.0 0.7 broadcast_in_dim.21.table
  11.7 2.8 %tail.1.refs_0_ = bf16[528,128]{1,0:T(8,128)(2,1)} custom-call(bf16[1024,512]{1,0:T(8,128)(2,1)} %k.7, bf16[1024,512]{1,0:T(8,128)(2,1)} %v.7, f32[1024,128]{1,0:T(8,128)} %broadcast_in_dim.8.dcol, f32[16,128]{1,0:T(8,128)} %broadcast_in_dim.21.table), custom_call_target="tpu_custom_call" | custom-call | tf_op jit(solution)/shard_map/tail/pallas_call | solution.py:320
  14.5 6.8 %collective-permute-start = (bf16[528,128]{1,0:T(8,128)(2,1)}, bf16[528,128]{1,0:T(8,128)(2,1)S(1)}, u32[]{:S(2)}, u32[]{:S(2)}) collective-permute-start(bf16[528,128]{1,0:T(8,128)(2,1)} %tail.1.refs_0_), channel_id=1, source_target_pairs={{0,8},{8,16},{16,24},{24,0},{1,9},{9,17},{17,25},{25,1},{2,10},{10... | collective-permute-start | bytes 405512 | tf_op jit(solution)/shard_map/ppermute | solution.py:256
  21.4 1.5 collective-permute-start.1
  22.8 2.6 %collective-permute-start.2 = (bf16[528,128]{1,0:T(8,128)(2,1)}, bf16[528,128]{1,0:T(8,128)(2,1)S(1)}, u32[]{:S(2)}, u32[]{:S(2)}) collective-permute-start(bf16[528,128]{1,0:T(8,128)(2,1)} %tail.1.refs_0_), channel_id=1, source_target_pairs={{0,24},{8,0},{16,8},{24,16},{1,25},{9,1},{17,9},{25,17},{2,26},{10... | collective-permute-start | bytes 405512 | tf_op jit(solution)/shard_map/ppermute | solution.py:256
  25.7 3.6 %collective-permute-done.1.refs_2_.refs_1_ = bf16[528,128]{1,0:T(8,128)(2,1)S(1)} collective-permute-done((bf16[528,128]{1,0:T(8,128)(2,1)}, bf16[528,128]{1,0:T(8,128)(2,1)S(1)}, u32[]{:S(2)}, u32[]{:S(2)}) %collective-permute-start.1) | collective-permute-done | bytes 135200 | tf_op jit(solution)/shard_map/ppermute | solution.py:256
  29.4 1.4 collective-permute-done.6
  30.9 1.6 collective-permute-start.7
  33.0 2.1 %collective-permute-start.8 = (bf16[2,128,768]{2,1,0:T(8,128)(2,1)S(1)}, bf16[2,128,768]{2,1,0:T(8,128)(2,1)S(1)}, u32[]{:S(2)}, u32[]{:S(2)}) collective-permute-start(bf16[2,128,768]{2,1,0:T(8,128)(2,1)S(1)} %get-tuple-element.116), channel_id=1, source_target_pairs={{0,64},{32,96},{64,0},{96,32},{1,65},{33,97},{65,1},{97,33},{2,66}... | collective-permute-start | bytes 1179656 | tf_op jit(solution)/shard_map/ppermute | solution.py:256
  35.1 1.9 row_state.2
  37.0 3.0 %collective-permute-start.4 = (bf16[528,128]{1,0:T(8,128)(2,1)}, bf16[528,128]{1,0:T(8,128)(2,1)S(1)}, u32[]{:S(2)}, u32[]{:S(2)}) collective-permute-start(bf16[528,128]{1,0:T(8,128)(2,1)} %row_state.2), channel_id=1, source_target_pairs={{0,32},{32,64},{64,96},{1,33},{33,65},{65,97},{2,34},{34,66},{66,9... | collective-permute-start | bytes 405512 | tf_op jit(solution)/shard_map/ppermute | solution.py:262
  40.0 1.6 collective-permute-start.5
  41.6 8.2 %collective-permute-done.7 = bf16[2,128,768]{2,1,0:T(8,128)(2,1)S(1)} collective-permute-done((bf16[2,128,768]{2,1,0:T(8,128)(2,1)S(1)}, bf16[2,128,768]{2,1,0:T(8,128)(2,1)S(1)}, u32[]{:S(2)}, u32[]{:S(2)}) %collective-permute-start.7) | collective-permute-done | bytes 393248 | tf_op jit(solution)/shard_map/ppermute | solution.py:256
  49.9 2.5 %collective-permute-done.8 = bf16[2,128,768]{2,1,0:T(8,128)(2,1)S(1)} collective-permute-done((bf16[2,128,768]{2,1,0:T(8,128)(2,1)S(1)}, bf16[2,128,768]{2,1,0:T(8,128)(2,1)S(1)}, u32[]{:S(2)}, u32[]{:S(2)}) %collective-permute-start.8) | collective-permute-done | bytes 393248 | tf_op jit(solution)/shard_map/ppermute | solution.py:256
  52.5 1.8 collective-permute-done.4.refs_3_
  54.3 2.9 %collective-permute-start.10 = (bf16[2,2,128,768]{3,2,1,0:T(8,128)(2,1)S(1)}, bf16[2,2,128,768]{3,2,1,0:T(8,128)(2,1)S(1)}, u32[]{:S(2)}, u32[]{:S(2)}) collective-permute-start(bf16[2,2,128,768]{3,2,1,0:T(8,128)(2,1)S(1)} %pad_maximum_fusion.refs_10_), channel_id=1, source_target_pairs={{0,24},{8,0},{16,8},{24,16},{1,25},{9,1},{17,9},{25,17},{2,26},{10... | collective-permute-start | bytes 2359304 | tf_op jit(solution)/shard_map/ppermute | solution.py:256
  57.2 3.2 %collective-permute-start.12 = (bf16[2,2,128,768]{3,2,1,0:T(8,128)(2,1)S(1)}, bf16[2,2,128,768]{3,2,1,0:T(8,128)(2,1)}, u32[]{:S(2)}, u32[]{:S(2)}) collective-permute-start(bf16[2,2,128,768]{3,2,1,0:T(8,128)(2,1)S(1)} %pad_maximum_fusion.1.refs_11_), channel_id=1, source_target_pairs={{0,24},{8,0},{16,8},{24,16},{1,25},{9,1},{17,9},{25,17},{2,26},{10... | collective-permute-start | bytes 2359304 | tf_op jit(solution)/shard_map/ppermute | solution.py:256
  60.4 6.8 %forward.1 = (f32[1024,512]{1,0:T(8,128)}, bf16[1024,512]{1,0:T(8,128)(2,1)}, bf16[512,1024]{1,0:T(8,128)(2,1)}, bf16[4,512,128]{2,1,0:T(8,128)(2,1)}) custom-call(bf16[1024,512]{1,0:T(8,128)(2,1)} %q.5, bf16[1024,512]{1,0:T(8,128)(2,1)} %k.7, bf16[1024,512]{1,0:T(8,128)(2,1)} %v.7, f32[1024,128]{1,0:T(8,128)} %broadcast_in_dim.8.dcol, f32[1,1024]{1,0:T(1,128)} %bitcast.41, ...), custom_call_target="tpu_custom_call" | custom-call | tf_op jit(solution)/shard_map/forward/pallas_call | solution.py:329
  67.2 12.4 %all-gather.3.cloned.1.call-done = bf16[8192,768]{1,0:T(8,128)(2,1)} async-done(((bf16[1024,768]{1,0:T(8,128)(2,1)}), bf16[8192,768]{1,0:T(8,128)(2,1)}) %all-gather.3.cloned.1.call-update) | async-done | bytes 12582928 | tf_op jit(solution)/shard_map/all_gather | solution.py:310
  79.7 13.0 %weight_grad.1 = bf16[16,512,384]{2,1,0:T(8,128)(2,1)} custom-call(bf16[512,1024]{1,0:T(8,128)(2,1)} %get-tuple-element.68.turned, bf16[8,1024,768]{2,1,0:T(8,128)(2,1)} %bitcast.35), custom_call_target="tpu_custom_call" | custom-call | tf_op jit(solution)/shard_map/weight_grad/pallas_call | solution.py:352
  93.5 0.8 copy-done.4
  94.3 0.8 collective-permute-start.14
  95.1 1.3 collective-permute-start.15
  96.4 2.6 %collective-permute-start.22 = (bf16[2,2,128,768]{3,2,1,0:T(8,128)(2,1)}, bf16[2,2,128,768]{3,2,1,0:T(8,128)(2,1)}, u32[]{:S(2)}, u32[]{:S(2)}) collective-permute-start(bf16[2,2,128,768]{3,2,1,0:T(8,128)(2,1)} %copy-done.5), channel_id=1, source_target_pairs={{0,24},{8,0},{16,8},{24,16},{1,25},{9,1},{17,9},{25,17},{2,26},{10... | collective-permute-start | bytes 2359304 | tf_op jit(solution)/shard_map/ppermute | solution.py:256
  98.9 14.9 %cotangent.1 = (f32[1024,512]{1,0:T(8,128)}, bf16[528,128]{1,0:T(8,128)(2,1)}) custom-call(bf16[8,1024,768]{2,1,0:T(8,128)(2,1)} %bitcast.36, bf16[512,6144]{1,0:T(8,128)(2,1)} %weight.1, f32[1024,512]{1,0:T(8,128)} %get-tuple-element.73.opened, bf16[1024,512]{1,0:T(8,128)(2,1)} %q.5, f32[1024,128]{1,0:T(8,128)} %broadcast_in_dim.8.dcol, ...), custom_call_target="tpu_custom_call" | custom-call | tf_op jit(solution)/shard_map/cotangent/pallas_call | solution.py:369
  113.9 5.6 %collective-permute-done.14.refs_2_ = bf16[1024,512]{1,0:T(8,128)(2,1)S(1)} collective-permute-done((bf16[1024,512]{1,0:T(8,128)(2,1)S(1)}, bf16[1024,512]{1,0:T(8,128)(2,1)S(1)}, u32[]{:S(2)}, u32[]{:S(2)}) %collective-permute-start.14) | collective-permute-done | bytes 1048608 | tf_op jit(solution)/shard_map/ppermute | solution.py:256
  119.5 1.9 collective-permute-done.15.refs_4_
  121.4 2.7 %collective-permute-start.16 = (bf16[528,128]{1,0:T(8,128)(2,1)}, bf16[528,128]{1,0:T(8,128)(2,1)S(1)}, u32[]{:S(2)}, u32[]{:S(2)}) collective-permute-start(bf16[528,128]{1,0:T(8,128)(2,1)} %get-tuple-element.76.refs_0_), channel_id=1, source_target_pairs={{0,24},{8,0},{16,8},{24,16},{1,25},{9,1},{17,9},{25,17},{2,26},{10... | collective-permute-start | bytes 405512 | tf_op jit(solution)/shard_map/ppermute | solution.py:256
  124.1 0.8 collective-permute-start.17
  124.9 0.9 collective-permute-start.18
  125.8 10.3 %collective-permute-done.16.refs_1_.refs_0_ = bf16[528,128]{1,0:T(8,128)(2,1)S(1)} collective-permute-done((bf16[528,128]{1,0:T(8,128)(2,1)}, bf16[528,128]{1,0:T(8,128)(2,1)S(1)}, u32[]{:S(2)}, u32[]{:S(2)}) %collective-permute-start.16) | collective-permute-done | bytes 135200 | tf_op jit(solution)/shard_map/ppermute | solution.py:256
  136.1 0.9 collective-permute-done.17.refs_2_.refs_1_
  137.0 4.3 %collective-permute-done.18.refs_3_.refs_2_ = bf16[528,128]{1,0:T(8,128)(2,1)S(1)} collective-permute-done((bf16[528,128]{1,0:T(8,128)(2,1)}, bf16[528,128]{1,0:T(8,128)(2,1)S(1)}, u32[]{:S(2)}, u32[]{:S(2)}) %collective-permute-start.18) | collective-permute-done | bytes 135200 | tf_op jit(solution)/shard_map/ppermute | solution.py:256
  141.9 1.9 row_state.3
  143.8 2.2 %collective-permute-start.24 = (bf16[528,128]{1,0:T(8,128)(2,1)}, bf16[528,128]{1,0:T(8,128)(2,1)S(1)}, u32[]{:S(2)}, u32[]{:S(2)}) collective-permute-start(bf16[528,128]{1,0:T(8,128)(2,1)} %row_state.3), channel_id=1, source_target_pairs={{32,0},{64,32},{96,64},{33,1},{65,33},{97,65},{34,2},{66,34},{98,6... | collective-permute-start | bytes 405512 | tf_op jit(solution)/shard_map/ppermute | solution.py:262
  146.0 1.3 collective-permute-start.25
  148.0 1.2 collective-permute-start.26
  149.3 5.0 %collective-permute-done.24.refs_3_ = bf16[528,128]{1,0:T(8,128)(2,1)S(1)} collective-permute-done((bf16[528,128]{1,0:T(8,128)(2,1)}, bf16[528,128]{1,0:T(8,128)(2,1)S(1)}, u32[]{:S(2)}, u32[]{:S(2)}) %collective-permute-start.24) | collective-permute-done | bytes 135200 | tf_op jit(solution)/shard_map/ppermute | solution.py:262
  154.3 2.3 %collective-permute-done.25.refs_4_ = bf16[528,128]{1,0:T(8,128)(2,1)S(1)} collective-permute-done((bf16[528,128]{1,0:T(8,128)(2,1)}, bf16[528,128]{1,0:T(8,128)(2,1)S(1)}, u32[]{:S(2)}, u32[]{:S(2)}) %collective-permute-start.25) | collective-permute-done | bytes 135200 | tf_op jit(solution)/shard_map/ppermute | solution.py:262
  156.6 6.0 %grad_query.1 = bf16[1024,512]{1,0:T(8,128)(2,1)} custom-call(f32[1024,512]{1,0:T(8,128)} %get-tuple-element.85.go, bf16[1024,512]{1,0:T(8,128)(2,1)} %k.7, bf16[1024,512]{1,0:T(8,128)(2,1)} %v.7, f32[1024,128]{1,0:T(8,128)} %broadcast_in_dim.8.dcol, f32[1,1024]{1,0:T(1,128)} %bitcast.42, f32[16,128]{1,0:T(8,128)} %broadcast_in_dim.21.table, ...), custom_call_target="tpu_custom_call" | custom-call | tf_op jit(solution)/shard_map/grad_query/pallas_call | solution.py:392
  162.6 2.2 %collective-permute-done.27.refs_7_ = bf16[512,512]{1,0:T(8,128)(2,1)} collective-permute-done((bf16[512,512]{1,0:T(8,128)(2,1)S(1)}, bf16[512,512]{1,0:T(8,128)(2,1)}, u32[]{:S(2)}, u32[]{:S(2)}) %collective-permute-start.27) | collective-permute-done | bytes 524320 | tf_op jit(solution)/shard_map/ppermute | solution.py:256
  165.9 7.4 %grad_key_value.1 = (bf16[1024,512]{1,0:T(8,128)(2,1)}, bf16[1024,512]{1,0:T(8,128)(2,1)}) custom-call(f32[1024,512]{1,0:T(8,128)} %get-tuple-element.85.go, bf16[1024,512]{1,0:T(8,128)(2,1)} %q.5, bf16[1024,512]{1,0:T(8,128)(2,1)} %k.7, bf16[1024,512]{1,0:T(8,128)(2,1)} %v.7, f32[1024,128]{1,0:T(8,128)} %broadcast_in_dim.8.dcol, f32[1,1024]{1,0:T(1,128)} %bitcast.43, ...), custom_call_target="tpu_custom_call" | custom-call | tf_op jit(solution)/shard_map/grad_key_value/pallas_call | solution.py:408
  173.4 13.8 %attended.1 = bf16[1024,768]{1,0:T(8,128)(2,1)} custom-call(s32[20]{0:T(128)} %stack.119.places, bf16[1024,512]{1,0:T(8,128)(2,1)} %get-tuple-element.96.refs_0_, bf16[1024,512]{1,0:T(8,128)(2,1)} %collective-permute-done.19.refs_1_, bf16[1024,512]{1,0:T(8,128)(2,1)} %copy-done.2, bf16[1024,512]{1,0:T(8,128)(2,1)} %collective-permute-done.20.refs_3_, ...), custom_call_target="tpu_custom_call" | custom-call | tf_op jit(solution)/shard_map/attended/pallas_call | solution.py:431
  187.2 1.9 bitcast_convert_fusion
  (79 shorter events, 4.9 us)
Async XLA Ops:
  7.2 2.5 %copy-start.17 = (s32[1024]{0:T(1024)S(1)}, s32[1024]{0:T(1024)}, u32[]{:S(2)}) copy-start(s32[1024]{0:T(1024)} %param.9) | copy-start | bytes 12292
  7.2 72.5 %all-gather.3.cloned.1.call-start = ((), (), s32[]{:S(2)}) async-start(), calls=%async_computation.1 | async-start | bytes 14155776 | tf_op jit(solution)/shard_map/all_gather | solution.py:310
  7.9 179.3 %reduce-scatter.4.cloned.1.call-start = ((), (), s32[]{:S(2)}) async-start(), calls=%async_computation.2 | async-start | bytes 6684672
  9.0 20.2 %collective-permute-start.3 = (bf16[128,1536]{1,0:T(8,128)(2,1)S(1)}, bf16[128,1536]{1,0:T(8,128)(2,1)S(1)}, u32[]{:S(2)}, u32[]{:S(2)}) collective-permute-start(bf16[128,1536]{1,0:T(8,128)(2,1)S(1)} %dynamic_slice.9), channel_id=1, source_target_pairs={{0,0},{2,2},{4,4},{6,6},{10,8},{12,10},{14,12},{8,14},{20,16},{22,... | collective-permute-start | bytes 1179656 | tf_op jit(solution)/shard_map/ppermute | solution.py:289
  9.7 21.1 %copy-start.12 = (f32[1024]{0:T(1024)}, f32[1024]{0:T(1024)S(1)}, u32[]{:S(2)}) copy-start(f32[1024]{0:T(1024)S(1)} %convert_element_type.12) | copy-start | bytes 12292
  14.5 11.1 %collective-permute-start = (bf16[528,128]{1,0:T(8,128)(2,1)}, bf16[528,128]{1,0:T(8,128)(2,1)S(1)}, u32[]{:S(2)}, u32[]{:S(2)}) collective-permute-start(bf16[528,128]{1,0:T(8,128)(2,1)} %tail.1.refs_0_), channel_id=1, source_target_pairs={{0,8},{8,16},{16,24},{24,0},{1,9},{9,17},{17,25},{25,1},{2,10},{10... | collective-permute-start | bytes 405512 | tf_op jit(solution)/shard_map/ppermute | solution.py:256
  21.4 7.9 %collective-permute-start.1 = (bf16[528,128]{1,0:T(8,128)(2,1)}, bf16[528,128]{1,0:T(8,128)(2,1)S(1)}, u32[]{:S(2)}, u32[]{:S(2)}) collective-permute-start(bf16[528,128]{1,0:T(8,128)(2,1)} %tail.1.refs_0_), channel_id=1, source_target_pairs={{0,16},{8,24},{16,0},{24,8},{1,17},{9,25},{17,1},{25,9},{2,18},{10... | collective-permute-start | bytes 405512 | tf_op jit(solution)/shard_map/ppermute | solution.py:256
  22.8 6.4 %collective-permute-start.2 = (bf16[528,128]{1,0:T(8,128)(2,1)}, bf16[528,128]{1,0:T(8,128)(2,1)S(1)}, u32[]{:S(2)}, u32[]{:S(2)}) collective-permute-start(bf16[528,128]{1,0:T(8,128)(2,1)} %tail.1.refs_0_), channel_id=1, source_target_pairs={{0,24},{8,0},{16,8},{24,16},{1,25},{9,1},{17,9},{25,17},{2,26},{10... | collective-permute-start | bytes 405512 | tf_op jit(solution)/shard_map/ppermute | solution.py:256
  25.7 9.4 %copy-start.9 = (bf16[528,128]{1,0:T(8,128)(2,1)}, bf16[528,128]{1,0:T(8,128)(2,1)S(1)}, u32[]{:S(2)}) copy-start(bf16[528,128]{1,0:T(8,128)(2,1)S(1)} %collective-permute-done.refs_1_.refs_0_) | copy-start | bytes 405508
  29.2 5.9 %copy-start.10 = (bf16[528,128]{1,0:T(8,128)(2,1)}, bf16[528,128]{1,0:T(8,128)(2,1)S(1)}, u32[]{:S(2)}) copy-start(bf16[528,128]{1,0:T(8,128)(2,1)S(1)} %collective-permute-done.1.refs_2_.refs_1_) | copy-start | bytes 405508
  29.2 5.9 %copy-start.11 = (bf16[528,128]{1,0:T(8,128)(2,1)}, bf16[528,128]{1,0:T(8,128)(2,1)S(1)}, u32[]{:S(2)}) copy-start(bf16[528,128]{1,0:T(8,128)(2,1)S(1)} %collective-permute-done.2.refs_3_.refs_2_) | copy-start | bytes 405508
  29.3 1.5 collective-permute-start.6
  30.9 18.9 %collective-permute-start.7 = (bf16[2,128,768]{2,1,0:T(8,128)(2,1)S(1)}, bf16[2,128,768]{2,1,0:T(8,128)(2,1)S(1)}, u32[]{:S(2)}, u32[]{:S(2)}) collective-permute-start(bf16[2,128,768]{2,1,0:T(8,128)(2,1)S(1)} %get-tuple-element.116), channel_id=1, source_target_pairs={{0,32},{32,64},{64,96},{96,0},{1,33},{33,65},{65,97},{97,1},{2,34}... | collective-permute-start | bytes 1179656 | tf_op jit(solution)/shard_map/ppermute | solution.py:256
  32.4 17.5 %collective-permute-start.9 = (bf16[2,128,768]{2,1,0:T(8,128)(2,1)S(1)}, bf16[2,128,768]{2,1,0:T(8,128)(2,1)S(1)}, u32[]{:S(2)}, u32[]{:S(2)}) collective-permute-start(bf16[2,128,768]{2,1,0:T(8,128)(2,1)S(1)} %get-tuple-element.116), channel_id=1, source_target_pairs={{0,96},{32,0},{64,32},{96,64},{1,97},{33,1},{65,33},{97,65},{2,98}... | collective-permute-start | bytes 1179656 | tf_op jit(solution)/shard_map/ppermute | solution.py:256
  33.0 19.4 %collective-permute-start.8 = (bf16[2,128,768]{2,1,0:T(8,128)(2,1)S(1)}, bf16[2,128,768]{2,1,0:T(8,128)(2,1)S(1)}, u32[]{:S(2)}, u32[]{:S(2)}) collective-permute-start(bf16[2,128,768]{2,1,0:T(8,128)(2,1)S(1)} %get-tuple-element.116), channel_id=1, source_target_pairs={{0,64},{32,96},{64,0},{96,32},{1,65},{33,97},{65,1},{97,33},{2,66}... | collective-permute-start | bytes 1179656 | tf_op jit(solution)/shard_map/ppermute | solution.py:256
  37.0 17.3 %collective-permute-start.4 = (bf16[528,128]{1,0:T(8,128)(2,1)}, bf16[528,128]{1,0:T(8,128)(2,1)S(1)}, u32[]{:S(2)}, u32[]{:S(2)}) collective-permute-start(bf16[528,128]{1,0:T(8,128)(2,1)} %row_state.2), channel_id=1, source_target_pairs={{0,32},{32,64},{64,96},{1,33},{33,65},{65,97},{2,34},{34,66},{66,9... | collective-permute-start | bytes 405512 | tf_op jit(solution)/shard_map/ppermute | solution.py:262
  40.0 14.3 %collective-permute-start.5 = (bf16[528,128]{1,0:T(8,128)(2,1)}, bf16[528,128]{1,0:T(8,128)(2,1)S(1)}, u32[]{:S(2)}, u32[]{:S(2)}) collective-permute-start(bf16[528,128]{1,0:T(8,128)(2,1)} %row_state.2), channel_id=1, source_target_pairs={{0,64},{32,96},{1,65},{33,97},{2,66},{34,98},{3,67},{35,99},{4,68}... | collective-permute-start | bytes 405512 | tf_op jit(solution)/shard_map/ppermute | solution.py:262
  49.9 17.3 %copy-start = (bf16[2,2,128,768]{3,2,1,0:T(8,128)(2,1)}, bf16[2,2,128,768]{3,2,1,0:T(8,128)(2,1)S(1)}, u32[]{:S(2)}) copy-start(bf16[2,2,128,768]{3,2,1,0:T(8,128)(2,1)S(1)} %pad_maximum_fusion.refs_10_) | copy-start | bytes 2359300
  52.5 14.7 %copy-start.1 = (bf16[2,2,128,768]{3,2,1,0:T(8,128)(2,1)}, bf16[2,2,128,768]{3,2,1,0:T(8,128)(2,1)S(1)}, u32[]{:S(2)}) copy-start(bf16[2,2,128,768]{3,2,1,0:T(8,128)(2,1)S(1)} %pad_maximum_fusion.1.refs_11_) | copy-start | bytes 2359300
  54.3 6.1 %copy-start.15 = (bf16[528,128]{1,0:T(8,128)(2,1)}, bf16[528,128]{1,0:T(8,128)(2,1)S(1)}, u32[]{:S(2)}) copy-start(bf16[528,128]{1,0:T(8,128)(2,1)S(1)} %collective-permute-done.4.refs_3_) | copy-start | bytes 405508
  54.3 6.1 %copy-start.16 = (bf16[528,128]{1,0:T(8,128)(2,1)}, bf16[528,128]{1,0:T(8,128)(2,1)S(1)}, u32[]{:S(2)}) copy-start(bf16[528,128]{1,0:T(8,128)(2,1)S(1)} %collective-permute-done.5.refs_4_) | copy-start | bytes 405508
  54.3 38.4 %collective-permute-start.10 = (bf16[2,2,128,768]{3,2,1,0:T(8,128)(2,1)S(1)}, bf16[2,2,128,768]{3,2,1,0:T(8,128)(2,1)S(1)}, u32[]{:S(2)}, u32[]{:S(2)}) collective-permute-start(bf16[2,2,128,768]{3,2,1,0:T(8,128)(2,1)S(1)} %pad_maximum_fusion.refs_10_), channel_id=1, source_target_pairs={{0,24},{8,0},{16,8},{24,16},{1,25},{9,1},{17,9},{25,17},{2,26},{10... | collective-permute-start | bytes 2359304 | tf_op jit(solution)/shard_map/ppermute | solution.py:256
  57.2 35.5 %collective-permute-start.11 = (bf16[2,2,128,768]{3,2,1,0:T(8,128)(2,1)S(1)}, bf16[2,2,128,768]{3,2,1,0:T(8,128)(2,1)}, u32[]{:S(2)}, u32[]{:S(2)}) collective-permute-start(bf16[2,2,128,768]{3,2,1,0:T(8,128)(2,1)S(1)} %pad_maximum_fusion.1.refs_11_), channel_id=1, source_target_pairs={{0,8},{8,16},{16,24},{24,0},{1,9},{9,17},{17,25},{25,1},{2,10},{10... | collective-permute-start | bytes 2359304 | tf_op jit(solution)/shard_map/ppermute | solution.py:256
  57.2 35.5 %collective-permute-start.12 = (bf16[2,2,128,768]{3,2,1,0:T(8,128)(2,1)S(1)}, bf16[2,2,128,768]{3,2,1,0:T(8,128)(2,1)}, u32[]{:S(2)}, u32[]{:S(2)}) collective-permute-start(bf16[2,2,128,768]{3,2,1,0:T(8,128)(2,1)S(1)} %pad_maximum_fusion.1.refs_11_), channel_id=1, source_target_pairs={{0,24},{8,0},{16,8},{24,16},{1,25},{9,1},{17,9},{25,17},{2,26},{10... | collective-permute-start | bytes 2359304 | tf_op jit(solution)/shard_map/ppermute | solution.py:256
  60.4 32.7 %collective-permute-start.13 = (bf16[2,2,128,768]{3,2,1,0:T(8,128)(2,1)S(1)}, bf16[2,2,128,768]{3,2,1,0:T(8,128)(2,1)}, u32[]{:S(2)}, u32[]{:S(2)}) collective-permute-start(bf16[2,2,128,768]{3,2,1,0:T(8,128)(2,1)S(1)} %pad_maximum_fusion.refs_10_), channel_id=1, source_target_pairs={{0,8},{8,16},{16,24},{24,0},{1,9},{9,17},{17,25},{25,1},{2,10},{10... | collective-permute-start | bytes 2359304 | tf_op jit(solution)/shard_map/ppermute | solution.py:256
  93.1 1.2 copy-start.4
  94.3 25.2 %collective-permute-start.14 = (bf16[1024,512]{1,0:T(8,128)(2,1)S(1)}, bf16[1024,512]{1,0:T(8,128)(2,1)S(1)}, u32[]{:S(2)}, u32[]{:S(2)}) collective-permute-start(bf16[1024,512]{1,0:T(8,128)(2,1)S(1)} %copy-done.4), channel_id=1, source_target_pairs={{0,6},{2,0},{4,2},{6,4},{1,7},{3,1},{5,3},{7,5},{8,14},{10,8},{12,... | collective-permute-start | bytes 3145736 | tf_op jit(solution)/shard_map/ppermute | solution.py:256
  95.1 26.3 %collective-permute-start.15 = (bf16[1024,512]{1,0:T(8,128)(2,1)S(1)}, bf16[1024,512]{1,0:T(8,128)(2,1)S(1)}, u32[]{:S(2)}, u32[]{:S(2)}) collective-permute-start(bf16[1024,512]{1,0:T(8,128)(2,1)S(1)} %copy-done.4), channel_id=1, source_target_pairs={{0,2},{2,4},{4,6},{6,0},{1,3},{3,5},{5,7},{7,1},{8,10},{10,12},{12... | collective-permute-start | bytes 3145736 | tf_op jit(solution)/shard_map/ppermute | solution.py:256
  96.4 51.1 %collective-permute-start.22 = (bf16[2,2,128,768]{3,2,1,0:T(8,128)(2,1)}, bf16[2,2,128,768]{3,2,1,0:T(8,128)(2,1)}, u32[]{:S(2)}, u32[]{:S(2)}) collective-permute-start(bf16[2,2,128,768]{3,2,1,0:T(8,128)(2,1)} %copy-done.5), channel_id=1, source_target_pairs={{0,24},{8,0},{16,8},{24,16},{1,25},{9,1},{17,9},{25,17},{2,26},{10... | collective-permute-start | bytes 2359304 | tf_op jit(solution)/shard_map/ppermute | solution.py:256
  98.9 49.1 %collective-permute-start.23 = (bf16[2,2,128,768]{3,2,1,0:T(8,128)(2,1)}, bf16[2,2,128,768]{3,2,1,0:T(8,128)(2,1)}, u32[]{:S(2)}, u32[]{:S(2)}) collective-permute-start(bf16[2,2,128,768]{3,2,1,0:T(8,128)(2,1)} %collective-permute-done.11.refs_17_), channel_id=1, source_target_pairs={{0,8},{8,16},{16,24},{24,0},{1,9},{9,17},{17,25},{25,1},{2,10},{10... | collective-permute-start | bytes 2359304 | tf_op jit(solution)/shard_map/ppermute | solution.py:256
  119.5 43.0 %copy-start.2 = (bf16[1024,512]{1,0:T(8,128)(2,1)}, bf16[1024,512]{1,0:T(8,128)(2,1)S(1)}, u32[]{:S(2)}) copy-start(bf16[1024,512]{1,0:T(8,128)(2,1)S(1)} %collective-permute-done.14.refs_2_) | copy-start | bytes 3145732
  121.4 41.2 %copy-start.3 = (bf16[1024,512]{1,0:T(8,128)(2,1)}, bf16[1024,512]{1,0:T(8,128)(2,1)S(1)}, u32[]{:S(2)}) copy-start(bf16[1024,512]{1,0:T(8,128)(2,1)S(1)} %collective-permute-done.15.refs_4_) | copy-start | bytes 3145732
  121.4 14.7 %collective-permute-start.16 = (bf16[528,128]{1,0:T(8,128)(2,1)}, bf16[528,128]{1,0:T(8,128)(2,1)S(1)}, u32[]{:S(2)}, u32[]{:S(2)}) collective-permute-start(bf16[528,128]{1,0:T(8,128)(2,1)} %get-tuple-element.76.refs_0_), channel_id=1, source_target_pairs={{0,24},{8,0},{16,8},{24,16},{1,25},{9,1},{17,9},{25,17},{2,26},{10... | collective-permute-start | bytes 405512 | tf_op jit(solution)/shard_map/ppermute | solution.py:256
  124.1 12.8 %collective-permute-start.17 = (bf16[528,128]{1,0:T(8,128)(2,1)}, bf16[528,128]{1,0:T(8,128)(2,1)S(1)}, u32[]{:S(2)}, u32[]{:S(2)}) collective-permute-start(bf16[528,128]{1,0:T(8,128)(2,1)} %get-tuple-element.76.refs_0_), channel_id=1, source_target_pairs={{0,16},{8,24},{16,0},{24,8},{1,17},{9,25},{17,1},{25,9},{2,18},{10... | collective-permute-start | bytes 405512 | tf_op jit(solution)/shard_map/ppermute | solution.py:256
  124.9 16.4 %collective-permute-start.18 = (bf16[528,128]{1,0:T(8,128)(2,1)}, bf16[528,128]{1,0:T(8,128)(2,1)S(1)}, u32[]{:S(2)}, u32[]{:S(2)}) collective-permute-start(bf16[528,128]{1,0:T(8,128)(2,1)} %get-tuple-element.76.refs_0_), channel_id=1, source_target_pairs={{0,8},{8,16},{16,24},{24,0},{1,9},{9,17},{17,25},{25,1},{2,10},{10... | collective-permute-start | bytes 405512 | tf_op jit(solution)/shard_map/ppermute | solution.py:256
  136.1 5.2 %copy-start.6 = (bf16[528,128]{1,0:T(8,128)(2,1)}, bf16[528,128]{1,0:T(8,128)(2,1)S(1)}, u32[]{:S(2)}) copy-start(bf16[528,128]{1,0:T(8,128)(2,1)S(1)} %collective-permute-done.16.refs_1_.refs_0_) | copy-start | bytes 405508
  137.0 4.3 %copy-start.7 = (bf16[528,128]{1,0:T(8,128)(2,1)}, bf16[528,128]{1,0:T(8,128)(2,1)S(1)}, u32[]{:S(2)}) copy-start(bf16[528,128]{1,0:T(8,128)(2,1)S(1)} %collective-permute-done.17.refs_2_.refs_1_) | copy-start | bytes 405508
  143.8 10.5 %collective-permute-start.24 = (bf16[528,128]{1,0:T(8,128)(2,1)}, bf16[528,128]{1,0:T(8,128)(2,1)S(1)}, u32[]{:S(2)}, u32[]{:S(2)}) collective-permute-start(bf16[528,128]{1,0:T(8,128)(2,1)} %row_state.3), channel_id=1, source_target_pairs={{32,0},{64,32},{96,64},{33,1},{65,33},{97,65},{34,2},{66,34},{98,6... | collective-permute-start | bytes 405512 | tf_op jit(solution)/shard_map/ppermute | solution.py:262
  146.0 10.6 %collective-permute-start.25 = (bf16[528,128]{1,0:T(8,128)(2,1)}, bf16[528,128]{1,0:T(8,128)(2,1)S(1)}, u32[]{:S(2)}, u32[]{:S(2)}) collective-permute-start(bf16[528,128]{1,0:T(8,128)(2,1)} %row_state.3), channel_id=1, source_target_pairs={{64,0},{96,32},{65,1},{97,33},{66,2},{98,34},{67,3},{99,35},{68,4}... | collective-permute-start | bytes 405512 | tf_op jit(solution)/shard_map/ppermute | solution.py:262
  147.3 26.1 %collective-permute-start.20 = (bf16[1024,512]{1,0:T(8,128)(2,1)S(1)}, bf16[1024,512]{1,0:T(8,128)(2,1)}, u32[]{:S(2)}, u32[]{:S(2)}) collective-permute-start(bf16[1024,512]{1,0:T(8,128)(2,1)S(1)} %collective-permute-done.14.refs_2_), channel_id=1, source_target_pairs={{0,1},{1,0},{2,3},{3,2},{4,5},{5,4},{6,7},{7,6},{8,9},{9,8},{10,11... | collective-permute-start | bytes 3145736 | tf_op jit(solution)/shard_map/ppermute | solution.py:266
  147.5 25.9 %collective-permute-start.19 = (bf16[1024,512]{1,0:T(8,128)(2,1)S(1)}, bf16[1024,512]{1,0:T(8,128)(2,1)}, u32[]{:S(2)}, u32[]{:S(2)}) collective-permute-start(bf16[1024,512]{1,0:T(8,128)(2,1)S(1)} %copy-done.4), channel_id=1, source_target_pairs={{0,1},{1,0},{2,3},{3,2},{4,5},{5,4},{6,7},{7,6},{8,9},{9,8},{10,11... | collective-permute-start | bytes 3145736 | tf_op jit(solution)/shard_map/ppermute | solution.py:266
  148.0 14.5 %collective-permute-start.26 = (bf16[512,512]{1,0:T(8,128)(2,1)S(1)}, bf16[512,512]{1,0:T(8,128)(2,1)}, u32[]{:S(2)}, u32[]{:S(2)}) collective-permute-start(bf16[512,512]{1,0:T(8,128)(2,1)S(1)} %slice.14), channel_id=1, source_target_pairs={{0,6},{2,0},{4,2},{6,4},{1,7},{3,1},{5,3},{7,5},{8,14},{10,8},{12,... | collective-permute-start | bytes 1572872 | tf_op jit(solution)/shard_map/ppermute | solution.py:256
  154.3 8.3 %copy-start.13 = (bf16[528,128]{1,0:T(8,128)(2,1)}, bf16[528,128]{1,0:T(8,128)(2,1)S(1)}, u32[]{:S(2)}) copy-start(bf16[528,128]{1,0:T(8,128)(2,1)S(1)} %collective-permute-done.24.refs_3_) | copy-start | bytes 405508
  154.3 10.5 %collective-permute-start.27 = (bf16[512,512]{1,0:T(8,128)(2,1)S(1)}, bf16[512,512]{1,0:T(8,128)(2,1)}, u32[]{:S(2)}, u32[]{:S(2)}) collective-permute-start(bf16[512,512]{1,0:T(8,128)(2,1)S(1)} %slice.15), channel_id=1, source_target_pairs={{0,2},{2,4},{4,6},{6,0},{1,3},{3,5},{5,7},{7,1},{8,10},{10,12},{12... | collective-permute-start | bytes 1572872 | tf_op jit(solution)/shard_map/ppermute | solution.py:256
  156.6 6.0 %copy-start.14 = (bf16[528,128]{1,0:T(8,128)(2,1)}, bf16[528,128]{1,0:T(8,128)(2,1)S(1)}, u32[]{:S(2)}) copy-start(bf16[528,128]{1,0:T(8,128)(2,1)S(1)} %collective-permute-done.25.refs_4_) | copy-start | bytes 405508
  156.6 16.8 %collective-permute-start.21 = (bf16[1024,512]{1,0:T(8,128)(2,1)S(1)}, bf16[1024,512]{1,0:T(8,128)(2,1)}, u32[]{:S(2)}, u32[]{:S(2)}) collective-permute-start(bf16[1024,512]{1,0:T(8,128)(2,1)S(1)} %collective-permute-done.15.refs_4_), channel_id=1, source_target_pairs={{0,1},{1,0},{2,3},{3,2},{4,5},{5,4},{6,7},{7,6},{8,9},{9,8},{10,11... | collective-permute-start | bytes 3145736 | tf_op jit(solution)/shard_map/ppermute | solution.py:266
  164.8 8.6 %collective-permute-start.28 = (bf16[512,512]{1,0:T(8,128)(2,1)}, bf16[512,512]{1,0:T(8,128)(2,1)}, u32[]{:S(2)}, u32[]{:S(2)}) collective-permute-start(bf16[512,512]{1,0:T(8,128)(2,1)} %collective-permute-done.26.refs_6_), channel_id=1, source_target_pairs={{0,1},{1,0},{2,3},{3,2},{4,5},{5,4},{6,7},{7,6},{8,9},{9,8},{10,11... | collective-permute-start | bytes 1572872 | tf_op jit(solution)/shard_map/ppermute | solution.py:266
  164.8 8.6 %collective-permute-start.29 = (bf16[512,512]{1,0:T(8,128)(2,1)}, bf16[512,512]{1,0:T(8,128)(2,1)}, u32[]{:S(2)}, u32[]{:S(2)}) collective-permute-start(bf16[512,512]{1,0:T(8,128)(2,1)} %collective-permute-done.27.refs_7_), channel_id=1, source_target_pairs={{0,1},{1,0},{2,3},{3,2},{4,5},{5,4},{6,7},{7,6},{8,9},{9,8},{10,11... | collective-permute-start | bytes 1572872 | tf_op jit(solution)/shard_map/ppermute | solution.py:266
  (2 other events, 1.5 us)
Sparse Core Ops, SparseCore 0:
  9.7 69.9 all-gather.2
  93.7 88.8 reduce-scatter.3

commit v8 on v3

--- a/solution.py
+++ b/solution.py
@@ -212,15 +212,12 @@
         carry[c, :] = jnp.where(keep, state, 0.0) + dot(kept, high, TN)
 
 
-def put_columns(part, out):
-    low = part.astype(BF16)
-    half = low.shape[1] // 2
-    out[0, 0] = low[:, :half]
-    out[0, 1] = low[:, half:]
-
-
 def weight_kernel(turned, grad, out):
-    put_columns(dot(turned[...], grad[0], NN), out)
+    for p in range(2):
+        low = dot(turned[...], grad[p], NN).astype(BF16)
+        half = low.shape[1] // 2
+        out[0, 2 * p] = low[:, :half]
+        out[0, 2 * p + 1] = low[:, half:]
 
 
 def sum_kernel(place, own, *refs):
@@ -242,7 +239,8 @@
                     group = places[2 * y + o]
                     row = pl.multiple_of(places[8 + x] * HEAD, HEAD)
                     to = columns.at[group, pl.ds(row, HEAD)]
-                    piece = columns_of[2 * y + x // 2].at[x % 2, o]
+                    cut = (3, 3, 2, 1)[y]
+                    piece = columns_of[2 * y + (x >= cut)].at[x if x < cut else x - cut, o]
                     yield pltpu.make_async_copy(piece, to, sems.at[8 * y + 2 * x + o])
 
     @pl.when(i == 0)
@@ -305,7 +303,7 @@
     other = lax.dynamic_slice(strip, (0, (1 - core) * share), (HEAD, share))
     both = jnp.stack([mine, swapped(other)])
     lines = [both] + [turned_by(both, "cx", s) for s in range(1, 4)]
-    return jnp.stack(lines[:2]), jnp.stack(lines[2:])
+    return jnp.stack(lines[:3]), jnp.stack(lines[1:]), lines[0][None], lines[3][None]
 
 
 def row_sum(mine, cy):
@@ -348,11 +346,10 @@
     table = jnp.broadcast_to(table[:, None], (16, HEAD))
 
     tail = pl.pallas_call(tail_kernel, out_shape=payload, name="tail")(keys, values, dcol, table)
-    own = column_pieces(column_strip(out_weight, share, cx), share, core)
-    arrived, own = exchanged(tail, 1, own)
+    arrived, strip = exchanged(tail, 1, column_strip(out_weight, share, cx))
+    own = column_pieces(strip, share, core)
+    arrived, own = lax.optimization_barrier((arrived, own))
     early = [turned_by(own[0], "cy", -1), turned_by(own[1], "cy", 1)]
-    arrived, early = lax.optimization_barrier((arrived, early))
-    later = [turned_by(own[1], "cy", -1), turned_by(own[0], "cy", 1)]
 
     row_block = pl.BlockSpec((1, CHUNK), lambda i: (0, i))
     state_block = pl.BlockSpec((1, size, HEAD), lambda i: (i, 0, 0))
@@ -379,19 +376,18 @@
         name="forward",
     )(queries, keys, values, dcol, drow, table, *arrived)
 
-    turned, later = lax.optimization_barrier((turned, later))
-    across = [turned_by(early[0], "cy", -1), turned_by(early[1], "cy", 1)]
-
     term = pl.pallas_call(
         weight_kernel,
-        grid=(groups,),
-        in_specs=[whole((width, rows)), pl.BlockSpec((1, rows, share), lambda j: (j, 0, 0))],
-        out_specs=pl.BlockSpec((1, 2, width, share // 2), lambda j: (j // 2, j % 2, 0, 0)),
+        grid=(groups // 2,),
+        in_specs=[whole((width, rows)), pl.BlockSpec((2, rows, share), lambda j: (j, 0, 0))],
+        out_specs=pl.BlockSpec((1, 4, width, share // 2), lambda j: (j, 0, 0, 0)),
         out_shape=jax.ShapeDtypeStruct((4, 4, width, share // 2), BF16),
         compiler_params=params(),
         name="weight_grad",
     )(turned, grad_whole)
-    term, low = lax.optimization_barrier((term, low))
+    term, low, early, own = lax.optimization_barrier((term, low, early, own))
+    across = [turned_by(early[0][:2], "cy", -1), turned_by(early[1][1:], "cy", 1)]
+    later = turned_by(own[3], "cy", -1)
     grad_part = lax.psum_scatter(term, "cx", scatter_dimension=0, tiled=True)[0]
 
     half_rows = rows // 2
@@ -415,14 +411,16 @@
         compiler_params=params(),
         name="cotangent",
     )(grad_whole, out_weight, opened, queries, dcol, table)
-    head, across, above, below = lax.optimization_barrier((head, across, above, below))
+    ready = (head, across, later, above, below)
+    head, across, later, above, below = lax.optimization_barrier(ready)
     far_a = turned_by(above[:half_rows], "z", -1)
     far_b = turned_by(below[half_rows:], "z", 1)
-    returned, (far_a, far_b, low) = exchanged(head, -1, (far_a, far_b, low))
+    moved = (far_a, far_b, low, above, below, own)
+    returned, (far_a, far_b, low, above, below, own) = exchanged(head, -1, moved)
     near = [low, swapped(low), above, swapped(above), below, swapped(below)]
     far = [far_a, far_b, swapped(far_a), swapped(far_b)]
-    columns = [*own, early[0], later[0], *across, later[1], early[1]]
-
+    near, far, own = lax.optimization_barrier((near, far, own))
+    last = turned_by(own[2], "cy", 1)
     grad_query = pl.pallas_call(
         query_kernel,
         grid=(blocks,),
@@ -433,6 +431,10 @@
         compiler_params=params(),
         name="grad_query",
     )(grad_opened, keys, values, dcol, drow, table, states)
+
+
+    last, grad_query = lax.optimization_barrier((last, grad_query))
+    columns = [own[0], own[3], early[0], later, *across, last, early[1]]
 
     sides = (core, 1 - core)
     around = [2 * ((z + cy + s) % 4) + side for s in range(4) for side in sides]
@@ -458,7 +460,8 @@
         compiler_params=params(),
         name="attended",
     )(jnp.stack(around + heads_at + groups_at), *near, *far, *columns)
-    returned, attended = lax.optimization_barrier((returned, attended))
+    ready = (returned, grad_opened, grad_part, attended)
+    returned, grad_opened, grad_part, attended = lax.optimization_barrier(ready)
 
     back_row = pl.BlockSpec((1, CHUNK), lambda i: (0, blocks - 1 - i))
     grad_key, grad_value = pl.pallas_call(
@@ -474,7 +477,6 @@
         name="grad_key_value",
     )(grad_opened, queries, keys, values, dcol, drow, table, *returned)
 
-    grad_part, grad_key = lax.optimization_barrier((grad_part, grad_key))
     grad_weight = row_sum(grad_part, cy)
     return attended, grad_query, grad_key, grad_value, grad_weight
 

time: 205 us -> 211 us (1.029)
  waiting for transfers between devices: 49.9 us -> 60.2 us
  starting transfers between devices: 59 us -> 52.2 us
    all_gather x1, waiting for transfers between devices: 0.01 us -> 13.5 us  [body(): grad_whole = lax.all_gather(grad_out, TENSOR, axis=0)]
    ppermute x4, starting transfers between devices: 12.6 us -> 8.35 us  [moved_by(): return lax.ppermute(value, axis, pairs)]
    ppermute x4, waiting for transfers between devices: 5.71 us -> 1.63 us  [moved_by(): return lax.ppermute(value, axis, pairs)]
    ppermute x6, waiting for transfers between devices: 3.68 us -> 7.49 us  [swapped(): return lax.ppermute(value, 'core', [(0, 1), (1, 0)])]
    ppermute x22, waiting for transfers between devices: 39.8 us -> 36.8 us  [turned_by(): lax.ppermute(value, axis, [(i, (i + step) % size) for i in range(size)])]
    ppermute x22, starting transfers between devices: 44.5 us -> 42 us  [turned_by(): lax.ppermute(value, axis, [(i, (i + step) % size) for i in range(size)])]
    unnamed x48 -> x74, local copies, waits for them, and re-layouts: 2.7 us -> 4.24 us
  transfers between devices with their start and end apart: 35 -> 35, of which waited for: 18 -> 15; matrix products, arithmetic and copies ran while one was open for 2% -> 2% of each run, Pallas kernels for 28% -> 33%
where the time goes in v8:
time: 211 us; the launch traced here: 208 us
  Pallas kernels  70 us (33%)
  waiting for transfers between devices  60.2 us (29%)
  starting transfers between devices  52.2 us (25%)
  between operations  14.8 us (7%)
  local copies, waits for them, and re-layouts  9.44 us (4%)
    ppermute x22, starting transfers between devices, turned_by(): lax.ppermute(value, axis, [(i, (i + step) % size) for i in range(size)])  42 us
    ppermute x22, waiting for transfers between devices, turned_by(): lax.ppermute(value, axis, [(i, (i + step) % size) for i in range(size)])  36.8 us
    pallas_call x1, Pallas kernels, body(): pl.pallas_call(cotangent_kernel, grid=(blocks,), in_specs=[pl.BlockSpec((...  16 us
    pallas_call x1, Pallas kernels, body(): pl.pallas_call(attended_kernel, grid_spec=pltpu.PrefetchScalarGridSpec(nu...  13.7 us
    all_gather x1, waiting for transfers between devices, body(): grad_whole = lax.all_gather(grad_out, TENSOR, axis=0)  13.5 us
    pallas_call x1, Pallas kernels, body(): pl.pallas_call(weight_kernel, grid=(groups // 2,), in_specs=[whole((width...  11.4 us
    ppermute x4, starting transfers between devices, moved_by(): return lax.ppermute(value, axis, pairs)  8.35 us
    ppermute x6, waiting for transfers between devices, swapped(): return lax.ppermute(value, 'core', [(0, 1), (1, 0)])  7.49 us
  transfers between devices with their start and end apart: 35, of which 15 were waited for; matrix products, arithmetic and copies ran while one was open for 2% of the time, Pallas kernels for 33%

profile of v8, /device:TPU:2, one launch (start us, length us, event | category | flops | bytes accessed | tf_op | source)
XLA Modules:
  0.0 207.9 jit_solution(15102417830304121654)
XLA Ops:
  8.0 1.0 dynamic_slice.19
  10.0 1.0 broadcast_in_dim.10.dcol
  11.7 2.8 %tail.1.refs_0_ = bf16[528,128]{1,0:T(8,128)(2,1)} custom-call(bf16[1024,512]{1,0:T(8,128)(2,1)} %k.7, bf16[1024,512]{1,0:T(8,128)(2,1)} %v.7, f32[1024,128]{1,0:T(8,128)} %broadcast_in_dim.10.dcol, f32[16,128]{1,0:T(8,128)} %broadcast_in_dim.26.table), custom_call_target="tpu_custom_call" | custom-call | tf_op jit(solution)/shard_map/tail/pallas_call | solution.py:348
  14.6 6.8 %collective-permute-start = (bf16[528,128]{1,0:T(8,128)(2,1)}, bf16[528,128]{1,0:T(8,128)(2,1)S(1)}, u32[]{:S(2)}, u32[]{:S(2)}) collective-permute-start(bf16[528,128]{1,0:T(8,128)(2,1)} %tail.1.refs_0_), channel_id=1, source_target_pairs={{0,8},{8,16},{16,24},{24,0},{1,9},{9,17},{17,25},{25,1},{2,10},{10... | collective-permute-start | bytes 405512 | tf_op jit(solution)/shard_map/ppermute | solution.py:265
  21.4 1.5 collective-permute-start.1
  22.9 2.6 %collective-permute-start.2 = (bf16[528,128]{1,0:T(8,128)(2,1)}, bf16[528,128]{1,0:T(8,128)(2,1)S(1)}, u32[]{:S(2)}, u32[]{:S(2)}) collective-permute-start(bf16[528,128]{1,0:T(8,128)(2,1)} %tail.1.refs_0_), channel_id=1, source_target_pairs={{0,24},{8,0},{16,8},{24,16},{1,25},{9,1},{17,9},{25,17},{2,26},{10... | collective-permute-start | bytes 405512 | tf_op jit(solution)/shard_map/ppermute | solution.py:265
  25.7 3.6 %collective-permute-done.1.refs_2_.refs_1_ = bf16[528,128]{1,0:T(8,128)(2,1)S(1)} collective-permute-done((bf16[528,128]{1,0:T(8,128)(2,1)}, bf16[528,128]{1,0:T(8,128)(2,1)S(1)}, u32[]{:S(2)}, u32[]{:S(2)}) %collective-permute-start.1) | collective-permute-done | bytes 135200 | tf_op jit(solution)/shard_map/ppermute | solution.py:265
  29.4 1.4 collective-permute-done.6
  31.5 2.4 %collective-permute-start.8 = (bf16[2,128,768]{2,1,0:T(8,128)(2,1)S(1)}, bf16[2,128,768]{2,1,0:T(8,128)(2,1)S(1)}, u32[]{:S(2)}, u32[]{:S(2)}) collective-permute-start(bf16[2,128,768]{2,1,0:T(8,128)(2,1)S(1)} %get-tuple-element.149), channel_id=1, source_target_pairs={{0,64},{32,96},{64,0},{96,32},{1,65},{33,97},{65,1},{97,33},{2,66}... | collective-permute-start | bytes 1179656 | tf_op jit(solution)/shard_map/ppermute | solution.py:265
  33.9 1.8 collective-permute-start.7
  35.7 1.9 row_state.2
  37.6 1.9 collective-permute-start.4
  39.5 2.7 %collective-permute-start.5 = (bf16[528,128]{1,0:T(8,128)(2,1)}, bf16[528,128]{1,0:T(8,128)(2,1)S(1)}, u32[]{:S(2)}, u32[]{:S(2)}) collective-permute-start(bf16[528,128]{1,0:T(8,128)(2,1)} %row_state.2), channel_id=1, source_target_pairs={{0,64},{32,96},{1,65},{33,97},{2,66},{34,98},{3,67},{35,99},{4,68}... | collective-permute-start | bytes 405512 | tf_op jit(solution)/shard_map/ppermute | solution.py:271
  42.2 9.3 %collective-permute-done.8 = bf16[2,128,768]{2,1,0:T(8,128)(2,1)S(1)} collective-permute-done((bf16[2,128,768]{2,1,0:T(8,128)(2,1)S(1)}, bf16[2,128,768]{2,1,0:T(8,128)(2,1)S(1)}, u32[]{:S(2)}, u32[]{:S(2)}) %collective-permute-start.8) | collective-permute-done | bytes 393248 | tf_op jit(solution)/shard_map/ppermute | solution.py:265
  51.5 2.0 collective-permute-done.7
  53.5 1.3 pad_maximum_fusion.1
  54.8 1.6 collective-permute-done.4.refs_3_
  56.4 2.9 %collective-permute-start.10 = (bf16[3,2,128,768]{3,2,1,0:T(8,128)(2,1)S(1)}, bf16[3,2,128,768]{3,2,1,0:T(8,128)(2,1)S(1)}, u32[]{:S(2)}, u32[]{:S(2)}) collective-permute-start(bf16[3,2,128,768]{3,2,1,0:T(8,128)(2,1)S(1)} %get-tuple-element.122.refs_10_), channel_id=1, source_target_pairs={{0,24},{8,0},{16,8},{24,16},{1,25},{9,1},{17,9},{25,17},{2,26},{10... | collective-permute-start | bytes 3538952 | tf_op jit(solution)/shard_map/ppermute | solution.py:265
  59.3 6.8 %forward.1 = (f32[1024,512]{1,0:T(8,128)}, bf16[1024,512]{1,0:T(8,128)(2,1)}, bf16[512,1024]{1,0:T(8,128)(2,1)}, bf16[4,512,128]{2,1,0:T(8,128)(2,1)}) custom-call(bf16[1024,512]{1,0:T(8,128)(2,1)} %q.5, bf16[1024,512]{1,0:T(8,128)(2,1)} %k.7, bf16[1024,512]{1,0:T(8,128)(2,1)} %v.7, f32[1024,128]{1,0:T(8,128)} %broadcast_in_dim.10.dcol, f32[1,1024]{1,0:T(1,128)} %bitcast.49, ...), custom_call_target="tpu_custom_call" | custom-call | tf_op jit(solution)/shard_map/forward/pallas_call | solution.py:356
  66.1 13.5 %all-gather.3.cloned.1.call-done = bf16[8192,768]{1,0:T(8,128)(2,1)} async-done(((bf16[1024,768]{1,0:T(8,128)(2,1)}), bf16[8192,768]{1,0:T(8,128)(2,1)}) %all-gather.3.cloned.1.call-update) | async-done | bytes 12582928 | tf_op jit(solution)/shard_map/all_gather | solution.py:338
  79.7 11.4 %weight_grad.1 = bf16[4,4,512,384]{3,2,1,0:T(8,128)(2,1)} custom-call(bf16[512,1024]{1,0:T(8,128)(2,1)} %get-tuple-element.84.turned, bf16[8,1024,768]{2,1,0:T(8,128)(2,1)} %bitcast.39), custom_call_target="tpu_custom_call" | custom-call | tf_op jit(solution)/shard_map/weight_grad/pallas_call | solution.py:379
  91.1 1.0 collective-permute-start.15
  92.1 1.1 collective-permute-start.16
  93.2 2.8 %collective-permute-start.12 = (bf16[2,2,128,768]{3,2,1,0:T(8,128)(2,1)S(1)}, bf16[2,2,128,768]{3,2,1,0:T(8,128)(2,1)S(1)}, u32[]{:S(2)}, u32[]{:S(2)}) collective-permute-start(bf16[2,2,128,768]{3,2,1,0:T(8,128)(2,1)S(1)} %slice.20), channel_id=1, source_target_pairs={{0,24},{8,0},{16,8},{24,16},{1,25},{9,1},{17,9},{25,17},{2,26},{10... | collective-permute-start | bytes 2359304 | tf_op jit(solution)/shard_map/ppermute | solution.py:265
  96.2 3.2 %collective-permute-start.14 = (bf16[1,2,128,768]{3,2,1,0:T(8,128)(2,1)S(1)}, bf16[1,2,128,768]{3,2,1,0:T(8,128)(2,1)S(1)}, u32[]{:S(2)}, u32[]{:S(2)}) collective-permute-start(bf16[1,2,128,768]{3,2,1,0:T(8,128)(2,1)S(1)} %bitcast.45), channel_id=1, source_target_pairs={{0,24},{8,0},{16,8},{24,16},{1,25},{9,1},{17,9},{25,17},{2,26},{10... | collective-permute-start | bytes 1179656 | tf_op jit(solution)/shard_map/ppermute | solution.py:265
  99.4 16.0 %cotangent.1 = (f32[1024,512]{1,0:T(8,128)}, bf16[528,128]{1,0:T(8,128)(2,1)}) custom-call(bf16[8,1024,768]{2,1,0:T(8,128)(2,1)} %bitcast.40, bf16[512,6144]{1,0:T(8,128)(2,1)} %weight.1, f32[1024,512]{1,0:T(8,128)} %get-tuple-element.82.opened, bf16[1024,512]{1,0:T(8,128)(2,1)} %q.5, f32[1024,128]{1,0:T(8,128)} %broadcast_in_dim.10.dcol, ...), custom_call_target="tpu_custom_call" | custom-call | tf_op jit(solution)/shard_map/cotangent/pallas_call | solution.py:397
  115.4 5.7 %collective-permute-done.14.refs_13_ = bf16[1,2,128,768]{3,2,1,0:T(8,128)(2,1)S(1)} collective-permute-done((bf16[1,2,128,768]{3,2,1,0:T(8,128)(2,1)S(1)}, bf16[1,2,128,768]{3,2,1,0:T(8,128)(2,1)S(1)}, u32[]{:S(2)}, u32[]{:S(2)}) %collective-permute-start.14) | collective-permute-done | bytes 393248 | tf_op jit(solution)/shard_map/ppermute | solution.py:265
  121.2 2.4 %collective-permute-start.20 = (bf16[512,512]{1,0:T(8,128)(2,1)S(1)}, bf16[512,512]{1,0:T(8,128)(2,1)S(1)}, u32[]{:S(2)}, u32[]{:S(2)}) collective-permute-start(bf16[512,512]{1,0:T(8,128)(2,1)S(1)} %slice.22), channel_id=1, source_target_pairs={{0,6},{2,0},{4,2},{6,4},{1,7},{3,1},{5,3},{7,5},{8,14},{10,8},{12,... | collective-permute-start | bytes 1572872 | tf_op jit(solution)/shard_map/ppermute | solution.py:265
  123.8 3.8 %collective-permute-start.17 = (bf16[528,128]{1,0:T(8,128)(2,1)S(1)}, bf16[528,128]{1,0:T(8,128)(2,1)S(1)}, u32[]{:S(2)}, u32[]{:S(2)}) collective-permute-start(bf16[528,128]{1,0:T(8,128)(2,1)S(1)} %copy-done.35), channel_id=1, source_target_pairs={{0,24},{8,0},{16,8},{24,16},{1,25},{9,1},{17,9},{25,17},{2,26},{10... | collective-permute-start | bytes 405512 | tf_op jit(solution)/shard_map/ppermute | solution.py:265
  128.5 3.5 %collective-permute-done.17.refs_1_.refs_0_ = bf16[528,128]{1,0:T(8,128)(2,1)S(1)} collective-permute-done((bf16[528,128]{1,0:T(8,128)(2,1)S(1)}, bf16[528,128]{1,0:T(8,128)(2,1)S(1)}, u32[]{:S(2)}, u32[]{:S(2)}) %collective-permute-start.17) | collective-permute-done | bytes 135200 | tf_op jit(solution)/shard_map/ppermute | solution.py:265
  132.0 2.4 %collective-permute-done.18.refs_2_.refs_1_ = bf16[528,128]{1,0:T(8,128)(2,1)S(1)} collective-permute-done((bf16[528,128]{1,0:T(8,128)(2,1)S(1)}, bf16[528,128]{1,0:T(8,128)(2,1)S(1)}, u32[]{:S(2)}, u32[]{:S(2)}) %collective-permute-start.18) | collective-permute-done | bytes 135200 | tf_op jit(solution)/shard_map/ppermute | solution.py:265
  134.4 1.0 collective-permute-done.19.refs_3_.refs_2_
  135.4 1.9 collective-permute-done.21.refs_7_
  138.4 5.3 %collective-permute-done.27.refs_8_ = bf16[512,512]{1,0:T(8,128)(2,1)S(1)} collective-permute-done((bf16[512,512]{1,0:T(8,128)(2,1)S(1)}, bf16[512,512]{1,0:T(8,128)(2,1)S(1)}, u32[]{:S(2)}, u32[]{:S(2)}) %collective-permute-start.27) | collective-permute-done | bytes 524320 | tf_op jit(solution)/shard_map/ppermute | solution.py:275
  146.0 1.0 copy-done.12
  147.0 1.3 collective-permute-start.29
  148.3 1.8 row_state.3
  150.2 2.5 %collective-permute-start.22 = (bf16[528,128]{1,0:T(8,128)(2,1)}, bf16[528,128]{1,0:T(8,128)(2,1)S(1)}, u32[]{:S(2)}, u32[]{:S(2)}) collective-permute-start(bf16[528,128]{1,0:T(8,128)(2,1)} %row_state.3), channel_id=1, source_target_pairs={{32,0},{64,32},{96,64},{33,1},{65,33},{97,65},{34,2},{66,34},{98,6... | collective-permute-start | bytes 405512 | tf_op jit(solution)/shard_map/ppermute | solution.py:271
  152.6 1.3 collective-permute-start.23
  154.7 5.9 %grad_query.1 = bf16[1024,512]{1,0:T(8,128)(2,1)} custom-call(f32[1024,512]{1,0:T(8,128)} %get-tuple-element.132.go, bf16[1024,512]{1,0:T(8,128)(2,1)} %k.7, bf16[1024,512]{1,0:T(8,128)(2,1)} %v.7, f32[1024,128]{1,0:T(8,128)} %broadcast_in_dim.10.dcol, f32[1,1024]{1,0:T(1,128)} %bitcast.50, f32[16,128]{1,0:T(8,128)} %broadcast_in_dim.26.table, ...), custom_call_target="tpu_custom_call" | custom-call | tf_op jit(solution)/shard_map/grad_query/pallas_call | solution.py:424
  161.4 13.7 %attended.1 = bf16[1024,768]{1,0:T(8,128)(2,1)} custom-call(s32[20]{0:T(128)} %stack.121.places, bf16[1024,512]{1,0:T(8,128)(2,1)} %get-tuple-element.112.refs_0_, bf16[1024,512]{1,0:T(8,128)(2,1)} %copy-done.10, bf16[1024,512]{1,0:T(8,128)(2,1)} %copy-done.3, bf16[1024,512]{1,0:T(8,128)(2,1)} %copy-done.11, bf16[1024,512]{1,0:T(8,128)(2,1)} %copy-done.4, ...), custom_call_target="tpu_custom_call" | custom-call | tf_op jit(solution)/shard_map/attended/pallas_call | solution.py:447
  175.1 1.4 dynamic-slice_bitcast_fusion
  176.6 1.5 collective-permute-start.30
  178.1 2.5 %collective-permute-start.31 = (bf16[512,384]{1,0:T(8,128)(2,1)S(1)}, bf16[512,384]{1,0:T(8,128)(2,1)S(1)}, u32[]{:S(2)}, u32[]{:S(2)}) collective-permute-start(bf16[512,384]{1,0:T(8,128)(2,1)S(1)} %get-tuple-element.144), channel_id=1, source_target_pairs={{0,16},{8,24},{16,0},{24,8},{1,17},{9,25},{17,1},{25,9},{2,18},{10... | collective-permute-start | bytes 1179656 | tf_op jit(solution)/shard_map/ppermute | solution.py:265
  180.6 2.5 %collective-permute-start.32 = (bf16[512,384]{1,0:T(8,128)(2,1)S(1)}, bf16[512,384]{1,0:T(8,128)(2,1)S(1)}, u32[]{:S(2)}, u32[]{:S(2)}) collective-permute-start(bf16[512,384]{1,0:T(8,128)(2,1)S(1)} %get-tuple-element.143), channel_id=1, source_target_pairs={{0,24},{8,0},{16,8},{24,16},{1,25},{9,1},{17,9},{25,17},{2,26},{10... | collective-permute-start | bytes 1179656 | tf_op jit(solution)/shard_map/ppermute | solution.py:265
  183.2 7.4 %grad_key_value.1 = (bf16[1024,512]{1,0:T(8,128)(2,1)}, bf16[1024,512]{1,0:T(8,128)(2,1)}) custom-call(f32[1024,512]{1,0:T(8,128)} %get-tuple-element.132.go, bf16[1024,512]{1,0:T(8,128)(2,1)} %q.5, bf16[1024,512]{1,0:T(8,128)(2,1)} %k.7, bf16[1024,512]{1,0:T(8,128)(2,1)} %v.7, f32[1024,128]{1,0:T(8,128)} %broadcast_in_dim.10.dcol, f32[1,1024]{1,0:T(1,128)} %bitcast.51, ...), custom_call_target="tpu_custom_call" | custom-call | tf_op jit(solution)/shard_map/grad_key_value/pallas_call | solution.py:467
  190.6 7.2 %collective-permute-done.31.refs_1_ = bf16[512,384]{1,0:T(8,128)(2,1)S(1)} collective-permute-done((bf16[512,384]{1,0:T(8,128)(2,1)S(1)}, bf16[512,384]{1,0:T(8,128)(2,1)S(1)}, u32[]{:S(2)}, u32[]{:S(2)}) %collective-permute-start.31) | collective-permute-done | bytes 393248 | tf_op jit(solution)/shard_map/ppermute | solution.py:265
  198.8 2.3 %last_sum.1 = f32[512,384]{1,0:T(8,128)} custom-call(s32[1]{0:T(128)} %bitcast.30.place, bf16[4,512,384]{2,1,0:T(8,128)(2,1)} %bitcast.42, bf16[512,384]{1,0:T(8,128)(2,1)} %copy-done.25, bf16[512,384]{1,0:T(8,128)(2,1)} %copy-done.26, bf16[512,384]{1,0:T(8,128)(2,1)} %copy-done.27), custom_call_target="tpu_custom_call" | custom-call | tf_op jit(solution)/shard_map/last_sum/pallas_call | solution.py:313
  (125 shorter events, 10.4 us)
Async XLA Ops:
  7.2 72.5 %all-gather.3.cloned.1.call-start = ((), (), s32[]{:S(2)}) async-start(), calls=%async_computation.2 | async-start | bytes 14155776 | tf_op jit(solution)/shard_map/all_gather | solution.py:338
  7.9 167.2 %reduce-scatter.2.cloned.1.call-start = ((), (), s32[]{:S(2)}) async-start(), calls=%async_computation.1 | async-start | bytes 7864320 | tf_op jit(solution)/shard_map/reduce_scatter | solution.py:391
  9.0 20.3 %collective-permute-start.3 = (bf16[128,1536]{1,0:T(8,128)(2,1)S(1)}, bf16[128,1536]{1,0:T(8,128)(2,1)S(1)}, u32[]{:S(2)}, u32[]{:S(2)}) collective-permute-start(bf16[128,1536]{1,0:T(8,128)(2,1)S(1)} %dynamic_slice.19), channel_id=1, source_target_pairs={{0,0},{2,2},{4,4},{6,6},{10,8},{12,10},{14,12},{8,14},{20,16},{22,... | collective-permute-start | bytes 1179656 | tf_op jit(solution)/shard_map/ppermute | solution.py:298
  14.6 11.1 %collective-permute-start = (bf16[528,128]{1,0:T(8,128)(2,1)}, bf16[528,128]{1,0:T(8,128)(2,1)S(1)}, u32[]{:S(2)}, u32[]{:S(2)}) collective-permute-start(bf16[528,128]{1,0:T(8,128)(2,1)} %tail.1.refs_0_), channel_id=1, source_target_pairs={{0,8},{8,16},{16,24},{24,0},{1,9},{9,17},{17,25},{25,1},{2,10},{10... | collective-permute-start | bytes 405512 | tf_op jit(solution)/shard_map/ppermute | solution.py:265
  21.4 7.9 %collective-permute-start.1 = (bf16[528,128]{1,0:T(8,128)(2,1)}, bf16[528,128]{1,0:T(8,128)(2,1)S(1)}, u32[]{:S(2)}, u32[]{:S(2)}) collective-permute-start(bf16[528,128]{1,0:T(8,128)(2,1)} %tail.1.refs_0_), channel_id=1, source_target_pairs={{0,16},{8,24},{16,0},{24,8},{1,17},{9,25},{17,1},{25,9},{2,18},{10... | collective-permute-start | bytes 405512 | tf_op jit(solution)/shard_map/ppermute | solution.py:265
  22.9 6.4 %collective-permute-start.2 = (bf16[528,128]{1,0:T(8,128)(2,1)}, bf16[528,128]{1,0:T(8,128)(2,1)S(1)}, u32[]{:S(2)}, u32[]{:S(2)}) collective-permute-start(bf16[528,128]{1,0:T(8,128)(2,1)} %tail.1.refs_0_), channel_id=1, source_target_pairs={{0,24},{8,0},{16,8},{24,16},{1,25},{9,1},{17,9},{25,17},{2,26},{10... | collective-permute-start | bytes 405512 | tf_op jit(solution)/shard_map/ppermute | solution.py:265
  29.3 1.5 collective-permute-start.6
  30.9 23.9 %copy-start.5 = (bf16[1,2,128,768]{3,2,1,0:T(8,128)(2,1)}, bf16[1,2,128,768]{3,2,1,0:T(8,128)(2,1)S(1)}, u32[]{:S(2)}) copy-start(bf16[1,2,128,768]{3,2,1,0:T(8,128)(2,1)S(1)} %get-tuple-element.127) | copy-start | bytes 1179652
  30.9 11.3 %collective-permute-start.9 = (bf16[2,128,768]{2,1,0:T(8,128)(2,1)S(1)}, bf16[2,128,768]{2,1,0:T(8,128)(2,1)S(1)}, u32[]{:S(2)}, u32[]{:S(2)}) collective-permute-start(bf16[2,128,768]{2,1,0:T(8,128)(2,1)S(1)} %get-tuple-element.149), channel_id=1, source_target_pairs={{0,96},{32,0},{64,32},{96,64},{1,97},{33,1},{65,33},{97,65},{2,98}... | collective-permute-start | bytes 1179656 | tf_op jit(solution)/shard_map/ppermute | solution.py:265
  31.5 20.0 %collective-permute-start.8 = (bf16[2,128,768]{2,1,0:T(8,128)(2,1)S(1)}, bf16[2,128,768]{2,1,0:T(8,128)(2,1)S(1)}, u32[]{:S(2)}, u32[]{:S(2)}) collective-permute-start(bf16[2,128,768]{2,1,0:T(8,128)(2,1)S(1)} %get-tuple-element.149), channel_id=1, source_target_pairs={{0,64},{32,96},{64,0},{96,32},{1,65},{33,97},{65,1},{97,33},{2,66}... | collective-permute-start | bytes 1179656 | tf_op jit(solution)/shard_map/ppermute | solution.py:265
  33.9 19.6 %collective-permute-start.7 = (bf16[2,128,768]{2,1,0:T(8,128)(2,1)S(1)}, bf16[2,128,768]{2,1,0:T(8,128)(2,1)S(1)}, u32[]{:S(2)}, u32[]{:S(2)}) collective-permute-start(bf16[2,128,768]{2,1,0:T(8,128)(2,1)S(1)} %get-tuple-element.149), channel_id=1, source_target_pairs={{0,32},{32,64},{64,96},{96,0},{1,33},{33,65},{65,97},{97,1},{2,34}... | collective-permute-start | bytes 1179656 | tf_op jit(solution)/shard_map/ppermute | solution.py:265
  37.6 18.8 %collective-permute-start.4 = (bf16[528,128]{1,0:T(8,128)(2,1)}, bf16[528,128]{1,0:T(8,128)(2,1)S(1)}, u32[]{:S(2)}, u32[]{:S(2)}) collective-permute-start(bf16[528,128]{1,0:T(8,128)(2,1)} %row_state.2), channel_id=1, source_target_pairs={{0,32},{32,64},{64,96},{1,33},{33,65},{65,97},{2,34},{34,66},{66,9... | collective-permute-start | bytes 405512 | tf_op jit(solution)/shard_map/ppermute | solution.py:271
  39.5 16.9 %collective-permute-start.5 = (bf16[528,128]{1,0:T(8,128)(2,1)}, bf16[528,128]{1,0:T(8,128)(2,1)S(1)}, u32[]{:S(2)}, u32[]{:S(2)}) collective-permute-start(bf16[528,128]{1,0:T(8,128)(2,1)} %row_state.2), channel_id=1, source_target_pairs={{0,64},{32,96},{1,65},{33,97},{2,66},{34,98},{3,67},{35,99},{4,68}... | collective-permute-start | bytes 405512 | tf_op jit(solution)/shard_map/ppermute | solution.py:271
  42.2 12.6 %copy-start.7 = (bf16[2,128,768]{2,1,0:T(8,128)(2,1)}, bf16[2,128,768]{2,1,0:T(8,128)(2,1)S(1)}, u32[]{:S(2)}) copy-start(bf16[2,128,768]{2,1,0:T(8,128)(2,1)S(1)} %collective-permute-done.9) | copy-start | bytes 1179652
  54.8 11.3 %copy-start = (bf16[3,2,128,768]{3,2,1,0:T(8,128)(2,1)}, bf16[3,2,128,768]{3,2,1,0:T(8,128)(2,1)S(1)}, u32[]{:S(2)}) copy-start(bf16[3,2,128,768]{3,2,1,0:T(8,128)(2,1)S(1)} %get-tuple-element.122.refs_10_) | copy-start | bytes 3538948
  56.4 34.6 %collective-permute-start.10 = (bf16[3,2,128,768]{3,2,1,0:T(8,128)(2,1)S(1)}, bf16[3,2,128,768]{3,2,1,0:T(8,128)(2,1)S(1)}, u32[]{:S(2)}, u32[]{:S(2)}) collective-permute-start(bf16[3,2,128,768]{3,2,1,0:T(8,128)(2,1)S(1)} %get-tuple-element.122.refs_10_), channel_id=1, source_target_pairs={{0,24},{8,0},{16,8},{24,16},{1,25},{9,1},{17,9},{25,17},{2,26},{10... | collective-permute-start | bytes 3538952 | tf_op jit(solution)/shard_map/ppermute | solution.py:265
  59.3 31.7 %collective-permute-start.11 = (bf16[3,2,128,768]{3,2,1,0:T(8,128)(2,1)}, bf16[3,2,128,768]{3,2,1,0:T(8,128)(2,1)S(1)}, u32[]{:S(2)}, u32[]{:S(2)}) collective-permute-start(bf16[3,2,128,768]{3,2,1,0:T(8,128)(2,1)} %get-tuple-element.87), channel_id=1, source_target_pairs={{0,8},{8,16},{16,24},{24,0},{1,9},{9,17},{17,25},{25,1},{2,10},{10... | collective-permute-start | bytes 3538952 | tf_op jit(solution)/shard_map/ppermute | solution.py:265
  91.1 30.1 %collective-permute-start.15 = (bf16[1024,512]{1,0:T(8,128)(2,1)}, bf16[1024,512]{1,0:T(8,128)(2,1)S(1)}, u32[]{:S(2)}, u32[]{:S(2)}) collective-permute-start(bf16[1024,512]{1,0:T(8,128)(2,1)} %get-tuple-element.112.refs_0_), channel_id=1, source_target_pairs={{0,6},{2,0},{4,2},{6,4},{1,7},{3,1},{5,3},{7,5},{8,14},{10,8},{12,... | collective-permute-start | bytes 3145736 | tf_op jit(solution)/shard_map/ppermute | solution.py:265
  92.1 29.1 %collective-permute-start.16 = (bf16[1024,512]{1,0:T(8,128)(2,1)}, bf16[1024,512]{1,0:T(8,128)(2,1)S(1)}, u32[]{:S(2)}, u32[]{:S(2)}) collective-permute-start(bf16[1024,512]{1,0:T(8,128)(2,1)} %get-tuple-element.112.refs_0_), channel_id=1, source_target_pairs={{0,2},{2,4},{4,6},{6,0},{1,3},{3,5},{5,7},{7,1},{8,10},{10,12},{12... | collective-permute-start | bytes 3145736 | tf_op jit(solution)/shard_map/ppermute | solution.py:265
  93.2 27.9 %collective-permute-start.12 = (bf16[2,2,128,768]{3,2,1,0:T(8,128)(2,1)S(1)}, bf16[2,2,128,768]{3,2,1,0:T(8,128)(2,1)S(1)}, u32[]{:S(2)}, u32[]{:S(2)}) collective-permute-start(bf16[2,2,128,768]{3,2,1,0:T(8,128)(2,1)S(1)} %slice.20), channel_id=1, source_target_pairs={{0,24},{8,0},{16,8},{24,16},{1,25},{9,1},{17,9},{25,17},{2,26},{10... | collective-permute-start | bytes 2359304 | tf_op jit(solution)/shard_map/ppermute | solution.py:265
  96.1 25.0 %collective-permute-start.13 = (bf16[2,2,128,768]{3,2,1,0:T(8,128)(2,1)S(1)}, bf16[2,2,128,768]{3,2,1,0:T(8,128)(2,1)S(1)}, u32[]{:S(2)}, u32[]{:S(2)}) collective-permute-start(bf16[2,2,128,768]{3,2,1,0:T(8,128)(2,1)S(1)} %slice.21), channel_id=1, source_target_pairs={{0,8},{8,16},{16,24},{24,0},{1,9},{9,17},{17,25},{25,1},{2,10},{10... | collective-permute-start | bytes 2359304 | tf_op jit(solution)/shard_map/ppermute | solution.py:265
  96.2 24.9 %collective-permute-start.14 = (bf16[1,2,128,768]{3,2,1,0:T(8,128)(2,1)S(1)}, bf16[1,2,128,768]{3,2,1,0:T(8,128)(2,1)S(1)}, u32[]{:S(2)}, u32[]{:S(2)}) collective-permute-start(bf16[1,2,128,768]{3,2,1,0:T(8,128)(2,1)S(1)} %bitcast.45), channel_id=1, source_target_pairs={{0,24},{8,0},{16,8},{24,16},{1,25},{9,1},{17,9},{25,17},{2,26},{10... | collective-permute-start | bytes 1179656 | tf_op jit(solution)/shard_map/ppermute | solution.py:265
  115.4 21.9 %copy-start.9 = (bf16[1024,512]{1,0:T(8,128)(2,1)S(1)}, bf16[1024,512]{1,0:T(8,128)(2,1)}, u32[]{:S(2)}) copy-start(bf16[1024,512]{1,0:T(8,128)(2,1)} %get-tuple-element.112.refs_0_) | copy-start | bytes 3145732
  115.4 31.6 %copy-start.6 = (bf16[1,2,128,768]{3,2,1,0:T(8,128)(2,1)S(1)}, bf16[1,2,128,768]{3,2,1,0:T(8,128)(2,1)}, u32[]{:S(2)}) copy-start(bf16[1,2,128,768]{3,2,1,0:T(8,128)(2,1)} %copy-done.5) | copy-start | bytes 1179652
  121.1 14.2 %copy-start.13 = (bf16[2,2,128,768]{3,2,1,0:T(8,128)(2,1)}, bf16[2,2,128,768]{3,2,1,0:T(8,128)(2,1)S(1)}, u32[]{:S(2)}) copy-start(bf16[2,2,128,768]{3,2,1,0:T(8,128)(2,1)S(1)} %collective-permute-done.12.refs_14_) | copy-start | bytes 2359300
  121.1 14.2 %copy-start.14 = (bf16[2,2,128,768]{3,2,1,0:T(8,128)(2,1)}, bf16[2,2,128,768]{3,2,1,0:T(8,128)(2,1)S(1)}, u32[]{:S(2)}) copy-start(bf16[2,2,128,768]{3,2,1,0:T(8,128)(2,1)S(1)} %collective-permute-done.13.refs_15_) | copy-start | bytes 2359300
  121.2 29.0 %copy-start.3 = (bf16[1024,512]{1,0:T(8,128)(2,1)}, bf16[1024,512]{1,0:T(8,128)(2,1)S(1)}, u32[]{:S(2)}) copy-start(bf16[1024,512]{1,0:T(8,128)(2,1)S(1)} %collective-permute-done.15.refs_2_) | copy-start | bytes 3145732
  121.2 23.3 %copy-start.4 = (bf16[1024,512]{1,0:T(8,128)(2,1)}, bf16[1024,512]{1,0:T(8,128)(2,1)S(1)}, u32[]{:S(2)}) copy-start(bf16[1024,512]{1,0:T(8,128)(2,1)S(1)} %collective-permute-done.16.refs_4_) | copy-start | bytes 3145732
  121.2 14.1 %collective-permute-start.20 = (bf16[512,512]{1,0:T(8,128)(2,1)S(1)}, bf16[512,512]{1,0:T(8,128)(2,1)S(1)}, u32[]{:S(2)}, u32[]{:S(2)}) collective-permute-start(bf16[512,512]{1,0:T(8,128)(2,1)S(1)} %slice.22), channel_id=1, source_target_pairs={{0,6},{2,0},{4,2},{6,4},{1,7},{3,1},{5,3},{7,5},{8,14},{10,8},{12,... | collective-permute-start | bytes 1572872 | tf_op jit(solution)/shard_map/ppermute | solution.py:265
  123.7 13.6 %collective-permute-start.21 = (bf16[512,512]{1,0:T(8,128)(2,1)S(1)}, bf16[512,512]{1,0:T(8,128)(2,1)S(1)}, u32[]{:S(2)}, u32[]{:S(2)}) collective-permute-start(bf16[512,512]{1,0:T(8,128)(2,1)S(1)} %slice.23), channel_id=1, source_target_pairs={{0,2},{2,4},{4,6},{6,0},{1,3},{3,5},{5,7},{7,1},{8,10},{10,12},{12... | collective-permute-start | bytes 1572872 | tf_op jit(solution)/shard_map/ppermute | solution.py:265
  123.8 8.2 %collective-permute-start.17 = (bf16[528,128]{1,0:T(8,128)(2,1)S(1)}, bf16[528,128]{1,0:T(8,128)(2,1)S(1)}, u32[]{:S(2)}, u32[]{:S(2)}) collective-permute-start(bf16[528,128]{1,0:T(8,128)(2,1)S(1)} %copy-done.35), channel_id=1, source_target_pairs={{0,24},{8,0},{16,8},{24,16},{1,25},{9,1},{17,9},{25,17},{2,26},{10... | collective-permute-start | bytes 405512 | tf_op jit(solution)/shard_map/ppermute | solution.py:265
  127.5 6.8 %collective-permute-start.18 = (bf16[528,128]{1,0:T(8,128)(2,1)S(1)}, bf16[528,128]{1,0:T(8,128)(2,1)S(1)}, u32[]{:S(2)}, u32[]{:S(2)}) collective-permute-start(bf16[528,128]{1,0:T(8,128)(2,1)S(1)} %copy-done.35), channel_id=1, source_target_pairs={{0,16},{8,24},{16,0},{24,8},{1,17},{9,25},{17,1},{25,9},{2,18},{10... | collective-permute-start | bytes 405512 | tf_op jit(solution)/shard_map/ppermute | solution.py:265
  127.5 7.8 %collective-permute-start.19 = (bf16[528,128]{1,0:T(8,128)(2,1)S(1)}, bf16[528,128]{1,0:T(8,128)(2,1)S(1)}, u32[]{:S(2)}, u32[]{:S(2)}) collective-permute-start(bf16[528,128]{1,0:T(8,128)(2,1)S(1)} %copy-done.35), channel_id=1, source_target_pairs={{0,8},{8,16},{16,24},{24,0},{1,9},{9,17},{17,25},{25,1},{2,10},{10... | collective-permute-start | bytes 405512 | tf_op jit(solution)/shard_map/ppermute | solution.py:265
  132.0 16.3 %copy-start.15 = (bf16[528,128]{1,0:T(8,128)(2,1)}, bf16[528,128]{1,0:T(8,128)(2,1)S(1)}, u32[]{:S(2)}) copy-start(bf16[528,128]{1,0:T(8,128)(2,1)S(1)} %collective-permute-done.17.refs_1_.refs_0_) | copy-start | bytes 405508
  134.4 14.0 %copy-start.16 = (bf16[528,128]{1,0:T(8,128)(2,1)}, bf16[528,128]{1,0:T(8,128)(2,1)S(1)}, u32[]{:S(2)}) copy-start(bf16[528,128]{1,0:T(8,128)(2,1)S(1)} %collective-permute-done.18.refs_2_.refs_1_) | copy-start | bytes 405508
  135.4 12.9 %copy-start.17 = (bf16[528,128]{1,0:T(8,128)(2,1)}, bf16[528,128]{1,0:T(8,128)(2,1)S(1)}, u32[]{:S(2)}) copy-start(bf16[528,128]{1,0:T(8,128)(2,1)S(1)} %collective-permute-done.19.refs_3_.refs_2_) | copy-start | bytes 405508
  135.4 25.2 %copy-start.21 = (bf16[512,512]{1,0:T(8,128)(2,1)}, bf16[512,512]{1,0:T(8,128)(2,1)S(1)}, u32[]{:S(2)}) copy-start(bf16[512,512]{1,0:T(8,128)(2,1)S(1)} %collective-permute-done.20.refs_6_) | copy-start | bytes 1572868
  137.3 7.2 %collective-permute-start.24 = (bf16[1024,512]{1,0:T(8,128)(2,1)S(1)}, bf16[1024,512]{1,0:T(8,128)(2,1)S(1)}, u32[]{:S(2)}, u32[]{:S(2)}) collective-permute-start(bf16[1024,512]{1,0:T(8,128)(2,1)S(1)} %copy-done.9), channel_id=1, source_target_pairs={{0,1},{1,0},{2,3},{3,2},{4,5},{5,4},{6,7},{7,6},{8,9},{9,8},{10,11... | collective-permute-start | bytes 3145736 | tf_op jit(solution)/shard_map/ppermute | solution.py:275
  137.3 7.2 %collective-permute-start.25 = (bf16[1024,512]{1,0:T(8,128)(2,1)S(1)}, bf16[1024,512]{1,0:T(8,128)(2,1)S(1)}, u32[]{:S(2)}, u32[]{:S(2)}) collective-permute-start(bf16[1024,512]{1,0:T(8,128)(2,1)S(1)} %collective-permute-done.15.refs_2_), channel_id=1, source_target_pairs={{0,1},{1,0},{2,3},{3,2},{4,5},{5,4},{6,7},{7,6},{8,9},{9,8},{10,11... | collective-permute-start | bytes 3145736 | tf_op jit(solution)/shard_map/ppermute | solution.py:275
  137.8 6.7 %collective-permute-start.26 = (bf16[1024,512]{1,0:T(8,128)(2,1)S(1)}, bf16[1024,512]{1,0:T(8,128)(2,1)S(1)}, u32[]{:S(2)}, u32[]{:S(2)}) collective-permute-start(bf16[1024,512]{1,0:T(8,128)(2,1)S(1)} %collective-permute-done.16.refs_4_), channel_id=1, source_target_pairs={{0,1},{1,0},{2,3},{3,2},{4,5},{5,4},{6,7},{7,6},{8,9},{9,8},{10,11... | collective-permute-start | bytes 3145736 | tf_op jit(solution)/shard_map/ppermute | solution.py:275
  137.9 5.8 %collective-permute-start.27 = (bf16[512,512]{1,0:T(8,128)(2,1)S(1)}, bf16[512,512]{1,0:T(8,128)(2,1)S(1)}, u32[]{:S(2)}, u32[]{:S(2)}) collective-permute-start(bf16[512,512]{1,0:T(8,128)(2,1)S(1)} %collective-permute-done.20.refs_6_), channel_id=1, source_target_pairs={{0,1},{1,0},{2,3},{3,2},{4,5},{5,4},{6,7},{7,6},{8,9},{9,8},{10,11... | collective-permute-start | bytes 1572872 | tf_op jit(solution)/shard_map/ppermute | solution.py:275
  138.3 6.1 %collective-permute-start.28 = (bf16[512,512]{1,0:T(8,128)(2,1)S(1)}, bf16[512,512]{1,0:T(8,128)(2,1)S(1)}, u32[]{:S(2)}, u32[]{:S(2)}) collective-permute-start(bf16[512,512]{1,0:T(8,128)(2,1)S(1)} %collective-permute-done.21.refs_7_), channel_id=1, source_target_pairs={{0,1},{1,0},{2,3},{3,2},{4,5},{5,4},{6,7},{7,6},{8,9},{9,8},{10,11... | collective-permute-start | bytes 1572872 | tf_op jit(solution)/shard_map/ppermute | solution.py:275
  147.0 13.6 %collective-permute-start.29 = (bf16[1,2,128,768]{3,2,1,0:T(8,128)(2,1)S(1)}, bf16[1,2,128,768]{3,2,1,0:T(8,128)(2,1)S(1)}, u32[]{:S(2)}, u32[]{:S(2)}) collective-permute-start(bf16[1,2,128,768]{3,2,1,0:T(8,128)(2,1)S(1)} %copy-done.6), channel_id=1, source_target_pairs={{0,8},{8,16},{16,24},{24,0},{1,9},{9,17},{17,25},{25,1},{2,10},{10... | collective-permute-start | bytes 1179656 | tf_op jit(solution)/shard_map/ppermute | solution.py:265
  150.2 24.9 %collective-permute-start.22 = (bf16[528,128]{1,0:T(8,128)(2,1)}, bf16[528,128]{1,0:T(8,128)(2,1)S(1)}, u32[]{:S(2)}, u32[]{:S(2)}) collective-permute-start(bf16[528,128]{1,0:T(8,128)(2,1)} %row_state.3), channel_id=1, source_target_pairs={{32,0},{64,32},{96,64},{33,1},{65,33},{97,65},{34,2},{66,34},{98,6... | collective-permute-start | bytes 405512 | tf_op jit(solution)/shard_map/ppermute | solution.py:271
  152.6 22.5 %collective-permute-start.23 = (bf16[528,128]{1,0:T(8,128)(2,1)}, bf16[528,128]{1,0:T(8,128)(2,1)S(1)}, u32[]{:S(2)}, u32[]{:S(2)}) collective-permute-start(bf16[528,128]{1,0:T(8,128)(2,1)} %row_state.3), channel_id=1, source_target_pairs={{64,0},{96,32},{65,1},{97,33},{66,2},{98,34},{67,3},{99,35},{68,4}... | collective-permute-start | bytes 405512 | tf_op jit(solution)/shard_map/ppermute | solution.py:271
  176.6 14.1 %collective-permute-start.30 = (bf16[512,384]{1,0:T(8,128)(2,1)S(1)}, bf16[512,384]{1,0:T(8,128)(2,1)S(1)}, u32[]{:S(2)}, u32[]{:S(2)}) collective-permute-start(bf16[512,384]{1,0:T(8,128)(2,1)S(1)} %get-tuple-element.145), channel_id=1, source_target_pairs={{0,8},{8,16},{16,24},{24,0},{1,9},{9,17},{17,25},{25,1},{2,10},{10... | collective-permute-start | bytes 1179656 | tf_op jit(solution)/shard_map/ppermute | solution.py:265
  178.1 19.7 %collective-permute-start.31 = (bf16[512,384]{1,0:T(8,128)(2,1)S(1)}, bf16[512,384]{1,0:T(8,128)(2,1)S(1)}, u32[]{:S(2)}, u32[]{:S(2)}) collective-permute-start(bf16[512,384]{1,0:T(8,128)(2,1)S(1)} %get-tuple-element.144), channel_id=1, source_target_pairs={{0,16},{8,24},{16,0},{24,8},{1,17},{9,25},{17,1},{25,9},{2,18},{10... | collective-permute-start | bytes 1179656 | tf_op jit(solution)/shard_map/ppermute | solution.py:265
  180.6 17.2 %collective-permute-start.32 = (bf16[512,384]{1,0:T(8,128)(2,1)S(1)}, bf16[512,384]{1,0:T(8,128)(2,1)S(1)}, u32[]{:S(2)}, u32[]{:S(2)}) collective-permute-start(bf16[512,384]{1,0:T(8,128)(2,1)S(1)} %get-tuple-element.143), channel_id=1, source_target_pairs={{0,24},{8,0},{16,8},{24,16},{1,25},{9,1},{17,9},{25,17},{2,26},{10... | collective-permute-start | bytes 1179656 | tf_op jit(solution)/shard_map/ppermute | solution.py:265
  (24 other events, 82.2 us)
Sparse Core Ops, SparseCore 0:
  9.7 69.9 all-gather.2
  91.2 62.9 reduce-scatter.1

commit v9 on v5

--- a/solution.py
+++ b/solution.py
@@ -212,15 +212,12 @@
         carry[c, :] = jnp.where(keep, state, 0.0) + dot(kept, high, TN)
 
 
-def put_columns(part, out):
-    low = part.astype(BF16)
-    half = low.shape[1] // 2
-    out[0, 0] = low[:, :half]
-    out[0, 1] = low[:, half:]
-
-
 def weight_kernel(turned, grad, out):
-    put_columns(dot(turned[...], grad[0], NN), out)
+    for p in range(2):
+        low = dot(turned[...], grad[p], NN).astype(BF16)
+        half = low.shape[1] // 2
+        out[0, 2 * p] = low[:, :half]
+        out[0, 2 * p + 1] = low[:, half:]
 
 
 def sum_kernel(place, own, *refs):
@@ -381,9 +378,9 @@
 
     term = pl.pallas_call(
         weight_kernel,
-        grid=(groups,),
-        in_specs=[whole((width, rows)), pl.BlockSpec((1, rows, share), lambda j: (j, 0, 0))],
-        out_specs=pl.BlockSpec((1, 2, width, share // 2), lambda j: (j // 2, j % 2, 0, 0)),
+        grid=(groups // 2,),
+        in_specs=[whole((width, rows)), pl.BlockSpec((2, rows, share), lambda j: (j, 0, 0))],
+        out_specs=pl.BlockSpec((1, 4, width, share // 2), lambda j: (j, 0, 0, 0)),
         out_shape=jax.ShapeDtypeStruct((4, 4, width, share // 2), BF16),
         compiler_params=params(),
         name="weight_grad",

time: 196 us -> 196 us (level)
  Pallas kernels: 70.9 us -> 68.9 us
  transfers between devices with their start and end apart: 35 -> 35, of which waited for: 19 -> 20; matrix products, arithmetic and copies ran while one was open for 2% -> 2% of each run, Pallas kernels for 35% -> 34%
where the time goes in v9:
time: 196 us; the launch traced here: 195 us
  Pallas kernels  68.9 us (35%)
  waiting for transfers between devices  55.6 us (28%)
  starting transfers between devices  48.4 us (25%)
  between operations  14.6 us (7%)
  local copies, waits for them, and re-layouts  7.31 us (4%)
    ppermute x22, starting transfers between devices, turned_by(): lax.ppermute(value, axis, [(i, (i + step) % size) for i in range(size)])  37.8 us
    ppermute x22, waiting for transfers between devices, turned_by(): lax.ppermute(value, axis, [(i, (i + step) % size) for i in range(size)])  32.4 us
    pallas_call x1, Pallas kernels, body(): pl.pallas_call(cotangent_kernel, grid=(blocks,), in_specs=[pl.BlockSpec((...  15 us
    pallas_call x1, Pallas kernels, body(): pl.pallas_call(attended_kernel, grid_spec=pltpu.PrefetchScalarGridSpec(nu...  13.7 us
    all_gather x1, waiting for transfers between devices, body(): grad_whole = lax.all_gather(grad_out, TENSOR, axis=0)  12.4 us
    pallas_call x1, Pallas kernels, body(): pl.pallas_call(weight_kernel, grid=(groups // 2,), in_specs=[whole((width...  11.4 us
    ppermute x4, starting transfers between devices, moved_by(): return lax.ppermute(value, axis, pairs)  8.7 us
    pallas_call x1, Pallas kernels, body(): pl.pallas_call(key_value_kernel, grid=(blocks,), in_specs=[rows_of(width,...  7.45 us
  transfers between devices with their start and end apart: 35, of which 20 were waited for; matrix products, arithmetic and copies ran while one was open for 2% of the time, Pallas kernels for 34%

profile of v9, /device:TPU:2, one launch (start us, length us, event | category | flops | bytes accessed | tf_op | source)
XLA Modules:
  0.0 195.0 jit_solution(2269517295661516807)
XLA Ops:
  8.0 1.0 dynamic_slice.19
  10.0 1.0 broadcast_in_dim.10.dcol
  11.7 2.8 %tail.1.refs_0_ = bf16[528,128]{1,0:T(8,128)(2,1)} custom-call(bf16[1024,512]{1,0:T(8,128)(2,1)} %k.7, bf16[1024,512]{1,0:T(8,128)(2,1)} %v.7, f32[1024,128]{1,0:T(8,128)} %broadcast_in_dim.10.dcol, f32[16,128]{1,0:T(8,128)} %broadcast_in_dim.24.table), custom_call_target="tpu_custom_call" | custom-call | tf_op jit(solution)/shard_map/tail/pallas_call | solution.py:347
  14.6 6.8 %collective-permute-start = (bf16[528,128]{1,0:T(8,128)(2,1)}, bf16[528,128]{1,0:T(8,128)(2,1)S(1)}, u32[]{:S(2)}, u32[]{:S(2)}) collective-permute-start(bf16[528,128]{1,0:T(8,128)(2,1)} %tail.1.refs_0_), channel_id=1, source_target_pairs={{0,8},{8,16},{16,24},{24,0},{1,9},{9,17},{17,25},{25,1},{2,10},{10... | collective-permute-start | bytes 405512 | tf_op jit(solution)/shard_map/ppermute | solution.py:264
  21.4 1.5 collective-permute-start.1
  22.9 2.6 %collective-permute-start.2 = (bf16[528,128]{1,0:T(8,128)(2,1)}, bf16[528,128]{1,0:T(8,128)(2,1)S(1)}, u32[]{:S(2)}, u32[]{:S(2)}) collective-permute-start(bf16[528,128]{1,0:T(8,128)(2,1)} %tail.1.refs_0_), channel_id=1, source_target_pairs={{0,24},{8,0},{16,8},{24,16},{1,25},{9,1},{17,9},{25,17},{2,26},{10... | collective-permute-start | bytes 405512 | tf_op jit(solution)/shard_map/ppermute | solution.py:264
  25.7 3.6 %collective-permute-done.1.refs_2_.refs_1_ = bf16[528,128]{1,0:T(8,128)(2,1)S(1)} collective-permute-done((bf16[528,128]{1,0:T(8,128)(2,1)}, bf16[528,128]{1,0:T(8,128)(2,1)S(1)}, u32[]{:S(2)}, u32[]{:S(2)}) %collective-permute-start.1) | collective-permute-done | bytes 135200 | tf_op jit(solution)/shard_map/ppermute | solution.py:264
  29.4 1.4 collective-permute-done.6
  30.9 1.6 collective-permute-start.7
  33.0 2.1 %collective-permute-start.8 = (bf16[2,128,768]{2,1,0:T(8,128)(2,1)S(1)}, bf16[2,128,768]{2,1,0:T(8,128)(2,1)S(1)}, u32[]{:S(2)}, u32[]{:S(2)}) collective-permute-start(bf16[2,128,768]{2,1,0:T(8,128)(2,1)S(1)} %get-tuple-element.103), channel_id=1, source_target_pairs={{0,64},{32,96},{64,0},{96,32},{1,65},{33,97},{65,1},{97,33},{2,66}... | collective-permute-start | bytes 1179656 | tf_op jit(solution)/shard_map/ppermute | solution.py:264
  35.1 1.9 row_state.2
  37.0 3.0 %collective-permute-start.4 = (bf16[528,128]{1,0:T(8,128)(2,1)}, bf16[528,128]{1,0:T(8,128)(2,1)S(1)}, u32[]{:S(2)}, u32[]{:S(2)}) collective-permute-start(bf16[528,128]{1,0:T(8,128)(2,1)} %row_state.2), channel_id=1, source_target_pairs={{0,32},{32,64},{64,96},{1,33},{33,65},{65,97},{2,34},{34,66},{66,9... | collective-permute-start | bytes 405512 | tf_op jit(solution)/shard_map/ppermute | solution.py:270
  40.0 1.6 collective-permute-start.5
  41.6 8.2 %collective-permute-done.7 = bf16[2,128,768]{2,1,0:T(8,128)(2,1)S(1)} collective-permute-done((bf16[2,128,768]{2,1,0:T(8,128)(2,1)S(1)}, bf16[2,128,768]{2,1,0:T(8,128)(2,1)S(1)}, u32[]{:S(2)}, u32[]{:S(2)}) %collective-permute-start.7) | collective-permute-done | bytes 393248 | tf_op jit(solution)/shard_map/ppermute | solution.py:264
  50.0 2.5 %collective-permute-done.8 = bf16[2,128,768]{2,1,0:T(8,128)(2,1)S(1)} collective-permute-done((bf16[2,128,768]{2,1,0:T(8,128)(2,1)S(1)}, bf16[2,128,768]{2,1,0:T(8,128)(2,1)S(1)}, u32[]{:S(2)}, u32[]{:S(2)}) %collective-permute-start.8) | collective-permute-done | bytes 393248 | tf_op jit(solution)/shard_map/ppermute | solution.py:264
  52.5 1.8 collective-permute-done.4.refs_3_
  54.3 2.9 %collective-permute-start.10 = (bf16[2,2,128,768]{3,2,1,0:T(8,128)(2,1)S(1)}, bf16[2,2,128,768]{3,2,1,0:T(8,128)(2,1)S(1)}, u32[]{:S(2)}, u32[]{:S(2)}) collective-permute-start(bf16[2,2,128,768]{3,2,1,0:T(8,128)(2,1)S(1)} %pad_maximum_fusion.refs_10_), channel_id=1, source_target_pairs={{0,24},{8,0},{16,8},{24,16},{1,25},{9,1},{17,9},{25,17},{2,26},{10... | collective-permute-start | bytes 2359304 | tf_op jit(solution)/shard_map/ppermute | solution.py:264
  57.2 3.2 %collective-permute-start.12 = (bf16[2,2,128,768]{3,2,1,0:T(8,128)(2,1)S(1)}, bf16[2,2,128,768]{3,2,1,0:T(8,128)(2,1)}, u32[]{:S(2)}, u32[]{:S(2)}) collective-permute-start(bf16[2,2,128,768]{3,2,1,0:T(8,128)(2,1)S(1)} %pad_maximum_fusion.1.refs_11_), channel_id=1, source_target_pairs={{0,24},{8,0},{16,8},{24,16},{1,25},{9,1},{17,9},{25,17},{2,26},{10... | collective-permute-start | bytes 2359304 | tf_op jit(solution)/shard_map/ppermute | solution.py:264
  60.4 6.8 %forward.1 = (f32[1024,512]{1,0:T(8,128)}, bf16[1024,512]{1,0:T(8,128)(2,1)}, bf16[512,1024]{1,0:T(8,128)(2,1)}, bf16[4,512,128]{2,1,0:T(8,128)(2,1)}) custom-call(bf16[1024,512]{1,0:T(8,128)(2,1)} %q.5, bf16[1024,512]{1,0:T(8,128)(2,1)} %k.7, bf16[1024,512]{1,0:T(8,128)(2,1)} %v.7, f32[1024,128]{1,0:T(8,128)} %broadcast_in_dim.10.dcol, f32[1,1024]{1,0:T(1,128)} %bitcast.47, ...), custom_call_target="tpu_custom_call" | custom-call | tf_op jit(solution)/shard_map/forward/pallas_call | solution.py:356
  67.2 12.4 %all-gather.3.cloned.1.call-done = bf16[8192,768]{1,0:T(8,128)(2,1)} async-done(((bf16[1024,768]{1,0:T(8,128)(2,1)}), bf16[8192,768]{1,0:T(8,128)(2,1)}) %all-gather.3.cloned.1.call-update) | async-done | bytes 12582928 | tf_op jit(solution)/shard_map/all_gather | solution.py:337
  79.7 11.4 %weight_grad.1 = bf16[4,4,512,384]{3,2,1,0:T(8,128)(2,1)} custom-call(bf16[512,1024]{1,0:T(8,128)(2,1)} %get-tuple-element.62.turned, bf16[8,1024,768]{2,1,0:T(8,128)(2,1)} %bitcast.39), custom_call_target="tpu_custom_call" | custom-call | tf_op jit(solution)/shard_map/weight_grad/pallas_call | solution.py:379
  91.0 2.1 %collective-permute-done.13.refs_16_ = bf16[2,2,128,768]{3,2,1,0:T(8,128)(2,1)} collective-permute-done((bf16[2,2,128,768]{3,2,1,0:T(8,128)(2,1)S(1)}, bf16[2,2,128,768]{3,2,1,0:T(8,128)(2,1)}, u32[]{:S(2)}, u32[]{:S(2)}) %collective-permute-start.13) | collective-permute-done | bytes 786464 | tf_op jit(solution)/shard_map/ppermute | solution.py:264
  93.2 1.2 copy-done.4
  95.1 1.3 collective-permute-start.17
  96.4 0.9 collective-permute-start.14
  97.3 1.1 collective-permute-start.15
  98.4 15.0 %cotangent.1 = (f32[1024,512]{1,0:T(8,128)}, bf16[528,128]{1,0:T(8,128)(2,1)}) custom-call(bf16[8,1024,768]{2,1,0:T(8,128)(2,1)} %bitcast.40, bf16[512,6144]{1,0:T(8,128)(2,1)} %weight.1, f32[1024,512]{1,0:T(8,128)} %get-tuple-element.60.opened, bf16[1024,512]{1,0:T(8,128)(2,1)} %q.5, f32[1024,128]{1,0:T(8,128)} %broadcast_in_dim.10.dcol, ...), custom_call_target="tpu_custom_call" | custom-call | tf_op jit(solution)/shard_map/cotangent/pallas_call | solution.py:396
  114.3 3.3 %collective-permute-done.15.refs_15_ = bf16[2,2,128,768]{3,2,1,0:T(8,128)(2,1)S(1)} collective-permute-done((bf16[2,2,128,768]{3,2,1,0:T(8,128)(2,1)}, bf16[2,2,128,768]{3,2,1,0:T(8,128)(2,1)S(1)}, u32[]{:S(2)}, u32[]{:S(2)}) %collective-permute-start.15) | collective-permute-done | bytes 786464 | tf_op jit(solution)/shard_map/ppermute | solution.py:264
  117.9 1.9 collective-permute-done.17.refs_4_
  120.6 1.6 collective-permute-start.22
  122.2 2.7 %collective-permute-start.18 = (bf16[528,128]{1,0:T(8,128)(2,1)S(1)}, bf16[528,128]{1,0:T(8,128)(2,1)S(1)}, u32[]{:S(2)}, u32[]{:S(2)}) collective-permute-start(bf16[528,128]{1,0:T(8,128)(2,1)S(1)} %copy-done.22), channel_id=1, source_target_pairs={{0,24},{8,0},{16,8},{24,16},{1,25},{9,1},{17,9},{25,17},{2,26},{10... | collective-permute-start | bytes 405512 | tf_op jit(solution)/shard_map/ppermute | solution.py:264
  126.6 2.8 %collective-permute-done.18.refs_1_.refs_0_ = bf16[528,128]{1,0:T(8,128)(2,1)S(1)} collective-permute-done((bf16[528,128]{1,0:T(8,128)(2,1)S(1)}, bf16[528,128]{1,0:T(8,128)(2,1)S(1)}, u32[]{:S(2)}, u32[]{:S(2)}) %collective-permute-start.18) | collective-permute-done | bytes 135200 | tf_op jit(solution)/shard_map/ppermute | solution.py:264
  129.4 2.3 %collective-permute-done.19.refs_2_.refs_1_ = bf16[528,128]{1,0:T(8,128)(2,1)S(1)} collective-permute-done((bf16[528,128]{1,0:T(8,128)(2,1)S(1)}, bf16[528,128]{1,0:T(8,128)(2,1)S(1)}, u32[]{:S(2)}, u32[]{:S(2)}) %collective-permute-start.19) | collective-permute-done | bytes 135200 | tf_op jit(solution)/shard_map/ppermute | solution.py:264
  131.7 1.3 collective-permute-done.20.refs_3_.refs_2_
  134.7 1.9 row_state.3
  136.5 1.5 collective-permute-done.28.refs_8_
  138.0 2.8 %collective-permute-start.23 = (bf16[528,128]{1,0:T(8,128)(2,1)}, bf16[528,128]{1,0:T(8,128)(2,1)S(1)}, u32[]{:S(2)}, u32[]{:S(2)}) collective-permute-start(bf16[528,128]{1,0:T(8,128)(2,1)} %row_state.3), channel_id=1, source_target_pairs={{32,0},{64,32},{96,64},{33,1},{65,33},{97,65},{34,2},{66,34},{98,6... | collective-permute-start | bytes 405512 | tf_op jit(solution)/shard_map/ppermute | solution.py:270
  140.9 1.3 collective-permute-start.24
  143.1 13.7 %attended.1 = bf16[1024,768]{1,0:T(8,128)(2,1)} custom-call(s32[20]{0:T(128)} %stack.119.places, bf16[1024,512]{1,0:T(8,128)(2,1)} %get-tuple-element.77.refs_0_, bf16[1024,512]{1,0:T(8,128)(2,1)} %collective-permute-done.25.refs_1_, bf16[1024,512]{1,0:T(8,128)(2,1)} %copy-done.2, bf16[1024,512]{1,0:T(8,128)(2,1)} %collective-permute-done.26.refs_3_, ...), custom_call_target="tpu_custom_call" | custom-call | tf_op jit(solution)/shard_map/attended/pallas_call | solution.py:430
  157.4 4.6 %reduce-scatter.2.cloned.1.call-done = bf16[1,4,512,384]{3,2,1,0:T(8,128)(2,1)} async-done(((bf16[4,4,512,384]{3,2,1,0:T(8,128)(2,1)}), bf16[1,4,512,384]{3,2,1,0:T(8,128)(2,1)}) %reduce-scatter.2.cloned.1.call-update) | async-done | bytes 1572880 | tf_op jit(solution)/shard_map/reduce_scatter | solution.py:390
  162.1 1.4 dynamic-slice_bitcast_fusion
  163.4 1.5 collective-permute-start.30
  165.0 2.7 %collective-permute-start.31 = (bf16[512,384]{1,0:T(8,128)(2,1)S(1)}, bf16[512,384]{1,0:T(8,128)(2,1)S(1)}, u32[]{:S(2)}, u32[]{:S(2)}) collective-permute-start(bf16[512,384]{1,0:T(8,128)(2,1)S(1)} %get-tuple-element.100), channel_id=1, source_target_pairs={{0,16},{8,24},{16,0},{24,8},{1,17},{9,25},{17,1},{25,9},{2,18},{10... | collective-permute-start | bytes 1179656 | tf_op jit(solution)/shard_map/ppermute | solution.py:264
  167.7 1.4 collective-permute-start.32
  169.1 5.9 %grad_query.1 = bf16[1024,512]{1,0:T(8,128)(2,1)} custom-call(f32[1024,512]{1,0:T(8,128)} %get-tuple-element.87.go, bf16[1024,512]{1,0:T(8,128)(2,1)} %k.7, bf16[1024,512]{1,0:T(8,128)(2,1)} %v.7, f32[1024,128]{1,0:T(8,128)} %broadcast_in_dim.10.dcol, f32[1,1024]{1,0:T(1,128)} %bitcast.48, f32[16,128]{1,0:T(8,128)} %broadcast_in_dim.24.table, ...), custom_call_target="tpu_custom_call" | custom-call | tf_op jit(solution)/shard_map/grad_query/pallas_call | solution.py:449
  175.0 7.4 %grad_key_value.1 = (bf16[1024,512]{1,0:T(8,128)(2,1)}, bf16[1024,512]{1,0:T(8,128)(2,1)}) custom-call(f32[1024,512]{1,0:T(8,128)} %get-tuple-element.87.go, bf16[1024,512]{1,0:T(8,128)(2,1)} %q.5, bf16[1024,512]{1,0:T(8,128)(2,1)} %k.7, bf16[1024,512]{1,0:T(8,128)(2,1)} %v.7, f32[1024,128]{1,0:T(8,128)} %broadcast_in_dim.10.dcol, f32[1,1024]{1,0:T(1,128)} %bitcast.49, ...), custom_call_target="tpu_custom_call" | custom-call | tf_op jit(solution)/shard_map/grad_key_value/pallas_call | solution.py:462
  182.5 2.5 %collective-permute-done.31.refs_1_ = bf16[512,384]{1,0:T(8,128)(2,1)S(1)} collective-permute-done((bf16[512,384]{1,0:T(8,128)(2,1)S(1)}, bf16[512,384]{1,0:T(8,128)(2,1)S(1)}, u32[]{:S(2)}, u32[]{:S(2)}) %collective-permute-start.31) | collective-permute-done | bytes 393248 | tf_op jit(solution)/shard_map/ppermute | solution.py:264
  185.9 2.3 %last_sum.1 = f32[512,384]{1,0:T(8,128)} custom-call(s32[1]{0:T(128)} %bitcast.30.place, bf16[4,512,384]{2,1,0:T(8,128)(2,1)} %bitcast.42, bf16[512,384]{1,0:T(8,128)(2,1)} %copy-done.14, bf16[512,384]{1,0:T(8,128)(2,1)} %copy-done.15, bf16[512,384]{1,0:T(8,128)(2,1)} %copy-done.16), custom_call_target="tpu_custom_call" | custom-call | tf_op jit(solution)/shard_map/last_sum/pallas_call | solution.py:312
  (98 shorter events, 11.9 us)
Async XLA Ops:
  7.2 72.5 %all-gather.3.cloned.1.call-start = ((), (), s32[]{:S(2)}) async-start(), calls=%async_computation.2 | async-start | bytes 14155776 | tf_op jit(solution)/shard_map/all_gather | solution.py:337
  7.9 154.2 %reduce-scatter.2.cloned.1.call-start = ((), (), s32[]{:S(2)}) async-start(), calls=%async_computation.1 | async-start | bytes 7864320 | tf_op jit(solution)/shard_map/reduce_scatter | solution.py:390
  9.0 20.3 %collective-permute-start.3 = (bf16[128,1536]{1,0:T(8,128)(2,1)S(1)}, bf16[128,1536]{1,0:T(8,128)(2,1)S(1)}, u32[]{:S(2)}, u32[]{:S(2)}) collective-permute-start(bf16[128,1536]{1,0:T(8,128)(2,1)S(1)} %dynamic_slice.19), channel_id=1, source_target_pairs={{0,0},{2,2},{4,4},{6,6},{10,8},{12,10},{14,12},{8,14},{20,16},{22,... | collective-permute-start | bytes 1179656 | tf_op jit(solution)/shard_map/ppermute | solution.py:297
  9.7 21.2 %copy-start.17 = (f32[1024]{0:T(1024)}, f32[1024]{0:T(1024)S(1)}, u32[]{:S(2)}) copy-start(f32[1024]{0:T(1024)S(1)} %convert_element_type.6) | copy-start | bytes 12292
  14.6 11.1 %collective-permute-start = (bf16[528,128]{1,0:T(8,128)(2,1)}, bf16[528,128]{1,0:T(8,128)(2,1)S(1)}, u32[]{:S(2)}, u32[]{:S(2)}) collective-permute-start(bf16[528,128]{1,0:T(8,128)(2,1)} %tail.1.refs_0_), channel_id=1, source_target_pairs={{0,8},{8,16},{16,24},{24,0},{1,9},{9,17},{17,25},{25,1},{2,10},{10... | collective-permute-start | bytes 405512 | tf_op jit(solution)/shard_map/ppermute | solution.py:264
  21.4 7.9 %collective-permute-start.1 = (bf16[528,128]{1,0:T(8,128)(2,1)}, bf16[528,128]{1,0:T(8,128)(2,1)S(1)}, u32[]{:S(2)}, u32[]{:S(2)}) collective-permute-start(bf16[528,128]{1,0:T(8,128)(2,1)} %tail.1.refs_0_), channel_id=1, source_target_pairs={{0,16},{8,24},{16,0},{24,8},{1,17},{9,25},{17,1},{25,9},{2,18},{10... | collective-permute-start | bytes 405512 | tf_op jit(solution)/shard_map/ppermute | solution.py:264
  22.9 6.4 %collective-permute-start.2 = (bf16[528,128]{1,0:T(8,128)(2,1)}, bf16[528,128]{1,0:T(8,128)(2,1)S(1)}, u32[]{:S(2)}, u32[]{:S(2)}) collective-permute-start(bf16[528,128]{1,0:T(8,128)(2,1)} %tail.1.refs_0_), channel_id=1, source_target_pairs={{0,24},{8,0},{16,8},{24,16},{1,25},{9,1},{17,9},{25,17},{2,26},{10... | collective-permute-start | bytes 405512 | tf_op jit(solution)/shard_map/ppermute | solution.py:264
  25.7 9.4 %copy-start.11 = (bf16[528,128]{1,0:T(8,128)(2,1)}, bf16[528,128]{1,0:T(8,128)(2,1)S(1)}, u32[]{:S(2)}) copy-start(bf16[528,128]{1,0:T(8,128)(2,1)S(1)} %collective-permute-done.refs_1_.refs_0_) | copy-start | bytes 405508
  29.3 1.5 collective-permute-start.6
  30.9 18.9 %collective-permute-start.7 = (bf16[2,128,768]{2,1,0:T(8,128)(2,1)S(1)}, bf16[2,128,768]{2,1,0:T(8,128)(2,1)S(1)}, u32[]{:S(2)}, u32[]{:S(2)}) collective-permute-start(bf16[2,128,768]{2,1,0:T(8,128)(2,1)S(1)} %get-tuple-element.103), channel_id=1, source_target_pairs={{0,32},{32,64},{64,96},{96,0},{1,33},{33,65},{65,97},{97,1},{2,34}... | collective-permute-start | bytes 1179656 | tf_op jit(solution)/shard_map/ppermute | solution.py:264
  32.5 17.5 %collective-permute-start.9 = (bf16[2,128,768]{2,1,0:T(8,128)(2,1)S(1)}, bf16[2,128,768]{2,1,0:T(8,128)(2,1)S(1)}, u32[]{:S(2)}, u32[]{:S(2)}) collective-permute-start(bf16[2,128,768]{2,1,0:T(8,128)(2,1)S(1)} %get-tuple-element.103), channel_id=1, source_target_pairs={{0,96},{32,0},{64,32},{96,64},{1,97},{33,1},{65,33},{97,65},{2,98}... | collective-permute-start | bytes 1179656 | tf_op jit(solution)/shard_map/ppermute | solution.py:264
  33.0 19.4 %collective-permute-start.8 = (bf16[2,128,768]{2,1,0:T(8,128)(2,1)S(1)}, bf16[2,128,768]{2,1,0:T(8,128)(2,1)S(1)}, u32[]{:S(2)}, u32[]{:S(2)}) collective-permute-start(bf16[2,128,768]{2,1,0:T(8,128)(2,1)S(1)} %get-tuple-element.103), channel_id=1, source_target_pairs={{0,64},{32,96},{64,0},{96,32},{1,65},{33,97},{65,1},{97,33},{2,66}... | collective-permute-start | bytes 1179656 | tf_op jit(solution)/shard_map/ppermute | solution.py:264
  37.0 17.3 %collective-permute-start.4 = (bf16[528,128]{1,0:T(8,128)(2,1)}, bf16[528,128]{1,0:T(8,128)(2,1)S(1)}, u32[]{:S(2)}, u32[]{:S(2)}) collective-permute-start(bf16[528,128]{1,0:T(8,128)(2,1)} %row_state.2), channel_id=1, source_target_pairs={{0,32},{32,64},{64,96},{1,33},{33,65},{65,97},{2,34},{34,66},{66,9... | collective-permute-start | bytes 405512 | tf_op jit(solution)/shard_map/ppermute | solution.py:270
  40.0 14.3 %collective-permute-start.5 = (bf16[528,128]{1,0:T(8,128)(2,1)}, bf16[528,128]{1,0:T(8,128)(2,1)S(1)}, u32[]{:S(2)}, u32[]{:S(2)}) collective-permute-start(bf16[528,128]{1,0:T(8,128)(2,1)} %row_state.2), channel_id=1, source_target_pairs={{0,64},{32,96},{1,65},{33,97},{2,66},{34,98},{3,67},{35,99},{4,68}... | collective-permute-start | bytes 405512 | tf_op jit(solution)/shard_map/ppermute | solution.py:270
  49.9 17.3 %copy-start = (bf16[2,2,128,768]{3,2,1,0:T(8,128)(2,1)}, bf16[2,2,128,768]{3,2,1,0:T(8,128)(2,1)S(1)}, u32[]{:S(2)}) copy-start(bf16[2,2,128,768]{3,2,1,0:T(8,128)(2,1)S(1)} %pad_maximum_fusion.refs_10_) | copy-start | bytes 2359300
  52.5 14.7 %copy-start.1 = (bf16[2,2,128,768]{3,2,1,0:T(8,128)(2,1)}, bf16[2,2,128,768]{3,2,1,0:T(8,128)(2,1)S(1)}, u32[]{:S(2)}) copy-start(bf16[2,2,128,768]{3,2,1,0:T(8,128)(2,1)S(1)} %pad_maximum_fusion.1.refs_11_) | copy-start | bytes 2359300
  54.3 6.1 %copy-start.20 = (bf16[528,128]{1,0:T(8,128)(2,1)}, bf16[528,128]{1,0:T(8,128)(2,1)S(1)}, u32[]{:S(2)}) copy-start(bf16[528,128]{1,0:T(8,128)(2,1)S(1)} %collective-permute-done.4.refs_3_) | copy-start | bytes 405508
  54.3 6.1 %copy-start.21 = (bf16[528,128]{1,0:T(8,128)(2,1)}, bf16[528,128]{1,0:T(8,128)(2,1)S(1)}, u32[]{:S(2)}) copy-start(bf16[528,128]{1,0:T(8,128)(2,1)S(1)} %collective-permute-done.5.refs_4_) | copy-start | bytes 405508
  54.3 36.7 %collective-permute-start.10 = (bf16[2,2,128,768]{3,2,1,0:T(8,128)(2,1)S(1)}, bf16[2,2,128,768]{3,2,1,0:T(8,128)(2,1)S(1)}, u32[]{:S(2)}, u32[]{:S(2)}) collective-permute-start(bf16[2,2,128,768]{3,2,1,0:T(8,128)(2,1)S(1)} %pad_maximum_fusion.refs_10_), channel_id=1, source_target_pairs={{0,24},{8,0},{16,8},{24,16},{1,25},{9,1},{17,9},{25,17},{2,26},{10... | collective-permute-start | bytes 2359304 | tf_op jit(solution)/shard_map/ppermute | solution.py:264
  57.2 33.8 %collective-permute-start.11 = (bf16[2,2,128,768]{3,2,1,0:T(8,128)(2,1)S(1)}, bf16[2,2,128,768]{3,2,1,0:T(8,128)(2,1)}, u32[]{:S(2)}, u32[]{:S(2)}) collective-permute-start(bf16[2,2,128,768]{3,2,1,0:T(8,128)(2,1)S(1)} %pad_maximum_fusion.1.refs_11_), channel_id=1, source_target_pairs={{0,8},{8,16},{16,24},{24,0},{1,9},{9,17},{17,25},{25,1},{2,10},{10... | collective-permute-start | bytes 2359304 | tf_op jit(solution)/shard_map/ppermute | solution.py:264
  57.2 33.8 %collective-permute-start.12 = (bf16[2,2,128,768]{3,2,1,0:T(8,128)(2,1)S(1)}, bf16[2,2,128,768]{3,2,1,0:T(8,128)(2,1)}, u32[]{:S(2)}, u32[]{:S(2)}) collective-permute-start(bf16[2,2,128,768]{3,2,1,0:T(8,128)(2,1)S(1)} %pad_maximum_fusion.1.refs_11_), channel_id=1, source_target_pairs={{0,24},{8,0},{16,8},{24,16},{1,25},{9,1},{17,9},{25,17},{2,26},{10... | collective-permute-start | bytes 2359304 | tf_op jit(solution)/shard_map/ppermute | solution.py:264
  60.4 32.7 %collective-permute-start.13 = (bf16[2,2,128,768]{3,2,1,0:T(8,128)(2,1)S(1)}, bf16[2,2,128,768]{3,2,1,0:T(8,128)(2,1)}, u32[]{:S(2)}, u32[]{:S(2)}) collective-permute-start(bf16[2,2,128,768]{3,2,1,0:T(8,128)(2,1)S(1)} %pad_maximum_fusion.refs_10_), channel_id=1, source_target_pairs={{0,8},{8,16},{16,24},{24,0},{1,9},{9,17},{17,25},{25,1},{2,10},{10... | collective-permute-start | bytes 2359304 | tf_op jit(solution)/shard_map/ppermute | solution.py:264
  94.4 23.5 %collective-permute-start.16 = (bf16[1024,512]{1,0:T(8,128)(2,1)S(1)}, bf16[1024,512]{1,0:T(8,128)(2,1)S(1)}, u32[]{:S(2)}, u32[]{:S(2)}) collective-permute-start(bf16[1024,512]{1,0:T(8,128)(2,1)S(1)} %copy-done.4), channel_id=1, source_target_pairs={{0,6},{2,0},{4,2},{6,4},{1,7},{3,1},{5,3},{7,5},{8,14},{10,8},{12,... | collective-permute-start | bytes 3145736 | tf_op jit(solution)/shard_map/ppermute | solution.py:264
  95.1 24.6 %collective-permute-start.17 = (bf16[1024,512]{1,0:T(8,128)(2,1)S(1)}, bf16[1024,512]{1,0:T(8,128)(2,1)S(1)}, u32[]{:S(2)}, u32[]{:S(2)}) collective-permute-start(bf16[1024,512]{1,0:T(8,128)(2,1)S(1)} %copy-done.4), channel_id=1, source_target_pairs={{0,2},{2,4},{4,6},{6,0},{1,3},{3,5},{5,7},{7,1},{8,10},{10,12},{12... | collective-permute-start | bytes 3145736 | tf_op jit(solution)/shard_map/ppermute | solution.py:264
  96.4 17.9 %collective-permute-start.14 = (bf16[2,2,128,768]{3,2,1,0:T(8,128)(2,1)}, bf16[2,2,128,768]{3,2,1,0:T(8,128)(2,1)S(1)}, u32[]{:S(2)}, u32[]{:S(2)}) collective-permute-start(bf16[2,2,128,768]{3,2,1,0:T(8,128)(2,1)} %copy-done.5), channel_id=1, source_target_pairs={{0,24},{8,0},{16,8},{24,16},{1,25},{9,1},{17,9},{25,17},{2,26},{10... | collective-permute-start | bytes 2359304 | tf_op jit(solution)/shard_map/ppermute | solution.py:264
  97.3 20.3 %collective-permute-start.15 = (bf16[2,2,128,768]{3,2,1,0:T(8,128)(2,1)}, bf16[2,2,128,768]{3,2,1,0:T(8,128)(2,1)S(1)}, u32[]{:S(2)}, u32[]{:S(2)}) collective-permute-start(bf16[2,2,128,768]{3,2,1,0:T(8,128)(2,1)} %collective-permute-done.11.refs_17_), channel_id=1, source_target_pairs={{0,8},{8,16},{16,24},{24,0},{1,9},{9,17},{17,25},{25,1},{2,10},{10... | collective-permute-start | bytes 2359304 | tf_op jit(solution)/shard_map/ppermute | solution.py:264
  113.4 8.8 %copy-start.22 = (bf16[528,128]{1,0:T(8,128)(2,1)S(1)}, bf16[528,128]{1,0:T(8,128)(2,1)}, u32[]{:S(2)}) copy-start(bf16[528,128]{1,0:T(8,128)(2,1)} %get-tuple-element.69.refs_0_) | copy-start | bytes 405508
  114.3 19.2 %copy-start.6 = (bf16[2,2,128,768]{3,2,1,0:T(8,128)(2,1)}, bf16[2,2,128,768]{3,2,1,0:T(8,128)(2,1)S(1)}, u32[]{:S(2)}) copy-start(bf16[2,2,128,768]{3,2,1,0:T(8,128)(2,1)S(1)} %collective-permute-done.14.refs_14_) | copy-start | bytes 2359300
  117.6 16.4 %copy-start.7 = (bf16[2,2,128,768]{3,2,1,0:T(8,128)(2,1)}, bf16[2,2,128,768]{3,2,1,0:T(8,128)(2,1)S(1)}, u32[]{:S(2)}) copy-start(bf16[2,2,128,768]{3,2,1,0:T(8,128)(2,1)S(1)} %collective-permute-done.15.refs_15_) | copy-start | bytes 2359300
  117.9 25.2 %copy-start.2 = (bf16[1024,512]{1,0:T(8,128)(2,1)}, bf16[1024,512]{1,0:T(8,128)(2,1)S(1)}, u32[]{:S(2)}) copy-start(bf16[1024,512]{1,0:T(8,128)(2,1)S(1)} %collective-permute-done.16.refs_2_) | copy-start | bytes 3145732
  119.7 23.3 %copy-start.3 = (bf16[1024,512]{1,0:T(8,128)(2,1)}, bf16[1024,512]{1,0:T(8,128)(2,1)S(1)}, u32[]{:S(2)}) copy-start(bf16[1024,512]{1,0:T(8,128)(2,1)S(1)} %collective-permute-done.17.refs_4_) | copy-start | bytes 3145732
  119.8 13.3 %collective-permute-start.21 = (bf16[512,512]{1,0:T(8,128)(2,1)S(1)}, bf16[512,512]{1,0:T(8,128)(2,1)}, u32[]{:S(2)}, u32[]{:S(2)}) collective-permute-start(bf16[512,512]{1,0:T(8,128)(2,1)S(1)} %slice.14), channel_id=1, source_target_pairs={{0,6},{2,0},{4,2},{6,4},{1,7},{3,1},{5,3},{7,5},{8,14},{10,8},{12,... | collective-permute-start | bytes 1572872 | tf_op jit(solution)/shard_map/ppermute | solution.py:264
  120.6 12.9 %collective-permute-start.22 = (bf16[512,512]{1,0:T(8,128)(2,1)S(1)}, bf16[512,512]{1,0:T(8,128)(2,1)}, u32[]{:S(2)}, u32[]{:S(2)}) collective-permute-start(bf16[512,512]{1,0:T(8,128)(2,1)S(1)} %slice.15), channel_id=1, source_target_pairs={{0,2},{2,4},{4,6},{6,0},{1,3},{3,5},{5,7},{7,1},{8,10},{10,12},{12... | collective-permute-start | bytes 1572872 | tf_op jit(solution)/shard_map/ppermute | solution.py:264
  122.2 7.3 %collective-permute-start.18 = (bf16[528,128]{1,0:T(8,128)(2,1)S(1)}, bf16[528,128]{1,0:T(8,128)(2,1)S(1)}, u32[]{:S(2)}, u32[]{:S(2)}) collective-permute-start(bf16[528,128]{1,0:T(8,128)(2,1)S(1)} %copy-done.22), channel_id=1, source_target_pairs={{0,24},{8,0},{16,8},{24,16},{1,25},{9,1},{17,9},{25,17},{2,26},{10... | collective-permute-start | bytes 405512 | tf_op jit(solution)/shard_map/ppermute | solution.py:264
  124.9 6.8 %collective-permute-start.19 = (bf16[528,128]{1,0:T(8,128)(2,1)S(1)}, bf16[528,128]{1,0:T(8,128)(2,1)S(1)}, u32[]{:S(2)}, u32[]{:S(2)}) collective-permute-start(bf16[528,128]{1,0:T(8,128)(2,1)S(1)} %copy-done.22), channel_id=1, source_target_pairs={{0,16},{8,24},{16,0},{24,8},{1,17},{9,25},{17,1},{25,9},{2,18},{10... | collective-permute-start | bytes 405512 | tf_op jit(solution)/shard_map/ppermute | solution.py:264
  125.7 7.4 %collective-permute-start.20 = (bf16[528,128]{1,0:T(8,128)(2,1)S(1)}, bf16[528,128]{1,0:T(8,128)(2,1)S(1)}, u32[]{:S(2)}, u32[]{:S(2)}) collective-permute-start(bf16[528,128]{1,0:T(8,128)(2,1)S(1)} %copy-done.22), channel_id=1, source_target_pairs={{0,8},{8,16},{16,24},{24,0},{1,9},{9,17},{17,25},{25,1},{2,10},{10... | collective-permute-start | bytes 405512 | tf_op jit(solution)/shard_map/ppermute | solution.py:264
  133.5 9.5 %collective-permute-start.25 = (bf16[1024,512]{1,0:T(8,128)(2,1)S(1)}, bf16[1024,512]{1,0:T(8,128)(2,1)}, u32[]{:S(2)}, u32[]{:S(2)}) collective-permute-start(bf16[1024,512]{1,0:T(8,128)(2,1)S(1)} %copy-done.4), channel_id=1, source_target_pairs={{0,1},{1,0},{2,3},{3,2},{4,5},{5,4},{6,7},{7,6},{8,9},{9,8},{10,11... | collective-permute-start | bytes 3145736 | tf_op jit(solution)/shard_map/ppermute | solution.py:274
  133.5 9.5 %collective-permute-start.26 = (bf16[1024,512]{1,0:T(8,128)(2,1)S(1)}, bf16[1024,512]{1,0:T(8,128)(2,1)}, u32[]{:S(2)}, u32[]{:S(2)}) collective-permute-start(bf16[1024,512]{1,0:T(8,128)(2,1)S(1)} %collective-permute-done.16.refs_2_), channel_id=1, source_target_pairs={{0,1},{1,0},{2,3},{3,2},{4,5},{5,4},{6,7},{7,6},{8,9},{9,8},{10,11... | collective-permute-start | bytes 3145736 | tf_op jit(solution)/shard_map/ppermute | solution.py:274
  134.0 9.0 %collective-permute-start.27 = (bf16[1024,512]{1,0:T(8,128)(2,1)S(1)}, bf16[1024,512]{1,0:T(8,128)(2,1)}, u32[]{:S(2)}, u32[]{:S(2)}) collective-permute-start(bf16[1024,512]{1,0:T(8,128)(2,1)S(1)} %collective-permute-done.17.refs_4_), channel_id=1, source_target_pairs={{0,1},{1,0},{2,3},{3,2},{4,5},{5,4},{6,7},{7,6},{8,9},{9,8},{10,11... | collective-permute-start | bytes 3145736 | tf_op jit(solution)/shard_map/ppermute | solution.py:274
  134.1 3.9 %collective-permute-start.28 = (bf16[512,512]{1,0:T(8,128)(2,1)}, bf16[512,512]{1,0:T(8,128)(2,1)}, u32[]{:S(2)}, u32[]{:S(2)}) collective-permute-start(bf16[512,512]{1,0:T(8,128)(2,1)} %collective-permute-done.21.refs_6_), channel_id=1, source_target_pairs={{0,1},{1,0},{2,3},{3,2},{4,5},{5,4},{6,7},{7,6},{8,9},{9,8},{10,11... | collective-permute-start | bytes 1572872 | tf_op jit(solution)/shard_map/ppermute | solution.py:274
  134.6 6.3 %collective-permute-start.29 = (bf16[512,512]{1,0:T(8,128)(2,1)}, bf16[512,512]{1,0:T(8,128)(2,1)}, u32[]{:S(2)}, u32[]{:S(2)}) collective-permute-start(bf16[512,512]{1,0:T(8,128)(2,1)} %collective-permute-done.22.refs_7_), channel_id=1, source_target_pairs={{0,1},{1,0},{2,3},{3,2},{4,5},{5,4},{6,7},{7,6},{8,9},{9,8},{10,11... | collective-permute-start | bytes 1572872 | tf_op jit(solution)/shard_map/ppermute | solution.py:274
  138.0 18.7 %collective-permute-start.23 = (bf16[528,128]{1,0:T(8,128)(2,1)}, bf16[528,128]{1,0:T(8,128)(2,1)S(1)}, u32[]{:S(2)}, u32[]{:S(2)}) collective-permute-start(bf16[528,128]{1,0:T(8,128)(2,1)} %row_state.3), channel_id=1, source_target_pairs={{32,0},{64,32},{96,64},{33,1},{65,33},{97,65},{34,2},{66,34},{98,6... | collective-permute-start | bytes 405512 | tf_op jit(solution)/shard_map/ppermute | solution.py:270
  140.9 16.6 %collective-permute-start.24 = (bf16[528,128]{1,0:T(8,128)(2,1)}, bf16[528,128]{1,0:T(8,128)(2,1)S(1)}, u32[]{:S(2)}, u32[]{:S(2)}) collective-permute-start(bf16[528,128]{1,0:T(8,128)(2,1)} %row_state.3), channel_id=1, source_target_pairs={{64,0},{96,32},{65,1},{97,33},{66,2},{98,34},{67,3},{99,35},{68,4}... | collective-permute-start | bytes 405512 | tf_op jit(solution)/shard_map/ppermute | solution.py:270
  156.8 18.2 %copy-start.18 = (bf16[528,128]{1,0:T(8,128)(2,1)}, bf16[528,128]{1,0:T(8,128)(2,1)S(1)}, u32[]{:S(2)}) copy-start(bf16[528,128]{1,0:T(8,128)(2,1)S(1)} %collective-permute-done.23.refs_3_) | copy-start | bytes 405508
  157.4 17.6 %copy-start.19 = (bf16[528,128]{1,0:T(8,128)(2,1)}, bf16[528,128]{1,0:T(8,128)(2,1)S(1)}, u32[]{:S(2)}) copy-start(bf16[528,128]{1,0:T(8,128)(2,1)S(1)} %collective-permute-done.24.refs_4_) | copy-start | bytes 405508
  163.4 19.0 %collective-permute-start.30 = (bf16[512,384]{1,0:T(8,128)(2,1)S(1)}, bf16[512,384]{1,0:T(8,128)(2,1)S(1)}, u32[]{:S(2)}, u32[]{:S(2)}) collective-permute-start(bf16[512,384]{1,0:T(8,128)(2,1)S(1)} %get-tuple-element.101), channel_id=1, source_target_pairs={{0,8},{8,16},{16,24},{24,0},{1,9},{9,17},{17,25},{25,1},{2,10},{10... | collective-permute-start | bytes 1179656 | tf_op jit(solution)/shard_map/ppermute | solution.py:264
  165.0 20.0 %collective-permute-start.31 = (bf16[512,384]{1,0:T(8,128)(2,1)S(1)}, bf16[512,384]{1,0:T(8,128)(2,1)S(1)}, u32[]{:S(2)}, u32[]{:S(2)}) collective-permute-start(bf16[512,384]{1,0:T(8,128)(2,1)S(1)} %get-tuple-element.100), channel_id=1, source_target_pairs={{0,16},{8,24},{16,0},{24,8},{1,17},{9,25},{17,1},{25,9},{2,18},{10... | collective-permute-start | bytes 1179656 | tf_op jit(solution)/shard_map/ppermute | solution.py:264
  167.7 17.3 %collective-permute-start.32 = (bf16[512,384]{1,0:T(8,128)(2,1)S(1)}, bf16[512,384]{1,0:T(8,128)(2,1)S(1)}, u32[]{:S(2)}, u32[]{:S(2)}) collective-permute-start(bf16[512,384]{1,0:T(8,128)(2,1)S(1)} %get-tuple-element.99), channel_id=1, source_target_pairs={{0,24},{8,0},{16,8},{24,16},{1,25},{9,1},{17,9},{25,17},{2,26},{10... | collective-permute-start | bytes 1179656 | tf_op jit(solution)/shard_map/ppermute | solution.py:264
  (11 other events, 31.5 us)
Sparse Core Ops, SparseCore 0:
  9.7 69.9 all-gather.2
  93.3 68.7 reduce-scatter.1
